TPU v7x, 256 devices: a whole 4x4x8 slice. The times are simulated.
256 devices in a mesh: grp: 4 (over z_lo), row: 8 (over z_hi, y), col: 8 (over x, core).
Axes of the slice: x: 4, y: 4, z: 8 (z_hi: 2, z_lo: 4; z = z_hi * 4 + z_lo), core: 2. Of those that a mesh axis runs over, the one named last changes fastest.
Arguments:
- amplitudes: bfloat16 [1024, 16384], P(('grp', 'row'), 'col'), may hold values from -6 to 6
- ladder_ints: bfloat16 [16384, 16384], P('col', ('grp', 'row')), may hold values from -0.0625 to 0.0625
- tile_live: int32 [128, 128], P('col', ('grp', 'row')), may hold values 0 or 1
- cycle_direct: bfloat16 [4096, 4096], P('col', ('grp', 'row')), may hold values from -0.0625 to 0.0625
- cycle_exchange: bfloat16 [4096, 4096], P('col', ('grp', 'row')), may hold values from -0.0625 to 0.0625
- eps_occ: float32 [32], replicated, may hold values from -2 to -0.5
- eps_vir: float32 [128], replicated, may hold values from 0.5 to 3
Outputs:
- update: bfloat16 [1024, 16384], P('col', ('grp', 'row'))
All inputs are finite; a program needn't handle non-finite values. No bound on the sum of `tile_live` on one device may be relied on, other than what follows from the above.
Results may differ from a plain program's by a relative error of at most 0.001.
Values may be sent and summed in bfloat16 or wider, within the bound.
No kernel may reach another device: no remote copies, remote signals or barrier semaphores. Data moves between devices by JAX's collectives and lax.ppermute only.
A program may use at most 64 MiB of HBM per device.

v0:
```python
import jax
import jax.numpy as jnp
from jax import lax
from jax.sharding import PartitionSpec as P


def local(amplitudes, ladder_ints, tile_live, cycle_direct, cycle_exchange, eps_occ, eps_vir):
    groups = lax.axis_size(("grp", "row"))
    columns = lax.axis_size("col")
    occ = eps_occ.shape[0]
    vir = eps_vir.shape[0]
    per_dev = occ // groups
    tile_edge = ladder_ints.shape[0] // tile_live.shape[0]
    expanded = jnp.repeat(jnp.repeat(tile_live, tile_edge, axis=0), tile_edge, axis=1).astype(
        jnp.bfloat16
    )
    masked = ladder_ints * expanded
    ladder = jnp.dot(
        lax.all_gather(amplitudes, ("grp", "row"), axis=0, tiled=True),
        masked,
        preferred_element_type=jnp.float32,
    )
    ladder = lax.psum_scatter(ladder, "col", scatter_dimension=0, tiled=True)
    whole = lax.all_gather(amplitudes, "col", axis=1, tiled=True)
    amp_four = whole.reshape(per_dev, occ, vir, vir)
    u_one = amp_four.transpose(0, 2, 1, 3).reshape(per_dev * vir, occ * vir)
    u_two = amp_four.transpose(0, 3, 1, 2).reshape(per_dev * vir, occ * vir)
    partial_value = jnp.dot(cycle_direct, u_one, preferred_element_type=jnp.float32)
    partial_value = partial_value + jnp.dot(
        cycle_exchange, u_two, preferred_element_type=jnp.float32
    )
    cycle = lax.psum_scatter(partial_value, ("grp", "row"), scatter_dimension=1, tiled=True)
    i_count = occ // columns
    a_count = vir // groups
    arranged = cycle.reshape(i_count, vir, per_dev, vir)
    arranged = lax.all_to_all(arranged, ("grp", "row"), split_axis=1, concat_axis=2, tiled=True)
    cycle_pairs = arranged.transpose(0, 2, 1, 3).reshape(i_count * occ, a_count * vir)
    occ_local = lax.dynamic_slice_in_dim(eps_occ, lax.axis_index("col") * i_count, i_count)
    vir_local = lax.dynamic_slice_in_dim(eps_vir, lax.axis_index(("grp", "row")) * a_count, a_count)
    denom = (
        vir_local[None, None, :, None]
        + eps_vir[None, None, None, :]
        - occ_local[:, None, None, None]
        - eps_occ[None, :, None, None]
    ).reshape(i_count * occ, a_count * vir)
    return ((ladder + cycle_pairs) / denom).astype(jnp.bfloat16)


def solution(mesh):
    placed = (
        P(("grp", "row"), "col"),
        P("col", ("grp", "row")),
        P("col", ("grp", "row")),
        P("col", ("grp", "row")),
        P("col", ("grp", "row")),
        P(),
        P(),
    )
    return jax.shard_map(
        local, mesh=mesh, in_specs=placed, out_specs=P("col", ("grp", "row")), check_vma=False
    )
```

profile of v0, /device:TPU:1, one launch (start us, length us, event | category | flops | bytes accessed | tf_op | source)
XLA Modules:
  0.0 578.3 jit_solution(7033893818952339657)
XLA Ops:
  6.5 0.7 all-gather.5.cloned.1.call-update
  7.3 0.0 all-gather.3.cloned.1.call-start
  7.3 0.7 all-gather.3.cloned.1.call-update
  8.0 0.0 reduce-scatter.5.cloned.1.call-start
  8.1 31.3 %all-gather.5.cloned.1.call-done = bf16[32,16384]{1,0:T(8,128)(2,1)} async-done(((bf16[32,2048]{1,0:T(8,128)(2,1)}), bf16[32,16384]{1,0:T(8,128)(2,1)}) %all-gather.5.cloned.1.call-update) | async-done | bytes 1048592 | tf_op jit(solution)/shard_map/all_gather | solution.py:24
  39.3 1.5 copy.27
  40.8 0.1 bitcast_bitcast_fusion
  40.9 0.7 copy.20
  41.6 1.3 fusion.3
  42.9 4.5 convolution_add_fusion
  47.4 0.0 reduce-scatter.5.cloned.1.call-update
  47.4 0.0 reduce-scatter.3.cloned.1.call-start
  47.5 0.6 copy-done.2
  48.1 0.1 copy.19
  48.2 160.6 %all-gather.3.cloned.1.call-done = bf16[1024,2048]{1,0:T(8,128)(2,1)} async-done(((bf16[32,2048]{1,0:T(8,128)(2,1)}), bf16[1024,2048]{1,0:T(8,128)(2,1)}) %all-gather.3.cloned.1.call-update) | async-done | bytes 4194320 | tf_op jit(solution)/shard_map/all_gather | solution.py:19
  208.8 0.1 broadcast_in_dim.4
  208.9 5.8 broadcast_in_dim.5
  214.7 6.0 %fusion.2 = f32[1024,512]{0,1:T(8,128)} fusion(bf16[1024,2048]{1,0:T(8,128)(2,1)} %all-gather.3.cloned.1.call-done, bf16[2048,512]{1,0:T(8,128)(2,1)S(1)} %copy-done.5, bf16[256,8,4,128]{3,2,1,0:T(4,128)(2,1)S(1)} %bitcast.47), kind=kOutput, calls=%fused_computation.4 | convolution fusion | flops 2148532224 | bytes 10485760 | tf_op jit(solution)/shard_map/dot_general | solution.py:18
  220.7 293.4 %reduce-scatter.5.cloned.1.call-done = f32[512,128]{1,0:T(8,128)} async-done(((f32[512,4096]{1,0:T(8,128)}), f32[512,128]{1,0:T(8,128)}) %reduce-scatter.5.cloned.1.call-update) | async-done | bytes 262160 | tf_op jit(solution)/shard_map/reduce_scatter | solution.py:32
  514.1 1.8 copy.21
  515.9 13.7 %all-to-all-start = ((f32[4,128,1,128]{3,0,2,1:T(4,128)}), f32[4,128,1,128]{3,0,2,1:T(4,128)S(1)}, u32[]{:S(2)}, u32[]{:S(2)}) async-start(f32[4,128,1,128]{3,0,2,1:T(4,128)} %copy.21), calls=%async_computation.2 | async-start | bytes 524288 | tf_op jit(solution)/shard_map/all_to_all | solution.py:36
  529.6 0.1 dynamic_slice.6
  529.7 0.1 dynamic_slice.7
  529.8 0.1 broadcast_add_fusion
  529.8 0.1 broadcast_subtract_fusion
  530.0 0.1 copy.24
  530.1 0.1 sub.44
  530.2 10.0 %all-to-all-done = f32[4,128,1,128]{3,0,2,1:T(4,128)S(1)} async-done(((f32[4,128,1,128]{3,0,2,1:T(4,128)}), f32[4,128,1,128]{3,0,2,1:T(4,128)S(1)}, u32[]{:S(2)}, u32[]{:S(2)}) %all-to-all-start) | async-done | bytes 262176 | tf_op jit(solution)/shard_map/all_to_all | solution.py:36
  540.2 0.1 copy.23
  540.4 29.6 %reduce-scatter.3.cloned.1.call-done = f32[128,512]{0,1:T(8,128)} async-done(((f32[1024,512]{0,1:T(8,128)}), f32[128,512]{0,1:T(8,128)}) %reduce-scatter.3.cloned.1.call-update) | async-done | bytes 262160 | tf_op jit(solution)/shard_map/reduce_scatter | solution.py:23
  570.0 1.0 divide_convert_fusion
  571.0 0.8 copy.25
  (19 shorter events, 0.1 us)
Async XLA Ops:
  6.5 35.1 %copy-start = (bf16[512,128]{1,0:T(8,128)(2,1)S(1)}, bf16[512,128]{1,0:T(8,128)(2,1)}, u32[]{:S(2)}) copy-start(bf16[512,128]{1,0:T(8,128)(2,1)} %param.10) | copy-start | bytes 393220
  6.5 32.8 %all-gather.5.cloned.1.call-start = ((), (), s32[]{:S(2)}) async-start(), calls=%async_computation.5 | async-start | bytes 1179648 | tf_op jit(solution)/shard_map/all_gather | solution.py:24
  7.3 201.6 %all-gather.3.cloned.1.call-start = ((), (), s32[]{:S(2)}) async-start(), calls=%async_computation.3 | async-start | bytes 4325376 | tf_op jit(solution)/shard_map/all_gather | solution.py:19
  8.0 506.0 %reduce-scatter.5.cloned.1.call-start = ((), (), s32[]{:S(2)}) async-start(), calls=%async_computation.6 | async-start | bytes 8650752 | tf_op jit(solution)/shard_map/reduce_scatter | solution.py:32
  41.6 1.3 copy-start.1
  47.4 0.7 copy-start.2
  47.4 167.3 %copy-start.5 = (bf16[2048,512]{1,0:T(8,128)(2,1)S(1)}, bf16[2048,512]{1,0:T(8,128)(2,1)}, u32[]{:S(2)}) copy-start(bf16[2048,512]{1,0:T(8,128)(2,1)} %param.8) | copy-start | bytes 6291460
  47.4 522.5 %reduce-scatter.3.cloned.1.call-start = ((), (), s32[]{:S(2)}) async-start(), calls=%async_computation.4 | async-start | bytes 2359296 | tf_op jit(solution)/shard_map/reduce_scatter | solution.py:23
  220.7 308.9 %copy-start.4 = (f32[128]{0:T(128)S(1)}, f32[128]{0:T(128)}, u32[]{:S(2)}) copy-start(f32[128]{0:T(128)} %param.13) | copy-start | bytes 1540
  220.7 309.0 %copy-start.3 = (f32[32]{0:T(128)S(1)}, f32[32]{0:T(128)}, u32[]{:S(2)}) copy-start(f32[32]{0:T(128)} %param.12) | copy-start | bytes 388
  515.9 24.3 %all-to-all-start = ((f32[4,128,1,128]{3,0,2,1:T(4,128)}), f32[4,128,1,128]{3,0,2,1:T(4,128)S(1)}, u32[]{:S(2)}, u32[]{:S(2)}) async-start(f32[4,128,1,128]{3,0,2,1:T(4,128)} %copy.21), calls=%async_computation.2 | async-start | bytes 524288 | tf_op jit(solution)/shard_map/all_to_all | solution.py:36
Sparse Core Ops, SparseCore 0:
  9.2 30.1 all-gather.4
  41.1 167.6 all-gather.2
  211.4 302.6 reduce-scatter.4
  516.5 53.4 reduce-scatter.2
where the time goes:
time: 580 us; the launch traced here: 578 us
  waiting for transfers between devices  526 us (91%)
  starting transfers between devices  13.8 us (2%)
  between operations  13.3 us (2%)
  local copies, waits for them, and re-layouts  12 us (2%)
  matrix products  11.7 us (2%)
    reduce_scatter x1, waiting for transfers between devices, local(): lax.psum_scatter(partial_value, ('grp', 'row'), scatter_dimension=1, tile...  293 us
    all_gather x1, waiting for transfers between devices, local(): lax.all_gather(amplitudes, ('grp', 'row'), axis=0, tiled=True)  161 us
    all_gather x1, waiting for transfers between devices, local(): whole = lax.all_gather(amplitudes, 'col', axis=1, tiled=True)  31.3 us
    reduce_scatter x1, waiting for transfers between devices, local(): ladder = lax.psum_scatter(ladder, 'col', scatter_dimension=0, tiled=True)  29.6 us
    all_to_all x1, starting transfers between devices, local(): lax.all_to_all(arranged, ('grp', 'row'), split_axis=1, concat_axis=2, til...  13.7 us
  transfers between devices with their start and end apart: 5, of which 5 were waited for; matrix products, arithmetic and copies ran while one was open for 4% of the time, Pallas kernels for 0%

commit v1 on v0

v1 whole, which is shorter than its diff:
```python
import jax
import jax.numpy as jnp
from jax import lax
from jax.sharding import Mesh, PartitionSpec as P

G = ("zl", "zh", "y")
C = ("x", "core")
Z = ("zl", "zh")


def shift(n, s):
    return [(i, (i + s) % n) for i in range(n)]


def z_shift(s):
    at = lambda z: (z % 4) * 2 + z // 4
    return [(at(z), at((z + s) % 8)) for z in range(8)]


def gather_pairs(t):
    z0 = lax.axis_index("zh") * 4 + lax.axis_index("zl")
    y0 = lax.axis_index("y")
    parts = [(0, t)]
    fwd = bwd = t
    for k in range(1, 5):
        fwd = lax.ppermute(fwd, Z, z_shift(1))
        parts.append((-k, fwd))
        if k < 4:
            bwd = lax.ppermute(bwd, Z, z_shift(-1))
            parts.append((k, bwd))
    mine = jnp.zeros((8,) + t.shape, t.dtype)
    for d, part in parts:
        z = (z0 + (d & 7)) & 7
        mine = lax.dynamic_update_slice(mine, part[None], ((z & 3) * 2 + (z >> 2), 0, 0))
    whole = jnp.zeros((8, 4) + t.shape, t.dtype)
    whole = lax.dynamic_update_slice(whole, mine[:, None], (0, y0, 0, 0))
    for s in range(1, 4):
        got = lax.ppermute(mine, "y", shift(4, s))
        whole = lax.dynamic_update_slice(whole, got[:, None], (0, (y0 + 4 - s) & 3, 0, 0))
    return whole.reshape((32,) + t.shape)


def scatter_sum(p):
    x0 = lax.axis_index("x")
    c0 = lax.axis_index("core")
    p = p.reshape(4, 2, 128, 512)
    away = lax.dynamic_slice_in_dim(p, 1 - c0, 1, 1)
    got = lax.ppermute(away, "core", shift(2, 1))
    p = (lax.dynamic_slice_in_dim(p, c0, 1, 1) + got)[:, 0]
    out = lax.dynamic_slice_in_dim(p, x0, 1, 0)
    for s in (1, 3, 2):
        block = lax.dynamic_slice_in_dim(p, (x0 + s) & 3, 1, 0)
        out = out + lax.ppermute(block, "x", shift(4, s))
    return out[0]


def local(amplitudes, ladder_ints, tile_live, cycle_direct, cycle_exchange, eps_occ, eps_vir):
    occ, vir = 32, 128
    col = lax.axis_index(C)
    g = lax.axis_index(G)
    both = jnp.stack([cycle_direct, cycle_exchange]).reshape(2, 4, 32, 4, vir)
    both = both.transpose(2, 0, 1, 3, 4)
    both = lax.all_to_all(both, G, 0, 0, tiled=True)
    w = both[:, 0].reshape(512, vir).T.reshape(8, 16, 512)
    w = lax.all_to_all(w, C, 0, 0, tiled=True)
    w = w.reshape(8, 16, occ, 4, 4)
    x = lax.all_gather(both[:, 1], C, axis=0, tiled=False)
    t = gather_pairs(amplitudes)
    expanded = jnp.repeat(jnp.repeat(tile_live, 128, axis=0), 128, axis=1).astype(jnp.bfloat16)
    ladder = jnp.dot(t.reshape(1024, 2048), ladder_ints * expanded, preferred_element_type=jnp.float32)
    four = t.reshape(occ, occ, 16, vir)
    wm = w.transpose(0, 3, 4, 2, 1).reshape(128, 512)
    u1 = four.transpose(0, 2, 1, 3).reshape(512, occ * vir)
    one = jnp.dot(wm, u1, preferred_element_type=jnp.float32).reshape(occ, 4, occ, vir)
    xm = x.transpose(0, 2, 3, 1, 4).reshape(128, occ * vir)
    two = lax.dot_general(
        xm.reshape(128, occ, vir), four, (((1, 2), (0, 3)), ((), ())), preferred_element_type=jnp.float32
    ).reshape(occ, 4, occ, 16)
    one = lax.dynamic_update_slice_in_dim(
        one, lax.dynamic_slice_in_dim(one, col * 16, 16, 3) + two, col * 16, 3
    )
    part = ladder + one.transpose(0, 2, 1, 3).reshape(1024, 512)
    total = scatter_sum(part.reshape(8, 128, 512))
    occ_local = lax.dynamic_slice_in_dim(eps_occ, col * 4, 4)
    vir_local = lax.dynamic_slice_in_dim(eps_vir, g * 4, 4)
    denom = (
        vir_local[None, None, :, None]
        + eps_vir[None, None, None, :]
        - occ_local[:, None, None, None]
        - eps_occ[None, :, None, None]
    ).reshape(128, 512)
    return (total / denom).astype(jnp.bfloat16)


def solution(mesh):
    fine = Mesh(mesh.devices.reshape(4, 2, 4, 4, 2), ("zl", "zh", "y", "x", "core"))
    placed = (P(G, C), P(C, G), P(C, G), P(C, G), P(C, G), P(), P())
    return jax.shard_map(local, mesh=fine, in_specs=placed, out_specs=P(C, G), check_vma=False)
```

time: 580 us -> 196 us (0.34)
  waiting for transfers between devices: 526 us -> 48.8 us
  local copies, waits for them, and re-layouts: 12 us -> 70.3 us
  starting transfers between devices: 13.8 us -> 42.7 us
    reduce_scatter x2 -> x0, waiting for transfers between devices: 323 us -> none  [the longest x1 293 us: local(): lax.psum_scatter(partial_value, ('grp', 'row'), scatter_dimension=1, tile...]
    all_gather x2 -> x1, waiting for transfers between devices: 192 us -> 0.02 us  [local(): x = lax.all_gather(both[:, 1], C, axis=0, tiled=False)]
    ppermute x0 -> x14, waiting for transfers between devices: none -> 48.7 us  [the longest x3 21.3 us: gather_pairs(): got = lax.ppermute(mine, 'y', shift(4, s))]
    dynamic_update_slice x0 -> x13, local copies, waits for them, and re-layouts: none -> 33.1 us  [the longest x1 24 us: local(): lax.dynamic_update_slice_in_dim(one, lax.dynamic_slice_in_dim(one, col *...]
    ppermute x0 -> x14, starting transfers between devices: none -> 25.7 us  [the longest x3 8.25 us: scatter_sum(): out = out + lax.ppermute(block, 'x', shift(4, s))]
    all_to_all x1 -> x2, waiting for transfers between devices: 9.99 us -> 0.01 us  [the longest x1 0.01 us: local(): w = lax.all_to_all(w, C, 0, 0, tiled=True)]
    unnamed x15 -> x13, local copies, waits for them, and re-layouts: 2.12 us -> 11.2 us
    dot_general x0 -> x2, local copies, waits for them, and re-layouts: none -> 8.24 us  [local(): jnp.dot(wm, u1, preferred_element_type=jnp.float32)]
  transfers between devices with their start and end apart: 5 -> 17, of which waited for: 5 -> 8; matrix products, arithmetic and copies ran while one was open for 4% -> 21% of each run, Pallas kernels for 0% -> 0%
where the time goes in v1:
time: 196 us; the launch traced here: 195 us
  local copies, waits for them, and re-layouts  70.3 us (36%)
  waiting for transfers between devices  48.8 us (25%)
  starting transfers between devices  42.7 us (22%)
  matrix products  16.1 us (8%)
  between operations  13.7 us (7%)
  other arithmetic  3.51 us (2%)
    dynamic_update_slice x1, local copies, waits for them, and re-layouts, local(): lax.dynamic_update_slice_in_dim(one, lax.dynamic_slice_in_dim(one, col *...  24 us
    ppermute x3, waiting for transfers between devices, gather_pairs(): got = lax.ppermute(mine, 'y', shift(4, s))  21.3 us
    ppermute x4, waiting for transfers between devices, gather_pairs(): fwd = lax.ppermute(fwd, Z, z_shift(1))  13.9 us
    unnamed x13, local copies, waits for them, and re-layouts  11.2 us
    ppermute x3, waiting for transfers between devices, scatter_sum(): out = out + lax.ppermute(block, 'x', shift(4, s))  10.8 us
    all_to_all x1, starting transfers between devices, local(): w = lax.all_to_all(w, C, 0, 0, tiled=True)  8.73 us
    all_to_all x1, starting transfers between devices, local(): both = lax.all_to_all(both, G, 0, 0, tiled=True)  8.3 us
    ppermute x3, starting transfers between devices, scatter_sum(): out = out + lax.ppermute(block, 'x', shift(4, s))  8.25 us
  transfers between devices with their start and end apart: 17, of which 8 were waited for; matrix products, arithmetic and copies ran while one was open for 21% of the time, Pallas kernels for 0%

profile of v1, /device:TPU:1, one launch (start us, length us, event | category | flops | bytes accessed | tf_op | source)
XLA Modules:
  0.0 195.2 jit_solution(18413258195114012232)
XLA Ops:
  6.5 2.5 %collective-permute-start = (bf16[32,2048]{1,0:T(8,128)(2,1)}, bf16[32,2048]{1,0:T(8,128)(2,1)S(1)}, u32[]{:S(2)}, u32[]{:S(2)}) collective-permute-start(bf16[32,2048]{1,0:T(8,128)(2,1)} %param.7), channel_id=1, source_target_pairs={{0,64},{64,128},{128,192},{192,32},{32,96},{96,160},{160,224},{224... | collective-permute-start | bytes 393224 | tf_op jit(solution)/shard_map/ppermute | solution.py:26
  9.0 3.9 %collective-permute-start.1 = (bf16[32,2048]{1,0:T(8,128)(2,1)}, bf16[32,2048]{1,0:T(8,128)(2,1)S(1)}, u32[]{:S(2)}, u32[]{:S(2)}) collective-permute-start(bf16[32,2048]{1,0:T(8,128)(2,1)} %param.7), channel_id=1, source_target_pairs={{0,224},{64,0},{128,64},{192,128},{32,192},{96,32},{160,96},{224,1... | collective-permute-start | bytes 393224 | tf_op jit(solution)/shard_map/ppermute | solution.py:29
  14.9 8.3 %all-to-all-start = ((bf16[32,2,4,4,128]{4,3,2,1,0:T(4,128)(2,1)}), bf16[32,2,4,4,128]{4,3,2,1,0:T(4,128)(2,1)S(1)}, u32[]{:S(2)}, u32[]{:S(2)}) async-start(bf16[32,2,4,4,128]{4,3,2,1,0:T(4,128)(2,1)} %copy.44), calls=%async_computation | async-start | bytes 524288 | tf_op jit(solution)/shard_map/all_to_all | solution.py:63
  25.6 1.4 collective-permute-start.3
  27.1 6.6 %collective-permute-done.2 = bf16[32,2048]{1,0:T(8,128)(2,1)S(1)} collective-permute-done((bf16[32,2048]{1,0:T(8,128)(2,1)S(1)}, bf16[32,2048]{1,0:T(8,128)(2,1)S(1)}, u32[]{:S(2)}, u32[]{:S(2)}) %collective-permute-start.2) | collective-permute-done | bytes 131104 | tf_op jit(solution)/shard_map/ppermute | solution.py:26
  33.7 2.7 %collective-permute-start.5 = (bf16[32,2048]{1,0:T(8,128)(2,1)S(1)}, bf16[32,2048]{1,0:T(8,128)(2,1)S(1)}, u32[]{:S(2)}, u32[]{:S(2)}) collective-permute-start(bf16[32,2048]{1,0:T(8,128)(2,1)S(1)} %collective-permute-done.3), channel_id=1, source_target_pairs={{0,224},{64,0},{128,64},{192,128},{32,192},{96,32},{160,96},{224,1... | collective-permute-start | bytes 393224 | tf_op jit(solution)/shard_map/ppermute | solution.py:29
  36.4 2.3 %collective-permute-done.4 = bf16[32,2048]{1,0:T(8,128)(2,1)S(1)} collective-permute-done((bf16[32,2048]{1,0:T(8,128)(2,1)S(1)}, bf16[32,2048]{1,0:T(8,128)(2,1)S(1)}, u32[]{:S(2)}, u32[]{:S(2)}) %collective-permute-start.4) | collective-permute-done | bytes 131104 | tf_op jit(solution)/shard_map/ppermute | solution.py:26
  38.8 5.0 %collective-permute-done.6 = bf16[32,2048]{1,0:T(8,128)(2,1)S(1)} collective-permute-done((bf16[32,2048]{1,0:T(8,128)(2,1)S(1)}, bf16[32,2048]{1,0:T(8,128)(2,1)S(1)}, u32[]{:S(2)}, u32[]{:S(2)}) %collective-permute-start.6) | collective-permute-done | bytes 131104 | tf_op jit(solution)/shard_map/ppermute | solution.py:26
  43.8 1.7 collective-permute-start.7
  45.6 2.5 %collective-permute-start.8 = (bf16[8,32,2048]{2,1,0:T(8,128)(2,1)S(1)}, bf16[8,32,2048]{2,1,0:T(8,128)(2,1)}, u32[]{:S(2)}, u32[]{:S(2)}) collective-permute-start(bf16[8,32,2048]{2,1,0:T(8,128)(2,1)S(1)} %bitcast_dynamic-update-slice_fusion.4), channel_id=1, source_target_pairs={{0,16},{8,24},{16,0},{24,8},{1,17},{9,25},{17,1},{25,9},{2,18},{10... | collective-permute-start | bytes 3145736 | tf_op jit(solution)/shard_map/ppermute | solution.py:38
  48.9 8.7 %all-to-all-start.1 = ((bf16[8,16,512]{2,1,0:T(8,128)(2,1)}), bf16[8,16,512]{2,1,0:T(8,128)(2,1)S(1)}, u32[]{:S(2)}, u32[]{:S(2)}) async-start(bf16[8,16,512]{2,1,0:T(8,128)(2,1)} %bitcast.22), calls=%async_computation.1 | async-start | bytes 262144 | tf_op jit(solution)/shard_map/all_to_all | solution.py:65
  59.7 2.5 %broadcast_in_dim.52 = bf16[8,4,32,2048]{3,2,1,0:T(8,128)(2,1)} broadcast(bf16[]{:T(256)} %constant.40.clone.1), dimensions={} | broadcast | bytes 4194306 | tf_op jit(solution)/shard_map/broadcast_in_dim | solution.py:35
  64.8 1.8 reshape.81
  66.6 2.4 %bitcast_dynamic-update-slice_fusion.1 = bf16[8,4,32,2048]{3,2,1,0:T(8,128)(2,1)} fusion(bf16[8,4,32,2048]{3,2,1,0:T(8,128)(2,1)} %bitcast_dynamic-update-slice_fusion.2, s32[]{:T(128)S(6)} %select_n.73, bf16[8,32,2048]{2,1,0:T(8,128)(2,1)} %collective-permute-done.7), kind=kLoop, calls=%fused_computation.10 | loop fusion | bytes 2097156 | tf_op jit(solution)/shard_map/dynamic_update_slice | solution.py:39
  69.0 20.8 %collective-permute-done.8 = bf16[8,32,2048]{2,1,0:T(8,128)(2,1)} collective-permute-done((bf16[8,32,2048]{2,1,0:T(8,128)(2,1)S(1)}, bf16[8,32,2048]{2,1,0:T(8,128)(2,1)}, u32[]{:S(2)}, u32[]{:S(2)}) %collective-permute-start.8) | collective-permute-done | bytes 1048608 | tf_op jit(solution)/shard_map/ppermute | solution.py:38
  89.9 2.3 %bitcast_dynamic-update-slice_fusion = bf16[8,4,32,2048]{3,2,1,0:T(8,128)(2,1)} fusion(bf16[8,4,32,2048]{3,2,1,0:T(8,128)(2,1)} %bitcast_dynamic-update-slice_fusion.1, s32[]{:T(128)S(6)} %select_n.74, bf16[8,32,2048]{2,1,0:T(8,128)(2,1)} %collective-permute-done.8), kind=kLoop, calls=%fused_computation.9 | loop fusion | bytes 2097156 | tf_op jit(solution)/shard_map/dynamic_update_slice | solution.py:39
  92.6 2.3 %bitcast_dynamic-update-slice_fusion.3 = bf16[8,4,32,2048]{3,2,1,0:T(8,128)(2,1)} fusion(bf16[8,4,32,2048]{3,2,1,0:T(8,128)(2,1)} %bitcast_dynamic-update-slice_fusion, s32[]{:T(128)S(6)} %select_n.75, bf16[8,32,2048]{2,1,0:T(8,128)(2,1)} %collective-permute-done.9), kind=kLoop, calls=%fused_computation.12 | loop fusion | bytes 2097156 | tf_op jit(solution)/shard_map/dynamic_update_slice | solution.py:39
  94.9 3.6 %copy.65 = bf16[128,8,16,128]{3,2,1,0:T(8,128)(2,1)S(1)} copy(bf16[128,8,16,128]{3,1,2,0:T(8,128)(2,1)} %bitcast.63) | data formatting | bytes 8388608
  101.6 6.1 %copy.78 = bf16[64,8,32,128]{3,1,2,0:T(8,128)(2,1)} copy(bf16[64,8,32,128]{3,2,1,0:T(8,128)(2,1)S(1)} %bitcast.137) | data formatting | bytes 8388608
  107.7 6.5 %copy.59 = bf16[4096,512]{1,0:T(8,128)(2,1)} copy(bf16[4096,512]{0,1:T(8,128)(2,1)} %bitcast.138) | data formatting | bytes 8388608 | tf_op jit(solution)/shard_map/dot_general | solution.py:74
  114.2 3.7 %fusion.7 = f32[32,4,32,128]{3,0,2,1:T(8,128)S(1)} fusion(bf16[32,128,512,1]{2,1,0,3:T(8,128)(2,1)} %bitcast.136, bf16[32,4,512,1]{2,0,1,3:T(8,128)(2,1)S(1)} %reshape.81), kind=kOutput, calls=%fused_computation.24 | convolution fusion | flops 536870912 | bytes 6422528 | tf_op jit(solution)/shard_map/dot_general | solution.py:74
  117.9 2.0 %copy.51 = bf16[8,4,4,32,128]{4,1,0,3,2:T(4,128)(2,1)S(1)} copy(bf16[8,4,4,32,128]{4,3,0,2,1:T(8,128)(2,1)} %bitcast.147) | data formatting | bytes 2097152 | tf_op jit(solution)/shard_map/transpose | solution.py:75
  119.9 7.9 %bitcast_add_fusion.1 = f32[32,4,32,16]{3,0,2,1:T(8,128)} fusion(f32[32,4,32,128]{3,0,2,1:T(8,128)S(1)} %fusion.7, s32[]{:T(128)S(6)} %select_n.76, bf16[32,4,32,128,1]{3,0,4,2,1:T(8,128)(2,1)S(1)} %bitcast.148, bf16[32,32,16,128]{3,2,1,0:T(8,128)(2,1)} %bitcast.135), kind=kOutput, calls=%fused_computation.8 | convolution fusion | flops 536936448 | bytes 5767172 | tf_op jit(solution)/shard_map/dot_general | solution.py:76
  127.8 24.0 %dynamic_update_slice.51 = f32[32,4,32,128]{3,0,2,1:T(8,128)S(1)} dynamic-update-slice(f32[32,4,32,128]{3,0,2,1:T(8,128)S(1)} %fusion.7, f32[32,4,32,16]{3,0,2,1:T(8,128)} %bitcast_add_fusion.1, s32[]{:T(128)} %constant.49.clone.1, s32[]{:T(128)} %constant.49.clone.1, s32[]{:T(128)} %constant.49.clone.1, s32[]{:T(128)S(6)} %select_n.76) | dynamic-update-slice | bytes 524292 | tf_op jit(solution)/shard_map/dynamic_update_slice | solution.py:79
  153.3 5.8 %broadcast_in_dim.67 = bf16[2048,4,128]{2,1,0:T(4,128)(2,1)S(1)} broadcast(bf16[2048,4]{1,0:T(8,128)(2,1)S(1)} %bitcast.142), dimensions={0,1} | broadcast | bytes 2113536 | tf_op jit(solution)/shard_map/broadcast_in_dim | solution.py:69
  159.1 4.6 %bitcast_add_fusion = f32[1024,512]{1,0:T(8,128)S(1)} fusion(f32[128,8,4,128]{3,2,1,0:T(4,128)S(1)} %bitcast.145, bf16[1024,2048]{1,0:T(8,128)(2,1)} %bitcast.15, bf16[2048,512]{1,0:T(8,128)(2,1)S(1)} %copy-done.4, bf16[256,8,4,128]{3,2,1,0:T(4,128)(2,1)S(1)} %bitcast.141), kind=kOutput, calls=%fused_computation.4 | convolution fusion | flops 2149056512 | bytes 12582912 | tf_op jit(solution)/shard_map/dot_general | solution.py:70
  164.0 2.7 %collective-permute-done.10 = f32[4,1,128,512]{3,2,1,0:T(8,128)} collective-permute-done((f32[4,1,128,512]{3,2,1,0:T(8,128)S(1)}, f32[4,1,128,512]{3,2,1,0:T(8,128)}, u32[]{:S(2)}, u32[]{:S(2)}) %collective-permute-start.10) | collective-permute-done | bytes 1048608 | tf_op jit(solution)/shard_map/ppermute | solution.py:48
  166.6 1.4 dynamic-slice_add_fusion
  168.1 5.2 %collective-permute-start.11 = (f32[1,128,512]{2,1,0:T(8,128)S(1)}, f32[1,128,512]{2,1,0:T(8,128)S(1)}, u32[]{:S(2)}, u32[]{:S(2)}) collective-permute-start(f32[1,128,512]{2,1,0:T(8,128)S(1)} %get-tuple-element.5), channel_id=1, source_target_pairs={{0,2},{2,4},{4,6},{6,0},{1,3},{3,5},{5,7},{7,1},{8,10},{10,12},{12... | collective-permute-start | bytes 786440 | tf_op jit(solution)/shard_map/ppermute | solution.py:53
  174.7 1.7 collective-permute-start.13
  176.7 4.3 %collective-permute-done.11 = f32[1,128,512]{2,1,0:T(8,128)S(1)} collective-permute-done((f32[1,128,512]{2,1,0:T(8,128)S(1)}, f32[1,128,512]{2,1,0:T(8,128)S(1)}, u32[]{:S(2)}, u32[]{:S(2)}) %collective-permute-start.11) | collective-permute-done | bytes 262176 | tf_op jit(solution)/shard_map/ppermute | solution.py:53
  181.0 6.5 %collective-permute-done.13 = f32[1,128,512]{2,1,0:T(8,128)S(1)} collective-permute-done((f32[1,128,512]{2,1,0:T(8,128)S(1)}, f32[1,128,512]{2,1,0:T(8,128)S(1)}, u32[]{:S(2)}, u32[]{:S(2)}) %collective-permute-start.13) | collective-permute-done | bytes 262176 | tf_op jit(solution)/shard_map/ppermute | solution.py:53
  (61 shorter events, 17.7 us)
Async XLA Ops:
  6.5 39.0 %copy-start.1 = (s32[16,4]{0,1:T(4,128)S(1)}, s32[16,4]{0,1:T(4,128)}, u32[]{:S(2)}) copy-start(s32[16,4]{0,1:T(4,128)} %param.9) | copy-start | bytes 772
  6.5 17.8 %collective-permute-start = (bf16[32,2048]{1,0:T(8,128)(2,1)}, bf16[32,2048]{1,0:T(8,128)(2,1)S(1)}, u32[]{:S(2)}, u32[]{:S(2)}) collective-permute-start(bf16[32,2048]{1,0:T(8,128)(2,1)} %param.7), channel_id=1, source_target_pairs={{0,64},{64,128},{128,192},{192,32},{32,96},{96,160},{160,224},{224... | collective-permute-start | bytes 393224 | tf_op jit(solution)/shard_map/ppermute | solution.py:26
  9.0 16.6 %collective-permute-start.1 = (bf16[32,2048]{1,0:T(8,128)(2,1)}, bf16[32,2048]{1,0:T(8,128)(2,1)S(1)}, u32[]{:S(2)}, u32[]{:S(2)}) collective-permute-start(bf16[32,2048]{1,0:T(8,128)(2,1)} %param.7), channel_id=1, source_target_pairs={{0,224},{64,0},{128,64},{192,128},{32,192},{96,32},{160,96},{224,1... | collective-permute-start | bytes 393224 | tf_op jit(solution)/shard_map/ppermute | solution.py:29
  14.9 33.2 %all-to-all-start = ((bf16[32,2,4,4,128]{4,3,2,1,0:T(4,128)(2,1)}), bf16[32,2,4,4,128]{4,3,2,1,0:T(4,128)(2,1)S(1)}, u32[]{:S(2)}, u32[]{:S(2)}) async-start(bf16[32,2,4,4,128]{4,3,2,1,0:T(4,128)(2,1)} %copy.44), calls=%async_computation | async-start | bytes 524288 | tf_op jit(solution)/shard_map/all_to_all | solution.py:63
  24.3 9.4 %collective-permute-start.2 = (bf16[32,2048]{1,0:T(8,128)(2,1)S(1)}, bf16[32,2048]{1,0:T(8,128)(2,1)S(1)}, u32[]{:S(2)}, u32[]{:S(2)}) collective-permute-start(bf16[32,2048]{1,0:T(8,128)(2,1)S(1)} %collective-permute-done), channel_id=1, source_target_pairs={{0,64},{64,128},{128,192},{192,32},{32,96},{96,160},{160,224},{224... | collective-permute-start | bytes 393224 | tf_op jit(solution)/shard_map/ppermute | solution.py:26
  25.6 8.1 %collective-permute-start.3 = (bf16[32,2048]{1,0:T(8,128)(2,1)S(1)}, bf16[32,2048]{1,0:T(8,128)(2,1)S(1)}, u32[]{:S(2)}, u32[]{:S(2)}) collective-permute-start(bf16[32,2048]{1,0:T(8,128)(2,1)S(1)} %collective-permute-done.1), channel_id=1, source_target_pairs={{0,224},{64,0},{128,64},{192,128},{32,192},{96,32},{160,96},{224,1... | collective-permute-start | bytes 393224 | tf_op jit(solution)/shard_map/ppermute | solution.py:29
  33.7 5.0 %collective-permute-start.4 = (bf16[32,2048]{1,0:T(8,128)(2,1)S(1)}, bf16[32,2048]{1,0:T(8,128)(2,1)S(1)}, u32[]{:S(2)}, u32[]{:S(2)}) collective-permute-start(bf16[32,2048]{1,0:T(8,128)(2,1)S(1)} %collective-permute-done.2), channel_id=1, source_target_pairs={{0,64},{64,128},{128,192},{192,32},{32,96},{96,160},{160,224},{224... | collective-permute-start | bytes 393224 | tf_op jit(solution)/shard_map/ppermute | solution.py:26
  33.7 5.0 %collective-permute-start.5 = (bf16[32,2048]{1,0:T(8,128)(2,1)S(1)}, bf16[32,2048]{1,0:T(8,128)(2,1)S(1)}, u32[]{:S(2)}, u32[]{:S(2)}) collective-permute-start(bf16[32,2048]{1,0:T(8,128)(2,1)S(1)} %collective-permute-done.3), channel_id=1, source_target_pairs={{0,224},{64,0},{128,64},{192,128},{32,192},{96,32},{160,96},{224,1... | collective-permute-start | bytes 393224 | tf_op jit(solution)/shard_map/ppermute | solution.py:29
  38.8 5.0 %collective-permute-start.6 = (bf16[32,2048]{1,0:T(8,128)(2,1)S(1)}, bf16[32,2048]{1,0:T(8,128)(2,1)S(1)}, u32[]{:S(2)}, u32[]{:S(2)}) collective-permute-start(bf16[32,2048]{1,0:T(8,128)(2,1)S(1)} %collective-permute-done.4), channel_id=1, source_target_pairs={{0,64},{64,128},{128,192},{192,32},{32,96},{96,160},{160,224},{224... | collective-permute-start | bytes 393224 | tf_op jit(solution)/shard_map/ppermute | solution.py:26
  43.8 22.8 %collective-permute-start.7 = (bf16[8,32,2048]{2,1,0:T(8,128)(2,1)S(1)}, bf16[8,32,2048]{2,1,0:T(8,128)(2,1)}, u32[]{:S(2)}, u32[]{:S(2)}) collective-permute-start(bf16[8,32,2048]{2,1,0:T(8,128)(2,1)S(1)} %bitcast_dynamic-update-slice_fusion.4), channel_id=1, source_target_pairs={{0,8},{8,16},{16,24},{24,0},{1,9},{9,17},{17,25},{25,1},{2,10},{10... | collective-permute-start | bytes 3145736 | tf_op jit(solution)/shard_map/ppermute | solution.py:38
  45.6 44.3 %collective-permute-start.8 = (bf16[8,32,2048]{2,1,0:T(8,128)(2,1)S(1)}, bf16[8,32,2048]{2,1,0:T(8,128)(2,1)}, u32[]{:S(2)}, u32[]{:S(2)}) collective-permute-start(bf16[8,32,2048]{2,1,0:T(8,128)(2,1)S(1)} %bitcast_dynamic-update-slice_fusion.4), channel_id=1, source_target_pairs={{0,16},{8,24},{16,0},{24,8},{1,17},{9,25},{17,1},{25,9},{2,18},{10... | collective-permute-start | bytes 3145736 | tf_op jit(solution)/shard_map/ppermute | solution.py:38
  48.9 14.4 %all-to-all-start.1 = ((bf16[8,16,512]{2,1,0:T(8,128)(2,1)}), bf16[8,16,512]{2,1,0:T(8,128)(2,1)S(1)}, u32[]{:S(2)}, u32[]{:S(2)}) async-start(bf16[8,16,512]{2,1,0:T(8,128)(2,1)} %bitcast.22), calls=%async_computation.1 | async-start | bytes 262144 | tf_op jit(solution)/shard_map/all_to_all | solution.py:65
  57.7 60.2 %all-gather.3.cloned.1.call-start = ((), (), s32[]{:S(2)}) async-start(), calls=%async_computation.2 | async-start | bytes 1179648 | tf_op jit(solution)/shard_map/all_gather | solution.py:67
  58.4 34.2 %collective-permute-start.9 = (bf16[8,32,2048]{2,1,0:T(8,128)(2,1)S(1)}, bf16[8,32,2048]{2,1,0:T(8,128)(2,1)}, u32[]{:S(2)}, u32[]{:S(2)}) collective-permute-start(bf16[8,32,2048]{2,1,0:T(8,128)(2,1)S(1)} %bitcast_dynamic-update-slice_fusion.4), channel_id=1, source_target_pairs={{0,24},{8,0},{16,8},{24,16},{1,25},{9,1},{17,9},{25,17},{2,26},{10... | collective-permute-start | bytes 3145736 | tf_op jit(solution)/shard_map/ppermute | solution.py:38
  98.5 2.0 %copy-start = (bf16[128,8,16,128]{3,2,1,0:T(8,128)(2,1)}, bf16[128,8,16,128]{3,2,1,0:T(8,128)(2,1)S(1)}, u32[]{:S(2)}) copy-start(bf16[128,8,16,128]{3,2,1,0:T(8,128)(2,1)S(1)} %copy.65) | copy-start | bytes 12582916
  151.8 7.2 %copy-start.4 = (bf16[2048,512]{1,0:T(8,128)(2,1)S(1)}, bf16[2048,512]{1,0:T(8,128)(2,1)}, u32[]{:S(2)}) copy-start(bf16[2048,512]{1,0:T(8,128)(2,1)} %param.8) | copy-start | bytes 6291460
  159.1 4.8 %copy-start.3 = (f32[128]{0:T(128)S(1)}, f32[128]{0:T(128)}, u32[]{:S(2)}) copy-start(f32[128]{0:T(128)} %param.13) | copy-start | bytes 1540
  163.7 12.8 %copy-start.2 = (f32[32]{0:T(128)S(1)}, f32[32]{0:T(128)}, u32[]{:S(2)}) copy-start(f32[32]{0:T(128)} %param.12) | copy-start | bytes 388
  163.8 2.9 %collective-permute-start.10 = (f32[4,1,128,512]{3,2,1,0:T(8,128)S(1)}, f32[4,1,128,512]{3,2,1,0:T(8,128)}, u32[]{:S(2)}, u32[]{:S(2)}) collective-permute-start(f32[4,1,128,512]{3,2,1,0:T(8,128)S(1)} %constant_dynamic-slice_fusion), channel_id=1, source_target_pairs={{0,1},{1,0},{2,3},{3,2},{4,5},{5,4},{6,7},{7,6},{8,9},{9,8},{10,11... | collective-permute-start | bytes 3145736 | tf_op jit(solution)/shard_map/ppermute | solution.py:48
  168.1 12.9 %collective-permute-start.11 = (f32[1,128,512]{2,1,0:T(8,128)S(1)}, f32[1,128,512]{2,1,0:T(8,128)S(1)}, u32[]{:S(2)}, u32[]{:S(2)}) collective-permute-start(f32[1,128,512]{2,1,0:T(8,128)S(1)} %get-tuple-element.5), channel_id=1, source_target_pairs={{0,2},{2,4},{4,6},{6,0},{1,3},{3,5},{5,7},{7,1},{8,10},{10,12},{12... | collective-permute-start | bytes 786440 | tf_op jit(solution)/shard_map/ppermute | solution.py:53
  173.4 7.6 %collective-permute-start.12 = (f32[1,128,512]{2,1,0:T(8,128)S(1)}, f32[1,128,512]{2,1,0:T(8,128)S(1)}, u32[]{:S(2)}, u32[]{:S(2)}) collective-permute-start(f32[1,128,512]{2,1,0:T(8,128)S(1)} %get-tuple-element.7), channel_id=1, source_target_pairs={{0,6},{2,0},{4,2},{6,4},{1,7},{3,1},{5,3},{7,5},{8,14},{10,8},{12,... | collective-permute-start | bytes 786440 | tf_op jit(solution)/shard_map/ppermute | solution.py:53
  174.7 12.8 %collective-permute-start.13 = (f32[1,128,512]{2,1,0:T(8,128)S(1)}, f32[1,128,512]{2,1,0:T(8,128)S(1)}, u32[]{:S(2)}, u32[]{:S(2)}) collective-permute-start(f32[1,128,512]{2,1,0:T(8,128)S(1)} %get-tuple-element.6), channel_id=1, source_target_pairs={{0,4},{2,6},{4,0},{6,2},{1,5},{3,7},{5,1},{7,3},{8,12},{10,14},{12... | collective-permute-start | bytes 786440 | tf_op jit(solution)/shard_map/ppermute | solution.py:53
Sparse Core Ops, SparseCore 0:
  60.3 23.5 all-gather.2

commit v2 on v1

v2 whole, which is shorter than its diff:
```python
import jax
import jax.numpy as jnp
from jax import lax
from jax.experimental import pallas as pl
from jax.experimental.pallas import tpu as pltpu
from jax.sharding import Mesh, PartitionSpec as P

G = ("zl", "zh", "y")
C = ("x", "core")
Z = ("zl", "zh")
F32 = jnp.float32
BF16 = jnp.bfloat16


def shift(n, s):
    return [(i, (i + s) % n) for i in range(n)]


def z_shift(s):
    at = lambda z: (z % 4) * 2 + z // 4
    return [(at(z), at((z + s) % 8)) for z in range(8)]


def gather_z(t):
    z0 = lax.axis_index("zh") * 4 + lax.axis_index("zl")
    parts = [(0, t)]
    fwd = bwd = t
    for k in range(1, 5):
        fwd = lax.ppermute(fwd, Z, z_shift(1))
        parts.append((-k, fwd))
        if k < 4:
            bwd = lax.ppermute(bwd, Z, z_shift(-1))
            parts.append((k, bwd))
    mine = jnp.zeros((8,) + t.shape, t.dtype)
    for d, part in parts:
        z = (z0 + (d & 7)) & 7
        mine = lax.dynamic_update_slice(mine, part[None], ((z & 3) * 2 + (z >> 2), 0, 0))
    return mine


def ladder_kernel(meta, live, t0, t1, t2, t3, u0, u1, u2, u3, v, wa, wb, keep, away, vm, wm, o2):
    x0, c0, y0, col = meta[0], meta[1], meta[2], meta[3]
    ts, us = (t0, t1, t2, t3), (u0, u1, u2, u3)
    ys = [(y0 + 4 - q) & 3 for q in range(4)]

    @pl.loop(0, 16)
    def _(kt):
        rows = pl.ds(pl.multiple_of(kt * 128, 128), 128)
        for n in range(4):
            tile = v[rows, n * 128 : n * 128 + 128]
            vm[rows, n * 128 : n * 128 + 128] = jnp.where(live[kt, n] != 0, tile, jnp.zeros_like(tile))

    for q in range(4):
        rows = []
        for r in range(8):
            h = (((x0 + r % 4) & 3) << 1) | (c0 ^ (r // 4))
            rows.append(ts[q][h])
        part = jnp.dot(jnp.concatenate(rows, 0), vm[...], preferred_element_type=F32)
        for r in range(8):
            out = (keep, away)[r // 4]
            for a in range(4):
                out[r % 4, pl.ds(ys[q] * 4 + a, 32, stride=16), :] = part[
                    r * 32 : r * 32 + 32, a * 128 : a * 128 + 128
                ]

    lane = lax.broadcasted_iota(jnp.int32, (128, 128), 1)
    acc = jnp.zeros((512, 128), F32)
    for q in range(4):
        w_all = jnp.zeros((128, 128), F32)
        xs = []
        for h in range(8):
            k = h * 4 + ys[q]
            wk = jnp.concatenate([wa[s, k, 0] for s in range(4)] + [wb[s, k, 0] for s in range(4)], 0)
            wk = pltpu.roll(wk.astype(F32), (16 * h + 128 - 16 * col) & 127, 1)
            w_all = jnp.where((lane >> 4) == h, wk, w_all)
            xs.append(jnp.concatenate([wa[s, k, 1] for s in range(4)] + [wb[s, k, 1] for s in range(4)], 0))
        wm[:, q * 128 : q * 128 + 128] = w_all.astype(BF16)
        for h in range(0, 8, 2):
            lhs = jnp.concatenate(
                [us[q][:, (h + e) * 16 : (h + e) * 16 + 16, :].reshape(512, 128) for e in range(2)], 1
            )
            rhs = jnp.concatenate([xs[h], xs[h + 1]], 1)
            acc = acc + lax.dot_general(lhs, rhs, (((1,), (1,)), ((), ())), preferred_element_type=F32)
    o2[...] = acc.T

    own = (lane >> 4) == col

    @pl.loop(0, 16)
    def _(jj):
        j = jj * 2
        rhs = jnp.concatenate(
            [jnp.concatenate([us[q][j + e] for q in range(4)], 0) for e in range(2)], 1
        )
        one = jnp.dot(wm[...], rhs, preferred_element_type=F32)
        two = o2[:, pl.ds(pl.multiple_of((jj >> 2) * 128, 128), 128)]
        for e in range(2):
            placed = pltpu.roll(two, (16 * col + 128 - 16 * ((j + e) & 7)) & 127, 1)
            both = one[:, e * 128 : e * 128 + 128] + jnp.where(own, placed, 0.0)
            rows = pl.ds(pl.multiple_of((j + e) * 16, 16), 16)
            for r in range(8):
                out = (keep, away)[r // 4]
                out[r % 4, rows, :] += both[r * 16 : r * 16 + 16]


def ladder_call(meta, live, ts, us, v, wa, wb):
    smem = pl.BlockSpec(memory_space=pltpu.SMEM)
    vmem = pl.BlockSpec(memory_space=pltpu.VMEM)
    out = jax.ShapeDtypeStruct((4, 512, 128), F32)
    return pl.pallas_call(
        ladder_kernel,
        out_shape=(out, out),
        in_specs=[smem, smem] + [vmem] * 11,
        out_specs=(vmem, vmem),
        scratch_shapes=[
            pltpu.VMEM((2048, 512), BF16),
            pltpu.VMEM((128, 512), BF16),
            pltpu.VMEM((128, 512), F32),
        ],
        cost_estimate=pl.CostEstimate(flops=3_300_000_000, bytes_accessed=15_000_000, transcendentals=0),
        compiler_params=pltpu.CompilerParams(vmem_limit_bytes=48 << 20),
        name="ladder",
    )(meta, live, *ts, *us, v, wa, wb)


def finish_kernel(meta, occ, vir, occ_col, vir_row, p0, p1, p2, p3, p4, out):
    col, g = meta[3], meta[4]
    for il in range(4):
        for a in range(4):
            rows = pl.ds(il * 4 + a, 32, stride=16)
            total = ((p0[rows, :] + p1[rows, :]) + p2[rows, :]) + (p3[rows, :] + p4[rows, :])
            denom = ((vir[g * 4 + a] + vir_row[...]) - occ[col * 4 + il]) - occ_col[...]
            out[il * 32 : il * 32 + 32, a * 128 : a * 128 + 128] = (total / denom).astype(BF16)


def finish_call(meta, eps_occ, eps_vir, parts):
    smem = pl.BlockSpec(memory_space=pltpu.SMEM)
    vmem = pl.BlockSpec(memory_space=pltpu.VMEM)
    return pl.pallas_call(
        finish_kernel,
        out_shape=jax.ShapeDtypeStruct((128, 512), BF16),
        in_specs=[smem] * 3 + [vmem] * 7,
        out_specs=vmem,
        cost_estimate=pl.CostEstimate(flops=400_000, bytes_accessed=1_500_000, transcendentals=0),
        name="finish",
    )(
        meta,
        eps_occ,
        eps_vir,
        jnp.broadcast_to(eps_occ[:, None], (32, 128)),
        eps_vir[None, :],
        *parts,
    )


def local(amplitudes, ladder_ints, tile_live, cycle_direct, cycle_exchange, eps_occ, eps_vir):
    x0, c0, y0 = lax.axis_index("x"), lax.axis_index("core"), lax.axis_index("y")
    meta = jnp.stack([x0, c0, y0, lax.axis_index(C), lax.axis_index(G)]).astype(jnp.int32)
    mine = gather_z(amplitudes)
    both = jnp.stack([cycle_direct, cycle_exchange]).reshape(2, 4, 32, 4, 128)
    both = both.transpose(2, 0, 1, 3, 4).reshape(32, 2, 16, 128)
    both = lax.all_to_all(both, G, 0, 0, tiled=True)
    wa = jnp.stack([both] + [lax.ppermute(both, "x", shift(4, -s)) for s in (1, 2, 3)])
    wb = lax.ppermute(wa, "core", shift(2, 1))
    ts = [mine] + [lax.ppermute(mine, "y", shift(4, s)) for s in (1, 2, 3)]
    us = [t.reshape(8, 32, 16, 128).transpose(1, 0, 2, 3).reshape(32, 128, 128) for t in ts]
    keep, away = ladder_call(meta, tile_live, ts, us, ladder_ints, wa, wb)
    got = lax.ppermute(away, "core", shift(2, 1))
    parts = [keep[0], got[0]]
    for s in (1, 2, 3):
        parts.append(lax.ppermute(keep[s] + got[s], "x", shift(4, s)))
    return finish_call(meta, eps_occ, eps_vir, parts)


def solution(mesh):
    fine = Mesh(mesh.devices.reshape(4, 2, 4, 4, 2), ("zl", "zh", "y", "x", "core"))
    placed = (P(G, C), P(C, G), P(C, G), P(C, G), P(C, G), P(), P())
    return jax.shard_map(local, mesh=fine, in_specs=placed, out_specs=P(C, G), check_vma=False)
```

time: 196 us -> 126 us (0.64)
  local copies, waits for them, and re-layouts: 70.3 us -> 9.29 us
  matrix products: 16.1 us -> 0 us
  Pallas kernels: 0 us -> 13.7 us
  between operations: 13.7 us -> 0.23 us
  waiting for transfers between devices: 48.8 us -> 58.7 us
  starting transfers between devices: 42.7 us -> 40.4 us
    dynamic_update_slice x13 -> x8, local copies, waits for them, and re-layouts: 33.1 us -> 0.11 us  [gather_z(): lax.dynamic_update_slice(mine, part[None], ((z & 3) * 2 + (z >> 2), 0, 0))]
    dot_general x3 -> x0, matrix products: 16.1 us -> none  [the longest x1 7.87 us: local(): lax.dot_general(xm.reshape(128, occ, vir), four, (((1, 2), (0, 3)), ((),...]
    pallas_call x0 -> x2, Pallas kernels: none -> 13.7 us  [the longest x1 11.2 us: ladder_call(): pl.pallas_call(ladder_kernel, out_shape=(out, out), in_specs=[smem, smem]...]
    ppermute x14 -> x18, waiting for transfers between devices: 48.7 us -> 58.7 us  [the longest x3 29.5 us: local(): ts = [mine] + [lax.ppermute(mine, 'y', shift(4, s)) for s in (1, 2, 3)]]
    unnamed x13 -> x19, local copies, waits for them, and re-layouts: 11.2 us -> 2.24 us
    all_to_all x1 -> x0, starting transfers between devices: 8.73 us -> none  [local(): w = lax.all_to_all(w, C, 0, 0, tiled=True)]
    dot_general x2 -> x0, local copies, waits for them, and re-layouts: 8.24 us -> none  [local(): jnp.dot(wm, u1, preferred_element_type=jnp.float32)]
    transpose x7 -> x0, local copies, waits for them, and re-layouts: 7.87 us -> none  [the longest x2 2.24 us: local(): u1 = four.transpose(0, 2, 1, 3).reshape(512, occ * vir)]
  transfers between devices with their start and end apart: 17 -> 19, of which waited for: 8 -> 10; matrix products, arithmetic and copies ran while one was open for 21% -> 9% of each run, Pallas kernels for 0% -> 0%
where the time goes in v2:
time: 126 us; the launch traced here: 125 us
  waiting for transfers between devices  58.7 us (47%)
  starting transfers between devices  40.4 us (32%)
  Pallas kernels  13.7 us (11%)
  local copies, waits for them, and re-layouts  9.29 us (7%)
  other arithmetic  3.17 us (3%)
    ppermute x3, waiting for transfers between devices, local(): ts = [mine] + [lax.ppermute(mine, 'y', shift(4, s)) for s in (1, 2, 3)]  29.5 us
    pallas_call x1, Pallas kernels, ladder_call(): pl.pallas_call(ladder_kernel, out_shape=(out, out), in_specs=[smem, smem]...  11.2 us
    ppermute x4, waiting for transfers between devices, gather_z(): fwd = lax.ppermute(fwd, Z, z_shift(1))  11.1 us
    ppermute x3, waiting for transfers between devices, local(): parts.append(lax.ppermute(keep[s] + got[s], 'x', shift(4, s)))  10.5 us
    all_to_all x1, starting transfers between devices, local(): both = lax.all_to_all(both, G, 0, 0, tiled=True)  8.23 us
    ppermute x3, starting transfers between devices, gather_z(): bwd = lax.ppermute(bwd, Z, z_shift(-1))  8.13 us
    ppermute x3, starting transfers between devices, local(): ts = [mine] + [lax.ppermute(mine, 'y', shift(4, s)) for s in (1, 2, 3)]  6.26 us
    ppermute x3, waiting for transfers between devices, local(): lax.ppermute(both, 'x', shift(4, -s))  5.25 us
  transfers between devices with their start and end apart: 19, of which 10 were waited for; matrix products, arithmetic and copies ran while one was open for 9% of the time, Pallas kernels for 0%

profile of v2, /device:TPU:1, one launch (start us, length us, event | category | flops | bytes accessed | tf_op | source)
XLA Modules:
  0.0 125.4 jit_solution(17613507853981762831)
XLA Ops:
  0.0 2.5 %collective-permute-start = (bf16[32,2048]{1,0:T(8,128)(2,1)}, bf16[32,2048]{1,0:T(8,128)(2,1)S(1)}, u32[]{:S(2)}, u32[]{:S(2)}) collective-permute-start(bf16[32,2048]{1,0:T(8,128)(2,1)} %param.7), channel_id=1, source_target_pairs={{0,64},{64,128},{128,192},{192,32},{32,96},{96,160},{160,224},{224... | collective-permute-start | bytes 393224 | tf_op jit(solution)/shard_map/ppermute | solution.py:29
  2.5 4.0 %collective-permute-start.1 = (bf16[32,2048]{1,0:T(8,128)(2,1)}, bf16[32,2048]{1,0:T(8,128)(2,1)S(1)}, u32[]{:S(2)}, u32[]{:S(2)}) collective-permute-start(bf16[32,2048]{1,0:T(8,128)(2,1)} %param.7), channel_id=1, source_target_pairs={{0,224},{64,0},{128,64},{192,128},{32,192},{96,32},{160,96},{224,1... | collective-permute-start | bytes 393224 | tf_op jit(solution)/shard_map/ppermute | solution.py:32
  6.5 1.2 pad_maximum_fusion.1
  8.5 8.2 %all-to-all-start = ((bf16[32,2,16,128]{3,2,1,0:T(8,128)(2,1)}), bf16[32,2,16,128]{3,2,1,0:T(8,128)(2,1)S(1)}, u32[]{:S(2)}, u32[]{:S(2)}) async-start(bf16[32,2,16,128]{3,2,1,0:T(8,128)(2,1)} %bitcast.25), calls=%async_computation | async-start | bytes 524288 | tf_op jit(solution)/shard_map/all_to_all | solution.py:161
  16.9 1.3 %collective-permute-start.2 = (bf16[32,2048]{1,0:T(8,128)(2,1)S(1)}, bf16[32,2048]{1,0:T(8,128)(2,1)S(1)}, u32[]{:S(2)}, u32[]{:S(2)}) collective-permute-start(bf16[32,2048]{1,0:T(8,128)(2,1)S(1)} %collective-permute-done), channel_id=1, source_target_pairs={{0,64},{64,128},{128,192},{192,32},{32,96},{96,160},{160,224},{224... | collective-permute-start | bytes 393224 | tf_op jit(solution)/shard_map/ppermute | solution.py:29
  18.2 1.4 %collective-permute-start.3 = (bf16[32,2048]{1,0:T(8,128)(2,1)S(1)}, bf16[32,2048]{1,0:T(8,128)(2,1)S(1)}, u32[]{:S(2)}, u32[]{:S(2)}) collective-permute-start(bf16[32,2048]{1,0:T(8,128)(2,1)S(1)} %collective-permute-done.1), channel_id=1, source_target_pairs={{0,224},{64,0},{128,64},{192,128},{32,192},{96,32},{160,96},{224,1... | collective-permute-start | bytes 393224 | tf_op jit(solution)/shard_map/ppermute | solution.py:32
  19.7 7.5 %collective-permute-done.2 = bf16[32,2048]{1,0:T(8,128)(2,1)S(1)} collective-permute-done((bf16[32,2048]{1,0:T(8,128)(2,1)S(1)}, bf16[32,2048]{1,0:T(8,128)(2,1)S(1)}, u32[]{:S(2)}, u32[]{:S(2)}) %collective-permute-start.2) | collective-permute-done | bytes 131104 | tf_op jit(solution)/shard_map/ppermute | solution.py:29
  27.2 2.7 %collective-permute-start.5 = (bf16[32,2048]{1,0:T(8,128)(2,1)S(1)}, bf16[32,2048]{1,0:T(8,128)(2,1)S(1)}, u32[]{:S(2)}, u32[]{:S(2)}) collective-permute-start(bf16[32,2048]{1,0:T(8,128)(2,1)S(1)} %collective-permute-done.3), channel_id=1, source_target_pairs={{0,224},{64,0},{128,64},{192,128},{32,192},{96,32},{160,96},{224,1... | collective-permute-start | bytes 393224 | tf_op jit(solution)/shard_map/ppermute | solution.py:32
  29.9 2.3 %collective-permute-done.4 = bf16[32,2048]{1,0:T(8,128)(2,1)S(1)} collective-permute-done((bf16[32,2048]{1,0:T(8,128)(2,1)S(1)}, bf16[32,2048]{1,0:T(8,128)(2,1)S(1)}, u32[]{:S(2)}, u32[]{:S(2)}) %collective-permute-start.4) | collective-permute-done | bytes 131104 | tf_op jit(solution)/shard_map/ppermute | solution.py:29
  32.3 2.6 %collective-permute-start.10 = (bf16[32,2,16,128]{3,2,1,0:T(8,128)(2,1)S(1)}, bf16[32,2,16,128]{3,2,1,0:T(8,128)(2,1)S(1)}, u32[]{:S(2)}, u32[]{:S(2)}) collective-permute-start(bf16[32,2,16,128]{3,2,1,0:T(8,128)(2,1)S(1)} %all-to-all-done), channel_id=1, source_target_pairs={{0,6},{2,0},{4,2},{6,4},{1,7},{3,1},{5,3},{7,5},{8,14},{10,8},{12,... | collective-permute-start | bytes 786440 | tf_op jit(solution)/shard_map/ppermute | solution.py:162
  36.0 1.3 %collective-permute-done.6 = bf16[32,2048]{1,0:T(8,128)(2,1)S(1)} collective-permute-done((bf16[32,2048]{1,0:T(8,128)(2,1)S(1)}, bf16[32,2048]{1,0:T(8,128)(2,1)S(1)}, u32[]{:S(2)}, u32[]{:S(2)}) %collective-permute-start.6) | collective-permute-done | bytes 131104 | tf_op jit(solution)/shard_map/ppermute | solution.py:29
  37.3 1.7 %collective-permute-start.7 = (bf16[8,32,2048]{2,1,0:T(8,128)(2,1)S(1)}, bf16[8,32,2048]{2,1,0:T(8,128)(2,1)S(1)}, u32[]{:S(2)}, u32[]{:S(2)}) collective-permute-start(bf16[8,32,2048]{2,1,0:T(8,128)(2,1)S(1)} %bitcast_dynamic-update-slice_fusion.t0), channel_id=1, source_target_pairs={{0,8},{8,16},{16,24},{24,0},{1,9},{9,17},{17,25},{25,1},{2,10},{10... | collective-permute-start | bytes 3145736 | tf_op jit(solution)/shard_map/ppermute | solution.py:164
  39.0 2.5 %collective-permute-start.8 = (bf16[8,32,2048]{2,1,0:T(8,128)(2,1)S(1)}, bf16[8,32,2048]{2,1,0:T(8,128)(2,1)S(1)}, u32[]{:S(2)}, u32[]{:S(2)}) collective-permute-start(bf16[8,32,2048]{2,1,0:T(8,128)(2,1)S(1)} %bitcast_dynamic-update-slice_fusion.t0), channel_id=1, source_target_pairs={{0,16},{8,24},{16,0},{24,8},{1,17},{9,25},{17,1},{25,9},{2,18},{10... | collective-permute-start | bytes 3145736 | tf_op jit(solution)/shard_map/ppermute | solution.py:164
  41.5 2.1 %collective-permute-start.9 = (bf16[8,32,2048]{2,1,0:T(8,128)(2,1)S(1)}, bf16[8,32,2048]{2,1,0:T(8,128)(2,1)}, u32[]{:S(2)}, u32[]{:S(2)}) collective-permute-start(bf16[8,32,2048]{2,1,0:T(8,128)(2,1)S(1)} %bitcast_dynamic-update-slice_fusion.t0), channel_id=1, source_target_pairs={{0,24},{8,0},{16,8},{24,16},{1,25},{9,1},{17,9},{25,17},{2,26},{10... | collective-permute-start | bytes 3145736 | tf_op jit(solution)/shard_map/ppermute | solution.py:164
  43.6 5.2 %collective-permute-done.12 = bf16[32,2,16,128]{3,2,1,0:T(8,128)(2,1)S(1)} collective-permute-done((bf16[32,2,16,128]{3,2,1,0:T(8,128)(2,1)S(1)}, bf16[32,2,16,128]{3,2,1,0:T(8,128)(2,1)S(1)}, u32[]{:S(2)}, u32[]{:S(2)}) %collective-permute-start.12) | collective-permute-done | bytes 262176 | tf_op jit(solution)/shard_map/ppermute | solution.py:162
  49.9 1.9 %collective-permute-start.13 = (bf16[4,32,2,16,128]{4,3,2,1,0:T(8,128)(2,1)}, bf16[4,32,2,16,128]{4,3,2,1,0:T(8,128)(2,1)}, u32[]{:S(2)}, u32[]{:S(2)}) collective-permute-start(bf16[4,32,2,16,128]{4,3,2,1,0:T(8,128)(2,1)} %pad_maximum_fusion.wa), channel_id=1, source_target_pairs={{0,1},{1,0},{2,3},{3,2},{4,5},{5,4},{6,7},{7,6},{8,9},{9,8},{10,11... | collective-permute-start | bytes 3145736 | tf_op jit(solution)/shard_map/ppermute | solution.py:163
  52.2 1.3 %copy.8 = bf16[8,32,16,128]{3,2,0,1:T(8,128)(2,1)} copy(bf16[8,32,16,128]{3,2,1,0:T(8,128)(2,1)S(1)} %bitcast.72) | data formatting | bytes 2097152 | tf_op jit(solution)/shard_map/reshape | solution.py:165
  53.5 5.9 %collective-permute-done.7.t1 = bf16[8,32,2048]{2,1,0:T(8,128)(2,1)S(1)} collective-permute-done((bf16[8,32,2048]{2,1,0:T(8,128)(2,1)S(1)}, bf16[8,32,2048]{2,1,0:T(8,128)(2,1)S(1)}, u32[]{:S(2)}, u32[]{:S(2)}) %collective-permute-start.7) | collective-permute-done | bytes 1048608 | tf_op jit(solution)/shard_map/ppermute | solution.py:164
  59.6 1.3 %copy.9 = bf16[8,32,16,128]{3,2,0,1:T(8,128)(2,1)} copy(bf16[8,32,16,128]{3,2,1,0:T(8,128)(2,1)S(1)} %bitcast.73) | data formatting | bytes 2097152 | tf_op jit(solution)/shard_map/reshape | solution.py:165
  60.9 22.4 %collective-permute-done.8.t2 = bf16[8,32,2048]{2,1,0:T(8,128)(2,1)S(1)} collective-permute-done((bf16[8,32,2048]{2,1,0:T(8,128)(2,1)S(1)}, bf16[8,32,2048]{2,1,0:T(8,128)(2,1)S(1)}, u32[]{:S(2)}, u32[]{:S(2)}) %collective-permute-start.8) | collective-permute-done | bytes 1048608 | tf_op jit(solution)/shard_map/ppermute | solution.py:164
  83.5 1.3 %copy.10 = bf16[8,32,16,128]{3,2,0,1:T(8,128)(2,1)} copy(bf16[8,32,16,128]{3,2,1,0:T(8,128)(2,1)S(1)} %bitcast.74) | data formatting | bytes 2097152 | tf_op jit(solution)/shard_map/reshape | solution.py:165
  84.7 1.3 %collective-permute-done.9.t3 = bf16[8,32,2048]{2,1,0:T(8,128)(2,1)} collective-permute-done((bf16[8,32,2048]{2,1,0:T(8,128)(2,1)S(1)}, bf16[8,32,2048]{2,1,0:T(8,128)(2,1)}, u32[]{:S(2)}, u32[]{:S(2)}) %collective-permute-start.9) | collective-permute-done | bytes 1048608 | tf_op jit(solution)/shard_map/ppermute | solution.py:164
  86.0 1.4 %copy.19 = bf16[32,8,16,128]{3,2,1,0:T(8,128)(2,1)S(1)} copy(bf16[32,8,16,128]{3,1,2,0:T(8,128)(2,1)} %bitcast.53) | data formatting | bytes 2097152
  87.5 1.3 %copy.11 = bf16[8,32,16,128]{3,2,0,1:T(8,128)(2,1)} copy(bf16[8,32,16,128]{3,2,1,0:T(8,128)(2,1)S(1)} %bitcast.75) | data formatting | bytes 2097152 | tf_op jit(solution)/shard_map/reshape | solution.py:165
  88.7 11.2 %ladder.1 = (f32[4,512,128]{2,1,0:T(8,128)S(1)}, f32[4,512,128]{2,1,0:T(8,128)S(1)}) custom-call(s32[5]{0:T(128)S(1)} %stack.47.meta, s32[16,4]{1,0:T(8,128)S(1)} %copy.14.live, bf16[8,32,2048]{2,1,0:T(8,128)(2,1)S(1)} %bitcast_dynamic-update-slice_fusion.t0, bf16[8,32,2048]{2,1,0:T(8,128)(2,1)S(1)} %collective-permute-done.7.t1, ...), custom_call_target="tpu_custom_call" | custom-call | flops 3300000000 | bytes 15000000 | tf_op jit(solution)/shard_map/ladder/pallas_call | solution.py:109
  100.0 3.6 %collective-permute-start.14 = (f32[4,512,128]{2,1,0:T(8,128)S(1)}, f32[4,512,128]{2,1,0:T(8,128)S(1)}, u32[]{:S(2)}, u32[]{:S(2)}) collective-permute-start(f32[4,512,128]{2,1,0:T(8,128)S(1)} %get-tuple-element.8), channel_id=1, source_target_pairs={{0,1},{1,0},{2,3},{3,2},{4,5},{5,4},{6,7},{7,6},{8,9},{9,8},{10,11... | collective-permute-start | bytes 3145736 | tf_op jit(solution)/shard_map/ppermute | solution.py:167
  103.6 2.3 %collective-permute-done.14 = f32[4,512,128]{2,1,0:T(8,128)S(1)} collective-permute-done((f32[4,512,128]{2,1,0:T(8,128)S(1)}, f32[4,512,128]{2,1,0:T(8,128)S(1)}, u32[]{:S(2)}, u32[]{:S(2)}) %collective-permute-start.14) | collective-permute-done | bytes 1048608 | tf_op jit(solution)/shard_map/ppermute | solution.py:167
  106.8 1.2 collective-permute-start.15
  108.0 2.4 %collective-permute-start.16 = (f32[512,128]{1,0:T(8,128)S(1)}, f32[512,128]{1,0:T(8,128)S(1)}, u32[]{:S(2)}, u32[]{:S(2)}) collective-permute-start(f32[512,128]{1,0:T(8,128)S(1)} %get-tuple-element.10), channel_id=1, source_target_pairs={{0,4},{2,6},{4,0},{6,2},{1,5},{3,7},{5,1},{7,3},{8,12},{10,14},{12... | collective-permute-start | bytes 786440 | tf_op jit(solution)/shard_map/ppermute | solution.py:170
  111.6 3.9 %collective-permute-done.15.p2 = f32[512,128]{1,0:T(8,128)S(1)} collective-permute-done((f32[512,128]{1,0:T(8,128)S(1)}, f32[512,128]{1,0:T(8,128)S(1)}, u32[]{:S(2)}, u32[]{:S(2)}) %collective-permute-start.15) | collective-permute-done | bytes 262176 | tf_op jit(solution)/shard_map/ppermute | solution.py:170
  115.6 6.6 %collective-permute-done.16.p3 = f32[512,128]{1,0:T(8,128)S(1)} collective-permute-done((f32[512,128]{1,0:T(8,128)S(1)}, f32[512,128]{1,0:T(8,128)S(1)}, u32[]{:S(2)}, u32[]{:S(2)}) %collective-permute-start.16) | collective-permute-done | bytes 262176 | tf_op jit(solution)/shard_map/ppermute | solution.py:170
  123.0 2.4 %finish.1 = bf16[128,512]{1,0:T(8,128)(2,1)} custom-call(s32[5]{0:T(128)} %copy-done, f32[32]{0:T(128)} %occ.1, f32[128]{0:T(128)} %vir.1, f32[32,128]{1,0:T(8,128)} %broadcast_in_dim.36.occ_col, f32[1,128]{1,0:T(1,128)} %bitcast.86, f32[512,128]{1,0:T(8,128)} %get-tuple-element.12.p0, f32[512,128]{1,0:T(8,128)} %get-tuple-element.13.p1, ...), custom_call_target="tpu_custom_call" | custom-call | flops 400000 | bytes 1500000 | tf_op jit(solution)/shard_map/finish/pallas_call | solution.py:138
  (46 shorter events, 7.0 us)
Async XLA Ops:
  0.0 16.8 %copy-start.4 = (bf16[32,2048]{1,0:T(8,128)(2,1)S(1)}, bf16[32,2048]{1,0:T(8,128)(2,1)}, u32[]{:S(2)}) copy-start(bf16[32,2048]{1,0:T(8,128)(2,1)} %param.7) | copy-start | bytes 393220
  0.0 16.9 %collective-permute-start = (bf16[32,2048]{1,0:T(8,128)(2,1)}, bf16[32,2048]{1,0:T(8,128)(2,1)S(1)}, u32[]{:S(2)}, u32[]{:S(2)}) collective-permute-start(bf16[32,2048]{1,0:T(8,128)(2,1)} %param.7), channel_id=1, source_target_pairs={{0,64},{64,128},{128,192},{192,32},{32,96},{96,160},{160,224},{224... | collective-permute-start | bytes 393224 | tf_op jit(solution)/shard_map/ppermute | solution.py:29
  2.5 15.8 %collective-permute-start.1 = (bf16[32,2048]{1,0:T(8,128)(2,1)}, bf16[32,2048]{1,0:T(8,128)(2,1)S(1)}, u32[]{:S(2)}, u32[]{:S(2)}) collective-permute-start(bf16[32,2048]{1,0:T(8,128)(2,1)} %param.7), channel_id=1, source_target_pairs={{0,224},{64,0},{128,64},{192,128},{32,192},{96,32},{160,96},{224,1... | collective-permute-start | bytes 393224 | tf_op jit(solution)/shard_map/ppermute | solution.py:32
  8.5 23.8 %all-to-all-start = ((bf16[32,2,16,128]{3,2,1,0:T(8,128)(2,1)}), bf16[32,2,16,128]{3,2,1,0:T(8,128)(2,1)S(1)}, u32[]{:S(2)}, u32[]{:S(2)}) async-start(bf16[32,2,16,128]{3,2,1,0:T(8,128)(2,1)} %bitcast.25), calls=%async_computation | async-start | bytes 524288 | tf_op jit(solution)/shard_map/all_to_all | solution.py:161
  16.9 34.9 %copy-start.6 = (s32[16,4]{0,1:T(4,128)S(1)}, s32[16,4]{0,1:T(4,128)}, u32[]{:S(2)}) copy-start(s32[16,4]{0,1:T(4,128)} %param.9) | copy-start | bytes 772
  16.9 10.3 %collective-permute-start.2 = (bf16[32,2048]{1,0:T(8,128)(2,1)S(1)}, bf16[32,2048]{1,0:T(8,128)(2,1)S(1)}, u32[]{:S(2)}, u32[]{:S(2)}) collective-permute-start(bf16[32,2048]{1,0:T(8,128)(2,1)S(1)} %collective-permute-done), channel_id=1, source_target_pairs={{0,64},{64,128},{128,192},{192,32},{32,96},{96,160},{160,224},{224... | collective-permute-start | bytes 393224 | tf_op jit(solution)/shard_map/ppermute | solution.py:29
  18.2 9.0 %collective-permute-start.3 = (bf16[32,2048]{1,0:T(8,128)(2,1)S(1)}, bf16[32,2048]{1,0:T(8,128)(2,1)S(1)}, u32[]{:S(2)}, u32[]{:S(2)}) collective-permute-start(bf16[32,2048]{1,0:T(8,128)(2,1)S(1)} %collective-permute-done.1), channel_id=1, source_target_pairs={{0,224},{64,0},{128,64},{192,128},{32,192},{96,32},{160,96},{224,1... | collective-permute-start | bytes 393224 | tf_op jit(solution)/shard_map/ppermute | solution.py:32
  27.2 5.0 %collective-permute-start.4 = (bf16[32,2048]{1,0:T(8,128)(2,1)S(1)}, bf16[32,2048]{1,0:T(8,128)(2,1)S(1)}, u32[]{:S(2)}, u32[]{:S(2)}) collective-permute-start(bf16[32,2048]{1,0:T(8,128)(2,1)S(1)} %collective-permute-done.2), channel_id=1, source_target_pairs={{0,64},{64,128},{128,192},{192,32},{32,96},{96,160},{160,224},{224... | collective-permute-start | bytes 393224 | tf_op jit(solution)/shard_map/ppermute | solution.py:29
  27.2 5.0 %collective-permute-start.5 = (bf16[32,2048]{1,0:T(8,128)(2,1)S(1)}, bf16[32,2048]{1,0:T(8,128)(2,1)S(1)}, u32[]{:S(2)}, u32[]{:S(2)}) collective-permute-start(bf16[32,2048]{1,0:T(8,128)(2,1)S(1)} %collective-permute-done.3), channel_id=1, source_target_pairs={{0,224},{64,0},{128,64},{192,128},{32,192},{96,32},{160,96},{224,1... | collective-permute-start | bytes 393224 | tf_op jit(solution)/shard_map/ppermute | solution.py:32
  32.2 5.0 %collective-permute-start.6 = (bf16[32,2048]{1,0:T(8,128)(2,1)S(1)}, bf16[32,2048]{1,0:T(8,128)(2,1)S(1)}, u32[]{:S(2)}, u32[]{:S(2)}) collective-permute-start(bf16[32,2048]{1,0:T(8,128)(2,1)S(1)} %collective-permute-done.4), channel_id=1, source_target_pairs={{0,64},{64,128},{128,192},{192,32},{32,96},{96,160},{160,224},{224... | collective-permute-start | bytes 393224 | tf_op jit(solution)/shard_map/ppermute | solution.py:29
  32.3 9.2 %collective-permute-start.10 = (bf16[32,2,16,128]{3,2,1,0:T(8,128)(2,1)S(1)}, bf16[32,2,16,128]{3,2,1,0:T(8,128)(2,1)S(1)}, u32[]{:S(2)}, u32[]{:S(2)}) collective-permute-start(bf16[32,2,16,128]{3,2,1,0:T(8,128)(2,1)S(1)} %all-to-all-done), channel_id=1, source_target_pairs={{0,6},{2,0},{4,2},{6,4},{1,7},{3,1},{5,3},{7,5},{8,14},{10,8},{12,... | collective-permute-start | bytes 786440 | tf_op jit(solution)/shard_map/ppermute | solution.py:162
  34.9 8.7 %collective-permute-start.11 = (bf16[32,2,16,128]{3,2,1,0:T(8,128)(2,1)S(1)}, bf16[32,2,16,128]{3,2,1,0:T(8,128)(2,1)S(1)}, u32[]{:S(2)}, u32[]{:S(2)}) collective-permute-start(bf16[32,2,16,128]{3,2,1,0:T(8,128)(2,1)S(1)} %all-to-all-done), channel_id=1, source_target_pairs={{0,4},{2,6},{4,0},{6,2},{1,5},{3,7},{5,1},{7,3},{8,12},{10,14},{12... | collective-permute-start | bytes 786440 | tf_op jit(solution)/shard_map/ppermute | solution.py:162
  35.4 13.4 %collective-permute-start.12 = (bf16[32,2,16,128]{3,2,1,0:T(8,128)(2,1)S(1)}, bf16[32,2,16,128]{3,2,1,0:T(8,128)(2,1)S(1)}, u32[]{:S(2)}, u32[]{:S(2)}) collective-permute-start(bf16[32,2,16,128]{3,2,1,0:T(8,128)(2,1)S(1)} %all-to-all-done), channel_id=1, source_target_pairs={{0,2},{2,4},{4,6},{6,0},{1,3},{3,5},{5,7},{7,1},{8,10},{10,12},{12... | collective-permute-start | bytes 786440 | tf_op jit(solution)/shard_map/ppermute | solution.py:162
  37.3 22.0 %collective-permute-start.7 = (bf16[8,32,2048]{2,1,0:T(8,128)(2,1)S(1)}, bf16[8,32,2048]{2,1,0:T(8,128)(2,1)S(1)}, u32[]{:S(2)}, u32[]{:S(2)}) collective-permute-start(bf16[8,32,2048]{2,1,0:T(8,128)(2,1)S(1)} %bitcast_dynamic-update-slice_fusion.t0), channel_id=1, source_target_pairs={{0,8},{8,16},{16,24},{24,0},{1,9},{9,17},{17,25},{25,1},{2,10},{10... | collective-permute-start | bytes 3145736 | tf_op jit(solution)/shard_map/ppermute | solution.py:164
  39.0 44.3 %collective-permute-start.8 = (bf16[8,32,2048]{2,1,0:T(8,128)(2,1)S(1)}, bf16[8,32,2048]{2,1,0:T(8,128)(2,1)S(1)}, u32[]{:S(2)}, u32[]{:S(2)}) collective-permute-start(bf16[8,32,2048]{2,1,0:T(8,128)(2,1)S(1)} %bitcast_dynamic-update-slice_fusion.t0), channel_id=1, source_target_pairs={{0,16},{8,24},{16,0},{24,8},{1,17},{9,25},{17,1},{25,9},{2,18},{10... | collective-permute-start | bytes 3145736 | tf_op jit(solution)/shard_map/ppermute | solution.py:164
  41.5 44.6 %collective-permute-start.9 = (bf16[8,32,2048]{2,1,0:T(8,128)(2,1)S(1)}, bf16[8,32,2048]{2,1,0:T(8,128)(2,1)}, u32[]{:S(2)}, u32[]{:S(2)}) collective-permute-start(bf16[8,32,2048]{2,1,0:T(8,128)(2,1)S(1)} %bitcast_dynamic-update-slice_fusion.t0), channel_id=1, source_target_pairs={{0,24},{8,0},{16,8},{24,16},{1,25},{9,1},{17,9},{25,17},{2,26},{10... | collective-permute-start | bytes 3145736 | tf_op jit(solution)/shard_map/ppermute | solution.py:164
  49.9 38.8 %collective-permute-start.13 = (bf16[4,32,2,16,128]{4,3,2,1,0:T(8,128)(2,1)}, bf16[4,32,2,16,128]{4,3,2,1,0:T(8,128)(2,1)}, u32[]{:S(2)}, u32[]{:S(2)}) collective-permute-start(bf16[4,32,2,16,128]{4,3,2,1,0:T(8,128)(2,1)} %pad_maximum_fusion.wa), channel_id=1, source_target_pairs={{0,1},{1,0},{2,3},{3,2},{4,5},{5,4},{6,7},{7,6},{8,9},{9,8},{10,11... | collective-permute-start | bytes 3145736 | tf_op jit(solution)/shard_map/ppermute | solution.py:163
  52.0 36.8 %copy-start = (s32[5]{0:T(128)}, s32[5]{0:T(128)S(1)}, u32[]{:S(2)}) copy-start(s32[5]{0:T(128)S(1)} %stack.47.meta) | copy-start | bytes 64
  100.0 22.2 %copy-start.5 = (f32[32]{0:T(128)S(1)}, f32[32]{0:T(128)}, u32[]{:S(2)}) copy-start(f32[32]{0:T(128)} %occ.1) | copy-start | bytes 388
  100.0 5.9 %collective-permute-start.14 = (f32[4,512,128]{2,1,0:T(8,128)S(1)}, f32[4,512,128]{2,1,0:T(8,128)S(1)}, u32[]{:S(2)}, u32[]{:S(2)}) collective-permute-start(f32[4,512,128]{2,1,0:T(8,128)S(1)} %get-tuple-element.8), channel_id=1, source_target_pairs={{0,1},{1,0},{2,3},{3,2},{4,5},{5,4},{6,7},{7,6},{8,9},{9,8},{10,11... | collective-permute-start | bytes 3145736 | tf_op jit(solution)/shard_map/ppermute | solution.py:167
  106.8 8.7 %collective-permute-start.15 = (f32[512,128]{1,0:T(8,128)S(1)}, f32[512,128]{1,0:T(8,128)S(1)}, u32[]{:S(2)}, u32[]{:S(2)}) collective-permute-start(f32[512,128]{1,0:T(8,128)S(1)} %get-tuple-element.11), channel_id=1, source_target_pairs={{0,2},{2,4},{4,6},{6,0},{1,3},{3,5},{5,7},{7,1},{8,10},{10,12},{12... | collective-permute-start | bytes 786440 | tf_op jit(solution)/shard_map/ppermute | solution.py:170
  108.0 14.1 %collective-permute-start.16 = (f32[512,128]{1,0:T(8,128)S(1)}, f32[512,128]{1,0:T(8,128)S(1)}, u32[]{:S(2)}, u32[]{:S(2)}) collective-permute-start(f32[512,128]{1,0:T(8,128)S(1)} %get-tuple-element.10), channel_id=1, source_target_pairs={{0,4},{2,6},{4,0},{6,2},{1,5},{3,7},{5,1},{7,3},{8,12},{10,14},{12... | collective-permute-start | bytes 786440 | tf_op jit(solution)/shard_map/ppermute | solution.py:170
  110.5 11.7 %collective-permute-start.17 = (f32[512,128]{1,0:T(8,128)S(1)}, f32[512,128]{1,0:T(8,128)S(1)}, u32[]{:S(2)}, u32[]{:S(2)}) collective-permute-start(f32[512,128]{1,0:T(8,128)S(1)} %get-tuple-element.9), channel_id=1, source_target_pairs={{0,6},{2,0},{4,2},{6,4},{1,7},{3,1},{5,3},{7,5},{8,14},{10,8},{12,... | collective-permute-start | bytes 786440 | tf_op jit(solution)/shard_map/ppermute | solution.py:170
  115.6 7.4 %copy-start.1 = (f32[512,128]{1,0:T(8,128)}, f32[512,128]{1,0:T(8,128)S(1)}, u32[]{:S(2)}) copy-start(f32[512,128]{1,0:T(8,128)S(1)} %collective-permute-done.15.p2) | copy-start | bytes 786436
  122.2 0.8 copy-start.2
  122.2 0.8 copy-start.3

commit v3 on v2

v3 whole, which is shorter than its diff:
```python
import jax
import jax.numpy as jnp
from jax import lax
from jax.experimental import pallas as pl
from jax.experimental.pallas import tpu as pltpu
from jax.sharding import Mesh, PartitionSpec as P

G = ("zl", "zh", "y")
C = ("x", "core")
Z = ("zl", "zh")
J = 16
F32 = jnp.float32
BF16 = jnp.bfloat16


def shift(n, s):
    return [(i, (i + s) % n) for i in range(n)]


def z_shift(s):
    at = lambda z: (z % 4) * 2 + z // 4
    return [(at(z), at((z + s) % 8)) for z in range(8)]


def ladder_kernel(meta, live, t0, t1, t2, t3, u0, u1, u2, u3, v, wa, wb, keep, away, vm, wm, o2):
    x0, c0, y0, col = meta[0], meta[1], meta[2], meta[3]
    ts, us = (t0, t1, t2, t3), (u0, u1, u2, u3)
    ys = [(y0 + 4 - q) & 3 for q in range(4)]

    @pl.loop(0, 16)
    def _(kt):
        rows = pl.ds(pl.multiple_of(kt * 128, 128), 128)
        for n in range(4):
            tile = v[rows, n * 128 : n * 128 + 128]
            vm[rows, n * 128 : n * 128 + 128] = jnp.where(live[kt, n] != 0, tile, jnp.zeros_like(tile))

    for q in range(0, 4, 2):
        rows = []
        for e in range(2):
            for r in range(8):
                h = (((x0 + r % 4) & 3) << 1) | (c0 ^ (r // 4))
                rows.append(ts[q + e][h])
        part = jnp.dot(jnp.concatenate(rows, 0), vm[...], preferred_element_type=F32)
        for e in range(2):
            for r in range(8):
                out = (keep, away)[r // 4]
                at = (e * 8 + r) * J
                for a in range(4):
                    out[r % 4, pl.ds(ys[q + e] * 4 + a, J, stride=16), :] = part[
                        at : at + J, a * 128 : a * 128 + 128
                    ]

    lane = lax.broadcasted_iota(jnp.int32, (128, 128), 1)
    acc = jnp.zeros((J * 16, 128), F32)
    for q in range(4):
        w_all = jnp.zeros((128, 128), F32)
        xs = []
        for h in range(8):
            k = h * 4 + ys[q]
            wk = jnp.concatenate([wa[s, k, 0] for s in range(4)] + [wb[s, k, 0] for s in range(4)], 0)
            wk = pltpu.roll(wk.astype(F32), (16 * h + 128 - 16 * col) & 127, 1)
            w_all = jnp.where((lane >> 4) == h, wk, w_all)
            xs.append(jnp.concatenate([wa[s, k, 1] for s in range(4)] + [wb[s, k, 1] for s in range(4)], 0))
        wm[:, q * 128 : q * 128 + 128] = w_all.astype(BF16)
        for h in range(0, 8, 2):
            lhs = jnp.concatenate(
                [us[q][:, (h + e) * 16 : (h + e) * 16 + 16, :].reshape(J * 16, 128) for e in range(2)], 1
            )
            rhs = jnp.concatenate([xs[h], xs[h + 1]], 1)
            acc = acc + lax.dot_general(lhs, rhs, (((1,), (1,)), ((), ())), preferred_element_type=F32)
    o2[...] = acc.T

    own = (lane >> 4) == col

    @pl.loop(0, J // 2)
    def _(jj):
        j = jj * 2
        rhs = jnp.concatenate(
            [jnp.concatenate([us[q][j + e] for q in range(4)], 0) for e in range(2)], 1
        )
        one = jnp.dot(wm[...], rhs, preferred_element_type=F32)
        two = o2[:, pl.ds(pl.multiple_of((jj >> 2) * 128, 128), 128)]
        for e in range(2):
            placed = pltpu.roll(two, (16 * col + 128 - 16 * ((j + e) & 7)) & 127, 1)
            both = one[:, e * 128 : e * 128 + 128] + jnp.where(own, placed, 0.0)
            rows = pl.ds(pl.multiple_of((j + e) * 16, 16), 16)
            for r in range(8):
                out = (keep, away)[r // 4]
                out[r % 4, rows, :] += both[r * 16 : r * 16 + 16]


def ladder_call(meta, live, ts, us, v, wa, wb):
    smem = pl.BlockSpec(memory_space=pltpu.SMEM)
    vmem = pl.BlockSpec(memory_space=pltpu.VMEM)
    out = jax.ShapeDtypeStruct((4, J * 16, 128), F32)
    return pl.pallas_call(
        ladder_kernel,
        out_shape=(out, out),
        in_specs=[smem, smem] + [vmem] * 11,
        out_specs=(vmem, vmem),
        scratch_shapes=[
            pltpu.VMEM((2048, 512), BF16),
            pltpu.VMEM((128, 512), BF16),
            pltpu.VMEM((128, J * 16), F32),
        ],
        cost_estimate=pl.CostEstimate(flops=1_650_000_000, bytes_accessed=10_000_000, transcendentals=0),
        compiler_params=pltpu.CompilerParams(vmem_limit_bytes=24 << 20),
        name="ladder",
    )(meta, live, *ts, *us, v, wa, wb)


def finish_kernel(meta, occ, vir, occ_col, vir_row, *refs):
    col, g = meta[3], meta[4]
    out = refs[-1]
    for half in range(32 // J):
        p0, p1, p2, p3, p4 = refs[half * 5 : half * 5 + 5]
        for il in range(4):
            for a in range(4):
                rows = pl.ds(il * 4 + a, J, stride=16)
                total = ((p0[rows, :] + p1[rows, :]) + p2[rows, :]) + (p3[rows, :] + p4[rows, :])
                denom = ((vir[g * 4 + a] + vir_row[...]) - occ[col * 4 + il]) - occ_col[
                    half * J : half * J + J, :
                ]
                at = il * 32 + half * J
                out[at : at + J, a * 128 : a * 128 + 128] = (total / denom).astype(BF16)


def finish_call(meta, eps_occ, eps_vir, parts):
    smem = pl.BlockSpec(memory_space=pltpu.SMEM)
    vmem = pl.BlockSpec(memory_space=pltpu.VMEM)
    return pl.pallas_call(
        finish_kernel,
        out_shape=jax.ShapeDtypeStruct((128, 512), BF16),
        in_specs=[smem] * 3 + [vmem] * (2 + len(parts)),
        out_specs=vmem,
        cost_estimate=pl.CostEstimate(flops=400_000, bytes_accessed=1_500_000, transcendentals=0),
        name="finish",
    )(
        meta,
        eps_occ,
        eps_vir,
        jnp.broadcast_to(eps_occ[:, None], (32, 128)),
        eps_vir[None, :],
        *parts,
    )


def local(amplitudes, ladder_ints, tile_live, cycle_direct, cycle_exchange, eps_occ, eps_vir):
    x0, c0, y0 = lax.axis_index("x"), lax.axis_index("core"), lax.axis_index("y")
    meta = jnp.stack([x0, c0, y0, lax.axis_index(C), lax.axis_index(G)]).astype(jnp.int32)
    copies = [jnp.broadcast_to(amplitudes[n * J : n * J + J], (8, J, 2048)) for n in range(32 // J)]
    both = jnp.stack([cycle_direct, cycle_exchange]).reshape(2, 4, 32, 4, 128)
    both = both.transpose(2, 0, 1, 3, 4).reshape(32, 2, 16, 128)
    both = lax.all_to_all(both, G, 0, 0, tiled=True)
    xs = [both] + [lax.ppermute(both, "x", shift(4, -s)) for s in (1, 2, 3)]
    mines = [lax.all_to_all(c, Z, 0, 0, tiled=True) for c in copies]
    tss = [[mine] + [lax.ppermute(mine, "y", shift(4, s)) for s in (1, 2, 3)] for mine in mines]
    *xs, tss[0][1] = lax.optimization_barrier((*xs, tss[0][1]))
    wa = jnp.stack(xs)
    wb = lax.ppermute(wa, "core", shift(2, 1))
    parts = []
    for ts in tss:
        us = [t.reshape(8, J, 16, 128).transpose(1, 0, 2, 3).reshape(J, 128, 128) for t in ts]
        keep, away = ladder_call(meta, tile_live, ts, us, ladder_ints, wa, wb)
        away, *parts = lax.optimization_barrier((away, *parts))
        got = lax.ppermute(away, "core", shift(2, 1))
        sums = [keep[s] + got[s] for s in (1, 2, 3)]
        *sums, wa = lax.optimization_barrier((*sums, wa))
        parts += [keep[0], got[0]]
        parts += [lax.ppermute(block, "x", shift(4, s)) for s, block in zip((1, 2, 3), sums)]
    return finish_call(meta, eps_occ, eps_vir, parts)


def solution(mesh):
    fine = Mesh(mesh.devices.reshape(4, 2, 4, 4, 2), ("zl", "zh", "y", "x", "core"))
    placed = (P(G, C), P(C, G), P(C, G), P(C, G), P(C, G), P(), P())
    return jax.shard_map(local, mesh=fine, in_specs=placed, out_specs=P(C, G), check_vma=False)
```

time: 126 us -> 142 us (1.13)
  waiting for transfers between devices: 58.7 us -> 71.4 us
  starting transfers between devices: 40.4 us -> 43.7 us
    all_to_all x0 -> x2, waiting for transfers between devices: none -> 20.3 us  [local(): mines = [lax.all_to_all(c, Z, 0, 0, tiled=True) for c in copies]]
    ppermute x16 -> x15, waiting for transfers between devices: 56.4 us -> 39.5 us  [the longest x6 19.4 us: local(): lax.ppermute(mine, 'y', shift(4, s))]
    all_to_all x0 -> x2, starting transfers between devices: none -> 12.5 us  [local(): mines = [lax.all_to_all(c, Z, 0, 0, tiled=True) for c in copies]]
    ppermute x16 -> x15, starting transfers between devices: 26.7 us -> 15.9 us  [the longest x6 6.19 us: local(): lax.ppermute(block, 'x', shift(4, s))]
    all_to_all x1, waiting for transfers between devices: 0.01 us -> 10.1 us  [local(): both = lax.all_to_all(both, G, 0, 0, tiled=True)]
    reshape x4 -> x8, local copies, waits for them, and re-layouts: 5.12 us -> 1.19 us  [local(): t.reshape(8, J, 16, 128).transpose(1, 0, 2, 3).reshape(J, 128, 128)]
    unnamed x19 -> x35, local copies, waits for them, and re-layouts: 2.24 us -> 5.07 us
    all_to_all x1, starting transfers between devices: 8.23 us -> 9.91 us  [local(): both = lax.all_to_all(both, G, 0, 0, tiled=True)]
  transfers between devices with their start and end apart: 19 -> 21, of which waited for: 10 -> 12; matrix products, arithmetic and copies ran while one was open for 9% -> 6% of each run, Pallas kernels for 0% -> 7%
where the time goes in v3:
time: 142 us; the launch traced here: 141 us
  waiting for transfers between devices  71.4 us (50%)
  starting transfers between devices  43.7 us (31%)
  Pallas kernels  12.7 us (9%)
  local copies, waits for them, and re-layouts  10.4 us (7%)
  other arithmetic  2.83 us (2%)
    all_to_all x2, waiting for transfers between devices, local(): mines = [lax.all_to_all(c, Z, 0, 0, tiled=True) for c in copies]  20.3 us
    ppermute x6, waiting for transfers between devices, local(): lax.ppermute(mine, 'y', shift(4, s))  19.4 us
    ppermute x3, waiting for transfers between devices, local(): xs = [both] + [lax.ppermute(both, 'x', shift(4, -s)) for s in (1, 2, 3)]  13.3 us
    all_to_all x2, starting transfers between devices, local(): mines = [lax.all_to_all(c, Z, 0, 0, tiled=True) for c in copies]  12.5 us
    pallas_call x2, Pallas kernels, ladder_call(): pl.pallas_call(ladder_kernel, out_shape=(out, out), in_specs=[smem, smem]...  10.2 us
    all_to_all x1, waiting for transfers between devices, local(): both = lax.all_to_all(both, G, 0, 0, tiled=True)  10.1 us
    all_to_all x1, starting transfers between devices, local(): both = lax.all_to_all(both, G, 0, 0, tiled=True)  9.91 us
    ppermute x6, waiting for transfers between devices, local(): lax.ppermute(block, 'x', shift(4, s))  6.84 us
  transfers between devices with their start and end apart: 21, of which 12 were waited for; matrix products, arithmetic and copies ran while one was open for 6% of the time, Pallas kernels for 7%

profile of v3, /device:TPU:1, one launch (start us, length us, event | category | flops | bytes accessed | tf_op | source)
XLA Modules:
  0.0 141.4 jit_solution(17732569000360584728)
XLA Ops:
  1.7 9.0 %all-to-all-start.1 = ((bf16[8,16,2048]{2,1,0:T(8,128)(2,1)}), bf16[8,16,2048]{2,1,0:T(8,128)(2,1)S(1)}, u32[]{:S(2)}, u32[]{:S(2)}) async-start(bf16[8,16,2048]{2,1,0:T(8,128)(2,1)} %broadcast_in_dim.18), calls=%async_computation.1 | async-start | bytes 1048576 | tf_op jit(solution)/shard_map/all_to_all | solution.py:156
  10.7 1.2 pad_maximum_fusion.1
  12.7 10.5 %all-to-all-done.1.t0 = bf16[8,16,2048]{2,1,0:T(8,128)(2,1)S(1)} async-done(((bf16[8,16,2048]{2,1,0:T(8,128)(2,1)}), bf16[8,16,2048]{2,1,0:T(8,128)(2,1)S(1)}, u32[]{:S(2)}, u32[]{:S(2)}) %all-to-all-start.1) | async-done | bytes 524320 | tf_op jit(solution)/shard_map/all_to_all | solution.py:156
  23.2 9.9 %all-to-all-start.2 = ((bf16[32,2,16,128]{3,2,1,0:T(8,128)(2,1)}), bf16[32,2,16,128]{3,2,1,0:T(8,128)(2,1)S(1)}, u32[]{:S(2)}, u32[]{:S(2)}) async-start(bf16[32,2,16,128]{3,2,1,0:T(8,128)(2,1)} %bitcast.17), calls=%async_computation.2 | async-start | bytes 524288 | tf_op jit(solution)/shard_map/all_to_all | solution.py:154
  33.1 1.3 collective-permute-start.6
  34.4 10.1 %all-to-all-done.2 = bf16[32,2,16,128]{3,2,1,0:T(8,128)(2,1)S(1)} async-done(((bf16[32,2,16,128]{3,2,1,0:T(8,128)(2,1)}), bf16[32,2,16,128]{3,2,1,0:T(8,128)(2,1)S(1)}, u32[]{:S(2)}, u32[]{:S(2)}) %all-to-all-start.2) | async-done | bytes 262176 | tf_op jit(solution)/shard_map/all_to_all | solution.py:154
  44.5 2.5 %collective-permute-start.3 = (bf16[32,2,16,128]{3,2,1,0:T(8,128)(2,1)S(1)}, bf16[32,2,16,128]{3,2,1,0:T(8,128)(2,1)S(1)}, u32[]{:S(2)}, u32[]{:S(2)}) collective-permute-start(bf16[32,2,16,128]{3,2,1,0:T(8,128)(2,1)S(1)} %all-to-all-done.2), channel_id=1, source_target_pairs={{0,6},{2,0},{4,2},{6,4},{1,7},{3,1},{5,3},{7,5},{8,14},{10,8},{12,... | collective-permute-start | bytes 786440 | tf_op jit(solution)/shard_map/ppermute | solution.py:155
  48.1 4.7 %collective-permute-done.3 = bf16[32,2,16,128]{3,2,1,0:T(8,128)(2,1)S(1)} collective-permute-done((bf16[32,2,16,128]{3,2,1,0:T(8,128)(2,1)S(1)}, bf16[32,2,16,128]{3,2,1,0:T(8,128)(2,1)S(1)}, u32[]{:S(2)}, u32[]{:S(2)}) %collective-permute-start.3) | collective-permute-done | bytes 262176 | tf_op jit(solution)/shard_map/ppermute | solution.py:155
  53.8 7.6 %collective-permute-done.5 = bf16[32,2,16,128]{3,2,1,0:T(8,128)(2,1)S(1)} collective-permute-done((bf16[32,2,16,128]{3,2,1,0:T(8,128)(2,1)S(1)}, bf16[32,2,16,128]{3,2,1,0:T(8,128)(2,1)S(1)}, u32[]{:S(2)}, u32[]{:S(2)}) %collective-permute-start.5) | collective-permute-done | bytes 262176 | tf_op jit(solution)/shard_map/ppermute | solution.py:155
  62.3 1.5 %collective-permute-start.9 = (bf16[4,32,2,16,128]{4,3,2,1,0:T(8,128)(2,1)S(1)}, bf16[4,32,2,16,128]{4,3,2,1,0:T(8,128)(2,1)S(1)}, u32[]{:S(2)}, u32[]{:S(2)}) collective-permute-start(bf16[4,32,2,16,128]{4,3,2,1,0:T(8,128)(2,1)S(1)} %pad_maximum_fusion.wa), channel_id=1, source_target_pairs={{0,1},{1,0},{2,3},{3,2},{4,5},{5,4},{6,7},{7,6},{8,9},{9,8},{10,11... | collective-permute-start | bytes 3145736 | tf_op jit(solution)/shard_map/ppermute | solution.py:160
  64.7 3.5 %all-to-all-start = ((bf16[8,16,2048]{2,1,0:T(8,128)(2,1)}), bf16[8,16,2048]{2,1,0:T(8,128)(2,1)S(1)}, u32[]{:S(2)}, u32[]{:S(2)}) async-start(bf16[8,16,2048]{2,1,0:T(8,128)(2,1)} %broadcast_in_dim.17), calls=%async_computation | async-start | bytes 1048576 | tf_op jit(solution)/shard_map/all_to_all | solution.py:156
  68.2 1.2 collective-permute-start.7
  69.4 1.4 %collective-permute-start.8 = (bf16[8,16,2048]{2,1,0:T(8,128)(2,1)S(1)}, bf16[8,16,2048]{2,1,0:T(8,128)(2,1)}, u32[]{:S(2)}, u32[]{:S(2)}) collective-permute-start(bf16[8,16,2048]{2,1,0:T(8,128)(2,1)S(1)} %all-to-all-done.1.t0), channel_id=1, source_target_pairs={{0,24},{8,0},{16,8},{24,16},{1,25},{9,1},{17,9},{25,17},{2,26},{10... | collective-permute-start | bytes 1572872 | tf_op jit(solution)/shard_map/ppermute | solution.py:157
  72.0 9.8 %all-to-all-done.t0 = bf16[8,16,2048]{2,1,0:T(8,128)(2,1)S(1)} async-done(((bf16[8,16,2048]{2,1,0:T(8,128)(2,1)}), bf16[8,16,2048]{2,1,0:T(8,128)(2,1)S(1)}, u32[]{:S(2)}, u32[]{:S(2)}) %all-to-all-start) | async-done | bytes 524320 | tf_op jit(solution)/shard_map/all_to_all | solution.py:156
  82.4 1.4 %collective-permute-start.2 = (bf16[8,16,2048]{2,1,0:T(8,128)(2,1)S(1)}, bf16[8,16,2048]{2,1,0:T(8,128)(2,1)S(1)}, u32[]{:S(2)}, u32[]{:S(2)}) collective-permute-start(bf16[8,16,2048]{2,1,0:T(8,128)(2,1)S(1)} %all-to-all-done.t0), channel_id=1, source_target_pairs={{0,24},{8,0},{16,8},{24,16},{1,25},{9,1},{17,9},{25,17},{2,26},{10... | collective-permute-start | bytes 1572872 | tf_op jit(solution)/shard_map/ppermute | solution.py:157
  83.9 1.1 copy.26
  85.2 1.3 copy.27
  86.6 5.9 %collective-permute-done.8.t3 = bf16[8,16,2048]{2,1,0:T(8,128)(2,1)} collective-permute-done((bf16[8,16,2048]{2,1,0:T(8,128)(2,1)S(1)}, bf16[8,16,2048]{2,1,0:T(8,128)(2,1)}, u32[]{:S(2)}, u32[]{:S(2)}) %collective-permute-start.8) | collective-permute-done | bytes 524320 | tf_op jit(solution)/shard_map/ppermute | solution.py:157
  92.5 1.1 copy.28
  93.7 5.4 %ladder.2 = (f32[4,256,128]{2,1,0:T(8,128)S(1)}, f32[4,256,128]{2,1,0:T(8,128)S(1)}) custom-call(s32[5]{0:T(128)S(1)} %stack.47.meta, s32[16,4]{1,0:T(8,128)S(1)} %copy.19.live, bf16[8,16,2048]{2,1,0:T(8,128)(2,1)S(1)} %all-to-all-done.1.t0, bf16[8,16,2048]{2,1,0:T(8,128)(2,1)S(1)} %copy-done.2, bf16[8,16,2048]{2,1,0:T(8,128)(2,1)} %collective-permute-done.7.t2, ...), custom_call_target="tpu_custom_call" | custom-call | flops 1650000000 | bytes 10000000 | tf_op jit(solution)/shard_map/ladder/pallas_call | solution.py:96
  99.1 1.9 %collective-permute-start.10 = (f32[4,256,128]{2,1,0:T(8,128)S(1)}, f32[4,256,128]{2,1,0:T(8,128)S(1)}, u32[]{:S(2)}, u32[]{:S(2)}) collective-permute-start(f32[4,256,128]{2,1,0:T(8,128)S(1)} %get-tuple-element.33), channel_id=1, source_target_pairs={{0,1},{1,0},{2,3},{3,2},{4,5},{5,4},{6,7},{7,6},{8,9},{9,8},{10,11... | collective-permute-start | bytes 1572872 | tf_op jit(solution)/shard_map/ppermute | solution.py:166
  101.4 13.5 %collective-permute-done.2.t3 = bf16[8,16,2048]{2,1,0:T(8,128)(2,1)S(1)} collective-permute-done((bf16[8,16,2048]{2,1,0:T(8,128)(2,1)S(1)}, bf16[8,16,2048]{2,1,0:T(8,128)(2,1)S(1)}, u32[]{:S(2)}, u32[]{:S(2)}) %collective-permute-start.2) | collective-permute-done | bytes 524320 | tf_op jit(solution)/shard_map/ppermute | solution.py:157
  116.1 1.5 %collective-permute-start.12 = (f32[256,128]{1,0:T(8,128)S(1)}, f32[256,128]{1,0:T(8,128)S(1)}, u32[]{:S(2)}, u32[]{:S(2)}) collective-permute-start(f32[256,128]{1,0:T(8,128)S(1)} %get-tuple-element.37), channel_id=1, source_target_pairs={{0,4},{2,6},{4,0},{6,2},{1,5},{3,7},{5,1},{7,3},{8,12},{10,14},{12... | collective-permute-start | bytes 393224 | tf_op jit(solution)/shard_map/ppermute | solution.py:170
  117.6 1.2 collective-permute-start.13
  118.7 4.8 %ladder.3 = (f32[4,256,128]{2,1,0:T(8,128)S(1)}, f32[4,256,128]{2,1,0:T(8,128)S(1)}) custom-call(s32[5]{0:T(128)S(1)} %stack.47.meta, s32[16,4]{1,0:T(8,128)S(1)} %copy.19.live, bf16[8,16,2048]{2,1,0:T(8,128)(2,1)S(1)} %all-to-all-done.t0, bf16[8,16,2048]{2,1,0:T(8,128)(2,1)S(1)} %collective-permute-done.t1, ...), custom_call_target="tpu_custom_call" | custom-call | flops 1650000000 | bytes 10000000 | tf_op jit(solution)/shard_map/ladder/pallas_call | solution.py:96
  123.6 1.1 collective-permute-done.11.refs_2_
  124.7 1.9 %collective-permute-start.14 = (f32[4,256,128]{2,1,0:T(8,128)S(1)}, f32[4,256,128]{2,1,0:T(8,128)S(1)}, u32[]{:S(2)}, u32[]{:S(2)}) collective-permute-start(f32[4,256,128]{2,1,0:T(8,128)S(1)} %get-tuple-element.45), channel_id=1, source_target_pairs={{0,1},{1,0},{2,3},{3,2},{4,5},{5,4},{6,7},{7,6},{8,9},{9,8},{10,11... | collective-permute-start | bytes 1572872 | tf_op jit(solution)/shard_map/ppermute | solution.py:166
  126.6 1.5 %collective-permute-done.14 = f32[4,256,128]{2,1,0:T(8,128)S(1)} collective-permute-done((f32[4,256,128]{2,1,0:T(8,128)S(1)}, f32[4,256,128]{2,1,0:T(8,128)S(1)}, u32[]{:S(2)}, u32[]{:S(2)}) %collective-permute-start.14) | collective-permute-done | bytes 524320 | tf_op jit(solution)/shard_map/ppermute | solution.py:166
  128.9 3.2 %collective-permute-start.16 = (f32[256,128]{1,0:T(8,128)S(1)}, f32[256,128]{1,0:T(8,128)S(1)}, u32[]{:S(2)}, u32[]{:S(2)}) collective-permute-start(f32[256,128]{1,0:T(8,128)S(1)} %get-tuple-element.47), channel_id=1, source_target_pairs={{0,4},{2,6},{4,0},{6,2},{1,5},{3,7},{5,1},{7,3},{8,12},{10,14},{12... | collective-permute-start | bytes 393224 | tf_op jit(solution)/shard_map/ppermute | solution.py:170
  132.4 2.4 %collective-permute-done.15.refs_7_ = f32[256,128]{1,0:T(8,128)S(1)} collective-permute-done((f32[256,128]{1,0:T(8,128)S(1)}, f32[256,128]{1,0:T(8,128)S(1)}, u32[]{:S(2)}, u32[]{:S(2)}) %collective-permute-start.15) | collective-permute-done | bytes 131104 | tf_op jit(solution)/shard_map/ppermute | solution.py:170
  134.8 3.4 %collective-permute-done.16.refs_8_ = f32[256,128]{1,0:T(8,128)S(1)} collective-permute-done((f32[256,128]{1,0:T(8,128)S(1)}, f32[256,128]{1,0:T(8,128)S(1)}, u32[]{:S(2)}, u32[]{:S(2)}) %collective-permute-start.16) | collective-permute-done | bytes 131104 | tf_op jit(solution)/shard_map/ppermute | solution.py:170
  139.0 2.4 %finish.1 = bf16[128,512]{1,0:T(8,128)(2,1)} custom-call(s32[5]{0:T(128)} %copy-done.4, f32[32]{0:T(128)} %occ.1, f32[128]{0:T(128)} %vir.1, f32[32,128]{1,0:T(8,128)} %broadcast_in_dim.15.occ_col, f32[1,128]{1,0:T(1,128)} %bitcast.119, f32[256,128]{1,0:T(8,128)} %get-tuple-element.39.refs_0_, f32[256,128]{1,0:T(8,128)} %get-tuple-element.40.refs_1_, ...), custom_call_target="tpu_custom_call" | custom-call | flops 400000 | bytes 1500000 | tf_op jit(solution)/shard_map/finish/pallas_call | solution.py:131
  (66 shorter events, 11.7 us)
Async XLA Ops:
  1.7 21.5 %all-to-all-start.1 = ((bf16[8,16,2048]{2,1,0:T(8,128)(2,1)}), bf16[8,16,2048]{2,1,0:T(8,128)(2,1)S(1)}, u32[]{:S(2)}, u32[]{:S(2)}) async-start(bf16[8,16,2048]{2,1,0:T(8,128)(2,1)} %broadcast_in_dim.18), calls=%async_computation.1 | async-start | bytes 1048576 | tf_op jit(solution)/shard_map/all_to_all | solution.py:156
  23.2 47.6 %copy-start.12 = (s32[16,4]{0,1:T(4,128)S(1)}, s32[16,4]{0,1:T(4,128)}, u32[]{:S(2)}) copy-start(s32[16,4]{0,1:T(4,128)} %param.9) | copy-start | bytes 772
  23.2 21.3 %all-to-all-start.2 = ((bf16[32,2,16,128]{3,2,1,0:T(8,128)(2,1)}), bf16[32,2,16,128]{3,2,1,0:T(8,128)(2,1)S(1)}, u32[]{:S(2)}, u32[]{:S(2)}) async-start(bf16[32,2,16,128]{3,2,1,0:T(8,128)(2,1)} %bitcast.17), calls=%async_computation.2 | async-start | bytes 524288 | tf_op jit(solution)/shard_map/all_to_all | solution.py:154
  33.1 28.3 %collective-permute-start.6 = (bf16[8,16,2048]{2,1,0:T(8,128)(2,1)S(1)}, bf16[8,16,2048]{2,1,0:T(8,128)(2,1)S(1)}, u32[]{:S(2)}, u32[]{:S(2)}) collective-permute-start(bf16[8,16,2048]{2,1,0:T(8,128)(2,1)S(1)} %all-to-all-done.1.t0), channel_id=1, source_target_pairs={{0,8},{8,16},{16,24},{24,0},{1,9},{9,17},{17,25},{25,1},{2,10},{10... | collective-permute-start | bytes 1572872 | tf_op jit(solution)/shard_map/ppermute | solution.py:157
  44.5 8.3 %collective-permute-start.3 = (bf16[32,2,16,128]{3,2,1,0:T(8,128)(2,1)S(1)}, bf16[32,2,16,128]{3,2,1,0:T(8,128)(2,1)S(1)}, u32[]{:S(2)}, u32[]{:S(2)}) collective-permute-start(bf16[32,2,16,128]{3,2,1,0:T(8,128)(2,1)S(1)} %all-to-all-done.2), channel_id=1, source_target_pairs={{0,6},{2,0},{4,2},{6,4},{1,7},{3,1},{5,3},{7,5},{8,14},{10,8},{12,... | collective-permute-start | bytes 786440 | tf_op jit(solution)/shard_map/ppermute | solution.py:155
  47.0 6.8 %collective-permute-start.4 = (bf16[32,2,16,128]{3,2,1,0:T(8,128)(2,1)S(1)}, bf16[32,2,16,128]{3,2,1,0:T(8,128)(2,1)S(1)}, u32[]{:S(2)}, u32[]{:S(2)}) collective-permute-start(bf16[32,2,16,128]{3,2,1,0:T(8,128)(2,1)S(1)} %all-to-all-done.2), channel_id=1, source_target_pairs={{0,4},{2,6},{4,0},{6,2},{1,5},{3,7},{5,1},{7,3},{8,12},{10,14},{12... | collective-permute-start | bytes 786440 | tf_op jit(solution)/shard_map/ppermute | solution.py:155
  47.5 13.9 %collective-permute-start.5 = (bf16[32,2,16,128]{3,2,1,0:T(8,128)(2,1)S(1)}, bf16[32,2,16,128]{3,2,1,0:T(8,128)(2,1)S(1)}, u32[]{:S(2)}, u32[]{:S(2)}) collective-permute-start(bf16[32,2,16,128]{3,2,1,0:T(8,128)(2,1)S(1)} %all-to-all-done.2), channel_id=1, source_target_pairs={{0,2},{2,4},{4,6},{6,0},{1,3},{3,5},{5,7},{7,1},{8,10},{10,12},{12... | collective-permute-start | bytes 786440 | tf_op jit(solution)/shard_map/ppermute | solution.py:155
  61.4 0.8 copy-start.1
  62.3 31.4 %collective-permute-start.9 = (bf16[4,32,2,16,128]{4,3,2,1,0:T(8,128)(2,1)S(1)}, bf16[4,32,2,16,128]{4,3,2,1,0:T(8,128)(2,1)S(1)}, u32[]{:S(2)}, u32[]{:S(2)}) collective-permute-start(bf16[4,32,2,16,128]{4,3,2,1,0:T(8,128)(2,1)S(1)} %pad_maximum_fusion.wa), channel_id=1, source_target_pairs={{0,1},{1,0},{2,3},{3,2},{4,5},{5,4},{6,7},{7,6},{8,9},{9,8},{10,11... | collective-permute-start | bytes 3145736 | tf_op jit(solution)/shard_map/ppermute | solution.py:160
  64.7 17.1 %all-to-all-start = ((bf16[8,16,2048]{2,1,0:T(8,128)(2,1)}), bf16[8,16,2048]{2,1,0:T(8,128)(2,1)S(1)}, u32[]{:S(2)}, u32[]{:S(2)}) async-start(bf16[8,16,2048]{2,1,0:T(8,128)(2,1)} %broadcast_in_dim.17), calls=%async_computation | async-start | bytes 1048576 | tf_op jit(solution)/shard_map/all_to_all | solution.py:156
  68.2 16.9 %collective-permute-start.7 = (bf16[8,16,2048]{2,1,0:T(8,128)(2,1)S(1)}, bf16[8,16,2048]{2,1,0:T(8,128)(2,1)}, u32[]{:S(2)}, u32[]{:S(2)}) collective-permute-start(bf16[8,16,2048]{2,1,0:T(8,128)(2,1)S(1)} %all-to-all-done.1.t0), channel_id=1, source_target_pairs={{0,16},{8,24},{16,0},{24,8},{1,17},{9,25},{17,1},{25,9},{2,18},{10... | collective-permute-start | bytes 1572872 | tf_op jit(solution)/shard_map/ppermute | solution.py:157
  69.4 23.1 %collective-permute-start.8 = (bf16[8,16,2048]{2,1,0:T(8,128)(2,1)S(1)}, bf16[8,16,2048]{2,1,0:T(8,128)(2,1)}, u32[]{:S(2)}, u32[]{:S(2)}) collective-permute-start(bf16[8,16,2048]{2,1,0:T(8,128)(2,1)S(1)} %all-to-all-done.1.t0), channel_id=1, source_target_pairs={{0,24},{8,0},{16,8},{24,16},{1,25},{9,1},{17,9},{25,17},{2,26},{10... | collective-permute-start | bytes 1572872 | tf_op jit(solution)/shard_map/ppermute | solution.py:157
  71.0 47.7 %copy-start.4 = (s32[5]{0:T(128)}, s32[5]{0:T(128)S(1)}, u32[]{:S(2)}) copy-start(s32[5]{0:T(128)S(1)} %stack.47.meta) | copy-start | bytes 64
  81.8 19.4 %collective-permute-start.1 = (bf16[8,16,2048]{2,1,0:T(8,128)(2,1)S(1)}, bf16[8,16,2048]{2,1,0:T(8,128)(2,1)S(1)}, u32[]{:S(2)}, u32[]{:S(2)}) collective-permute-start(bf16[8,16,2048]{2,1,0:T(8,128)(2,1)S(1)} %all-to-all-done.t0), channel_id=1, source_target_pairs={{0,16},{8,24},{16,0},{24,8},{1,17},{9,25},{17,1},{25,9},{2,18},{10... | collective-permute-start | bytes 1572872 | tf_op jit(solution)/shard_map/ppermute | solution.py:157
  82.4 32.5 %collective-permute-start.2 = (bf16[8,16,2048]{2,1,0:T(8,128)(2,1)S(1)}, bf16[8,16,2048]{2,1,0:T(8,128)(2,1)S(1)}, u32[]{:S(2)}, u32[]{:S(2)}) collective-permute-start(bf16[8,16,2048]{2,1,0:T(8,128)(2,1)S(1)} %all-to-all-done.t0), channel_id=1, source_target_pairs={{0,24},{8,0},{16,8},{24,16},{1,25},{9,1},{17,9},{25,17},{2,26},{10... | collective-permute-start | bytes 1572872 | tf_op jit(solution)/shard_map/ppermute | solution.py:157
  85.1 30.0 %collective-permute-start = (bf16[8,16,2048]{2,1,0:T(8,128)(2,1)S(1)}, bf16[8,16,2048]{2,1,0:T(8,128)(2,1)S(1)}, u32[]{:S(2)}, u32[]{:S(2)}) collective-permute-start(bf16[8,16,2048]{2,1,0:T(8,128)(2,1)S(1)} %all-to-all-done.t0), channel_id=1, source_target_pairs={{0,8},{8,16},{16,24},{24,0},{1,9},{9,17},{17,25},{25,1},{2,10},{10... | collective-permute-start | bytes 1572872 | tf_op jit(solution)/shard_map/ppermute | solution.py:157
  85.2 8.5 %copy-start = (bf16[2048,512]{1,0:T(8,128)(2,1)S(1)}, bf16[2048,512]{1,0:T(8,128)(2,1)}, u32[]{:S(2)}) copy-start(bf16[2048,512]{1,0:T(8,128)(2,1)} %v.3) | copy-start | bytes 6291460
  85.2 8.5 %copy-start.2 = (bf16[8,16,2048]{2,1,0:T(8,128)(2,1)S(1)}, bf16[8,16,2048]{2,1,0:T(8,128)(2,1)}, u32[]{:S(2)}) copy-start(bf16[8,16,2048]{2,1,0:T(8,128)(2,1)} %copy-done.1) | copy-start | bytes 1572868
  85.2 8.5 %copy-start.3 = (bf16[8,16,16,128]{3,2,0,1:T(8,128)(2,1)S(1)}, bf16[8,16,16,128]{3,2,0,1:T(8,128)(2,1)}, u32[]{:S(2)}) copy-start(bf16[8,16,16,128]{3,2,0,1:T(8,128)(2,1)} %copy.14) | copy-start | bytes 1572868
  99.1 16.1 %collective-permute-start.10 = (f32[4,256,128]{2,1,0:T(8,128)S(1)}, f32[4,256,128]{2,1,0:T(8,128)S(1)}, u32[]{:S(2)}, u32[]{:S(2)}) collective-permute-start(f32[4,256,128]{2,1,0:T(8,128)S(1)} %get-tuple-element.33), channel_id=1, source_target_pairs={{0,1},{1,0},{2,3},{3,2},{4,5},{5,4},{6,7},{7,6},{8,9},{9,8},{10,11... | collective-permute-start | bytes 1572872 | tf_op jit(solution)/shard_map/ppermute | solution.py:166
  116.1 8.6 %collective-permute-start.11 = (f32[256,128]{1,0:T(8,128)S(1)}, f32[256,128]{1,0:T(8,128)S(1)}, u32[]{:S(2)}, u32[]{:S(2)}) collective-permute-start(f32[256,128]{1,0:T(8,128)S(1)} %get-tuple-element.36), channel_id=1, source_target_pairs={{0,2},{2,4},{4,6},{6,0},{1,3},{3,5},{5,7},{7,1},{8,10},{10,12},{12... | collective-permute-start | bytes 393224 | tf_op jit(solution)/shard_map/ppermute | solution.py:170
  116.1 8.6 %collective-permute-start.12 = (f32[256,128]{1,0:T(8,128)S(1)}, f32[256,128]{1,0:T(8,128)S(1)}, u32[]{:S(2)}, u32[]{:S(2)}) collective-permute-start(f32[256,128]{1,0:T(8,128)S(1)} %get-tuple-element.37), channel_id=1, source_target_pairs={{0,4},{2,6},{4,0},{6,2},{1,5},{3,7},{5,1},{7,3},{8,12},{10,14},{12... | collective-permute-start | bytes 393224 | tf_op jit(solution)/shard_map/ppermute | solution.py:170
  117.6 7.1 %collective-permute-start.13 = (f32[256,128]{1,0:T(8,128)S(1)}, f32[256,128]{1,0:T(8,128)S(1)}, u32[]{:S(2)}, u32[]{:S(2)}) collective-permute-start(f32[256,128]{1,0:T(8,128)S(1)} %get-tuple-element.38), channel_id=1, source_target_pairs={{0,6},{2,0},{4,2},{6,4},{1,7},{3,1},{5,3},{7,5},{8,14},{10,8},{12,... | collective-permute-start | bytes 393224 | tf_op jit(solution)/shard_map/ppermute | solution.py:170
  118.7 19.5 %copy-start.11 = (f32[32]{0:T(128)S(1)}, f32[32]{0:T(128)}, u32[]{:S(2)}) copy-start(f32[32]{0:T(128)} %occ.1) | copy-start | bytes 388
  124.6 14.3 %copy-start.5 = (f32[256,128]{1,0:T(8,128)}, f32[256,128]{1,0:T(8,128)S(1)}, u32[]{:S(2)}) copy-start(f32[256,128]{1,0:T(8,128)S(1)} %collective-permute-done.11.refs_2_) | copy-start | bytes 393220
  124.6 14.3 %copy-start.6 = (f32[256,128]{1,0:T(8,128)}, f32[256,128]{1,0:T(8,128)S(1)}, u32[]{:S(2)}) copy-start(f32[256,128]{1,0:T(8,128)S(1)} %collective-permute-done.12.refs_3_) | copy-start | bytes 393220
  124.7 14.3 %copy-start.7 = (f32[256,128]{1,0:T(8,128)}, f32[256,128]{1,0:T(8,128)S(1)}, u32[]{:S(2)}) copy-start(f32[256,128]{1,0:T(8,128)S(1)} %collective-permute-done.13.refs_4_) | copy-start | bytes 393220
  124.7 3.5 %collective-permute-start.14 = (f32[4,256,128]{2,1,0:T(8,128)S(1)}, f32[4,256,128]{2,1,0:T(8,128)S(1)}, u32[]{:S(2)}, u32[]{:S(2)}) collective-permute-start(f32[4,256,128]{2,1,0:T(8,128)S(1)} %get-tuple-element.45), channel_id=1, source_target_pairs={{0,1},{1,0},{2,3},{3,2},{4,5},{5,4},{6,7},{7,6},{8,9},{9,8},{10,11... | collective-permute-start | bytes 1572872 | tf_op jit(solution)/shard_map/ppermute | solution.py:166
  128.9 5.9 %collective-permute-start.15 = (f32[256,128]{1,0:T(8,128)S(1)}, f32[256,128]{1,0:T(8,128)S(1)}, u32[]{:S(2)}, u32[]{:S(2)}) collective-permute-start(f32[256,128]{1,0:T(8,128)S(1)} %get-tuple-element.46), channel_id=1, source_target_pairs={{0,2},{2,4},{4,6},{6,0},{1,3},{3,5},{5,7},{7,1},{8,10},{10,12},{12... | collective-permute-start | bytes 393224 | tf_op jit(solution)/shard_map/ppermute | solution.py:170
  128.9 9.3 %collective-permute-start.16 = (f32[256,128]{1,0:T(8,128)S(1)}, f32[256,128]{1,0:T(8,128)S(1)}, u32[]{:S(2)}, u32[]{:S(2)}) collective-permute-start(f32[256,128]{1,0:T(8,128)S(1)} %get-tuple-element.47), channel_id=1, source_target_pairs={{0,4},{2,6},{4,0},{6,2},{1,5},{3,7},{5,1},{7,3},{8,12},{10,14},{12... | collective-permute-start | bytes 393224 | tf_op jit(solution)/shard_map/ppermute | solution.py:170
  132.2 6.1 %collective-permute-start.17 = (f32[256,128]{1,0:T(8,128)S(1)}, f32[256,128]{1,0:T(8,128)S(1)}, u32[]{:S(2)}, u32[]{:S(2)}) collective-permute-start(f32[256,128]{1,0:T(8,128)S(1)} %get-tuple-element.48), channel_id=1, source_target_pairs={{0,6},{2,0},{4,2},{6,4},{1,7},{3,1},{5,3},{7,5},{8,14},{10,8},{12,... | collective-permute-start | bytes 393224 | tf_op jit(solution)/shard_map/ppermute | solution.py:170
  134.8 4.1 %copy-start.8 = (f32[256,128]{1,0:T(8,128)}, f32[256,128]{1,0:T(8,128)S(1)}, u32[]{:S(2)}) copy-start(f32[256,128]{1,0:T(8,128)S(1)} %collective-permute-done.15.refs_7_) | copy-start | bytes 393220
  (2 other events, 1.5 us)

commit v4 on v2

v4 whole, which is shorter than its diff:
```python
import functools

import jax
import jax.numpy as jnp
from jax import lax
from jax.experimental import pallas as pl
from jax.experimental.pallas import tpu as pltpu
from jax.sharding import Mesh, PartitionSpec as P

G = ("zl", "zh", "y")
C = ("x", "core")
Z = ("zl", "zh")
F32 = jnp.float32
BF16 = jnp.bfloat16


def shift(n, s):
    return [(i, (i + s) % n) for i in range(n)]


def z_shift(s):
    at = lambda z: (z % 4) * 2 + z // 4
    return [(at(z), at((z + s) % 8)) for z in range(8)]


EVEN = (6, 0, 2, 4)
ODD = (5, 7, 1, 3)


def ladder_kernel(slots, meta, live, *refs):
    ts, us, (v, wa, wb), refs = refs[:4], refs[4:8], refs[8:11], refs[11:]
    prev = None
    if slots is ODD:
        prev, refs = refs[0], refs[1:]
    outs, (ladder, vm, wm, o2) = refs[:-4], refs[-4:]
    x0, c0, y0, col, z0 = meta[0], meta[1], meta[2], meta[3], meta[5]
    ys = [(y0 + 4 - q) & 3 for q in range(4)]
    zs = [(z0 + d) & 7 for d in slots]
    hs = [((z & 3) << 1) | (z >> 2) for z in zs]
    at = [((((z >> 2) ^ c0) << 2) | (((z & 3) + 4 - x0) & 3)) for z in zs]

    @pl.loop(0, 16)
    def _(kt):
        rows = pl.ds(pl.multiple_of(kt * 128, 128), 128)
        for n in range(4):
            tile = v[rows, n * 128 : n * 128 + 128]
            vm[rows, n * 128 : n * 128 + 128] = jnp.where(live[kt, n] != 0, tile, jnp.zeros_like(tile))

    @pl.loop(0, 8)
    def _(r):
        ladder[r] = jnp.zeros((512, 128), F32) if prev is None else prev[r]

    for q in range(0, 4, 2):
        rows = jnp.concatenate([ts[q][...].reshape(128, 2048), ts[q + 1][...].reshape(128, 2048)], 0)
        part = jnp.dot(rows, vm[...], preferred_element_type=F32)
        for e in range(2):
            for d in range(4):
                top = e * 128 + d * 32
                for a in range(4):
                    rows = pl.ds(ys[q + e] * 4 + a, 32, stride=16)
                    ladder[at[d], rows, :] += part[top : top + 32, a * 128 : a * 128 + 128]

    lane = lax.broadcasted_iota(jnp.int32, (128, 128), 1)

    def spread(k, which):
        pieces = [w[(x0 + s) & 3, k, which] for w in (wa, wb) for s in range(4)]
        return jnp.concatenate(pieces, 0)

    acc = jnp.zeros((512, 128), F32)
    for p in range(2):
        w_all = jnp.zeros((128, 128), F32)
        for e in range(2):
            q = p * 2 + e
            ks = [h * 4 + ys[q] for h in hs]
            for d in range(4):
                wk = spread(ks[d], 0).astype(F32)
                wk = pltpu.roll(wk, (16 * (e * 4 + d) + 128 - 16 * col) & 127, 1)
                w_all = jnp.where((lane >> 4) == e * 4 + d, wk, w_all)
            for d in range(0, 4, 2):
                lhs = jnp.concatenate([us[q][d + f].reshape(512, 128) for f in range(2)], 1)
                rhs = jnp.concatenate([spread(ks[d + f], 1) for f in range(2)], 1)
                acc = acc + lax.dot_general(lhs, rhs, (((1,), (1,)), ((), ())), preferred_element_type=F32)
        wm[:, p * 128 : p * 128 + 128] = w_all.astype(BF16)
    o2[...] = acc.T

    own = (lane >> 4) == col

    @pl.loop(0, 16)
    def _(jj):
        j = jj * 2
        rhs = jnp.concatenate(
            [jnp.concatenate([us[q][d, j + e] for q in range(4) for d in range(4)], 0) for e in range(2)], 1
        )
        one = jnp.dot(wm[...], rhs, preferred_element_type=F32)
        two = o2[:, pl.ds(pl.multiple_of((jj >> 2) * 128, 128), 128)]
        for e in range(2):
            placed = pltpu.roll(two, (16 * col + 128 - 16 * ((j + e) & 7)) & 127, 1)
            both = one[:, e * 128 : e * 128 + 128] + jnp.where(own, placed, 0.0)
            rows = pl.ds(pl.multiple_of((j + e) * 16, 16), 16)
            for r in range(8):
                value = ladder[r, rows, :] + both[r * 16 : r * 16 + 16]
                if prev is None:
                    outs[0][r, rows, :] = value
                else:
                    outs[r // 4][r % 4, rows, :] = value


def ladder_call(slots, meta, live, ts, us, v, wa, wb, prev=()):
    smem = pl.BlockSpec(memory_space=pltpu.SMEM)
    vmem = pl.BlockSpec(memory_space=pltpu.VMEM)
    whole = jax.ShapeDtypeStruct((8, 512, 128), F32)
    half = jax.ShapeDtypeStruct((4, 512, 128), F32)
    return pl.pallas_call(
        functools.partial(ladder_kernel, slots),
        out_shape=(half, half) if prev else (whole,),
        in_specs=[smem, smem] + [vmem] * (11 + len(prev)),
        out_specs=(vmem, vmem) if prev else (vmem,),
        scratch_shapes=[
            pltpu.VMEM((8, 512, 128), F32),
            pltpu.VMEM((2048, 512), BF16),
            pltpu.VMEM((128, 256), BF16),
            pltpu.VMEM((128, 512), F32),
        ],
        cost_estimate=pl.CostEstimate(flops=1_650_000_000, bytes_accessed=10_000_000, transcendentals=0),
        compiler_params=pltpu.CompilerParams(vmem_limit_bytes=24 << 20),
        name="ladder",
    )(meta, live, *ts, *us, v, wa, wb, *prev)


def finish_kernel(meta, occ, vir, occ_col, vir_row, p0, p1, p2, p3, p4, out):
    col, g = meta[3], meta[4]
    for il in range(4):
        for a in range(4):
            rows = pl.ds(il * 4 + a, 32, stride=16)
            total = ((p0[rows, :] + p1[rows, :]) + p2[rows, :]) + (p3[rows, :] + p4[rows, :])
            denom = ((vir[g * 4 + a] + vir_row[...]) - occ[col * 4 + il]) - occ_col[...]
            out[il * 32 : il * 32 + 32, a * 128 : a * 128 + 128] = (total / denom).astype(BF16)


def finish_call(meta, eps_occ, eps_vir, parts):
    smem = pl.BlockSpec(memory_space=pltpu.SMEM)
    vmem = pl.BlockSpec(memory_space=pltpu.VMEM)
    return pl.pallas_call(
        finish_kernel,
        out_shape=jax.ShapeDtypeStruct((128, 512), BF16),
        in_specs=[smem] * 3 + [vmem] * 7,
        out_specs=vmem,
        cost_estimate=pl.CostEstimate(flops=400_000, bytes_accessed=1_500_000, transcendentals=0),
        name="finish",
    )(
        meta,
        eps_occ,
        eps_vir,
        jnp.broadcast_to(eps_occ[:, None], (32, 128)),
        eps_vir[None, :],
        *parts,
    )


def over_y(group):
    return [group] + [lax.ppermute(group, "y", shift(4, s)) for s in (1, 2, 3)]


def split_rows(ts):
    return [t.reshape(4, 32, 16, 128) for t in ts]


def local(amplitudes, ladder_ints, tile_live, cycle_direct, cycle_exchange, eps_occ, eps_vir):
    x0, c0, y0 = lax.axis_index("x"), lax.axis_index("core"), lax.axis_index("y")
    z0 = lax.axis_index("zh") * 4 + lax.axis_index("zl")
    meta = jnp.stack([x0, c0, y0, lax.axis_index(C), lax.axis_index(G), z0]).astype(jnp.int32)
    t = amplitudes
    below, above, across = (lax.ppermute(t, Z, z_shift(s)) for s in (2, -2, 4))
    both = jnp.stack([cycle_direct, cycle_exchange]).reshape(2, 4, 32, 4, 128)
    both = both.transpose(2, 0, 1, 3, 4).reshape(32, 2, 16, 128)
    both = lax.all_to_all(both, G, 0, 0, tiled=True)
    both, below, above, across = lax.optimization_barrier((both, below, above, across))
    even = jnp.stack([below, t, above, across])
    left = lax.ppermute(even[0:2], Z, z_shift(1))
    right = lax.ppermute(even[1:3], Z, z_shift(-1))
    ts_even = over_y(even)
    wa = lax.all_to_all(jnp.broadcast_to(both[None], (4, 32, 2, 16, 128)), "x", 0, 0, tiled=True)
    wa, left, right, ts_even[1] = lax.optimization_barrier((wa, left, right, ts_even[1]))
    wb = lax.ppermute(wa, "core", shift(2, 1))
    odd = jnp.concatenate([left, right])
    ts_odd = over_y(odd)
    prev = list(ladder_call(EVEN, meta, tile_live, ts_even, split_rows(ts_even), ladder_ints, wa, wb))
    *ts_odd, prev[0] = lax.optimization_barrier((*ts_odd, prev[0]))
    keep, away = ladder_call(ODD, meta, tile_live, ts_odd, split_rows(ts_odd), ladder_ints, wa, wb, tuple(prev))
    got = lax.ppermute(away, "core", shift(2, 1))
    parts = [keep[0], got[0]]
    for s in (1, 2, 3):
        parts.append(lax.ppermute(keep[s] + got[s], "x", shift(4, s)))
    return finish_call(meta, eps_occ, eps_vir, parts)


def solution(mesh):
    fine = Mesh(mesh.devices.reshape(4, 2, 4, 4, 2), ("zl", "zh", "y", "x", "core"))
    placed = (P(G, C), P(C, G), P(C, G), P(C, G), P(C, G), P(), P())
    return jax.shard_map(local, mesh=fine, in_specs=placed, out_specs=P(C, G), check_vma=False)
```

time: 126 us -> 139 us (1.10); the launches traced: 125 us -> 137 us
  starting transfers between devices: 40.4 us -> 44.5 us
  local copies, waits for them, and re-layouts: 9.29 us -> 13.1 us
  Pallas kernels: 13.7 us -> 16.6 us
    unnamed x19 -> x43, local copies, waits for them, and re-layouts: 2.24 us -> 9.34 us
    reshape x4 -> x0, local copies, waits for them, and re-layouts: 5.12 us -> none  [local(): t.reshape(8, 32, 16, 128).transpose(1, 0, 2, 3).reshape(32, 128, 128)]
    all_to_all x0 -> x1, starting transfers between devices: none -> 4.01 us  [local(): lax.all_to_all(jnp.broadcast_to(both[None], (4, 32, 2, 16, 128)), 'x', 0,...]
    all_to_all x1, starting transfers between devices: 8.23 us -> 12.2 us  [local(): both = lax.all_to_all(both, G, 0, 0, tiled=True)]
    pallas_call x1 -> x2, Pallas kernels: 11.2 us -> 14.2 us  [ladder_call(): pl.pallas_call(functools.partial(ladder_kernel, slots), out_shape=(half,...]
    ppermute x1, starting transfers between devices: 3.62 us -> 0.87 us  [local(): got = lax.ppermute(away, 'core', shift(2, 1))]
    ppermute x13 -> x11, starting transfers between devices: 21.9 us -> 19.9 us  [the longest x3 8.79 us: local(): below, above, across = (lax.ppermute(t, Z, z_shift(s)) for s in (2, -2, 4))]
    ppermute x1, starting transfers between devices: 1.9 us -> 3.29 us  [local(): wb = lax.ppermute(wa, 'core', shift(2, 1))]
  transfers between devices with their start and end apart: 19 -> 18, of which waited for: 10 -> 13; matrix products, arithmetic and copies ran while one was open for 9% -> 5% of each run, Pallas kernels for 0% -> 5%
where the time goes in v4:
time: 139 us; the launch traced here: 137 us
  waiting for transfers between devices  59.2 us (43%)
  starting transfers between devices  44.5 us (32%)
  Pallas kernels  16.6 us (12%)
  local copies, waits for them, and re-layouts  13.1 us (9%)
  other arithmetic  3.29 us (2%)
    ppermute x6, waiting for transfers between devices, over_y(): return [group] + [lax.ppermute(group, 'y', shift(4, s)) for s in (1, 2, 3)]  30 us
    pallas_call x2, Pallas kernels, ladder_call(): pl.pallas_call(functools.partial(ladder_kernel, slots), out_shape=(half,...  14.2 us
    all_to_all x1, starting transfers between devices, local(): both = lax.all_to_all(both, G, 0, 0, tiled=True)  12.2 us
    ppermute x3, waiting for transfers between devices, local(): below, above, across = (lax.ppermute(t, Z, z_shift(s)) for s in (2, -2, 4))  10.8 us
    ppermute x3, waiting for transfers between devices, local(): parts.append(lax.ppermute(keep[s] + got[s], 'x', shift(4, s)))  10.5 us
    unnamed x43, local copies, waits for them, and re-layouts  9.34 us
    ppermute x3, starting transfers between devices, local(): below, above, across = (lax.ppermute(t, Z, z_shift(s)) for s in (2, -2, 4))  8.79 us
    ppermute x6, starting transfers between devices, over_y(): return [group] + [lax.ppermute(group, 'y', shift(4, s)) for s in (1, 2, 3)]  8.07 us
  transfers between devices with their start and end apart: 18, of which 13 were waited for; matrix products, arithmetic and copies ran while one was open for 5% of the time, Pallas kernels for 5%

profile of v4, /device:TPU:1, one launch (start us, length us, event | category | flops | bytes accessed | tf_op | source)
XLA Modules:
  0.0 137.0 jit_solution(9835638024101889385)
XLA Ops:
  0.0 1.2 maximum_bitcast_fusion
  1.9 12.2 %all-to-all-start = ((bf16[32,2,16,128]{3,2,1,0:T(8,128)(2,1)}), bf16[32,2,16,128]{3,2,1,0:T(8,128)(2,1)S(1)}, u32[]{:S(2)}, u32[]{:S(2)}) async-start(bf16[32,2,16,128]{3,2,1,0:T(8,128)(2,1)} %bitcast.10), calls=%async_computation | async-start | bytes 524288 | tf_op jit(solution)/shard_map/all_to_all | solution.py:176
  14.1 2.2 %collective-permute-start = (bf16[32,2048]{1,0:T(8,128)(2,1)}, bf16[32,2048]{1,0:T(8,128)(2,1)S(1)}, u32[]{:S(2)}, u32[]{:S(2)}) collective-permute-start(bf16[32,2048]{1,0:T(8,128)(2,1)} %param.7), channel_id=1, source_target_pairs={{0,128},{64,192},{128,32},{192,96},{32,160},{96,224},{160,0},{224,... | collective-permute-start | bytes 393224 | tf_op jit(solution)/shard_map/ppermute | solution.py:173
  16.3 1.4 %collective-permute-start.1 = (bf16[32,2048]{1,0:T(8,128)(2,1)}, bf16[32,2048]{1,0:T(8,128)(2,1)S(1)}, u32[]{:S(2)}, u32[]{:S(2)}) collective-permute-start(bf16[32,2048]{1,0:T(8,128)(2,1)} %param.7), channel_id=1, source_target_pairs={{0,160},{64,224},{128,0},{192,64},{32,128},{96,192},{160,32},{224,... | collective-permute-start | bytes 393224 | tf_op jit(solution)/shard_map/ppermute | solution.py:173
  17.8 5.1 %collective-permute-start.2 = (bf16[32,2048]{1,0:T(8,128)(2,1)}, bf16[32,2048]{1,0:T(8,128)(2,1)S(1)}, u32[]{:S(2)}, u32[]{:S(2)}) collective-permute-start(bf16[32,2048]{1,0:T(8,128)(2,1)} %param.7), channel_id=1, source_target_pairs={{0,32},{64,96},{128,160},{192,224},{32,0},{96,64},{160,128},{224,1... | collective-permute-start | bytes 393224 | tf_op jit(solution)/shard_map/ppermute | solution.py:173
  22.9 4.4 %collective-permute-done = bf16[32,2048]{1,0:T(8,128)(2,1)S(1)} collective-permute-done((bf16[32,2048]{1,0:T(8,128)(2,1)}, bf16[32,2048]{1,0:T(8,128)(2,1)S(1)}, u32[]{:S(2)}, u32[]{:S(2)}) %collective-permute-start) | collective-permute-done | bytes 131104 | tf_op jit(solution)/shard_map/ppermute | solution.py:173
  27.3 2.1 %collective-permute-done.1 = bf16[32,2048]{1,0:T(8,128)(2,1)S(1)} collective-permute-done((bf16[32,2048]{1,0:T(8,128)(2,1)}, bf16[32,2048]{1,0:T(8,128)(2,1)S(1)}, u32[]{:S(2)}, u32[]{:S(2)}) %collective-permute-start.1) | collective-permute-done | bytes 131104 | tf_op jit(solution)/shard_map/ppermute | solution.py:173
  29.4 4.4 %collective-permute-done.2 = bf16[32,2048]{1,0:T(8,128)(2,1)S(1)} collective-permute-done((bf16[32,2048]{1,0:T(8,128)(2,1)}, bf16[32,2048]{1,0:T(8,128)(2,1)S(1)}, u32[]{:S(2)}, u32[]{:S(2)}) %collective-permute-start.2) | collective-permute-done | bytes 131104 | tf_op jit(solution)/shard_map/ppermute | solution.py:173
  34.9 4.0 %all-to-all-start.1 = ((bf16[4,32,2,16,128]{4,3,2,1,0:T(8,128)(2,1)}), bf16[4,32,2,16,128]{4,3,2,1,0:T(8,128)(2,1)S(1)}, u32[]{:S(2)}, u32[]{:S(2)}) async-start(bf16[4,32,2,16,128]{4,3,2,1,0:T(8,128)(2,1)} %broadcast_in_dim.8), calls=%async_computation.1 | async-start | bytes 2097152 | tf_op jit(solution)/shard_map/all_to_all | solution.py:182
  39.0 1.4 %collective-permute-start.5 = (bf16[4,32,2048]{2,1,0:T(8,128)(2,1)S(1)}, bf16[4,32,2048]{2,1,0:T(8,128)(2,1)S(1)}, u32[]{:S(2)}, u32[]{:S(2)}) collective-permute-start(bf16[4,32,2048]{2,1,0:T(8,128)(2,1)S(1)} %pad_maximum_fusion.refs_0_), channel_id=1, source_target_pairs={{0,8},{8,16},{16,24},{24,0},{1,9},{9,17},{17,25},{25,1},{2,10},{10... | collective-permute-start | bytes 1572872 | tf_op jit(solution)/shard_map/ppermute | solution.py:161
  40.4 3.0 %collective-permute-start.3 = (bf16[2,32,2048]{2,1,0:T(8,128)(2,1)S(1)}, bf16[2,32,2048]{2,1,0:T(8,128)(2,1)S(1)}, u32[]{:S(2)}, u32[]{:S(2)}) collective-permute-start(bf16[2,32,2048]{2,1,0:T(8,128)(2,1)S(1)} %get-tuple-element.41), channel_id=1, source_target_pairs={{0,64},{64,128},{128,192},{192,32},{32,96},{96,160},{160,224},{224... | collective-permute-start | bytes 786440 | tf_op jit(solution)/shard_map/ppermute | solution.py:179
  43.5 3.8 %collective-permute-done.3 = bf16[2,32,2048]{2,1,0:T(8,128)(2,1)S(1)} collective-permute-done((bf16[2,32,2048]{2,1,0:T(8,128)(2,1)S(1)}, bf16[2,32,2048]{2,1,0:T(8,128)(2,1)S(1)}, u32[]{:S(2)}, u32[]{:S(2)}) %collective-permute-start.3) | collective-permute-done | bytes 262176 | tf_op jit(solution)/shard_map/ppermute | solution.py:179
  47.3 1.9 %collective-permute-done.4 = bf16[2,32,2048]{2,1,0:T(8,128)(2,1)S(1)} collective-permute-done((bf16[2,32,2048]{2,1,0:T(8,128)(2,1)S(1)}, bf16[2,32,2048]{2,1,0:T(8,128)(2,1)S(1)}, u32[]{:S(2)}, u32[]{:S(2)}) %collective-permute-start.4) | collective-permute-done | bytes 262176 | tf_op jit(solution)/shard_map/ppermute | solution.py:180
  49.1 2.2 %collective-permute-done.5.refs_1_ = bf16[4,32,2048]{2,1,0:T(8,128)(2,1)S(1)} collective-permute-done((bf16[4,32,2048]{2,1,0:T(8,128)(2,1)S(1)}, bf16[4,32,2048]{2,1,0:T(8,128)(2,1)S(1)}, u32[]{:S(2)}, u32[]{:S(2)}) %collective-permute-start.5) | collective-permute-done | bytes 524320 | tf_op jit(solution)/shard_map/ppermute | solution.py:161
  52.1 3.3 %collective-permute-start.11 = (bf16[4,32,2,16,128]{4,3,2,1,0:T(8,128)(2,1)S(1)}, bf16[4,32,2,16,128]{4,3,2,1,0:T(8,128)(2,1)S(1)}, u32[]{:S(2)}, u32[]{:S(2)}) collective-permute-start(bf16[4,32,2,16,128]{4,3,2,1,0:T(8,128)(2,1)S(1)} %all-to-all-done.1.refs_9_), channel_id=1, source_target_pairs={{0,1},{1,0},{2,3},{3,2},{4,5},{5,4},{6,7},{7,6},{8,9},{9,8},{10,11... | collective-permute-start | bytes 3145736 | tf_op jit(solution)/shard_map/ppermute | solution.py:184
  55.4 2.8 %collective-permute-start.9 = (bf16[4,32,2048]{2,1,0:T(8,128)(2,1)S(1)}, bf16[4,32,2048]{2,1,0:T(8,128)(2,1)S(1)}, u32[]{:S(2)}, u32[]{:S(2)}) collective-permute-start(bf16[4,32,2048]{2,1,0:T(8,128)(2,1)S(1)} %pad_maximum_fusion.refs_0_), channel_id=1, source_target_pairs={{0,16},{8,24},{16,0},{24,8},{1,17},{9,25},{17,1},{25,9},{2,18},{10... | collective-permute-start | bytes 1572872 | tf_op jit(solution)/shard_map/ppermute | solution.py:161
  61.9 8.6 %collective-permute-done.9.refs_2_ = bf16[4,32,2048]{2,1,0:T(8,128)(2,1)S(1)} collective-permute-done((bf16[4,32,2048]{2,1,0:T(8,128)(2,1)S(1)}, bf16[4,32,2048]{2,1,0:T(8,128)(2,1)S(1)}, u32[]{:S(2)}, u32[]{:S(2)}) %collective-permute-start.9) | collective-permute-done | bytes 524320 | tf_op jit(solution)/shard_map/ppermute | solution.py:161
  71.3 2.0 %collective-permute-start.8 = (bf16[4,32,2048]{2,1,0:T(8,128)(2,1)S(1)}, bf16[4,32,2048]{2,1,0:T(8,128)(2,1)}, u32[]{:S(2)}, u32[]{:S(2)}) collective-permute-start(bf16[4,32,2048]{2,1,0:T(8,128)(2,1)S(1)} %constant_dynamic-update-slice_fusion.refs_0_), channel_id=1, source_target_pairs={{0,24},{8,0},{16,8},{24,16},{1,25},{9,1},{17,9},{25,17},{2,26},{10... | collective-permute-start | bytes 1572872 | tf_op jit(solution)/shard_map/ppermute | solution.py:161
  76.5 5.0 %collective-permute-done.10.refs_3_ = bf16[4,32,2048]{2,1,0:T(8,128)(2,1)} collective-permute-done((bf16[4,32,2048]{2,1,0:T(8,128)(2,1)S(1)}, bf16[4,32,2048]{2,1,0:T(8,128)(2,1)}, u32[]{:S(2)}, u32[]{:S(2)}) %collective-permute-start.10) | collective-permute-done | bytes 524320 | tf_op jit(solution)/shard_map/ppermute | solution.py:161
  82.8 6.9 %ladder.2.refs_11_ = f32[8,512,128]{2,1,0:T(8,128)S(1)} custom-call(s32[6]{0:T(128)S(1)} %stack.65.meta, s32[16,4]{1,0:T(8,128)S(1)} %copy.10.live, bf16[4,32,2048]{2,1,0:T(8,128)(2,1)S(1)} %pad_maximum_fusion.refs_0_, bf16[4,32,2048]{2,1,0:T(8,128)(2,1)S(1)} %copy-done.2, bf16[4,32,2048]{2,1,0:T(8,128)(2,1)S(1)} %copy-done.4, ...), custom_call_target="tpu_custom_call" | custom-call | flops 1650000000 | bytes 10000000 | tf_op jit(solution)/shard_map/ladder/pallas_call | solution.py:113
  89.7 3.3 %collective-permute-done.7.refs_2_ = bf16[4,32,2048]{2,1,0:T(8,128)(2,1)} collective-permute-done((bf16[4,32,2048]{2,1,0:T(8,128)(2,1)S(1)}, bf16[4,32,2048]{2,1,0:T(8,128)(2,1)}, u32[]{:S(2)}, u32[]{:S(2)}) %collective-permute-start.7) | collective-permute-done | bytes 524320 | tf_op jit(solution)/shard_map/ppermute | solution.py:161
  93.1 10.9 %collective-permute-done.8.refs_3_ = bf16[4,32,2048]{2,1,0:T(8,128)(2,1)} collective-permute-done((bf16[4,32,2048]{2,1,0:T(8,128)(2,1)S(1)}, bf16[4,32,2048]{2,1,0:T(8,128)(2,1)}, u32[]{:S(2)}, u32[]{:S(2)}) %collective-permute-start.8) | collective-permute-done | bytes 524320 | tf_op jit(solution)/shard_map/ppermute | solution.py:161
  104.1 1.2 copy.19
  105.3 1.1 copy.20
  106.4 1.1 copy.21
  107.6 7.3 %ladder.3 = (f32[4,512,128]{2,1,0:T(8,128)S(1)}, f32[4,512,128]{2,1,0:T(8,128)S(1)}) custom-call(s32[6]{0:T(128)S(1)} %stack.65.meta, s32[16,4]{1,0:T(8,128)S(1)} %copy.10.live, bf16[4,32,2048]{2,1,0:T(8,128)(2,1)S(1)} %constant_dynamic-update-slice_fusion.refs_0_, bf16[4,32,2048]{2,1,0:T(8,128)(2,1)} %collective-permute-done.6.refs_1_, ...), custom_call_target="tpu_custom_call" | custom-call | flops 1650000000 | bytes 10000000 | tf_op jit(solution)/shard_map/ladder/pallas_call | solution.py:113
  115.7 2.3 %collective-permute-done.12 = f32[4,512,128]{2,1,0:T(8,128)S(1)} collective-permute-done((f32[4,512,128]{2,1,0:T(8,128)S(1)}, f32[4,512,128]{2,1,0:T(8,128)S(1)}, u32[]{:S(2)}, u32[]{:S(2)}) %collective-permute-start.12) | collective-permute-done | bytes 1048608 | tf_op jit(solution)/shard_map/ppermute | solution.py:190
  119.6 2.4 %collective-permute-start.14 = (f32[512,128]{1,0:T(8,128)S(1)}, f32[512,128]{1,0:T(8,128)S(1)}, u32[]{:S(2)}, u32[]{:S(2)}) collective-permute-start(f32[512,128]{1,0:T(8,128)S(1)} %get-tuple-element.36), channel_id=1, source_target_pairs={{0,4},{2,6},{4,0},{6,2},{1,5},{3,7},{5,1},{7,3},{8,12},{10,14},{12... | collective-permute-start | bytes 786440 | tf_op jit(solution)/shard_map/ppermute | solution.py:193
  122.0 1.2 collective-permute-start.15
  123.2 4.4 %collective-permute-done.13.p2 = f32[512,128]{1,0:T(8,128)S(1)} collective-permute-done((f32[512,128]{1,0:T(8,128)S(1)}, f32[512,128]{1,0:T(8,128)S(1)}, u32[]{:S(2)}, u32[]{:S(2)}) %collective-permute-start.13) | collective-permute-done | bytes 262176 | tf_op jit(solution)/shard_map/ppermute | solution.py:193
  127.7 6.1 %collective-permute-done.14.p3 = f32[512,128]{1,0:T(8,128)S(1)} collective-permute-done((f32[512,128]{1,0:T(8,128)S(1)}, f32[512,128]{1,0:T(8,128)S(1)}, u32[]{:S(2)}, u32[]{:S(2)}) %collective-permute-start.14) | collective-permute-done | bytes 262176 | tf_op jit(solution)/shard_map/ppermute | solution.py:193
  134.5 2.4 %finish.1 = bf16[128,512]{1,0:T(8,128)(2,1)} custom-call(s32[6]{0:T(128)} %copy-done.5, f32[32]{0:T(128)} %occ.1, f32[128]{0:T(128)} %vir.1, f32[32,128]{1,0:T(8,128)} %broadcast_in_dim.6.occ_col, f32[1,128]{1,0:T(1,128)} %bitcast.93, f32[512,128]{1,0:T(8,128)} %get-tuple-element.38.p0, f32[512,128]{1,0:T(8,128)} %get-tuple-element.39.p1, ...), custom_call_target="tpu_custom_call" | custom-call | flops 400000 | bytes 1500000 | tf_op jit(solution)/shard_map/finish/pallas_call | solution.py:143
  (60 shorter events, 15.2 us)
Async XLA Ops:
  1.9 36.9 %copy-start.6 = (bf16[32,2048]{1,0:T(8,128)(2,1)S(1)}, bf16[32,2048]{1,0:T(8,128)(2,1)}, u32[]{:S(2)}) copy-start(bf16[32,2048]{1,0:T(8,128)(2,1)} %param.7) | copy-start | bytes 393220
  1.9 31.8 %all-to-all-start = ((bf16[32,2,16,128]{3,2,1,0:T(8,128)(2,1)}), bf16[32,2,16,128]{3,2,1,0:T(8,128)(2,1)S(1)}, u32[]{:S(2)}, u32[]{:S(2)}) async-start(bf16[32,2,16,128]{3,2,1,0:T(8,128)(2,1)} %bitcast.10), calls=%async_computation | async-start | bytes 524288 | tf_op jit(solution)/shard_map/all_to_all | solution.py:176
  14.1 13.2 %collective-permute-start = (bf16[32,2048]{1,0:T(8,128)(2,1)}, bf16[32,2048]{1,0:T(8,128)(2,1)S(1)}, u32[]{:S(2)}, u32[]{:S(2)}) collective-permute-start(bf16[32,2048]{1,0:T(8,128)(2,1)} %param.7), channel_id=1, source_target_pairs={{0,128},{64,192},{128,32},{192,96},{32,160},{96,224},{160,0},{224,... | collective-permute-start | bytes 393224 | tf_op jit(solution)/shard_map/ppermute | solution.py:173
  16.3 13.0 %collective-permute-start.1 = (bf16[32,2048]{1,0:T(8,128)(2,1)}, bf16[32,2048]{1,0:T(8,128)(2,1)S(1)}, u32[]{:S(2)}, u32[]{:S(2)}) collective-permute-start(bf16[32,2048]{1,0:T(8,128)(2,1)} %param.7), channel_id=1, source_target_pairs={{0,160},{64,224},{128,0},{192,64},{32,128},{96,192},{160,32},{224,... | collective-permute-start | bytes 393224 | tf_op jit(solution)/shard_map/ppermute | solution.py:173
  17.8 15.9 %collective-permute-start.2 = (bf16[32,2048]{1,0:T(8,128)(2,1)}, bf16[32,2048]{1,0:T(8,128)(2,1)S(1)}, u32[]{:S(2)}, u32[]{:S(2)}) collective-permute-start(bf16[32,2048]{1,0:T(8,128)(2,1)} %param.7), channel_id=1, source_target_pairs={{0,32},{64,96},{128,160},{192,224},{32,0},{96,64},{160,128},{224,1... | collective-permute-start | bytes 393224 | tf_op jit(solution)/shard_map/ppermute | solution.py:173
  33.7 5.2 %copy-start.7 = (bf16[32,2048]{1,0:T(8,128)(2,1)}, bf16[32,2048]{1,0:T(8,128)(2,1)S(1)}, u32[]{:S(2)}) copy-start(bf16[32,2048]{1,0:T(8,128)(2,1)S(1)} %collective-permute-done.2) | copy-start | bytes 393220
  34.9 17.2 %all-to-all-start.1 = ((bf16[4,32,2,16,128]{4,3,2,1,0:T(8,128)(2,1)}), bf16[4,32,2,16,128]{4,3,2,1,0:T(8,128)(2,1)S(1)}, u32[]{:S(2)}, u32[]{:S(2)}) async-start(bf16[4,32,2,16,128]{4,3,2,1,0:T(8,128)(2,1)} %broadcast_in_dim.8), calls=%async_computation.1 | async-start | bytes 2097152 | tf_op jit(solution)/shard_map/all_to_all | solution.py:182
  38.9 35.1 %copy-start.14 = (s32[16,4]{0,1:T(4,128)S(1)}, s32[16,4]{0,1:T(4,128)}, u32[]{:S(2)}) copy-start(s32[16,4]{0,1:T(4,128)} %param.9) | copy-start | bytes 772
  39.0 12.3 %collective-permute-start.5 = (bf16[4,32,2048]{2,1,0:T(8,128)(2,1)S(1)}, bf16[4,32,2048]{2,1,0:T(8,128)(2,1)S(1)}, u32[]{:S(2)}, u32[]{:S(2)}) collective-permute-start(bf16[4,32,2048]{2,1,0:T(8,128)(2,1)S(1)} %pad_maximum_fusion.refs_0_), channel_id=1, source_target_pairs={{0,8},{8,16},{16,24},{24,0},{1,9},{9,17},{17,25},{25,1},{2,10},{10... | collective-permute-start | bytes 1572872 | tf_op jit(solution)/shard_map/ppermute | solution.py:161
  40.4 6.8 %collective-permute-start.3 = (bf16[2,32,2048]{2,1,0:T(8,128)(2,1)S(1)}, bf16[2,32,2048]{2,1,0:T(8,128)(2,1)S(1)}, u32[]{:S(2)}, u32[]{:S(2)}) collective-permute-start(bf16[2,32,2048]{2,1,0:T(8,128)(2,1)S(1)} %get-tuple-element.41), channel_id=1, source_target_pairs={{0,64},{64,128},{128,192},{192,32},{32,96},{96,160},{160,224},{224... | collective-permute-start | bytes 786440 | tf_op jit(solution)/shard_map/ppermute | solution.py:179
  43.5 5.7 %collective-permute-start.4 = (bf16[2,32,2048]{2,1,0:T(8,128)(2,1)S(1)}, bf16[2,32,2048]{2,1,0:T(8,128)(2,1)S(1)}, u32[]{:S(2)}, u32[]{:S(2)}) collective-permute-start(bf16[2,32,2048]{2,1,0:T(8,128)(2,1)S(1)} %get-tuple-element.40), channel_id=1, source_target_pairs={{0,224},{64,0},{128,64},{192,128},{32,192},{96,32},{160,96},{224,1... | collective-permute-start | bytes 786440 | tf_op jit(solution)/shard_map/ppermute | solution.py:180
  47.3 10.9 %copy-start.8 = (bf16[2,32,2048]{2,1,0:T(8,128)(2,1)}, bf16[2,32,2048]{2,1,0:T(8,128)(2,1)S(1)}, u32[]{:S(2)}) copy-start(bf16[2,32,2048]{2,1,0:T(8,128)(2,1)S(1)} %collective-permute-done.3) | copy-start | bytes 786436
  49.1 2.2 %copy-start.9 = (bf16[2,32,2048]{2,1,0:T(8,128)(2,1)}, bf16[2,32,2048]{2,1,0:T(8,128)(2,1)S(1)}, u32[]{:S(2)}) copy-start(bf16[2,32,2048]{2,1,0:T(8,128)(2,1)S(1)} %collective-permute-done.4) | copy-start | bytes 786436
  51.3 0.8 copy-start.1
  52.1 30.7 %collective-permute-start.11 = (bf16[4,32,2,16,128]{4,3,2,1,0:T(8,128)(2,1)S(1)}, bf16[4,32,2,16,128]{4,3,2,1,0:T(8,128)(2,1)S(1)}, u32[]{:S(2)}, u32[]{:S(2)}) collective-permute-start(bf16[4,32,2,16,128]{4,3,2,1,0:T(8,128)(2,1)S(1)} %all-to-all-done.1.refs_9_), channel_id=1, source_target_pairs={{0,1},{1,0},{2,3},{3,2},{4,5},{5,4},{6,7},{7,6},{8,9},{9,8},{10,11... | collective-permute-start | bytes 3145736 | tf_op jit(solution)/shard_map/ppermute | solution.py:184
  55.4 15.1 %collective-permute-start.9 = (bf16[4,32,2048]{2,1,0:T(8,128)(2,1)S(1)}, bf16[4,32,2048]{2,1,0:T(8,128)(2,1)S(1)}, u32[]{:S(2)}, u32[]{:S(2)}) collective-permute-start(bf16[4,32,2048]{2,1,0:T(8,128)(2,1)S(1)} %pad_maximum_fusion.refs_0_), channel_id=1, source_target_pairs={{0,16},{8,24},{16,0},{24,8},{1,17},{9,25},{17,1},{25,9},{2,18},{10... | collective-permute-start | bytes 1572872 | tf_op jit(solution)/shard_map/ppermute | solution.py:161
  58.2 23.3 %collective-permute-start.10 = (bf16[4,32,2048]{2,1,0:T(8,128)(2,1)S(1)}, bf16[4,32,2048]{2,1,0:T(8,128)(2,1)}, u32[]{:S(2)}, u32[]{:S(2)}) collective-permute-start(bf16[4,32,2048]{2,1,0:T(8,128)(2,1)S(1)} %pad_maximum_fusion.refs_0_), channel_id=1, source_target_pairs={{0,24},{8,0},{16,8},{24,16},{1,25},{9,1},{17,9},{25,17},{2,26},{10... | collective-permute-start | bytes 1572872 | tf_op jit(solution)/shard_map/ppermute | solution.py:161
  60.6 29.1 %collective-permute-start.6 = (bf16[4,32,2048]{2,1,0:T(8,128)(2,1)S(1)}, bf16[4,32,2048]{2,1,0:T(8,128)(2,1)}, u32[]{:S(2)}, u32[]{:S(2)}) collective-permute-start(bf16[4,32,2048]{2,1,0:T(8,128)(2,1)S(1)} %constant_dynamic-update-slice_fusion.refs_0_), channel_id=1, source_target_pairs={{0,8},{8,16},{16,24},{24,0},{1,9},{9,17},{17,25},{25,1},{2,10},{10... | collective-permute-start | bytes 1572872 | tf_op jit(solution)/shard_map/ppermute | solution.py:161
  61.7 31.4 %collective-permute-start.7 = (bf16[4,32,2048]{2,1,0:T(8,128)(2,1)S(1)}, bf16[4,32,2048]{2,1,0:T(8,128)(2,1)}, u32[]{:S(2)}, u32[]{:S(2)}) collective-permute-start(bf16[4,32,2048]{2,1,0:T(8,128)(2,1)S(1)} %constant_dynamic-update-slice_fusion.refs_0_), channel_id=1, source_target_pairs={{0,16},{8,24},{16,0},{24,8},{1,17},{9,25},{17,1},{25,9},{2,18},{10... | collective-permute-start | bytes 1572872 | tf_op jit(solution)/shard_map/ppermute | solution.py:161
  70.5 0.8 copy-start.3
  71.3 32.7 %collective-permute-start.8 = (bf16[4,32,2048]{2,1,0:T(8,128)(2,1)S(1)}, bf16[4,32,2048]{2,1,0:T(8,128)(2,1)}, u32[]{:S(2)}, u32[]{:S(2)}) collective-permute-start(bf16[4,32,2048]{2,1,0:T(8,128)(2,1)S(1)} %constant_dynamic-update-slice_fusion.refs_0_), channel_id=1, source_target_pairs={{0,24},{8,0},{16,8},{24,16},{1,25},{9,1},{17,9},{25,17},{2,26},{10... | collective-permute-start | bytes 1572872 | tf_op jit(solution)/shard_map/ppermute | solution.py:161
  74.2 33.4 %copy-start.5 = (s32[6]{0:T(128)}, s32[6]{0:T(128)S(1)}, u32[]{:S(2)}) copy-start(s32[6]{0:T(128)S(1)} %stack.65.meta) | copy-start | bytes 76
  74.2 2.2 %copy-start.4 = (bf16[4,32,2048]{2,1,0:T(8,128)(2,1)S(1)}, bf16[4,32,2048]{2,1,0:T(8,128)(2,1)}, u32[]{:S(2)}) copy-start(bf16[4,32,2048]{2,1,0:T(8,128)(2,1)} %copy-done.3) | copy-start | bytes 1572868
  74.2 8.5 %copy-start.2 = (bf16[4,32,2048]{2,1,0:T(8,128)(2,1)S(1)}, bf16[4,32,2048]{2,1,0:T(8,128)(2,1)}, u32[]{:S(2)}) copy-start(bf16[4,32,2048]{2,1,0:T(8,128)(2,1)} %copy-done.1) | copy-start | bytes 1572868
  75.2 7.5 %copy-start = (bf16[2048,512]{1,0:T(8,128)(2,1)S(1)}, bf16[2048,512]{1,0:T(8,128)(2,1)}, u32[]{:S(2)}) copy-start(bf16[2048,512]{1,0:T(8,128)(2,1)} %refs_8_.3) | copy-start | bytes 6291460
  114.9 18.9 %copy-start.13 = (f32[32]{0:T(128)S(1)}, f32[32]{0:T(128)}, u32[]{:S(2)}) copy-start(f32[32]{0:T(128)} %occ.1) | copy-start | bytes 388
  114.9 3.2 %collective-permute-start.12 = (f32[4,512,128]{2,1,0:T(8,128)S(1)}, f32[4,512,128]{2,1,0:T(8,128)S(1)}, u32[]{:S(2)}, u32[]{:S(2)}) collective-permute-start(f32[4,512,128]{2,1,0:T(8,128)S(1)} %get-tuple-element.34), channel_id=1, source_target_pairs={{0,1},{1,0},{2,3},{3,2},{4,5},{5,4},{6,7},{7,6},{8,9},{9,8},{10,11... | collective-permute-start | bytes 3145736 | tf_op jit(solution)/shard_map/ppermute | solution.py:190
  118.9 8.7 %collective-permute-start.13 = (f32[512,128]{1,0:T(8,128)S(1)}, f32[512,128]{1,0:T(8,128)S(1)}, u32[]{:S(2)}, u32[]{:S(2)}) collective-permute-start(f32[512,128]{1,0:T(8,128)S(1)} %get-tuple-element.37), channel_id=1, source_target_pairs={{0,2},{2,4},{4,6},{6,0},{1,3},{3,5},{5,7},{7,1},{8,10},{10,12},{12... | collective-permute-start | bytes 786440 | tf_op jit(solution)/shard_map/ppermute | solution.py:193
  119.6 14.1 %collective-permute-start.14 = (f32[512,128]{1,0:T(8,128)S(1)}, f32[512,128]{1,0:T(8,128)S(1)}, u32[]{:S(2)}, u32[]{:S(2)}) collective-permute-start(f32[512,128]{1,0:T(8,128)S(1)} %get-tuple-element.36), channel_id=1, source_target_pairs={{0,4},{2,6},{4,0},{6,2},{1,5},{3,7},{5,1},{7,3},{8,12},{10,14},{12... | collective-permute-start | bytes 786440 | tf_op jit(solution)/shard_map/ppermute | solution.py:193
  122.0 11.7 %collective-permute-start.15 = (f32[512,128]{1,0:T(8,128)S(1)}, f32[512,128]{1,0:T(8,128)S(1)}, u32[]{:S(2)}, u32[]{:S(2)}) collective-permute-start(f32[512,128]{1,0:T(8,128)S(1)} %get-tuple-element.35), channel_id=1, source_target_pairs={{0,6},{2,0},{4,2},{6,4},{1,7},{3,1},{5,3},{7,5},{8,14},{10,8},{12,... | collective-permute-start | bytes 786440 | tf_op jit(solution)/shard_map/ppermute | solution.py:193
  127.7 6.8 %copy-start.10 = (f32[512,128]{1,0:T(8,128)}, f32[512,128]{1,0:T(8,128)S(1)}, u32[]{:S(2)}) copy-start(f32[512,128]{1,0:T(8,128)S(1)} %collective-permute-done.13.p2) | copy-start | bytes 786436
  133.7 0.8 copy-start.12
  (1 other events, 0.8 us)

commit v5 on v4

v5 whole, which is shorter than its diff:
```python
import functools

import jax
import jax.numpy as jnp
from jax import lax
from jax.experimental import pallas as pl
from jax.experimental.pallas import tpu as pltpu
from jax.sharding import Mesh, PartitionSpec as P

G = ("zl", "zh", "y")
C = ("x", "core")
Z = ("zl", "zh")
F32 = jnp.float32
BF16 = jnp.bfloat16


def shift(n, s):
    return [(i, (i + s) % n) for i in range(n)]


def z_shift(s):
    at = lambda z: (z % 4) * 2 + z // 4
    return [(at(z), at((z + s) % 8)) for z in range(8)]


NEAR = (0, -1, 1, -2, 2)
FAR = (-3, 3, 4)
CUTS = {NEAR: 3, FAR: 1}


def ladder_kernel(slots, meta, live, *refs):
    n = len(slots)
    cut = CUTS[slots]
    ts, us, (v, wa, wb), refs = refs[:5], refs[5:10], refs[10:13], refs[13:]
    blocks = [(p, d, q, d) for p, q in ((0, 0), (1, 1)) for d in range(n)]
    blocks += [(2, d, 2, d) for d in range(cut)] + [(3, d - cut, 2, d) for d in range(cut, n)]
    blocks += [(4, d, 3, d) for d in range(n)]
    prev = None
    if slots is FAR:
        prev, refs = refs[0], refs[1:]
    outs, (ladder, vm, wm, o2) = refs[:-4], refs[-4:]
    x0, c0, y0, col, z0 = meta[0], meta[1], meta[2], meta[3], meta[5]
    ys = [(y0 + 4 - q) & 3 for q in range(4)]
    zs = [(z0 + (d & 7)) & 7 for d in slots]
    hs = [((z & 3) << 1) | (z >> 2) for z in zs]
    at = [((((z >> 2) ^ c0) << 2) | (((z & 3) + 4 - x0) & 3)) for z in zs]

    @pl.loop(0, 16)
    def _(kt):
        rows = pl.ds(pl.multiple_of(kt * 128, 128), 128)
        for n in range(4):
            tile = v[rows, n * 128 : n * 128 + 128]
            vm[rows, n * 128 : n * 128 + 128] = jnp.where(live[kt, n] != 0, tile, jnp.zeros_like(tile))

    @pl.loop(0, 8)
    def _(r):
        ladder[r] = jnp.zeros((512, 128), F32) if prev is None else prev[r]

    half = 2 * n
    for part_of in (blocks[:half], blocks[half:]):
        rows = jnp.concatenate([ts[p][e] for p, e, _, _ in part_of], 0)
        part = jnp.dot(rows, vm[...], preferred_element_type=F32)
        for m, (_, _, q, d) in enumerate(part_of):
            for a in range(4):
                rows = pl.ds(ys[q] * 4 + a, 32, stride=16)
                ladder[at[d], rows, :] += part[m * 32 : m * 32 + 32, a * 128 : a * 128 + 128]

    lane = lax.broadcasted_iota(jnp.int32, (128, 128), 1)

    def spread(k, which):
        pieces = [w[(x0 + s) & 3, k, which] for w in (wa, wb) for s in range(4)]
        return jnp.concatenate(pieces, 0)

    acc = jnp.zeros((512, 128), F32)
    w_all = None
    for m in range(0, 4 * n, 2):
        pair = blocks[m : m + 2]
        lhs = jnp.concatenate([us[p][e].reshape(512, 128) for p, e, _, _ in pair], 1)
        rhs = jnp.concatenate([spread(hs[d] * 4 + ys[q], 1) for _, _, q, d in pair], 1)
        acc = acc + lax.dot_general(lhs, rhs, (((1,), (1,)), ((), ())), preferred_element_type=F32)
        if m % 8 == 0:
            w_all = jnp.zeros((128, 128), F32)
        for f, (_, _, q, d) in enumerate(pair):
            place = m % 8 + f
            wk = spread(hs[d] * 4 + ys[q], 0).astype(F32)
            wk = pltpu.roll(wk, (16 * place + 128 - 16 * col) & 127, 1)
            w_all = jnp.where((lane >> 4) == place, wk, w_all)
        if m % 8 == 6 or m + 2 == 4 * n:
            top = m // 8 * 128
            width = min(128, 64 * n - top)
            wm[:, top : top + width] = w_all[:, :width].astype(BF16)
    o2[...] = acc.T

    own = (lane >> 4) == col

    @pl.loop(0, 16)
    def _(jj):
        j = jj * 2
        rhs = jnp.concatenate(
            [jnp.concatenate([us[p][e, j + f] for p, e, _, _ in blocks], 0) for f in range(2)], 1
        )
        one = jnp.dot(wm[...], rhs, preferred_element_type=F32)
        two = o2[:, pl.ds(pl.multiple_of((jj >> 2) * 128, 128), 128)]
        for f in range(2):
            placed = pltpu.roll(two, (16 * col + 128 - 16 * ((j + f) & 7)) & 127, 1)
            both = one[:, f * 128 : f * 128 + 128] + jnp.where(own, placed, 0.0)
            rows = pl.ds(pl.multiple_of((j + f) * 16, 16), 16)
            for r in range(8):
                value = ladder[r, rows, :] + both[r * 16 : r * 16 + 16]
                if prev is None:
                    outs[0][r, rows, :] = value
                else:
                    outs[r // 4][r % 4, rows, :] = value


def ladder_call(slots, meta, live, ts, us, v, wa, wb, prev=()):
    smem = pl.BlockSpec(memory_space=pltpu.SMEM)
    vmem = pl.BlockSpec(memory_space=pltpu.VMEM)
    whole = jax.ShapeDtypeStruct((8, 512, 128), F32)
    half = jax.ShapeDtypeStruct((4, 512, 128), F32)
    return pl.pallas_call(
        functools.partial(ladder_kernel, slots),
        out_shape=(half, half) if prev else (whole,),
        in_specs=[smem, smem] + [vmem] * (13 + len(prev)),
        out_specs=(vmem, vmem) if prev else (vmem,),
        scratch_shapes=[
            pltpu.VMEM((8, 512, 128), F32),
            pltpu.VMEM((2048, 512), BF16),
            pltpu.VMEM((128, 64 * len(slots)), BF16),
            pltpu.VMEM((128, 512), F32),
        ],
        cost_estimate=pl.CostEstimate(flops=400_000_000 * len(slots), bytes_accessed=10_000_000, transcendentals=0),
        compiler_params=pltpu.CompilerParams(vmem_limit_bytes=24 << 20),
        name="ladder",
    )(meta, live, *ts, *us, v, wa, wb, *prev)


def finish_kernel(meta, occ, vir, occ_col, vir_row, p0, p1, p2, p3, p4, out):
    col, g = meta[3], meta[4]
    for il in range(4):
        for a in range(4):
            rows = pl.ds(il * 4 + a, 32, stride=16)
            total = ((p0[rows, :] + p1[rows, :]) + p2[rows, :]) + (p3[rows, :] + p4[rows, :])
            denom = ((vir[g * 4 + a] + vir_row[...]) - occ[col * 4 + il]) - occ_col[...]
            out[il * 32 : il * 32 + 32, a * 128 : a * 128 + 128] = (total / denom).astype(BF16)


def finish_call(meta, eps_occ, eps_vir, parts):
    smem = pl.BlockSpec(memory_space=pltpu.SMEM)
    vmem = pl.BlockSpec(memory_space=pltpu.VMEM)
    return pl.pallas_call(
        finish_kernel,
        out_shape=jax.ShapeDtypeStruct((128, 512), BF16),
        in_specs=[smem] * 3 + [vmem] * 7,
        out_specs=vmem,
        cost_estimate=pl.CostEstimate(flops=400_000, bytes_accessed=1_500_000, transcendentals=0),
        name="finish",
    )(
        meta,
        eps_occ,
        eps_vir,
        jnp.broadcast_to(eps_occ[:, None], (32, 128)),
        eps_vir[None, :],
        *parts,
    )


def over_y(group, cut):
    down = lax.ppermute(group, "y", shift(4, 1))
    up = lax.ppermute(group, "y", shift(4, -1))
    first = lax.ppermute(down[:cut], "y", shift(4, 1))
    rest = lax.ppermute(up[cut:], "y", shift(4, -1))
    return [group, down, first, rest, up]


def split_rows(ts):
    return [t.reshape(-1, 32, 16, 128) for t in ts]


def local(amplitudes, ladder_ints, tile_live, cycle_direct, cycle_exchange, eps_occ, eps_vir):
    x0, c0, y0 = lax.axis_index("x"), lax.axis_index("core"), lax.axis_index("y")
    z0 = lax.axis_index("zh") * 4 + lax.axis_index("zl")
    meta = jnp.stack([x0, c0, y0, lax.axis_index(C), lax.axis_index(G), z0]).astype(jnp.int32)
    both = jnp.stack([cycle_direct, cycle_exchange]).reshape(2, 4, 32, 4, 128)
    both = both.transpose(2, 0, 1, 3, 4).reshape(32, 2, 16, 128)
    fwd = bwd = amplitudes
    ring = [amplitudes]
    for k in range(1, 4):
        fwd, bwd = lax.ppermute(fwd, Z, z_shift(1)), lax.ppermute(bwd, Z, z_shift(-1))
        ring += [fwd, bwd]
    ring.append(lax.ppermute(fwd, Z, z_shift(1)))
    near = jnp.stack(ring[:5])
    both = lax.all_to_all(both, G, 0, 0, tiled=True)
    wa = lax.all_to_all(jnp.broadcast_to(both[None], (4, 32, 2, 16, 128)), "x", 0, 0, tiled=True)
    wa, ring[7] = lax.optimization_barrier((wa, ring[7]))
    wb = lax.ppermute(wa, "core", shift(2, 1))
    far = jnp.stack(ring[5:])
    ts_near, ts_far = over_y(near, CUTS[NEAR]), over_y(far, CUTS[FAR])
    prev = list(ladder_call(NEAR, meta, tile_live, ts_near, split_rows(ts_near), ladder_ints, wa, wb))
    *ts_far, prev[0] = lax.optimization_barrier((*ts_far, prev[0]))
    keep, away = ladder_call(FAR, meta, tile_live, ts_far, split_rows(ts_far), ladder_ints, wa, wb, tuple(prev))
    got = lax.ppermute(away, "core", shift(2, 1))
    parts = [keep[0], got[0]]
    for s in (1, 2, 3):
        parts.append(lax.ppermute(keep[s] + got[s], "x", shift(4, s)))
    return finish_call(meta, eps_occ, eps_vir, parts)


def solution(mesh):
    fine = Mesh(mesh.devices.reshape(4, 2, 4, 4, 2), ("zl", "zh", "y", "x", "core"))
    placed = (P(G, C), P(C, G), P(C, G), P(C, G), P(C, G), P(), P())
    return jax.shard_map(local, mesh=fine, in_specs=placed, out_specs=P(C, G), check_vma=False)
```

time: 139 us -> 122 us (0.88)
  waiting for transfers between devices: 59.2 us -> 35.2 us
  starting transfers between devices: 44.5 us -> 49.3 us
  local copies, waits for them, and re-layouts: 13.1 us -> 15.4 us
    ppermute x11 -> x15, waiting for transfers between devices: 46.5 us -> 16.8 us  [the longest x2 6.58 us: over_y(): up = lax.ppermute(group, 'y', shift(4, -1))]
    ppermute x11 -> x15, starting transfers between devices: 19.9 us -> 25.8 us  [the longest x3 8.06 us: local(): lax.ppermute(bwd, Z, z_shift(-1))]
    all_to_all x1, waiting for transfers between devices: 0.01 us -> 3.97 us  [local(): lax.all_to_all(jnp.broadcast_to(both[None], (4, 32, 2, 16, 128)), 'x', 0,...]
    all_to_all x1, starting transfers between devices: 12.2 us -> 8.3 us  [local(): both = lax.all_to_all(both, G, 0, 0, tiled=True)]
    ppermute x1, starting transfers between devices: 3.29 us -> 6.69 us  [local(): wb = lax.ppermute(wa, 'core', shift(2, 1))]
    ppermute x3, starting transfers between devices: 4.29 us -> 2.68 us  [local(): parts.append(lax.ppermute(keep[s] + got[s], 'x', shift(4, s)))]
    ppermute x3, waiting for transfers between devices: 10.5 us -> 12 us  [local(): parts.append(lax.ppermute(keep[s] + got[s], 'x', shift(4, s)))]
    unnamed x43 -> x59, local copies, waits for them, and re-layouts: 9.34 us -> 10.3 us
  transfers between devices with their start and end apart: 18 -> 22, of which waited for: 13 -> 11; matrix products, arithmetic and copies ran while one was open for 5% -> 12% of each run, Pallas kernels for 5% -> 6%
where the time goes in v5:
time: 122 us; the launch traced here: 121 us
  starting transfers between devices  49.3 us (40%)
  waiting for transfers between devices  35.2 us (29%)
  Pallas kernels  16.7 us (14%)
  local copies, waits for them, and re-layouts  15.4 us (13%)
  other arithmetic  3.86 us (3%)
    pallas_call x2, Pallas kernels, ladder_call(): pl.pallas_call(functools.partial(ladder_kernel, slots), out_shape=(half,...  14.3 us
    ppermute x3, waiting for transfers between devices, local(): parts.append(lax.ppermute(keep[s] + got[s], 'x', shift(4, s)))  12 us
    unnamed x59, local copies, waits for them, and re-layouts  10.3 us
    all_to_all x1, starting transfers between devices, local(): both = lax.all_to_all(both, G, 0, 0, tiled=True)  8.3 us
    ppermute x3, starting transfers between devices, local(): lax.ppermute(bwd, Z, z_shift(-1))  8.06 us
    ppermute x2, starting transfers between devices, over_y(): rest = lax.ppermute(up[cut:], 'y', shift(4, -1))  7.05 us
    ppermute x1, starting transfers between devices, local(): wb = lax.ppermute(wa, 'core', shift(2, 1))  6.69 us
    ppermute x2, waiting for transfers between devices, over_y(): up = lax.ppermute(group, 'y', shift(4, -1))  6.58 us
  transfers between devices with their start and end apart: 22, of which 11 were waited for; matrix products, arithmetic and copies ran while one was open for 12% of the time, Pallas kernels for 6%

profile of v5, /device:TPU:1, one launch (start us, length us, event | category | flops | bytes accessed | tf_op | source)
XLA Modules:
  0.0 120.8 jit_solution(3091523449824118137)
XLA Ops:
  0.0 2.5 %collective-permute-start = (bf16[32,2048]{1,0:T(8,128)(2,1)}, bf16[32,2048]{1,0:T(8,128)(2,1)S(1)}, u32[]{:S(2)}, u32[]{:S(2)}) collective-permute-start(bf16[32,2048]{1,0:T(8,128)(2,1)} %param.7), channel_id=1, source_target_pairs={{0,64},{64,128},{128,192},{192,32},{32,96},{96,160},{160,224},{224... | collective-permute-start | bytes 393224 | tf_op jit(solution)/shard_map/ppermute | solution.py:189
  2.5 3.9 %collective-permute-start.3 = (bf16[32,2048]{1,0:T(8,128)(2,1)}, bf16[32,2048]{1,0:T(8,128)(2,1)S(1)}, u32[]{:S(2)}, u32[]{:S(2)}) collective-permute-start(bf16[32,2048]{1,0:T(8,128)(2,1)} %param.7), channel_id=1, source_target_pairs={{0,224},{64,0},{128,64},{192,128},{32,192},{96,32},{160,96},{224,1... | collective-permute-start | bytes 393224 | tf_op jit(solution)/shard_map/ppermute | solution.py:189
  6.4 1.2 maximum_bitcast_fusion
  8.4 8.3 %all-to-all-start = ((bf16[32,2,16,128]{3,2,1,0:T(8,128)(2,1)}), bf16[32,2,16,128]{3,2,1,0:T(8,128)(2,1)S(1)}, u32[]{:S(2)}, u32[]{:S(2)}) async-start(bf16[32,2,16,128]{3,2,1,0:T(8,128)(2,1)} %bitcast.12), calls=%async_computation | async-start | bytes 524288 | tf_op jit(solution)/shard_map/all_to_all | solution.py:193
  16.7 1.6 %bitcast_dynamic-update-slice_fusion.9 = bf16[5,32,2048]{2,1,0:T(8,128)(2,1)} fusion(bf16[32,2048]{1,0:T(8,128)(2,1)} %param.7), kind=kLoop, calls=%fused_computation.19 | loop fusion | bytes 262144
  18.3 1.2 %collective-permute-start.1 = (bf16[32,2048]{1,0:T(8,128)(2,1)S(1)}, bf16[32,2048]{1,0:T(8,128)(2,1)S(1)}, u32[]{:S(2)}, u32[]{:S(2)}) collective-permute-start(bf16[32,2048]{1,0:T(8,128)(2,1)S(1)} %collective-permute-done), channel_id=1, source_target_pairs={{0,64},{64,128},{128,192},{192,32},{32,96},{96,160},{160,224},{224... | collective-permute-start | bytes 393224 | tf_op jit(solution)/shard_map/ppermute | solution.py:189
  20.2 1.4 %collective-permute-start.4 = (bf16[32,2048]{1,0:T(8,128)(2,1)S(1)}, bf16[32,2048]{1,0:T(8,128)(2,1)S(1)}, u32[]{:S(2)}, u32[]{:S(2)}) collective-permute-start(bf16[32,2048]{1,0:T(8,128)(2,1)S(1)} %collective-permute-done.3), channel_id=1, source_target_pairs={{0,224},{64,0},{128,64},{192,128},{32,192},{96,32},{160,96},{224,1... | collective-permute-start | bytes 393224 | tf_op jit(solution)/shard_map/ppermute | solution.py:189
  22.3 4.9 %collective-permute-done.1 = bf16[32,2048]{1,0:T(8,128)(2,1)S(1)} collective-permute-done((bf16[32,2048]{1,0:T(8,128)(2,1)S(1)}, bf16[32,2048]{1,0:T(8,128)(2,1)S(1)}, u32[]{:S(2)}, u32[]{:S(2)}) %collective-permute-start.1) | collective-permute-done | bytes 131104 | tf_op jit(solution)/shard_map/ppermute | solution.py:189
  27.3 1.2 broadcast_in_dim.8
  28.5 4.1 %all-to-all-start.1 = ((bf16[4,32,2,16,128]{4,3,2,1,0:T(8,128)(2,1)}), bf16[4,32,2,16,128]{4,3,2,1,0:T(8,128)(2,1)S(1)}, u32[]{:S(2)}, u32[]{:S(2)}) async-start(bf16[4,32,2,16,128]{4,3,2,1,0:T(8,128)(2,1)} %broadcast_in_dim.8), calls=%async_computation.1 | async-start | bytes 2097152 | tf_op jit(solution)/shard_map/all_to_all | solution.py:194
  33.3 1.2 %collective-permute-start.6 = (bf16[32,2048]{1,0:T(8,128)(2,1)S(1)}, bf16[32,2048]{1,0:T(8,128)(2,1)S(1)}, u32[]{:S(2)}, u32[]{:S(2)}) collective-permute-start(bf16[32,2048]{1,0:T(8,128)(2,1)S(1)} %collective-permute-done.2), channel_id=1, source_target_pairs={{0,64},{64,128},{128,192},{192,32},{32,96},{96,160},{160,224},{224... | collective-permute-start | bytes 393224 | tf_op jit(solution)/shard_map/ppermute | solution.py:191
  35.9 2.5 %collective-permute-done.6 = bf16[32,2048]{1,0:T(8,128)(2,1)S(1)} collective-permute-done((bf16[32,2048]{1,0:T(8,128)(2,1)S(1)}, bf16[32,2048]{1,0:T(8,128)(2,1)S(1)}, u32[]{:S(2)}, u32[]{:S(2)}) %collective-permute-start.6) | collective-permute-done | bytes 131104 | tf_op jit(solution)/shard_map/ppermute | solution.py:191
  38.4 4.0 %all-to-all-done.1.refs_11_ = bf16[4,32,2,16,128]{4,3,2,1,0:T(8,128)(2,1)S(1)} async-done(((bf16[4,32,2,16,128]{4,3,2,1,0:T(8,128)(2,1)}), bf16[4,32,2,16,128]{4,3,2,1,0:T(8,128)(2,1)S(1)}, u32[]{:S(2)}, u32[]{:S(2)}) %all-to-all-start.1) | async-done | bytes 1048608 | tf_op jit(solution)/shard_map/all_to_all | solution.py:194
  42.4 6.7 %collective-permute-start.15 = (bf16[4,32,2,16,128]{4,3,2,1,0:T(8,128)(2,1)S(1)}, bf16[4,32,2,16,128]{4,3,2,1,0:T(8,128)(2,1)S(1)}, u32[]{:S(2)}, u32[]{:S(2)}) collective-permute-start(bf16[4,32,2,16,128]{4,3,2,1,0:T(8,128)(2,1)S(1)} %all-to-all-done.1.refs_11_), channel_id=1, source_target_pairs={{0,1},{1,0},{2,3},{3,2},{4,5},{5,4},{6,7},{7,6},{8,9},{9,8},{10,11... | collective-permute-start | bytes 3145736 | tf_op jit(solution)/shard_map/ppermute | solution.py:196
  49.1 2.5 %collective-permute-start.13 = (bf16[5,32,2048]{2,1,0:T(8,128)(2,1)}, bf16[5,32,2048]{2,1,0:T(8,128)(2,1)S(1)}, u32[]{:S(2)}, u32[]{:S(2)}) collective-permute-start(bf16[5,32,2048]{2,1,0:T(8,128)(2,1)} %bitcast_dynamic-update-slice_fusion.5.refs_0_), channel_id=1, source_target_pairs={{0,24},{8,0},{16,8},{24,16},{1,25},{9,1},{17,9},{25,17},{2,26},{10... | collective-permute-start | bytes 1966088 | tf_op jit(solution)/shard_map/ppermute | solution.py:170
  51.6 2.7 %collective-permute-start.5 = (bf16[32,2048]{1,0:T(8,128)(2,1)}, bf16[32,2048]{1,0:T(8,128)(2,1)S(1)}, u32[]{:S(2)}, u32[]{:S(2)}) collective-permute-start(bf16[32,2048]{1,0:T(8,128)(2,1)} %copy-done.8), channel_id=1, source_target_pairs={{0,224},{64,0},{128,64},{192,128},{32,192},{96,32},{160,96},{224,1... | collective-permute-start | bytes 393224 | tf_op jit(solution)/shard_map/ppermute | solution.py:189
  54.3 2.8 %collective-permute-done.5 = bf16[32,2048]{1,0:T(8,128)(2,1)S(1)} collective-permute-done((bf16[32,2048]{1,0:T(8,128)(2,1)}, bf16[32,2048]{1,0:T(8,128)(2,1)S(1)}, u32[]{:S(2)}, u32[]{:S(2)}) %collective-permute-start.5) | collective-permute-done | bytes 131104 | tf_op jit(solution)/shard_map/ppermute | solution.py:189
  57.1 1.8 %pad_maximum_fusion.refs_0_ = bf16[3,32,2048]{2,1,0:T(8,128)(2,1)} fusion(bf16[1,32,2048]{2,1,0:T(8,128)(2,1)} %bitcast.125, bf16[1,32,2048]{2,1,0:T(8,128)(2,1)S(1)} %bitcast.126, bf16[1,32,2048]{2,1,0:T(8,128)(2,1)} %bitcast.124), kind=kLoop, calls=%fused_computation | loop fusion | flops 393216 | bytes 786432 | tf_op jit(solution)/shard_map/stack | solution.py:197
  61.2 1.1 collective-permute-start.12
  63.0 2.9 %collective-permute-done.13.refs_4_ = bf16[5,32,2048]{2,1,0:T(8,128)(2,1)S(1)} collective-permute-done((bf16[5,32,2048]{2,1,0:T(8,128)(2,1)}, bf16[5,32,2048]{2,1,0:T(8,128)(2,1)S(1)}, u32[]{:S(2)}, u32[]{:S(2)}) %collective-permute-start.13) | collective-permute-done | bytes 655392 | tf_op jit(solution)/shard_map/ppermute | solution.py:170
  66.0 3.4 %collective-permute-start.14 = (bf16[2,32,2048]{2,1,0:T(8,128)(2,1)S(1)}, bf16[2,32,2048]{2,1,0:T(8,128)(2,1)S(1)}, u32[]{:S(2)}, u32[]{:S(2)}) collective-permute-start(bf16[2,32,2048]{2,1,0:T(8,128)(2,1)S(1)} %slice.51), channel_id=1, source_target_pairs={{0,24},{8,0},{16,8},{24,16},{1,25},{9,1},{17,9},{25,17},{2,26},{10... | collective-permute-start | bytes 786440 | tf_op jit(solution)/shard_map/ppermute | solution.py:172
  70.8 3.6 %collective-permute-done.9.refs_4_ = bf16[3,32,2048]{2,1,0:T(8,128)(2,1)} collective-permute-done((bf16[3,32,2048]{2,1,0:T(8,128)(2,1)}, bf16[3,32,2048]{2,1,0:T(8,128)(2,1)}, u32[]{:S(2)}, u32[]{:S(2)}) %collective-permute-start.9) | collective-permute-done | bytes 393248 | tf_op jit(solution)/shard_map/ppermute | solution.py:170
  75.4 3.7 %collective-permute-start.10 = (bf16[2,32,2048]{2,1,0:T(8,128)(2,1)S(1)}, bf16[2,32,2048]{2,1,0:T(8,128)(2,1)S(1)}, u32[]{:S(2)}, u32[]{:S(2)}) collective-permute-start(bf16[2,32,2048]{2,1,0:T(8,128)(2,1)S(1)} %slice.49), channel_id=1, source_target_pairs={{0,24},{8,0},{16,8},{24,16},{1,25},{9,1},{17,9},{25,17},{2,26},{10... | collective-permute-start | bytes 786440 | tf_op jit(solution)/shard_map/ppermute | solution.py:172
  81.4 7.8 %ladder.2.refs_13_ = f32[8,512,128]{2,1,0:T(8,128)S(1)} custom-call(s32[6]{0:T(128)S(1)} %stack.78.meta, s32[16,4]{1,0:T(8,128)S(1)} %copy.10.live, bf16[5,32,2048]{2,1,0:T(8,128)(2,1)} %bitcast_dynamic-update-slice_fusion.5.refs_0_, bf16[5,32,2048]{2,1,0:T(8,128)(2,1)S(1)} %collective-permute-done.11.refs_1_, ...), custom_call_target="tpu_custom_call" | custom-call | flops 2000000000 | bytes 10000000 | tf_op jit(solution)/shard_map/ladder/pallas_call | solution.py:121
  89.3 1.1 copy.20
  91.6 6.4 %ladder.3 = (f32[4,512,128]{2,1,0:T(8,128)S(1)}, f32[4,512,128]{2,1,0:T(8,128)S(1)}) custom-call(s32[6]{0:T(128)S(1)} %stack.78.meta, s32[16,4]{1,0:T(8,128)S(1)} %copy.10.live, bf16[3,32,2048]{2,1,0:T(8,128)(2,1)} %pad_maximum_fusion.refs_0_, bf16[3,32,2048]{2,1,0:T(8,128)(2,1)S(1)} %collective-permute-done.7.refs_1_, ...), custom_call_target="tpu_custom_call" | custom-call | flops 1200000000 | bytes 10000000 | tf_op jit(solution)/shard_map/ladder/pallas_call | solution.py:121
  98.0 1.7 %collective-permute-start.16 = (f32[4,512,128]{2,1,0:T(8,128)S(1)}, f32[4,512,128]{2,1,0:T(8,128)S(1)}, u32[]{:S(2)}, u32[]{:S(2)}) collective-permute-start(f32[4,512,128]{2,1,0:T(8,128)S(1)} %get-tuple-element.24), channel_id=1, source_target_pairs={{0,1},{1,0},{2,3},{3,2},{4,5},{5,4},{6,7},{7,6},{8,9},{9,8},{10,11... | collective-permute-start | bytes 3145736 | tf_op jit(solution)/shard_map/ppermute | solution.py:202
  99.7 2.3 %collective-permute-done.16 = f32[4,512,128]{2,1,0:T(8,128)S(1)} collective-permute-done((f32[4,512,128]{2,1,0:T(8,128)S(1)}, f32[4,512,128]{2,1,0:T(8,128)S(1)}, u32[]{:S(2)}, u32[]{:S(2)}) %collective-permute-start.16) | collective-permute-done | bytes 1048608 | tf_op jit(solution)/shard_map/ppermute | solution.py:202
  103.2 1.8 %collective-permute-start.18 = (f32[512,128]{1,0:T(8,128)S(1)}, f32[512,128]{1,0:T(8,128)S(1)}, u32[]{:S(2)}, u32[]{:S(2)}) collective-permute-start(f32[512,128]{1,0:T(8,128)S(1)} %get-tuple-element.26), channel_id=1, source_target_pairs={{0,4},{2,6},{4,0},{6,2},{1,5},{3,7},{5,1},{7,3},{8,12},{10,14},{12... | collective-permute-start | bytes 786440 | tf_op jit(solution)/shard_map/ppermute | solution.py:205
  105.6 6.6 %collective-permute-done.17.p2 = f32[512,128]{1,0:T(8,128)S(1)} collective-permute-done((f32[512,128]{1,0:T(8,128)S(1)}, f32[512,128]{1,0:T(8,128)S(1)}, u32[]{:S(2)}, u32[]{:S(2)}) %collective-permute-start.17) | collective-permute-done | bytes 262176 | tf_op jit(solution)/shard_map/ppermute | solution.py:205
  112.2 4.5 %collective-permute-done.18.p3 = f32[512,128]{1,0:T(8,128)S(1)} collective-permute-done((f32[512,128]{1,0:T(8,128)S(1)}, f32[512,128]{1,0:T(8,128)S(1)}, u32[]{:S(2)}, u32[]{:S(2)}) %collective-permute-start.18) | collective-permute-done | bytes 262176 | tf_op jit(solution)/shard_map/ppermute | solution.py:205
  118.3 2.4 %finish.1 = bf16[128,512]{1,0:T(8,128)(2,1)} custom-call(s32[6]{0:T(128)} %copy-done.2, f32[32]{0:T(128)} %occ.1, f32[128]{0:T(128)} %vir.1, f32[32,128]{1,0:T(8,128)} %broadcast_in_dim.6.occ_col, f32[1,128]{1,0:T(1,128)} %bitcast.127, f32[512,128]{1,0:T(8,128)} %get-tuple-element.28.p0, f32[512,128]{1,0:T(8,128)} %get-tuple-element.29.p1, ...), custom_call_target="tpu_custom_call" | custom-call | flops 400000 | bytes 1500000 | tf_op jit(solution)/shard_map/finish/pallas_call | solution.py:151
  (87 shorter events, 16.6 us)
Async XLA Ops:
  0.0 18.3 %collective-permute-start = (bf16[32,2048]{1,0:T(8,128)(2,1)}, bf16[32,2048]{1,0:T(8,128)(2,1)S(1)}, u32[]{:S(2)}, u32[]{:S(2)}) collective-permute-start(bf16[32,2048]{1,0:T(8,128)(2,1)} %param.7), channel_id=1, source_target_pairs={{0,64},{64,128},{128,192},{192,32},{32,96},{96,160},{160,224},{224... | collective-permute-start | bytes 393224 | tf_op jit(solution)/shard_map/ppermute | solution.py:189
  2.5 17.7 %collective-permute-start.3 = (bf16[32,2048]{1,0:T(8,128)(2,1)}, bf16[32,2048]{1,0:T(8,128)(2,1)S(1)}, u32[]{:S(2)}, u32[]{:S(2)}) collective-permute-start(bf16[32,2048]{1,0:T(8,128)(2,1)} %param.7), channel_id=1, source_target_pairs={{0,224},{64,0},{128,64},{192,128},{32,192},{96,32},{160,96},{224,1... | collective-permute-start | bytes 393224 | tf_op jit(solution)/shard_map/ppermute | solution.py:189
  8.4 18.9 %all-to-all-start = ((bf16[32,2,16,128]{3,2,1,0:T(8,128)(2,1)}), bf16[32,2,16,128]{3,2,1,0:T(8,128)(2,1)S(1)}, u32[]{:S(2)}, u32[]{:S(2)}) async-start(bf16[32,2,16,128]{3,2,1,0:T(8,128)(2,1)} %bitcast.12), calls=%async_computation | async-start | bytes 524288 | tf_op jit(solution)/shard_map/all_to_all | solution.py:193
  18.3 15.0 %copy-start.10 = (bf16[32,2048]{1,0:T(8,128)(2,1)}, bf16[32,2048]{1,0:T(8,128)(2,1)S(1)}, u32[]{:S(2)}) copy-start(bf16[32,2048]{1,0:T(8,128)(2,1)S(1)} %collective-permute-done) | copy-start | bytes 393220
  18.3 8.9 %collective-permute-start.1 = (bf16[32,2048]{1,0:T(8,128)(2,1)S(1)}, bf16[32,2048]{1,0:T(8,128)(2,1)S(1)}, u32[]{:S(2)}, u32[]{:S(2)}) collective-permute-start(bf16[32,2048]{1,0:T(8,128)(2,1)S(1)} %collective-permute-done), channel_id=1, source_target_pairs={{0,64},{64,128},{128,192},{192,32},{32,96},{96,160},{160,224},{224... | collective-permute-start | bytes 393224 | tf_op jit(solution)/shard_map/ppermute | solution.py:189
  20.2 34.1 %copy-start.3 = (bf16[32,2048]{1,0:T(8,128)(2,1)S(1)}, bf16[32,2048]{1,0:T(8,128)(2,1)}, u32[]{:S(2)}) copy-start(bf16[32,2048]{1,0:T(8,128)(2,1)} %param.7) | copy-start | bytes 393220
  20.2 15.0 %copy-start.4 = (bf16[32,2048]{1,0:T(8,128)(2,1)}, bf16[32,2048]{1,0:T(8,128)(2,1)S(1)}, u32[]{:S(2)}) copy-start(bf16[32,2048]{1,0:T(8,128)(2,1)S(1)} %collective-permute-done.3) | copy-start | bytes 393220
  20.2 14.3 %collective-permute-start.4 = (bf16[32,2048]{1,0:T(8,128)(2,1)S(1)}, bf16[32,2048]{1,0:T(8,128)(2,1)S(1)}, u32[]{:S(2)}, u32[]{:S(2)}) collective-permute-start(bf16[32,2048]{1,0:T(8,128)(2,1)S(1)} %collective-permute-done.3), channel_id=1, source_target_pairs={{0,224},{64,0},{128,64},{192,128},{32,192},{96,32},{160,96},{224,1... | collective-permute-start | bytes 393224 | tf_op jit(solution)/shard_map/ppermute | solution.py:189
  27.2 11.2 %copy-start.6 = (bf16[32,2048]{1,0:T(8,128)(2,1)}, bf16[32,2048]{1,0:T(8,128)(2,1)S(1)}, u32[]{:S(2)}) copy-start(bf16[32,2048]{1,0:T(8,128)(2,1)S(1)} %collective-permute-done.1) | copy-start | bytes 393220
  27.2 6.1 %collective-permute-start.2 = (bf16[32,2048]{1,0:T(8,128)(2,1)S(1)}, bf16[32,2048]{1,0:T(8,128)(2,1)S(1)}, u32[]{:S(2)}, u32[]{:S(2)}) collective-permute-start(bf16[32,2048]{1,0:T(8,128)(2,1)S(1)} %collective-permute-done.1), channel_id=1, source_target_pairs={{0,64},{64,128},{128,192},{192,32},{32,96},{96,160},{160,224},{224... | collective-permute-start | bytes 393224 | tf_op jit(solution)/shard_map/ppermute | solution.py:189
  28.5 31.5 %copy-start.17 = (s32[16,4]{0,1:T(4,128)S(1)}, s32[16,4]{0,1:T(4,128)}, u32[]{:S(2)}) copy-start(s32[16,4]{0,1:T(4,128)} %param.9) | copy-start | bytes 772
  28.5 13.9 %all-to-all-start.1 = ((bf16[4,32,2,16,128]{4,3,2,1,0:T(8,128)(2,1)}), bf16[4,32,2,16,128]{4,3,2,1,0:T(8,128)(2,1)S(1)}, u32[]{:S(2)}, u32[]{:S(2)}) async-start(bf16[4,32,2,16,128]{4,3,2,1,0:T(8,128)(2,1)} %broadcast_in_dim.8), calls=%async_computation.1 | async-start | bytes 2097152 | tf_op jit(solution)/shard_map/all_to_all | solution.py:194
  33.3 9.1 %copy-start.14 = (bf16[32,2048]{1,0:T(8,128)(2,1)}, bf16[32,2048]{1,0:T(8,128)(2,1)S(1)}, u32[]{:S(2)}) copy-start(bf16[32,2048]{1,0:T(8,128)(2,1)S(1)} %collective-permute-done.2) | copy-start | bytes 393220
  33.3 5.1 %collective-permute-start.6 = (bf16[32,2048]{1,0:T(8,128)(2,1)S(1)}, bf16[32,2048]{1,0:T(8,128)(2,1)S(1)}, u32[]{:S(2)}, u32[]{:S(2)}) collective-permute-start(bf16[32,2048]{1,0:T(8,128)(2,1)S(1)} %collective-permute-done.2), channel_id=1, source_target_pairs={{0,64},{64,128},{128,192},{192,32},{32,96},{96,160},{160,224},{224... | collective-permute-start | bytes 393224 | tf_op jit(solution)/shard_map/ppermute | solution.py:191
  35.2 25.9 %collective-permute-start.11 = (bf16[5,32,2048]{2,1,0:T(8,128)(2,1)}, bf16[5,32,2048]{2,1,0:T(8,128)(2,1)S(1)}, u32[]{:S(2)}, u32[]{:S(2)}) collective-permute-start(bf16[5,32,2048]{2,1,0:T(8,128)(2,1)} %bitcast_dynamic-update-slice_fusion.5.refs_0_), channel_id=1, source_target_pairs={{0,8},{8,16},{16,24},{24,0},{1,9},{9,17},{17,25},{25,1},{2,10},{10... | collective-permute-start | bytes 1966088 | tf_op jit(solution)/shard_map/ppermute | solution.py:169
  42.4 38.7 %collective-permute-start.15 = (bf16[4,32,2,16,128]{4,3,2,1,0:T(8,128)(2,1)S(1)}, bf16[4,32,2,16,128]{4,3,2,1,0:T(8,128)(2,1)S(1)}, u32[]{:S(2)}, u32[]{:S(2)}) collective-permute-start(bf16[4,32,2,16,128]{4,3,2,1,0:T(8,128)(2,1)S(1)} %all-to-all-done.1.refs_11_), channel_id=1, source_target_pairs={{0,1},{1,0},{2,3},{3,2},{4,5},{5,4},{6,7},{7,6},{8,9},{9,8},{10,11... | collective-permute-start | bytes 3145736 | tf_op jit(solution)/shard_map/ppermute | solution.py:196
  49.1 16.9 %collective-permute-start.13 = (bf16[5,32,2048]{2,1,0:T(8,128)(2,1)}, bf16[5,32,2048]{2,1,0:T(8,128)(2,1)S(1)}, u32[]{:S(2)}, u32[]{:S(2)}) collective-permute-start(bf16[5,32,2048]{2,1,0:T(8,128)(2,1)} %bitcast_dynamic-update-slice_fusion.5.refs_0_), channel_id=1, source_target_pairs={{0,24},{8,0},{16,8},{24,16},{1,25},{9,1},{17,9},{25,17},{2,26},{10... | collective-permute-start | bytes 1966088 | tf_op jit(solution)/shard_map/ppermute | solution.py:170
  51.6 5.5 %collective-permute-start.5 = (bf16[32,2048]{1,0:T(8,128)(2,1)}, bf16[32,2048]{1,0:T(8,128)(2,1)S(1)}, u32[]{:S(2)}, u32[]{:S(2)}) collective-permute-start(bf16[32,2048]{1,0:T(8,128)(2,1)} %copy-done.8), channel_id=1, source_target_pairs={{0,224},{64,0},{128,64},{192,128},{32,192},{96,32},{160,96},{224,1... | collective-permute-start | bytes 393224 | tf_op jit(solution)/shard_map/ppermute | solution.py:189
  58.9 15.5 %collective-permute-start.9 = (bf16[3,32,2048]{2,1,0:T(8,128)(2,1)}, bf16[3,32,2048]{2,1,0:T(8,128)(2,1)}, u32[]{:S(2)}, u32[]{:S(2)}) collective-permute-start(bf16[3,32,2048]{2,1,0:T(8,128)(2,1)} %pad_maximum_fusion.refs_0_), channel_id=1, source_target_pairs={{0,24},{8,0},{16,8},{24,16},{1,25},{9,1},{17,9},{25,17},{2,26},{10... | collective-permute-start | bytes 1179656 | tf_op jit(solution)/shard_map/ppermute | solution.py:170
  60.1 31.4 %copy-start.2 = (s32[6]{0:T(128)}, s32[6]{0:T(128)S(1)}, u32[]{:S(2)}) copy-start(s32[6]{0:T(128)S(1)} %stack.78.meta) | copy-start | bytes 76
  60.1 9.9 %copy-start.7 = (bf16[32,2048]{1,0:T(8,128)(2,1)S(1)}, bf16[32,2048]{1,0:T(8,128)(2,1)}, u32[]{:S(2)}) copy-start(bf16[32,2048]{1,0:T(8,128)(2,1)} %copy-done.6) | copy-start | bytes 393220
  60.1 9.9 %copy-start.9 = (bf16[32,2048]{1,0:T(8,128)(2,1)S(1)}, bf16[32,2048]{1,0:T(8,128)(2,1)}, u32[]{:S(2)}) copy-start(bf16[32,2048]{1,0:T(8,128)(2,1)} %copy-done.8) | copy-start | bytes 393220
  61.2 18.9 %collective-permute-start.12 = (bf16[3,32,2048]{2,1,0:T(8,128)(2,1)S(1)}, bf16[3,32,2048]{2,1,0:T(8,128)(2,1)S(1)}, u32[]{:S(2)}, u32[]{:S(2)}) collective-permute-start(bf16[3,32,2048]{2,1,0:T(8,128)(2,1)S(1)} %slice.50), channel_id=1, source_target_pairs={{0,8},{8,16},{16,24},{24,0},{1,9},{9,17},{17,25},{25,1},{2,10},{10... | collective-permute-start | bytes 1179656 | tf_op jit(solution)/shard_map/ppermute | solution.py:171
  62.3 17.8 %collective-permute-start.7 = (bf16[3,32,2048]{2,1,0:T(8,128)(2,1)}, bf16[3,32,2048]{2,1,0:T(8,128)(2,1)S(1)}, u32[]{:S(2)}, u32[]{:S(2)}) collective-permute-start(bf16[3,32,2048]{2,1,0:T(8,128)(2,1)} %pad_maximum_fusion.refs_0_), channel_id=1, source_target_pairs={{0,8},{8,16},{16,24},{24,0},{1,9},{9,17},{17,25},{25,1},{2,10},{10... | collective-permute-start | bytes 1179656 | tf_op jit(solution)/shard_map/ppermute | solution.py:169
  66.0 14.0 %collective-permute-start.14 = (bf16[2,32,2048]{2,1,0:T(8,128)(2,1)S(1)}, bf16[2,32,2048]{2,1,0:T(8,128)(2,1)S(1)}, u32[]{:S(2)}, u32[]{:S(2)}) collective-permute-start(bf16[2,32,2048]{2,1,0:T(8,128)(2,1)S(1)} %slice.51), channel_id=1, source_target_pairs={{0,24},{8,0},{16,8},{24,16},{1,25},{9,1},{17,9},{25,17},{2,26},{10... | collective-permute-start | bytes 786440 | tf_op jit(solution)/shard_map/ppermute | solution.py:172
  75.4 13.9 %collective-permute-start.10 = (bf16[2,32,2048]{2,1,0:T(8,128)(2,1)S(1)}, bf16[2,32,2048]{2,1,0:T(8,128)(2,1)S(1)}, u32[]{:S(2)}, u32[]{:S(2)}) collective-permute-start(bf16[2,32,2048]{2,1,0:T(8,128)(2,1)S(1)} %slice.49), channel_id=1, source_target_pairs={{0,24},{8,0},{16,8},{24,16},{1,25},{9,1},{17,9},{25,17},{2,26},{10... | collective-permute-start | bytes 786440 | tf_op jit(solution)/shard_map/ppermute | solution.py:172
  80.1 9.1 %collective-permute-start.8 = (bf16[1,32,2048]{2,1,0:T(8,128)(2,1)S(1)}, bf16[1,32,2048]{2,1,0:T(8,128)(2,1)S(1)}, u32[]{:S(2)}, u32[]{:S(2)}) collective-permute-start(bf16[1,32,2048]{2,1,0:T(8,128)(2,1)S(1)} %slice.48), channel_id=1, source_target_pairs={{0,8},{8,16},{16,24},{24,0},{1,9},{9,17},{17,25},{25,1},{2,10},{10... | collective-permute-start | bytes 393224 | tf_op jit(solution)/shard_map/ppermute | solution.py:171
  98.0 19.6 %copy-start.16 = (f32[32]{0:T(128)S(1)}, f32[32]{0:T(128)}, u32[]{:S(2)}) copy-start(f32[32]{0:T(128)} %occ.1) | copy-start | bytes 388
  98.0 4.0 %collective-permute-start.16 = (f32[4,512,128]{2,1,0:T(8,128)S(1)}, f32[4,512,128]{2,1,0:T(8,128)S(1)}, u32[]{:S(2)}, u32[]{:S(2)}) collective-permute-start(f32[4,512,128]{2,1,0:T(8,128)S(1)} %get-tuple-element.24), channel_id=1, source_target_pairs={{0,1},{1,0},{2,3},{3,2},{4,5},{5,4},{6,7},{7,6},{8,9},{9,8},{10,11... | collective-permute-start | bytes 3145736 | tf_op jit(solution)/shard_map/ppermute | solution.py:202
  102.9 9.3 %collective-permute-start.17 = (f32[512,128]{1,0:T(8,128)S(1)}, f32[512,128]{1,0:T(8,128)S(1)}, u32[]{:S(2)}, u32[]{:S(2)}) collective-permute-start(f32[512,128]{1,0:T(8,128)S(1)} %get-tuple-element.27), channel_id=1, source_target_pairs={{0,2},{2,4},{4,6},{6,0},{1,3},{3,5},{5,7},{7,1},{8,10},{10,12},{12... | collective-permute-start | bytes 786440 | tf_op jit(solution)/shard_map/ppermute | solution.py:205
  103.2 13.5 %collective-permute-start.18 = (f32[512,128]{1,0:T(8,128)S(1)}, f32[512,128]{1,0:T(8,128)S(1)}, u32[]{:S(2)}, u32[]{:S(2)}) collective-permute-start(f32[512,128]{1,0:T(8,128)S(1)} %get-tuple-element.26), channel_id=1, source_target_pairs={{0,4},{2,6},{4,0},{6,2},{1,5},{3,7},{5,1},{7,3},{8,12},{10,14},{12... | collective-permute-start | bytes 786440 | tf_op jit(solution)/shard_map/ppermute | solution.py:205
  105.0 12.6 %collective-permute-start.19 = (f32[512,128]{1,0:T(8,128)S(1)}, f32[512,128]{1,0:T(8,128)S(1)}, u32[]{:S(2)}, u32[]{:S(2)}) collective-permute-start(f32[512,128]{1,0:T(8,128)S(1)} %get-tuple-element.25), channel_id=1, source_target_pairs={{0,6},{2,0},{4,2},{6,4},{1,7},{3,1},{5,3},{7,5},{8,14},{10,8},{12,... | collective-permute-start | bytes 786440 | tf_op jit(solution)/shard_map/ppermute | solution.py:205
  (8 other events, 32.3 us)

commit v6 on v5

v6 whole, which is shorter than its diff:
```python
import functools

import jax
import jax.numpy as jnp
from jax import lax
from jax.experimental import pallas as pl
from jax.experimental.pallas import tpu as pltpu
from jax.sharding import Mesh, PartitionSpec as P

G = ("zl", "zh", "y")
C = ("x", "core")
Z = ("zl", "zh")
F32 = jnp.float32
BF16 = jnp.bfloat16


def shift(n, s):
    return [(i, (i + s) % n) for i in range(n)]


def z_shift(s):
    at = lambda z: (z % 4) * 2 + z // 4
    return [(at(z), at((z + s) % 8)) for z in range(8)]


FIRST = ((0, 0, 8), (1, 0, 8), (3, 0, 8))
LAST = ((2, 0, 4), (2, 4, 4))


def ladder_kernel(pieces, meta, live, *refs):
    n = len(pieces)
    ts, us, (v, wa, wb), refs = refs[:n], refs[n : 2 * n], refs[2 * n : 2 * n + 3], refs[2 * n + 3 :]
    blocks = [(p, e, q, top + e) for p, (q, top, count) in enumerate(pieces) for e in range(count)]
    prev = None
    if pieces is LAST:
        prev, refs = refs[0], refs[1:]
    outs, (ladder, vm, wm, o2) = refs[:-4], refs[-4:]
    x0, c0, y0, col = meta[0], meta[1], meta[2], meta[3]
    ys = [(y0 + 4 - q) & 3 for q in range(4)]
    at = [(((h & 1) ^ c0) << 2) | (((h >> 1) + 4 - x0) & 3) for h in range(8)]

    @pl.loop(0, 16)
    def _(kt):
        rows = pl.ds(pl.multiple_of(kt * 128, 128), 128)
        for n in range(4):
            tile = v[rows, n * 128 : n * 128 + 128]
            vm[rows, n * 128 : n * 128 + 128] = jnp.where(live[kt, n] != 0, tile, jnp.zeros_like(tile))

    @pl.loop(0, 8)
    def _(r):
        ladder[r] = jnp.zeros((512, 128), F32) if prev is None else prev[r]

    for m0 in range(0, len(blocks), 8):
        part_of = blocks[m0 : m0 + 8]
        rows = jnp.concatenate([ts[p][e] for p, e, _, _ in part_of], 0)
        part = jnp.dot(rows, vm[...], preferred_element_type=F32)
        for m, (_, _, q, h) in enumerate(part_of):
            for a in range(4):
                rows = pl.ds(ys[q] * 4 + a, 32, stride=16)
                ladder[at[h], rows, :] += part[m * 32 : m * 32 + 32, a * 128 : a * 128 + 128]

    lane = lax.broadcasted_iota(jnp.int32, (128, 128), 1)

    def spread(k, which):
        pieces = [w[s, k, which] for w in (wa, wb) for s in range(4)]
        return jnp.concatenate(pieces, 0)

    acc = jnp.zeros((512, 128), F32)
    w_all = None
    for m in range(0, len(blocks), 2):
        pair = blocks[m : m + 2]
        lhs = jnp.concatenate([us[p][e].reshape(512, 128) for p, e, _, _ in pair], 1)
        rhs = jnp.concatenate([spread(h * 4 + ys[q], 1) for _, _, q, h in pair], 1)
        acc = acc + lax.dot_general(lhs, rhs, (((1,), (1,)), ((), ())), preferred_element_type=F32)
        if m % 8 == 0:
            w_all = jnp.zeros((128, 128), F32)
        for f, (_, _, q, h) in enumerate(pair):
            place = m % 8 + f
            wk = spread(h * 4 + ys[q], 0).astype(F32)
            wk = pltpu.roll(wk, (16 * place + 128 - 16 * col) & 127, 1)
            w_all = jnp.where((lane >> 4) == place, wk, w_all)
        if m % 8 == 6:
            wm[:, m // 8 * 128 : m // 8 * 128 + 128] = w_all.astype(BF16)
    o2[...] = acc.T

    own = (lane >> 4) == col

    @pl.loop(0, 16)
    def _(jj):
        j = jj * 2
        rhs = jnp.concatenate(
            [jnp.concatenate([us[p][e, j + f] for p, e, _, _ in blocks], 0) for f in range(2)], 1
        )
        one = jnp.dot(wm[...], rhs, preferred_element_type=F32)
        two = o2[:, pl.ds(pl.multiple_of((jj >> 2) * 128, 128), 128)]
        for f in range(2):
            placed = pltpu.roll(two, (16 * col + 128 - 16 * ((j + f) & 7)) & 127, 1)
            both = one[:, f * 128 : f * 128 + 128] + jnp.where(own, placed, 0.0)
            rows = pl.ds(pl.multiple_of((j + f) * 16, 16), 16)
            for r in range(8):
                value = ladder[r, rows, :] + both[r * 16 : r * 16 + 16]
                if prev is None:
                    outs[0][r, rows, :] = value
                else:
                    outs[r // 4][r % 4, rows, :] = value


def ladder_call(pieces, meta, live, ts, us, v, wa, wb, prev=()):
    smem = pl.BlockSpec(memory_space=pltpu.SMEM)
    vmem = pl.BlockSpec(memory_space=pltpu.VMEM)
    whole = jax.ShapeDtypeStruct((8, 512, 128), F32)
    half = jax.ShapeDtypeStruct((4, 512, 128), F32)
    return pl.pallas_call(
        functools.partial(ladder_kernel, pieces),
        out_shape=(half, half) if prev else (whole,),
        in_specs=[smem, smem] + [vmem] * (len(ts) + len(us) + 3 + len(prev)),
        out_specs=(vmem, vmem) if prev else (vmem,),
        scratch_shapes=[
            pltpu.VMEM((8, 512, 128), F32),
            pltpu.VMEM((2048, 512), BF16),
            pltpu.VMEM((128, 384 if prev == () else 128), BF16),
            pltpu.VMEM((128, 512), F32),
        ],
        cost_estimate=pl.CostEstimate(flops=400_000_000 * (9 if prev == () else 3), bytes_accessed=10_000_000, transcendentals=0),
        compiler_params=pltpu.CompilerParams(vmem_limit_bytes=24 << 20),
        name="ladder",
    )(meta, live, *ts, *us, v, wa, wb, *prev)


def finish_kernel(meta, occ, vir, occ_col, vir_row, p0, p1, p2, p3, p4, out):
    col, g = meta[3], meta[4]
    for il in range(4):
        for a in range(4):
            rows = pl.ds(il * 4 + a, 32, stride=16)
            total = ((p0[rows, :] + p1[rows, :]) + p2[rows, :]) + (p3[rows, :] + p4[rows, :])
            denom = ((vir[g * 4 + a] + vir_row[...]) - occ[col * 4 + il]) - occ_col[...]
            out[il * 32 : il * 32 + 32, a * 128 : a * 128 + 128] = (total / denom).astype(BF16)


def finish_call(meta, occ_col, eps_occ, eps_vir, parts):
    smem = pl.BlockSpec(memory_space=pltpu.SMEM)
    vmem = pl.BlockSpec(memory_space=pltpu.VMEM)
    return pl.pallas_call(
        finish_kernel,
        out_shape=jax.ShapeDtypeStruct((128, 512), BF16),
        in_specs=[smem] * 3 + [vmem] * 7,
        out_specs=vmem,
        cost_estimate=pl.CostEstimate(flops=400_000, bytes_accessed=1_500_000, transcendentals=0),
        name="finish",
    )(
        meta,
        eps_occ,
        eps_vir,
        occ_col,
        eps_vir[None, :],
        *parts,
    )


def gather_z(t, early):
    z0 = lax.axis_index("zh") * 4 + lax.axis_index("zl")
    parts = [(0, t)]
    fwd = bwd = t
    for k in range(1, 5):
        fwd = lax.ppermute(fwd, Z, z_shift(1))
        if k == 1:
            fwd, *early = lax.optimization_barrier((fwd, *early))
        parts.append((-k, fwd))
        if k < 4:
            bwd = lax.ppermute(bwd, Z, z_shift(-1))
            parts.append((k, bwd))
    mine = jnp.zeros((8,) + t.shape, t.dtype)
    for d, part in parts:
        z = (z0 + (d & 7)) & 7
        mine = lax.dynamic_update_slice(mine, part[None], ((z & 3) * 2 + (z >> 2), 0, 0))
    return mine, early


def split_rows(ts):
    return [t.reshape(-1, 32, 16, 128) for t in ts]


def local(amplitudes, ladder_ints, tile_live, cycle_direct, cycle_exchange, eps_occ, eps_vir):
    x0, c0, y0 = lax.axis_index("x"), lax.axis_index("core"), lax.axis_index("y")
    meta = jnp.stack([x0, c0, y0, lax.axis_index(C), lax.axis_index(G)]).astype(jnp.int32)
    both = jnp.stack([cycle_direct, cycle_exchange]).reshape(2, 4, 32, 4, 128)
    both = both.transpose(2, 0, 1, 3, 4).reshape(32, 2, 16, 128)
    occ_col = jnp.broadcast_to(eps_occ[:, None], (32, 128))
    mine, (both, occ_col, meta) = gather_z(amplitudes, (both, occ_col, meta))
    down = lax.ppermute(mine, "y", shift(4, 1))
    up = lax.ppermute(mine, "y", shift(4, -1))
    both, mine = lax.optimization_barrier((both, mine))
    both = lax.all_to_all(both, G, 0, 0, tiled=True)
    xs = [both] + [lax.ppermute(both, "x", shift(4, -s)) for s in (1, 2, 3)]
    *xs, down, up = lax.optimization_barrier((*xs, down, up))
    wa = jnp.stack(xs)
    wb = lax.ppermute(wa, "core", shift(2, 1))
    low = lax.ppermute(down[:4], "y", shift(4, 1))
    high = lax.ppermute(up[4:], "y", shift(4, -1))
    first, last = [mine, down, up], [low, high]
    prev = list(ladder_call(FIRST, meta, tile_live, first, split_rows(first), ladder_ints, wa, wb))
    *last, prev[0] = lax.optimization_barrier((*last, prev[0]))
    keep, away = ladder_call(LAST, meta, tile_live, last, split_rows(last), ladder_ints, wa, wb, tuple(prev))
    got = lax.ppermute(away, "core", shift(2, 1))
    parts = [keep[0], got[0]]
    for s in (1, 2, 3):
        parts.append(lax.ppermute(keep[s] + got[s], "x", shift(4, s)))
    return finish_call(meta, occ_col, eps_occ, eps_vir, parts)


def solution(mesh):
    fine = Mesh(mesh.devices.reshape(4, 2, 4, 4, 2), ("zl", "zh", "y", "x", "core"))
    placed = (P(G, C), P(C, G), P(C, G), P(C, G), P(C, G), P(), P())
    return jax.shard_map(local, mesh=fine, in_specs=placed, out_specs=P(C, G), check_vma=False)
```

time: 122 us -> 118 us (0.967)
  blocking collectives: 0 us -> 22.3 us
  starting transfers between devices: 49.3 us -> 32.3 us
  local copies, waits for them, and re-layouts: 15.4 us -> 8.66 us
  other arithmetic: 3.86 us -> 2.22 us
    all_to_all x0 -> x1, blocking collectives: none -> 22.3 us  [local(): both = lax.all_to_all(both, G, 0, 0, tiled=True)]
    all_to_all x2 -> x0, starting transfers between devices: 12.4 us -> none  [the longest x1 8.3 us: local(): both = lax.all_to_all(both, G, 0, 0, tiled=True)]
    unnamed x59 -> x24, local copies, waits for them, and re-layouts: 10.3 us -> 5.03 us
    ppermute x15 -> x14, starting transfers between devices: 25.8 us -> 21.2 us  [the longest x3 9.54 us: gather_z(): bwd = lax.ppermute(bwd, Z, z_shift(-1))]
    all_to_all x2 -> x0, waiting for transfers between devices: 4.08 us -> none  [the longest x1 3.97 us: local(): lax.all_to_all(jnp.broadcast_to(both[None], (4, 32, 2, 16, 128)), 'x', 0,...]
    ppermute x15 -> x14, waiting for transfers between devices: 16.8 us -> 19.8 us  [the longest x4 10.3 us: gather_z(): fwd = lax.ppermute(fwd, Z, z_shift(1))]
    another operation x3 -> x2, local copies, waits for them, and re-layouts: 1.41 us -> 0.18 us  [the longest x1 0.09 us: local(): both = jnp.stack([cycle_direct, cycle_exchange]).reshape(2, 4, 32, 4, 128)]
  transfers between devices with their start and end apart: 22 -> 19, of which waited for: 11 -> 12; matrix products, arithmetic and copies ran while one was open for 12% -> 5% of each run, Pallas kernels for 6% -> 7%
where the time goes in v6:
time: 118 us; the launch traced here: 117 us
  waiting for transfers between devices  34.1 us (29%)
  starting transfers between devices  32.3 us (27%)
  blocking collectives  22.3 us (19%)
  Pallas kernels  17 us (14%)
  local copies, waits for them, and re-layouts  8.66 us (7%)
  other arithmetic  2.22 us (2%)
    all_to_all x1, blocking collectives, local(): both = lax.all_to_all(both, G, 0, 0, tiled=True)  22.3 us
    pallas_call x2, Pallas kernels, ladder_call(): pl.pallas_call(functools.partial(ladder_kernel, pieces), out_shape=(half,...  14.6 us
    ppermute x3, waiting for transfers between devices, local(): parts.append(lax.ppermute(keep[s] + got[s], 'x', shift(4, s)))  12 us
    ppermute x4, waiting for transfers between devices, gather_z(): fwd = lax.ppermute(fwd, Z, z_shift(1))  10.3 us
    ppermute x3, starting transfers between devices, gather_z(): bwd = lax.ppermute(bwd, Z, z_shift(-1))  9.54 us
    ppermute x3, waiting for transfers between devices, local(): xs = [both] + [lax.ppermute(both, 'x', shift(4, -s)) for s in (1, 2, 3)]  8.41 us
    ppermute x1, starting transfers between devices, local(): wb = lax.ppermute(wa, 'core', shift(2, 1))  7.21 us
    unnamed x24, local copies, waits for them, and re-layouts  5.03 us
  transfers between devices with their start and end apart: 19, of which 12 were waited for; matrix products, arithmetic and copies ran while one was open for 5% of the time, Pallas kernels for 7%

profile of v6, /device:TPU:1, one launch (start us, length us, event | category | flops | bytes accessed | tf_op | source)
XLA Modules:
  0.0 116.9 jit_solution(4734123406413325678)
XLA Ops:
  0.0 2.5 %collective-permute-start = (bf16[32,2048]{1,0:T(8,128)(2,1)}, bf16[32,2048]{1,0:T(8,128)(2,1)S(1)}, u32[]{:S(2)}, u32[]{:S(2)}) collective-permute-start(bf16[32,2048]{1,0:T(8,128)(2,1)} %param.7), channel_id=1, source_target_pairs={{0,64},{64,128},{128,192},{192,32},{32,96},{96,160},{160,224},{224... | collective-permute-start | bytes 393224 | tf_op jit(solution)/shard_map/ppermute | solution.py:165
  2.5 4.0 %collective-permute-start.1 = (bf16[32,2048]{1,0:T(8,128)(2,1)}, bf16[32,2048]{1,0:T(8,128)(2,1)S(1)}, u32[]{:S(2)}, u32[]{:S(2)}) collective-permute-start(bf16[32,2048]{1,0:T(8,128)(2,1)} %param.7), channel_id=1, source_target_pairs={{0,224},{64,0},{128,64},{192,128},{32,192},{96,32},{160,96},{224,1... | collective-permute-start | bytes 393224 | tf_op jit(solution)/shard_map/ppermute | solution.py:170
  6.6 0.9 bitcast_dynamic-update-slice_fusion.7
  7.6 1.2 pad_maximum_fusion.1
  8.9 0.9 collective-permute-done
  10.5 2.7 %collective-permute-start.3 = (bf16[32,2048]{1,0:T(8,128)(2,1)S(1)}, bf16[32,2048]{1,0:T(8,128)(2,1)S(1)}, u32[]{:S(2)}, u32[]{:S(2)}) collective-permute-start(bf16[32,2048]{1,0:T(8,128)(2,1)S(1)} %collective-permute-done.1), channel_id=1, source_target_pairs={{0,224},{64,0},{128,64},{192,128},{32,192},{96,32},{160,96},{224,1... | collective-permute-start | bytes 393224 | tf_op jit(solution)/shard_map/ppermute | solution.py:170
  13.3 2.2 %collective-permute-done.2 = bf16[32,2048]{1,0:T(8,128)(2,1)S(1)} collective-permute-done((bf16[32,2048]{1,0:T(8,128)(2,1)S(1)}, bf16[32,2048]{1,0:T(8,128)(2,1)S(1)}, u32[]{:S(2)}, u32[]{:S(2)}) %collective-permute-start.2) | collective-permute-done | bytes 131104 | tf_op jit(solution)/shard_map/ppermute | solution.py:165
  15.6 2.8 %collective-permute-start.5 = (bf16[32,2048]{1,0:T(8,128)(2,1)S(1)}, bf16[32,2048]{1,0:T(8,128)(2,1)S(1)}, u32[]{:S(2)}, u32[]{:S(2)}) collective-permute-start(bf16[32,2048]{1,0:T(8,128)(2,1)S(1)} %collective-permute-done.3), channel_id=1, source_target_pairs={{0,224},{64,0},{128,64},{192,128},{32,192},{96,32},{160,96},{224,1... | collective-permute-start | bytes 393224 | tf_op jit(solution)/shard_map/ppermute | solution.py:170
  18.4 2.2 %collective-permute-done.4 = bf16[32,2048]{1,0:T(8,128)(2,1)S(1)} collective-permute-done((bf16[32,2048]{1,0:T(8,128)(2,1)S(1)}, bf16[32,2048]{1,0:T(8,128)(2,1)S(1)}, u32[]{:S(2)}, u32[]{:S(2)}) %collective-permute-start.4) | collective-permute-done | bytes 131104 | tf_op jit(solution)/shard_map/ppermute | solution.py:165
  20.6 5.0 %collective-permute-done.6 = bf16[32,2048]{1,0:T(8,128)(2,1)S(1)} collective-permute-done((bf16[32,2048]{1,0:T(8,128)(2,1)S(1)}, bf16[32,2048]{1,0:T(8,128)(2,1)S(1)}, u32[]{:S(2)}, u32[]{:S(2)}) %collective-permute-start.6) | collective-permute-done | bytes 131104 | tf_op jit(solution)/shard_map/ppermute | solution.py:165
  25.6 1.4 %collective-permute-start.10 = (bf16[8,32,2048]{2,1,0:T(8,128)(2,1)S(1)}, bf16[8,32,2048]{2,1,0:T(8,128)(2,1)S(1)}, u32[]{:S(2)}, u32[]{:S(2)}) collective-permute-start(bf16[8,32,2048]{2,1,0:T(8,128)(2,1)S(1)} %bitcast_dynamic-update-slice_fusion.refs_0_), channel_id=1, source_target_pairs={{0,8},{8,16},{16,24},{24,0},{1,9},{9,17},{17,25},{25,1},{2,10},{10... | collective-permute-start | bytes 3145736 | tf_op jit(solution)/shard_map/ppermute | solution.py:190
  27.0 1.5 %collective-permute-start.11 = (bf16[8,32,2048]{2,1,0:T(8,128)(2,1)S(1)}, bf16[8,32,2048]{2,1,0:T(8,128)(2,1)S(1)}, u32[]{:S(2)}, u32[]{:S(2)}) collective-permute-start(bf16[8,32,2048]{2,1,0:T(8,128)(2,1)S(1)} %bitcast_dynamic-update-slice_fusion.refs_0_), channel_id=1, source_target_pairs={{0,24},{8,0},{16,8},{24,16},{1,25},{9,1},{17,9},{25,17},{2,26},{10... | collective-permute-start | bytes 3145736 | tf_op jit(solution)/shard_map/ppermute | solution.py:191
  28.5 22.3 %all_to_all.5 = bf16[32,2,16,128]{3,2,1,0:T(8,128)(2,1)S(1)} all-to-all(bf16[32,2,16,128]{3,2,1,0:T(8,128)(2,1)S(1)} %bitcast.69), channel_id=1, replica_groups=mesh['zl'=4,'zh'=2,'y'=4,'x'=4,'core'=2] {'zl','zh','y'}, dimensions={0} | all-to-all | bytes 524288 | tf_op jit(solution)/shard_map/all_to_all | solution.py:193
  50.8 2.5 %collective-permute-start.7 = (bf16[32,2,16,128]{3,2,1,0:T(8,128)(2,1)S(1)}, bf16[32,2,16,128]{3,2,1,0:T(8,128)(2,1)S(1)}, u32[]{:S(2)}, u32[]{:S(2)}) collective-permute-start(bf16[32,2,16,128]{3,2,1,0:T(8,128)(2,1)S(1)} %all_to_all.5), channel_id=1, source_target_pairs={{0,6},{2,0},{4,2},{6,4},{1,7},{3,1},{5,3},{7,5},{8,14},{10,8},{12,... | collective-permute-start | bytes 786440 | tf_op jit(solution)/shard_map/ppermute | solution.py:194
  54.5 5.0 %collective-permute-done.7 = bf16[32,2,16,128]{3,2,1,0:T(8,128)(2,1)S(1)} collective-permute-done((bf16[32,2,16,128]{3,2,1,0:T(8,128)(2,1)S(1)}, bf16[32,2,16,128]{3,2,1,0:T(8,128)(2,1)S(1)}, u32[]{:S(2)}, u32[]{:S(2)}) %collective-permute-start.7) | collective-permute-done | bytes 262176 | tf_op jit(solution)/shard_map/ppermute | solution.py:194
  60.2 2.7 %collective-permute-done.9 = bf16[32,2,16,128]{3,2,1,0:T(8,128)(2,1)S(1)} collective-permute-done((bf16[32,2,16,128]{3,2,1,0:T(8,128)(2,1)S(1)}, bf16[32,2,16,128]{3,2,1,0:T(8,128)(2,1)S(1)}, u32[]{:S(2)}, u32[]{:S(2)}) %collective-permute-start.9) | collective-permute-done | bytes 262176 | tf_op jit(solution)/shard_map/ppermute | solution.py:194
  63.0 7.2 %collective-permute-start.14 = (bf16[4,32,2,16,128]{4,3,2,1,0:T(8,128)(2,1)S(1)}, bf16[4,32,2,16,128]{4,3,2,1,0:T(8,128)(2,1)}, u32[]{:S(2)}, u32[]{:S(2)}) collective-permute-start(bf16[4,32,2,16,128]{4,3,2,1,0:T(8,128)(2,1)S(1)} %pad_maximum_fusion.refs_7_.refs_5_), channel_id=1, source_target_pairs={{0,1},{1,0},{2,3},{3,2},{4,5},{5,4},{6,7},{7,6},{8,9},{9,8},{10,11... | collective-permute-start | bytes 3145736 | tf_op jit(solution)/shard_map/ppermute | solution.py:197
  70.2 0.8 slice.30
  71.8 0.8 slice.31
  72.7 1.9 %collective-permute-start.13 = (bf16[4,32,2048]{2,1,0:T(8,128)(2,1)}, bf16[4,32,2048]{2,1,0:T(8,128)(2,1)}, u32[]{:S(2)}, u32[]{:S(2)}) collective-permute-start(bf16[4,32,2048]{2,1,0:T(8,128)(2,1)} %slice.31), channel_id=1, source_target_pairs={{0,24},{8,0},{16,8},{24,16},{1,25},{9,1},{17,9},{25,17},{2,26},{10... | collective-permute-start | bytes 1572872 | tf_op jit(solution)/shard_map/ppermute | solution.py:199
  76.6 8.5 %ladder.2.refs_7_ = f32[8,512,128]{2,1,0:T(8,128)S(1)} custom-call(s32[5]{0:T(128)S(1)} %stack.50.meta, s32[16,4]{1,0:T(8,128)S(1)} %copy.11.live, bf16[8,32,2048]{2,1,0:T(8,128)(2,1)S(1)} %bitcast_dynamic-update-slice_fusion.refs_0_, bf16[8,32,2048]{2,1,0:T(8,128)(2,1)S(1)} %collective-permute-done.10.refs_1_, bf16[8,32,2048]{2,1,0:T(8,128)(2,1)S(1)} %copy-done.1, ...), custom_call_target="tpu_custom_call" | custom-call | flops 3600000000 | bytes 10000000 | tf_op jit(solution)/shard_map/ladder/pallas_call | solution.py:113
  85.1 1.0 collective-permute-done.12.refs_0_
  86.1 1.1 copy.16
  87.3 1.1 copy.17
  88.5 6.1 %ladder.3 = (f32[4,512,128]{2,1,0:T(8,128)S(1)}, f32[4,512,128]{2,1,0:T(8,128)S(1)}) custom-call(s32[5]{0:T(128)S(1)} %stack.50.meta, s32[16,4]{1,0:T(8,128)S(1)} %copy.11.live, bf16[4,32,2048]{2,1,0:T(8,128)(2,1)} %collective-permute-done.12.refs_0_, bf16[4,32,2048]{2,1,0:T(8,128)(2,1)} %collective-permute-done.13.refs_1_, ...), custom_call_target="tpu_custom_call" | custom-call | flops 1200000000 | bytes 10000000 | tf_op jit(solution)/shard_map/ladder/pallas_call | solution.py:113
  94.6 1.3 %collective-permute-start.15 = (f32[4,512,128]{2,1,0:T(8,128)S(1)}, f32[4,512,128]{2,1,0:T(8,128)S(1)}, u32[]{:S(2)}, u32[]{:S(2)}) collective-permute-start(f32[4,512,128]{2,1,0:T(8,128)S(1)} %get-tuple-element.38), channel_id=1, source_target_pairs={{0,1},{1,0},{2,3},{3,2},{4,5},{5,4},{6,7},{7,6},{8,9},{9,8},{10,11... | collective-permute-start | bytes 3145736 | tf_op jit(solution)/shard_map/ppermute | solution.py:204
  95.8 2.3 %collective-permute-done.15 = f32[4,512,128]{2,1,0:T(8,128)S(1)} collective-permute-done((f32[4,512,128]{2,1,0:T(8,128)S(1)}, f32[4,512,128]{2,1,0:T(8,128)S(1)}, u32[]{:S(2)}, u32[]{:S(2)}) %collective-permute-start.15) | collective-permute-done | bytes 1048608 | tf_op jit(solution)/shard_map/ppermute | solution.py:204
  98.1 0.9 fusion
  99.1 1.5 %collective-permute-start.17 = (f32[512,128]{1,0:T(8,128)S(1)}, f32[512,128]{1,0:T(8,128)S(1)}, u32[]{:S(2)}, u32[]{:S(2)}) collective-permute-start(f32[512,128]{1,0:T(8,128)S(1)} %get-tuple-element.40), channel_id=1, source_target_pairs={{0,4},{2,6},{4,0},{6,2},{1,5},{3,7},{5,1},{7,3},{8,12},{10,14},{12... | collective-permute-start | bytes 786440 | tf_op jit(solution)/shard_map/ppermute | solution.py:207
  100.6 1.2 collective-permute-start.18
  101.7 11.7 %collective-permute-done.16.p2 = f32[512,128]{1,0:T(8,128)S(1)} collective-permute-done((f32[512,128]{1,0:T(8,128)S(1)}, f32[512,128]{1,0:T(8,128)S(1)}, u32[]{:S(2)}, u32[]{:S(2)}) %collective-permute-start.16) | collective-permute-done | bytes 262176 | tf_op jit(solution)/shard_map/ppermute | solution.py:207
  114.4 2.4 %finish.1 = bf16[128,512]{1,0:T(8,128)(2,1)} custom-call(s32[5]{0:T(128)} %copy-done.3, f32[32]{0:T(128)} %occ.1, f32[128]{0:T(128)} %vir.1, f32[32,128]{1,0:T(8,128)} %broadcast_in_dim.36.occ_col, f32[1,128]{1,0:T(1,128)} %bitcast.76, f32[512,128]{1,0:T(8,128)} %get-tuple-element.42.p0, f32[512,128]{1,0:T(8,128)} %get-tuple-element.43.p1, ...), custom_call_target="tpu_custom_call" | custom-call | flops 400000 | bytes 1500000 | tf_op jit(solution)/shard_map/finish/pallas_call | solution.py:143
  (51 shorter events, 7.0 us)
Async XLA Ops:
  0.0 9.8 %copy-start.7 = (f32[32]{0:T(128)S(1)}, f32[32]{0:T(128)}, u32[]{:S(2)}) copy-start(f32[32]{0:T(128)} %occ.1) | copy-start | bytes 388
  0.0 9.8 %collective-permute-start = (bf16[32,2048]{1,0:T(8,128)(2,1)}, bf16[32,2048]{1,0:T(8,128)(2,1)S(1)}, u32[]{:S(2)}, u32[]{:S(2)}) collective-permute-start(bf16[32,2048]{1,0:T(8,128)(2,1)} %param.7), channel_id=1, source_target_pairs={{0,64},{64,128},{128,192},{192,32},{32,96},{96,160},{160,224},{224... | collective-permute-start | bytes 393224 | tf_op jit(solution)/shard_map/ppermute | solution.py:165
  2.5 8.1 %collective-permute-start.1 = (bf16[32,2048]{1,0:T(8,128)(2,1)}, bf16[32,2048]{1,0:T(8,128)(2,1)S(1)}, u32[]{:S(2)}, u32[]{:S(2)}) collective-permute-start(bf16[32,2048]{1,0:T(8,128)(2,1)} %param.7), channel_id=1, source_target_pairs={{0,224},{64,0},{128,64},{192,128},{32,192},{96,32},{160,96},{224,1... | collective-permute-start | bytes 393224 | tf_op jit(solution)/shard_map/ppermute | solution.py:170
  8.9 79.5 %copy-start.3 = (s32[5]{0:T(128)}, s32[5]{0:T(128)S(1)}, u32[]{:S(2)}) copy-start(s32[5]{0:T(128)S(1)} %stack.50.meta) | copy-start | bytes 64
  10.5 5.0 %collective-permute-start.2 = (bf16[32,2048]{1,0:T(8,128)(2,1)S(1)}, bf16[32,2048]{1,0:T(8,128)(2,1)S(1)}, u32[]{:S(2)}, u32[]{:S(2)}) collective-permute-start(bf16[32,2048]{1,0:T(8,128)(2,1)S(1)} %collective-permute-done), channel_id=1, source_target_pairs={{0,64},{64,128},{128,192},{192,32},{32,96},{96,160},{160,224},{224... | collective-permute-start | bytes 393224 | tf_op jit(solution)/shard_map/ppermute | solution.py:165
  10.5 5.0 %collective-permute-start.3 = (bf16[32,2048]{1,0:T(8,128)(2,1)S(1)}, bf16[32,2048]{1,0:T(8,128)(2,1)S(1)}, u32[]{:S(2)}, u32[]{:S(2)}) collective-permute-start(bf16[32,2048]{1,0:T(8,128)(2,1)S(1)} %collective-permute-done.1), channel_id=1, source_target_pairs={{0,224},{64,0},{128,64},{192,128},{32,192},{96,32},{160,96},{224,1... | collective-permute-start | bytes 393224 | tf_op jit(solution)/shard_map/ppermute | solution.py:170
  15.5 5.0 %collective-permute-start.4 = (bf16[32,2048]{1,0:T(8,128)(2,1)S(1)}, bf16[32,2048]{1,0:T(8,128)(2,1)S(1)}, u32[]{:S(2)}, u32[]{:S(2)}) collective-permute-start(bf16[32,2048]{1,0:T(8,128)(2,1)S(1)} %collective-permute-done.2), channel_id=1, source_target_pairs={{0,64},{64,128},{128,192},{192,32},{32,96},{96,160},{160,224},{224... | collective-permute-start | bytes 393224 | tf_op jit(solution)/shard_map/ppermute | solution.py:165
  15.6 5.0 %collective-permute-start.5 = (bf16[32,2048]{1,0:T(8,128)(2,1)S(1)}, bf16[32,2048]{1,0:T(8,128)(2,1)S(1)}, u32[]{:S(2)}, u32[]{:S(2)}) collective-permute-start(bf16[32,2048]{1,0:T(8,128)(2,1)S(1)} %collective-permute-done.3), channel_id=1, source_target_pairs={{0,224},{64,0},{128,64},{192,128},{32,192},{96,32},{160,96},{224,1... | collective-permute-start | bytes 393224 | tf_op jit(solution)/shard_map/ppermute | solution.py:170
  20.6 5.0 %collective-permute-start.6 = (bf16[32,2048]{1,0:T(8,128)(2,1)S(1)}, bf16[32,2048]{1,0:T(8,128)(2,1)S(1)}, u32[]{:S(2)}, u32[]{:S(2)}) collective-permute-start(bf16[32,2048]{1,0:T(8,128)(2,1)S(1)} %collective-permute-done.4), channel_id=1, source_target_pairs={{0,64},{64,128},{128,192},{192,32},{32,96},{96,160},{160,224},{224... | collective-permute-start | bytes 393224 | tf_op jit(solution)/shard_map/ppermute | solution.py:165
  25.6 37.2 %collective-permute-start.10 = (bf16[8,32,2048]{2,1,0:T(8,128)(2,1)S(1)}, bf16[8,32,2048]{2,1,0:T(8,128)(2,1)S(1)}, u32[]{:S(2)}, u32[]{:S(2)}) collective-permute-start(bf16[8,32,2048]{2,1,0:T(8,128)(2,1)S(1)} %bitcast_dynamic-update-slice_fusion.refs_0_), channel_id=1, source_target_pairs={{0,8},{8,16},{16,24},{24,0},{1,9},{9,17},{17,25},{25,1},{2,10},{10... | collective-permute-start | bytes 3145736 | tf_op jit(solution)/shard_map/ppermute | solution.py:190
  27.0 35.9 %collective-permute-start.11 = (bf16[8,32,2048]{2,1,0:T(8,128)(2,1)S(1)}, bf16[8,32,2048]{2,1,0:T(8,128)(2,1)S(1)}, u32[]{:S(2)}, u32[]{:S(2)}) collective-permute-start(bf16[8,32,2048]{2,1,0:T(8,128)(2,1)S(1)} %bitcast_dynamic-update-slice_fusion.refs_0_), channel_id=1, source_target_pairs={{0,24},{8,0},{16,8},{24,16},{1,25},{9,1},{17,9},{25,17},{2,26},{10... | collective-permute-start | bytes 3145736 | tf_op jit(solution)/shard_map/ppermute | solution.py:191
  50.8 8.6 %collective-permute-start.7 = (bf16[32,2,16,128]{3,2,1,0:T(8,128)(2,1)S(1)}, bf16[32,2,16,128]{3,2,1,0:T(8,128)(2,1)S(1)}, u32[]{:S(2)}, u32[]{:S(2)}) collective-permute-start(bf16[32,2,16,128]{3,2,1,0:T(8,128)(2,1)S(1)} %all_to_all.5), channel_id=1, source_target_pairs={{0,6},{2,0},{4,2},{6,4},{1,7},{3,1},{5,3},{7,5},{8,14},{10,8},{12,... | collective-permute-start | bytes 786440 | tf_op jit(solution)/shard_map/ppermute | solution.py:194
  53.3 6.8 %collective-permute-start.8 = (bf16[32,2,16,128]{3,2,1,0:T(8,128)(2,1)S(1)}, bf16[32,2,16,128]{3,2,1,0:T(8,128)(2,1)S(1)}, u32[]{:S(2)}, u32[]{:S(2)}) collective-permute-start(bf16[32,2,16,128]{3,2,1,0:T(8,128)(2,1)S(1)} %all_to_all.5), channel_id=1, source_target_pairs={{0,4},{2,6},{4,0},{6,2},{1,5},{3,7},{5,1},{7,3},{8,12},{10,14},{12... | collective-permute-start | bytes 786440 | tf_op jit(solution)/shard_map/ppermute | solution.py:194
  53.8 9.0 %collective-permute-start.9 = (bf16[32,2,16,128]{3,2,1,0:T(8,128)(2,1)S(1)}, bf16[32,2,16,128]{3,2,1,0:T(8,128)(2,1)S(1)}, u32[]{:S(2)}, u32[]{:S(2)}) collective-permute-start(bf16[32,2,16,128]{3,2,1,0:T(8,128)(2,1)S(1)} %all_to_all.5), channel_id=1, source_target_pairs={{0,2},{2,4},{4,6},{6,0},{1,3},{3,5},{5,7},{7,1},{8,10},{10,12},{12... | collective-permute-start | bytes 786440 | tf_op jit(solution)/shard_map/ppermute | solution.py:194
  62.9 9.8 %copy-start = (bf16[8,32,2048]{2,1,0:T(8,128)(2,1)}, bf16[8,32,2048]{2,1,0:T(8,128)(2,1)S(1)}, u32[]{:S(2)}) copy-start(bf16[8,32,2048]{2,1,0:T(8,128)(2,1)S(1)} %collective-permute-done.11.refs_2_) | copy-start | bytes 3145732
  62.9 11.7 %copy-start.8 = (s32[16,4]{0,1:T(4,128)S(1)}, s32[16,4]{0,1:T(4,128)}, u32[]{:S(2)}) copy-start(s32[16,4]{0,1:T(4,128)} %param.9) | copy-start | bytes 772
  63.0 13.1 %collective-permute-start.14 = (bf16[4,32,2,16,128]{4,3,2,1,0:T(8,128)(2,1)S(1)}, bf16[4,32,2,16,128]{4,3,2,1,0:T(8,128)(2,1)}, u32[]{:S(2)}, u32[]{:S(2)}) collective-permute-start(bf16[4,32,2,16,128]{4,3,2,1,0:T(8,128)(2,1)S(1)} %pad_maximum_fusion.refs_7_.refs_5_), channel_id=1, source_target_pairs={{0,1},{1,0},{2,3},{3,2},{4,5},{5,4},{6,7},{7,6},{8,9},{9,8},{10,11... | collective-permute-start | bytes 3145736 | tf_op jit(solution)/shard_map/ppermute | solution.py:197
  71.1 15.0 %collective-permute-start.12 = (bf16[4,32,2048]{2,1,0:T(8,128)(2,1)}, bf16[4,32,2048]{2,1,0:T(8,128)(2,1)}, u32[]{:S(2)}, u32[]{:S(2)}) collective-permute-start(bf16[4,32,2048]{2,1,0:T(8,128)(2,1)} %slice.30), channel_id=1, source_target_pairs={{0,8},{8,16},{16,24},{24,0},{1,9},{9,17},{17,25},{25,1},{2,10},{10... | collective-permute-start | bytes 1572872 | tf_op jit(solution)/shard_map/ppermute | solution.py:198
  72.7 13.5 %collective-permute-start.13 = (bf16[4,32,2048]{2,1,0:T(8,128)(2,1)}, bf16[4,32,2048]{2,1,0:T(8,128)(2,1)}, u32[]{:S(2)}, u32[]{:S(2)}) collective-permute-start(bf16[4,32,2048]{2,1,0:T(8,128)(2,1)} %slice.31), channel_id=1, source_target_pairs={{0,24},{8,0},{16,8},{24,16},{1,25},{9,1},{17,9},{25,17},{2,26},{10... | collective-permute-start | bytes 1572872 | tf_op jit(solution)/shard_map/ppermute | solution.py:199
  74.7 1.2 %copy-start.1 = (bf16[8,32,2048]{2,1,0:T(8,128)(2,1)S(1)}, bf16[8,32,2048]{2,1,0:T(8,128)(2,1)}, u32[]{:S(2)}) copy-start(bf16[8,32,2048]{2,1,0:T(8,128)(2,1)} %copy-done) | copy-start | bytes 3145732
  74.9 1.7 %copy-start.2 = (bf16[2048,512]{1,0:T(8,128)(2,1)S(1)}, bf16[2048,512]{1,0:T(8,128)(2,1)}, u32[]{:S(2)}) copy-start(bf16[2048,512]{1,0:T(8,128)(2,1)} %refs_4_.1) | copy-start | bytes 6291460
  94.6 3.5 %collective-permute-start.15 = (f32[4,512,128]{2,1,0:T(8,128)S(1)}, f32[4,512,128]{2,1,0:T(8,128)S(1)}, u32[]{:S(2)}, u32[]{:S(2)}) collective-permute-start(f32[4,512,128]{2,1,0:T(8,128)S(1)} %get-tuple-element.38), channel_id=1, source_target_pairs={{0,1},{1,0},{2,3},{3,2},{4,5},{5,4},{6,7},{7,6},{8,9},{9,8},{10,11... | collective-permute-start | bytes 3145736 | tf_op jit(solution)/shard_map/ppermute | solution.py:204
  99.1 14.3 %collective-permute-start.16 = (f32[512,128]{1,0:T(8,128)S(1)}, f32[512,128]{1,0:T(8,128)S(1)}, u32[]{:S(2)}, u32[]{:S(2)}) collective-permute-start(f32[512,128]{1,0:T(8,128)S(1)} %get-tuple-element.41), channel_id=1, source_target_pairs={{0,2},{2,4},{4,6},{6,0},{1,3},{3,5},{5,7},{7,1},{8,10},{10,12},{12... | collective-permute-start | bytes 786440 | tf_op jit(solution)/shard_map/ppermute | solution.py:207
  99.1 14.3 %collective-permute-start.17 = (f32[512,128]{1,0:T(8,128)S(1)}, f32[512,128]{1,0:T(8,128)S(1)}, u32[]{:S(2)}, u32[]{:S(2)}) collective-permute-start(f32[512,128]{1,0:T(8,128)S(1)} %get-tuple-element.40), channel_id=1, source_target_pairs={{0,4},{2,6},{4,0},{6,2},{1,5},{3,7},{5,1},{7,3},{8,12},{10,14},{12... | collective-permute-start | bytes 786440 | tf_op jit(solution)/shard_map/ppermute | solution.py:207
  100.6 13.2 %collective-permute-start.18 = (f32[512,128]{1,0:T(8,128)S(1)}, f32[512,128]{1,0:T(8,128)S(1)}, u32[]{:S(2)}, u32[]{:S(2)}) collective-permute-start(f32[512,128]{1,0:T(8,128)S(1)} %get-tuple-element.39), channel_id=1, source_target_pairs={{0,6},{2,0},{4,2},{6,4},{1,7},{3,1},{5,3},{7,5},{8,14},{10,8},{12,... | collective-permute-start | bytes 786440 | tf_op jit(solution)/shard_map/ppermute | solution.py:207
  113.4 0.7 copy-start.4
  113.4 0.8 copy-start.5
  113.7 0.7 copy-start.6

commit v7 on v5

--- a/solution.py
+++ b/solution.py
@@ -23,34 +23,40 @@
     return [(at(z), at((z + s) % 8)) for z in range(8)]
 
 
-NEAR = (0, -1, 1, -2, 2)
-FAR = (-3, 3, 4)
+NEAR = (-2, 5)
+FAR = (3, 3)
 CUTS = {NEAR: 3, FAR: 1}
 
 
-def ladder_kernel(slots, meta, live, *refs):
-    n = len(slots)
-    cut = CUTS[slots]
+def ladder_kernel(group, meta, live, *refs):
+    low, n = group
+    cut = CUTS[group]
     ts, us, (v, wa, wb), refs = refs[:5], refs[5:10], refs[10:13], refs[13:]
     blocks = [(p, d, q, d) for p, q in ((0, 0), (1, 1)) for d in range(n)]
     blocks += [(2, d, 2, d) for d in range(cut)] + [(3, d - cut, 2, d) for d in range(cut, n)]
     blocks += [(4, d, 3, d) for d in range(n)]
     prev = None
-    if slots is FAR:
+    if group is FAR:
+        vm = v
         prev, refs = refs[0], refs[1:]
-    outs, (ladder, vm, wm, o2) = refs[:-4], refs[-4:]
+    outs, (ladder, wm, o2) = refs[:-3], refs[-3:]
+    if group is NEAR:
+        vm = outs[1]
     x0, c0, y0, col, z0 = meta[0], meta[1], meta[2], meta[3], meta[5]
     ys = [(y0 + 4 - q) & 3 for q in range(4)]
-    zs = [(z0 + (d & 7)) & 7 for d in slots]
+    zs = [(z0 + low + 8 + lax.rem(e + 4 * n - z0, n)) & 7 for e in range(n)]
     hs = [((z & 3) << 1) | (z >> 2) for z in zs]
     at = [((((z >> 2) ^ c0) << 2) | (((z & 3) + 4 - x0) & 3)) for z in zs]
 
-    @pl.loop(0, 16)
-    def _(kt):
-        rows = pl.ds(pl.multiple_of(kt * 128, 128), 128)
-        for n in range(4):
-            tile = v[rows, n * 128 : n * 128 + 128]
-            vm[rows, n * 128 : n * 128 + 128] = jnp.where(live[kt, n] != 0, tile, jnp.zeros_like(tile))
+    if group is NEAR:
+
+        @pl.loop(0, 16)
+        def _(kt):
+            rows = pl.ds(pl.multiple_of(kt * 128, 128), 128)
+            for c in range(4):
+                cols = slice(c * 128, c * 128 + 128)
+                tile = v[rows, cols]
+                vm[rows, cols] = jnp.where(live[kt, c] != 0, tile, jnp.zeros_like(tile))
 
     @pl.loop(0, 8)
     def _(r):
@@ -68,7 +74,7 @@
     lane = lax.broadcasted_iota(jnp.int32, (128, 128), 1)
 
     def spread(k, which):
-        pieces = [w[(x0 + s) & 3, k, which] for w in (wa, wb) for s in range(4)]
+        pieces = [w[s, k, which] for w in (wa, wb) for s in range(4)]
         return jnp.concatenate(pieces, 0)
 
     acc = jnp.zeros((512, 128), F32)
@@ -113,23 +119,23 @@
                     outs[r // 4][r % 4, rows, :] = value
 
 
-def ladder_call(slots, meta, live, ts, us, v, wa, wb, prev=()):
+def ladder_call(group, meta, live, ts, us, v, wa, wb, prev=()):
     smem = pl.BlockSpec(memory_space=pltpu.SMEM)
     vmem = pl.BlockSpec(memory_space=pltpu.VMEM)
     whole = jax.ShapeDtypeStruct((8, 512, 128), F32)
     half = jax.ShapeDtypeStruct((4, 512, 128), F32)
+    masked = jax.ShapeDtypeStruct((2048, 512), BF16)
     return pl.pallas_call(
-        functools.partial(ladder_kernel, slots),
-        out_shape=(half, half) if prev else (whole,),
+        functools.partial(ladder_kernel, group),
+        out_shape=(half, half) if prev else (whole, masked),
         in_specs=[smem, smem] + [vmem] * (13 + len(prev)),
-        out_specs=(vmem, vmem) if prev else (vmem,),
+        out_specs=(vmem, vmem),
         scratch_shapes=[
             pltpu.VMEM((8, 512, 128), F32),
-            pltpu.VMEM((2048, 512), BF16),
-            pltpu.VMEM((128, 64 * len(slots)), BF16),
+            pltpu.VMEM((128, 64 * group[1]), BF16),
             pltpu.VMEM((128, 512), F32),
         ],
-        cost_estimate=pl.CostEstimate(flops=400_000_000 * len(slots), bytes_accessed=10_000_000, transcendentals=0),
+        cost_estimate=pl.CostEstimate(flops=400_000_000 * group[1], bytes_accessed=10_000_000, transcendentals=0),
         compiler_params=pltpu.CompilerParams(vmem_limit_bytes=24 << 20),
         name="ladder",
     )(meta, live, *ts, *us, v, wa, wb, *prev)
@@ -145,7 +151,7 @@
             out[il * 32 : il * 32 + 32, a * 128 : a * 128 + 128] = (total / denom).astype(BF16)
 
 
-def finish_call(meta, eps_occ, eps_vir, parts):
+def finish_call(meta, occ_col, eps_occ, eps_vir, parts):
     smem = pl.BlockSpec(memory_space=pltpu.SMEM)
     vmem = pl.BlockSpec(memory_space=pltpu.VMEM)
     return pl.pallas_call(
@@ -159,7 +165,7 @@
         meta,
         eps_occ,
         eps_vir,
-        jnp.broadcast_to(eps_occ[:, None], (32, 128)),
+        occ_col,
         eps_vir[None, :],
         *parts,
     )
@@ -177,33 +183,43 @@
     return [t.reshape(-1, 32, 16, 128) for t in ts]
 
 
+def place(buffer, group, z0, d, block):
+    low, n = group
+    return lax.dynamic_update_slice(buffer, block[None], (lax.rem(z0 + (d - low) % n, n), 0, 0))
+
+
 def local(amplitudes, ladder_ints, tile_live, cycle_direct, cycle_exchange, eps_occ, eps_vir):
     x0, c0, y0 = lax.axis_index("x"), lax.axis_index("core"), lax.axis_index("y")
     z0 = lax.axis_index("zh") * 4 + lax.axis_index("zl")
     meta = jnp.stack([x0, c0, y0, lax.axis_index(C), lax.axis_index(G), z0]).astype(jnp.int32)
     both = jnp.stack([cycle_direct, cycle_exchange]).reshape(2, 4, 32, 4, 128)
     both = both.transpose(2, 0, 1, 3, 4).reshape(32, 2, 16, 128)
+    both = lax.all_to_all(both, G, 0, 0, tiled=True)
+    occ_col = jnp.broadcast_to(eps_occ[:, None], (32, 128))
+    near = place(jnp.zeros((5, 32, 2048), BF16), NEAR, z0, 0, amplitudes)
+    far = jnp.zeros((3, 32, 2048), BF16)
     fwd = bwd = amplitudes
-    ring = [amplitudes]
-    for k in range(1, 4):
+    for k in range(1, 3):
         fwd, bwd = lax.ppermute(fwd, Z, z_shift(1)), lax.ppermute(bwd, Z, z_shift(-1))
-        ring += [fwd, bwd]
-    ring.append(lax.ppermute(fwd, Z, z_shift(1)))
-    near = jnp.stack(ring[:5])
-    both = lax.all_to_all(both, G, 0, 0, tiled=True)
-    wa = lax.all_to_all(jnp.broadcast_to(both[None], (4, 32, 2, 16, 128)), "x", 0, 0, tiled=True)
-    wa, ring[7] = lax.optimization_barrier((wa, ring[7]))
+        near = place(place(near, NEAR, z0, -k, fwd), NEAR, z0, k, bwd)
+    ts_near = over_y(near, CUTS[NEAR])
+    xs = [both] + [lax.ppermute(both, "x", shift(4, -s)) for s in (1, 2, 3)]
+    fwd, bwd = lax.ppermute(fwd, Z, z_shift(1)), lax.ppermute(bwd, Z, z_shift(-1))
+    far = place(place(far, FAR, z0, 5, fwd), FAR, z0, 3, bwd)
+    far = place(far, FAR, z0, 4, lax.ppermute(fwd, Z, z_shift(1)))
+    ts_far = over_y(far, CUTS[FAR])
+    *xs, ts_near[1], ts_near[4], occ_col = lax.optimization_barrier((*xs, ts_near[1], ts_near[4], occ_col))
+    wa = jnp.stack(xs)
     wb = lax.ppermute(wa, "core", shift(2, 1))
-    far = jnp.stack(ring[5:])
-    ts_near, ts_far = over_y(near, CUTS[NEAR]), over_y(far, CUTS[FAR])
-    prev = list(ladder_call(NEAR, meta, tile_live, ts_near, split_rows(ts_near), ladder_ints, wa, wb))
-    *ts_far, prev[0] = lax.optimization_barrier((*ts_far, prev[0]))
-    keep, away = ladder_call(FAR, meta, tile_live, ts_far, split_rows(ts_far), ladder_ints, wa, wb, tuple(prev))
+    *ts_near, wb = lax.optimization_barrier((*ts_near, wb))
+    first, masked = ladder_call(NEAR, meta, tile_live, ts_near, split_rows(ts_near), ladder_ints, wa, wb)
+    *ts_far, first = lax.optimization_barrier((*ts_far, first))
+    keep, away = ladder_call(FAR, meta, tile_live, ts_far, split_rows(ts_far), masked, wa, wb, (first,))
     got = lax.ppermute(away, "core", shift(2, 1))
     parts = [keep[0], got[0]]
     for s in (1, 2, 3):
         parts.append(lax.ppermute(keep[s] + got[s], "x", shift(4, s)))
-    return finish_call(meta, eps_occ, eps_vir, parts)
+    return finish_call(meta, occ_col, eps_occ, eps_vir, parts)
 
 
 def solution(mesh):

time: 122 us -> 118 us (0.967)
  starting transfers between devices: 49.3 us -> 46.3 us
  local copies, waits for them, and re-layouts: 15.4 us -> 17.1 us
  other arithmetic: 3.86 us -> 2.21 us
    ppermute x2, waiting for transfers between devices: 6.58 us -> 0.28 us  [over_y(): up = lax.ppermute(group, 'y', shift(4, -1))]
    ppermute x3, waiting for transfers between devices: 4.94 us -> 9.85 us  [local(): lax.ppermute(fwd, Z, z_shift(1))]
    ppermute x1, starting transfers between devices: 1.7 us -> 6.56 us  [local(): got = lax.ppermute(away, 'core', shift(2, 1))]
    ppermute x2, waiting for transfers between devices: 0.01 us -> 4.81 us  [over_y(): first = lax.ppermute(down[:cut], 'y', shift(4, 1))]
    ppermute x1, starting transfers between devices: 6.69 us -> 2.28 us  [local(): wb = lax.ppermute(wa, 'core', shift(2, 1))]
    all_to_all x1 -> x0, starting transfers between devices: 4.14 us -> none  [local(): lax.all_to_all(jnp.broadcast_to(both[None], (4, 32, 2, 16, 128)), 'x', 0,...]
    all_to_all x1 -> x0, waiting for transfers between devices: 3.97 us -> none  [local(): lax.all_to_all(jnp.broadcast_to(both[None], (4, 32, 2, 16, 128)), 'x', 0,...]
    ppermute x1 -> x4, starting transfers between devices: 1.21 us -> 4.3 us  [the longest x3 4.21 us: local(): xs = [both] + [lax.ppermute(both, 'x', shift(4, -s)) for s in (1, 2, 3)]]
  transfers between devices with their start and end apart: 22 -> 24, of which waited for: 11 -> 9; matrix products, arithmetic and copies ran while one was open for 12% -> 12% of each run, Pallas kernels for 6% -> 7%
where the time goes in v7:
time: 118 us; the launch traced here: 117 us
  starting transfers between devices  46.3 us (39%)
  waiting for transfers between devices  35 us (30%)
  local copies, waits for them, and re-layouts  17.1 us (14%)
  Pallas kernels  16.4 us (14%)
  other arithmetic  2.21 us (2%)
    pallas_call x2, Pallas kernels, ladder_call(): pl.pallas_call(functools.partial(ladder_kernel, group), out_shape=(half,...  13.9 us
    ppermute x3, waiting for transfers between devices, local(): parts.append(lax.ppermute(keep[s] + got[s], 'x', shift(4, s)))  11.7 us
    ppermute x3, waiting for transfers between devices, local(): lax.ppermute(fwd, Z, z_shift(1))  9.85 us
    all_to_all x1, starting transfers between devices, local(): both = lax.all_to_all(both, G, 0, 0, tiled=True)  8.23 us
    unnamed x35, local copies, waits for them, and re-layouts  7.54 us
    ppermute x3, starting transfers between devices, local(): lax.ppermute(bwd, Z, z_shift(-1))  7.38 us
    ppermute x1, starting transfers between devices, local(): got = lax.ppermute(away, 'core', shift(2, 1))  6.56 us
    ppermute x3, waiting for transfers between devices, local(): xs = [both] + [lax.ppermute(both, 'x', shift(4, -s)) for s in (1, 2, 3)]  5.25 us
  transfers between devices with their start and end apart: 24, of which 9 were waited for; matrix products, arithmetic and copies ran while one was open for 12% of the time, Pallas kernels for 7%

profile of v7, /device:TPU:1, one launch (start us, length us, event | category | flops | bytes accessed | tf_op | source)
XLA Modules:
  0.0 117.4 jit_solution(11507419480241866222)
XLA Ops:
  0.0 2.5 %collective-permute-start.3 = (bf16[32,2048]{1,0:T(8,128)(2,1)}, bf16[32,2048]{1,0:T(8,128)(2,1)S(1)}, u32[]{:S(2)}, u32[]{:S(2)}) collective-permute-start(bf16[32,2048]{1,0:T(8,128)(2,1)} %param.7), channel_id=1, source_target_pairs={{0,64},{64,128},{128,192},{192,32},{32,96},{96,160},{160,224},{224... | collective-permute-start | bytes 393224 | tf_op jit(solution)/shard_map/ppermute | solution.py:203
  2.5 4.0 %collective-permute-start.4 = (bf16[32,2048]{1,0:T(8,128)(2,1)}, bf16[32,2048]{1,0:T(8,128)(2,1)S(1)}, u32[]{:S(2)}, u32[]{:S(2)}) collective-permute-start(bf16[32,2048]{1,0:T(8,128)(2,1)} %param.7), channel_id=1, source_target_pairs={{0,224},{64,0},{128,64},{192,128},{32,192},{96,32},{160,96},{224,1... | collective-permute-start | bytes 393224 | tf_op jit(solution)/shard_map/ppermute | solution.py:203
  6.5 1.2 pad_maximum_fusion.1
  8.4 8.2 %all-to-all-start = ((bf16[32,2,16,128]{3,2,1,0:T(8,128)(2,1)}), bf16[32,2,16,128]{3,2,1,0:T(8,128)(2,1)S(1)}, u32[]{:S(2)}, u32[]{:S(2)}) async-start(bf16[32,2,16,128]{3,2,1,0:T(8,128)(2,1)} %bitcast.9), calls=%async_computation | async-start | bytes 524288 | tf_op jit(solution)/shard_map/all_to_all | solution.py:197
  16.9 1.3 %collective-permute-start.5 = (bf16[32,2048]{1,0:T(8,128)(2,1)S(1)}, bf16[32,2048]{1,0:T(8,128)(2,1)S(1)}, u32[]{:S(2)}, u32[]{:S(2)}) collective-permute-start(bf16[32,2048]{1,0:T(8,128)(2,1)S(1)} %collective-permute-done.3), channel_id=1, source_target_pairs={{0,64},{64,128},{128,192},{192,32},{32,96},{96,160},{160,224},{224... | collective-permute-start | bytes 393224 | tf_op jit(solution)/shard_map/ppermute | solution.py:203
  18.2 1.4 %collective-permute-start.6 = (bf16[32,2048]{1,0:T(8,128)(2,1)S(1)}, bf16[32,2048]{1,0:T(8,128)(2,1)S(1)}, u32[]{:S(2)}, u32[]{:S(2)}) collective-permute-start(bf16[32,2048]{1,0:T(8,128)(2,1)S(1)} %collective-permute-done.4), channel_id=1, source_target_pairs={{0,224},{64,0},{128,64},{192,128},{32,192},{96,32},{160,96},{224,1... | collective-permute-start | bytes 393224 | tf_op jit(solution)/shard_map/ppermute | solution.py:203
  19.7 7.5 %collective-permute-done.5 = bf16[32,2048]{1,0:T(8,128)(2,1)S(1)} collective-permute-done((bf16[32,2048]{1,0:T(8,128)(2,1)S(1)}, bf16[32,2048]{1,0:T(8,128)(2,1)S(1)}, u32[]{:S(2)}, u32[]{:S(2)}) %collective-permute-start.5) | collective-permute-done | bytes 131104 | tf_op jit(solution)/shard_map/ppermute | solution.py:203
  27.3 1.7 %collective-permute-start.7 = (bf16[5,32,2048]{2,1,0:T(8,128)(2,1)S(1)}, bf16[5,32,2048]{2,1,0:T(8,128)(2,1)S(1)}, u32[]{:S(2)}, u32[]{:S(2)}) collective-permute-start(bf16[5,32,2048]{2,1,0:T(8,128)(2,1)S(1)} %bitcast_dynamic-update-slice_fusion.3.refs_0_), channel_id=1, source_target_pairs={{0,8},{8,16},{16,24},{24,0},{1,9},{9,17},{17,25},{25,1},{2,10},{10... | collective-permute-start | bytes 1966088 | tf_op jit(solution)/shard_map/ppermute | solution.py:175
  29.0 1.4 %collective-permute-start.8 = (bf16[5,32,2048]{2,1,0:T(8,128)(2,1)S(1)}, bf16[5,32,2048]{2,1,0:T(8,128)(2,1)S(1)}, u32[]{:S(2)}, u32[]{:S(2)}) collective-permute-start(bf16[5,32,2048]{2,1,0:T(8,128)(2,1)S(1)} %bitcast_dynamic-update-slice_fusion.3.refs_0_), channel_id=1, source_target_pairs={{0,24},{8,0},{16,8},{24,16},{1,25},{9,1},{17,9},{25,17},{2,26},{10... | collective-permute-start | bytes 1966088 | tf_op jit(solution)/shard_map/ppermute | solution.py:176
  30.3 2.5 %collective-permute-start = (bf16[32,2,16,128]{3,2,1,0:T(8,128)(2,1)S(1)}, bf16[32,2,16,128]{3,2,1,0:T(8,128)(2,1)S(1)}, u32[]{:S(2)}, u32[]{:S(2)}) collective-permute-start(bf16[32,2,16,128]{3,2,1,0:T(8,128)(2,1)S(1)} %all-to-all-done), channel_id=1, source_target_pairs={{0,6},{2,0},{4,2},{6,4},{1,7},{3,1},{5,3},{7,5},{8,14},{10,8},{12,... | collective-permute-start | bytes 786440 | tf_op jit(solution)/shard_map/ppermute | solution.py:206
  33.3 2.3 %collective-permute-done.9 = bf16[32,2048]{1,0:T(8,128)(2,1)} collective-permute-done((bf16[32,2048]{1,0:T(8,128)(2,1)S(1)}, bf16[32,2048]{1,0:T(8,128)(2,1)}, u32[]{:S(2)}, u32[]{:S(2)}) %collective-permute-start.9) | collective-permute-done | bytes 131104 | tf_op jit(solution)/shard_map/ppermute | solution.py:207
  35.7 1.2 %collective-permute-start.2 = (bf16[32,2,16,128]{3,2,1,0:T(8,128)(2,1)S(1)}, bf16[32,2,16,128]{3,2,1,0:T(8,128)(2,1)S(1)}, u32[]{:S(2)}, u32[]{:S(2)}) collective-permute-start(bf16[32,2,16,128]{3,2,1,0:T(8,128)(2,1)S(1)} %all-to-all-done), channel_id=1, source_target_pairs={{0,2},{2,4},{4,6},{6,0},{1,3},{3,5},{5,7},{7,1},{8,10},{10,12},{12... | collective-permute-start | bytes 786440 | tf_op jit(solution)/shard_map/ppermute | solution.py:206
  37.7 1.6 %bitcast_dynamic-update-slice_fusion.2 = bf16[3,32,2048]{2,1,0:T(8,128)(2,1)} fusion(bf16[3,32,2048]{2,1,0:T(8,128)(2,1)} %broadcast_in_dim.47, s32[]{:T(128)S(6)} %select_n.29, bf16[32,2048]{1,0:T(8,128)(2,1)} %collective-permute-done.9), kind=kLoop, calls=%fused_computation.12 | loop fusion | bytes 262148 | tf_op jit(solution)/shard_map/dynamic_update_slice | solution.py:188
  39.2 1.9 %collective-permute-start.10 = (bf16[32,2048]{1,0:T(8,128)(2,1)S(1)}, bf16[32,2048]{1,0:T(8,128)(2,1)S(1)}, u32[]{:S(2)}, u32[]{:S(2)}) collective-permute-start(bf16[32,2048]{1,0:T(8,128)(2,1)S(1)} %collective-permute-done.6), channel_id=1, source_target_pairs={{0,224},{64,0},{128,64},{192,128},{32,192},{96,32},{160,96},{224,1... | collective-permute-start | bytes 393224 | tf_op jit(solution)/shard_map/ppermute | solution.py:207
  41.2 5.2 %collective-permute-done.2 = bf16[32,2,16,128]{3,2,1,0:T(8,128)(2,1)S(1)} collective-permute-done((bf16[32,2,16,128]{3,2,1,0:T(8,128)(2,1)S(1)}, bf16[32,2,16,128]{3,2,1,0:T(8,128)(2,1)S(1)}, u32[]{:S(2)}, u32[]{:S(2)}) %collective-permute-start.2) | collective-permute-done | bytes 262176 | tf_op jit(solution)/shard_map/ppermute | solution.py:206
  47.5 2.3 %collective-permute-start.18 = (bf16[4,32,2,16,128]{4,3,2,1,0:T(8,128)(2,1)S(1)}, bf16[4,32,2,16,128]{4,3,2,1,0:T(8,128)(2,1)S(1)}, u32[]{:S(2)}, u32[]{:S(2)}) collective-permute-start(bf16[4,32,2,16,128]{4,3,2,1,0:T(8,128)(2,1)S(1)} %pad_maximum_fusion.refs_11_), channel_id=1, source_target_pairs={{0,1},{1,0},{2,3},{3,2},{4,5},{5,4},{6,7},{7,6},{8,9},{9,8},{10,11... | collective-permute-start | bytes 3145736 | tf_op jit(solution)/shard_map/ppermute | solution.py:213
  51.1 1.4 %collective-permute-start.14 = (bf16[3,32,2048]{2,1,0:T(8,128)(2,1)}, bf16[3,32,2048]{2,1,0:T(8,128)(2,1)S(1)}, u32[]{:S(2)}, u32[]{:S(2)}) collective-permute-start(bf16[3,32,2048]{2,1,0:T(8,128)(2,1)} %bitcast_dynamic-update-slice_fusion.refs_0_), channel_id=1, source_target_pairs={{0,24},{8,0},{16,8},{24,16},{1,25},{9,1},{17,9},{25,17},{2,26},{10... | collective-permute-start | bytes 1179656 | tf_op jit(solution)/shard_map/ppermute | solution.py:176
  53.4 1.6 %slice.51 = bf16[2,32,2048]{2,1,0:T(8,128)(2,1)} slice(bf16[5,32,2048]{2,1,0:T(8,128)(2,1)} %copy-done), slice={[3:5], [0:32], [0:2048]} | slice | bytes 524288 | tf_op jit(solution)/shard_map/slice | solution.py:178
  55.1 2.6 %collective-permute-start.17 = (bf16[2,32,2048]{2,1,0:T(8,128)(2,1)}, bf16[2,32,2048]{2,1,0:T(8,128)(2,1)}, u32[]{:S(2)}, u32[]{:S(2)}) collective-permute-start(bf16[2,32,2048]{2,1,0:T(8,128)(2,1)} %slice.51), channel_id=1, source_target_pairs={{0,24},{8,0},{16,8},{24,16},{1,25},{9,1},{17,9},{25,17},{2,26},{10... | collective-permute-start | bytes 786440 | tf_op jit(solution)/shard_map/ppermute | solution.py:178
  59.4 2.6 %collective-permute-start.15 = (bf16[2,32,2048]{2,1,0:T(8,128)(2,1)}, bf16[2,32,2048]{2,1,0:T(8,128)(2,1)}, u32[]{:S(2)}, u32[]{:S(2)}) collective-permute-start(bf16[2,32,2048]{2,1,0:T(8,128)(2,1)} %slice.49), channel_id=1, source_target_pairs={{0,24},{8,0},{16,8},{24,16},{1,25},{9,1},{17,9},{25,17},{2,26},{10... | collective-permute-start | bytes 786440 | tf_op jit(solution)/shard_map/ppermute | solution.py:178
  64.1 4.8 %collective-permute-done.16.refs_2_ = bf16[3,32,2048]{2,1,0:T(8,128)(2,1)} collective-permute-done((bf16[3,32,2048]{2,1,0:T(8,128)(2,1)}, bf16[3,32,2048]{2,1,0:T(8,128)(2,1)}, u32[]{:S(2)}, u32[]{:S(2)}) %collective-permute-start.16) | collective-permute-done | bytes 393248 | tf_op jit(solution)/shard_map/ppermute | solution.py:177
  69.3 1.2 %copy.15 = bf16[12,8,16,128]{3,2,1,0:T(8,128)(2,1)S(1)} copy(bf16[12,8,16,128]{3,1,2,0:T(8,128)(2,1)} %bitcast.38) | data formatting | bytes 786432
  71.6 7.9 %ladder.2 = (f32[8,512,128]{2,1,0:T(8,128)S(1)}, bf16[2048,512]{1,0:T(8,128)(2,1)S(1)}) custom-call(s32[6]{0:T(128)S(1)} %stack.51.meta, s32[16,4]{1,0:T(8,128)S(1)} %copy.11.live, bf16[5,32,2048]{2,1,0:T(8,128)(2,1)S(1)} %bitcast_dynamic-update-slice_fusion.3.refs_0_, bf16[5,32,2048]{2,1,0:T(8,128)(2,1)S(1)} %collective-permute-done.7.refs_1_, ...), custom_call_target="tpu_custom_call" | custom-call | flops 2000000000 | bytes 10000000 | tf_op jit(solution)/shard_map/ladder/pallas_call | solution.py:128
  79.5 1.1 copy.18
  80.6 1.1 copy.19
  82.8 6.0 %ladder.3 = (f32[4,512,128]{2,1,0:T(8,128)S(1)}, f32[4,512,128]{2,1,0:T(8,128)S(1)}) custom-call(s32[6]{0:T(128)S(1)} %stack.51.meta, s32[16,4]{1,0:T(8,128)S(1)} %copy.11.live, bf16[3,32,2048]{2,1,0:T(8,128)(2,1)} %bitcast_dynamic-update-slice_fusion.refs_0_, bf16[3,32,2048]{2,1,0:T(8,128)(2,1)} %collective-permute-done.12.refs_1_, ...), custom_call_target="tpu_custom_call" | custom-call | flops 1200000000 | bytes 10000000 | tf_op jit(solution)/shard_map/ladder/pallas_call | solution.py:128
  88.8 6.6 %collective-permute-start.19 = (f32[4,512,128]{2,1,0:T(8,128)S(1)}, f32[4,512,128]{2,1,0:T(8,128)S(1)}, u32[]{:S(2)}, u32[]{:S(2)}) collective-permute-start(f32[4,512,128]{2,1,0:T(8,128)S(1)} %get-tuple-element.50), channel_id=1, source_target_pairs={{0,1},{1,0},{2,3},{3,2},{4,5},{5,4},{6,7},{7,6},{8,9},{9,8},{10,11... | collective-permute-start | bytes 3145736 | tf_op jit(solution)/shard_map/ppermute | solution.py:218
  95.4 2.3 %collective-permute-done.19 = f32[4,512,128]{2,1,0:T(8,128)S(1)} collective-permute-done((f32[4,512,128]{2,1,0:T(8,128)S(1)}, f32[4,512,128]{2,1,0:T(8,128)S(1)}, u32[]{:S(2)}, u32[]{:S(2)}) %collective-permute-start.19) | collective-permute-done | bytes 1048608 | tf_op jit(solution)/shard_map/ppermute | solution.py:218
  98.6 3.9 %collective-permute-start.21 = (f32[512,128]{1,0:T(8,128)S(1)}, f32[512,128]{1,0:T(8,128)S(1)}, u32[]{:S(2)}, u32[]{:S(2)}) collective-permute-start(f32[512,128]{1,0:T(8,128)S(1)} %get-tuple-element.52), channel_id=1, source_target_pairs={{0,4},{2,6},{4,0},{6,2},{1,5},{3,7},{5,1},{7,3},{8,12},{10,14},{12... | collective-permute-start | bytes 786440 | tf_op jit(solution)/shard_map/ppermute | solution.py:221
  102.4 4.9 %collective-permute-done.20.p2 = f32[512,128]{1,0:T(8,128)S(1)} collective-permute-done((f32[512,128]{1,0:T(8,128)S(1)}, f32[512,128]{1,0:T(8,128)S(1)}, u32[]{:S(2)}, u32[]{:S(2)}) %collective-permute-start.20) | collective-permute-done | bytes 262176 | tf_op jit(solution)/shard_map/ppermute | solution.py:221
  107.3 6.8 %collective-permute-done.21.p3 = f32[512,128]{1,0:T(8,128)S(1)} collective-permute-done((f32[512,128]{1,0:T(8,128)S(1)}, f32[512,128]{1,0:T(8,128)S(1)}, u32[]{:S(2)}, u32[]{:S(2)}) %collective-permute-start.21) | collective-permute-done | bytes 262176 | tf_op jit(solution)/shard_map/ppermute | solution.py:221
  114.9 2.4 %finish.1 = bf16[128,512]{1,0:T(8,128)(2,1)} custom-call(s32[6]{0:T(128)} %copy-done.5, f32[32]{0:T(128)} %occ.1, f32[128]{0:T(128)} %vir.1, f32[32,128]{1,0:T(8,128)} %broadcast_in_dim.45.occ_col, f32[1,128]{1,0:T(1,128)} %bitcast.103, f32[512,128]{1,0:T(8,128)} %get-tuple-element.54.p0, f32[512,128]{1,0:T(8,128)} %get-tuple-element.55.p1, ...), custom_call_target="tpu_custom_call" | custom-call | flops 400000 | bytes 1500000 | tf_op jit(solution)/shard_map/finish/pallas_call | solution.py:157
  (74 shorter events, 13.6 us)
Async XLA Ops:
  0.0 16.8 %copy-start.9 = (bf16[32,2048]{1,0:T(8,128)(2,1)S(1)}, bf16[32,2048]{1,0:T(8,128)(2,1)}, u32[]{:S(2)}) copy-start(bf16[32,2048]{1,0:T(8,128)(2,1)} %param.7) | copy-start | bytes 393220
  0.0 16.9 %collective-permute-start.3 = (bf16[32,2048]{1,0:T(8,128)(2,1)}, bf16[32,2048]{1,0:T(8,128)(2,1)S(1)}, u32[]{:S(2)}, u32[]{:S(2)}) collective-permute-start(bf16[32,2048]{1,0:T(8,128)(2,1)} %param.7), channel_id=1, source_target_pairs={{0,64},{64,128},{128,192},{192,32},{32,96},{96,160},{160,224},{224... | collective-permute-start | bytes 393224 | tf_op jit(solution)/shard_map/ppermute | solution.py:203
  2.5 15.7 %collective-permute-start.4 = (bf16[32,2048]{1,0:T(8,128)(2,1)}, bf16[32,2048]{1,0:T(8,128)(2,1)S(1)}, u32[]{:S(2)}, u32[]{:S(2)}) collective-permute-start(bf16[32,2048]{1,0:T(8,128)(2,1)} %param.7), channel_id=1, source_target_pairs={{0,224},{64,0},{128,64},{192,128},{32,192},{96,32},{160,96},{224,1... | collective-permute-start | bytes 393224 | tf_op jit(solution)/shard_map/ppermute | solution.py:203
  6.5 40.0 %copy-start.10 = (f32[32]{0:T(128)S(1)}, f32[32]{0:T(128)}, u32[]{:S(2)}) copy-start(f32[32]{0:T(128)} %occ.1) | copy-start | bytes 388
  8.4 21.9 %all-to-all-start = ((bf16[32,2,16,128]{3,2,1,0:T(8,128)(2,1)}), bf16[32,2,16,128]{3,2,1,0:T(8,128)(2,1)S(1)}, u32[]{:S(2)}, u32[]{:S(2)}) async-start(bf16[32,2,16,128]{3,2,1,0:T(8,128)(2,1)} %bitcast.9), calls=%async_computation | async-start | bytes 524288 | tf_op jit(solution)/shard_map/all_to_all | solution.py:197
  16.9 10.3 %collective-permute-start.5 = (bf16[32,2048]{1,0:T(8,128)(2,1)S(1)}, bf16[32,2048]{1,0:T(8,128)(2,1)S(1)}, u32[]{:S(2)}, u32[]{:S(2)}) collective-permute-start(bf16[32,2048]{1,0:T(8,128)(2,1)S(1)} %collective-permute-done.3), channel_id=1, source_target_pairs={{0,64},{64,128},{128,192},{192,32},{32,96},{96,160},{160,224},{224... | collective-permute-start | bytes 393224 | tf_op jit(solution)/shard_map/ppermute | solution.py:203
  18.2 9.0 %collective-permute-start.6 = (bf16[32,2048]{1,0:T(8,128)(2,1)S(1)}, bf16[32,2048]{1,0:T(8,128)(2,1)S(1)}, u32[]{:S(2)}, u32[]{:S(2)}) collective-permute-start(bf16[32,2048]{1,0:T(8,128)(2,1)S(1)} %collective-permute-done.4), channel_id=1, source_target_pairs={{0,224},{64,0},{128,64},{192,128},{32,192},{96,32},{160,96},{224,1... | collective-permute-start | bytes 393224 | tf_op jit(solution)/shard_map/ppermute | solution.py:203
  27.3 19.2 %collective-permute-start.7 = (bf16[5,32,2048]{2,1,0:T(8,128)(2,1)S(1)}, bf16[5,32,2048]{2,1,0:T(8,128)(2,1)S(1)}, u32[]{:S(2)}, u32[]{:S(2)}) collective-permute-start(bf16[5,32,2048]{2,1,0:T(8,128)(2,1)S(1)} %bitcast_dynamic-update-slice_fusion.3.refs_0_), channel_id=1, source_target_pairs={{0,8},{8,16},{16,24},{24,0},{1,9},{9,17},{17,25},{25,1},{2,10},{10... | collective-permute-start | bytes 1966088 | tf_op jit(solution)/shard_map/ppermute | solution.py:175
  29.0 17.5 %collective-permute-start.8 = (bf16[5,32,2048]{2,1,0:T(8,128)(2,1)S(1)}, bf16[5,32,2048]{2,1,0:T(8,128)(2,1)S(1)}, u32[]{:S(2)}, u32[]{:S(2)}) collective-permute-start(bf16[5,32,2048]{2,1,0:T(8,128)(2,1)S(1)} %bitcast_dynamic-update-slice_fusion.3.refs_0_), channel_id=1, source_target_pairs={{0,24},{8,0},{16,8},{24,16},{1,25},{9,1},{17,9},{25,17},{2,26},{10... | collective-permute-start | bytes 1966088 | tf_op jit(solution)/shard_map/ppermute | solution.py:176
  30.3 5.3 %collective-permute-start.9 = (bf16[32,2048]{1,0:T(8,128)(2,1)S(1)}, bf16[32,2048]{1,0:T(8,128)(2,1)}, u32[]{:S(2)}, u32[]{:S(2)}) collective-permute-start(bf16[32,2048]{1,0:T(8,128)(2,1)S(1)} %collective-permute-done.5), channel_id=1, source_target_pairs={{0,64},{64,128},{128,192},{192,32},{32,96},{96,160},{160,224},{224... | collective-permute-start | bytes 393224 | tf_op jit(solution)/shard_map/ppermute | solution.py:207
  30.3 8.9 %collective-permute-start = (bf16[32,2,16,128]{3,2,1,0:T(8,128)(2,1)S(1)}, bf16[32,2,16,128]{3,2,1,0:T(8,128)(2,1)S(1)}, u32[]{:S(2)}, u32[]{:S(2)}) collective-permute-start(bf16[32,2,16,128]{3,2,1,0:T(8,128)(2,1)S(1)} %all-to-all-done), channel_id=1, source_target_pairs={{0,6},{2,0},{4,2},{6,4},{1,7},{3,1},{5,3},{7,5},{8,14},{10,8},{12,... | collective-permute-start | bytes 786440 | tf_op jit(solution)/shard_map/ppermute | solution.py:206
  32.8 8.3 %collective-permute-start.1 = (bf16[32,2,16,128]{3,2,1,0:T(8,128)(2,1)S(1)}, bf16[32,2,16,128]{3,2,1,0:T(8,128)(2,1)S(1)}, u32[]{:S(2)}, u32[]{:S(2)}) collective-permute-start(bf16[32,2,16,128]{3,2,1,0:T(8,128)(2,1)S(1)} %all-to-all-done), channel_id=1, source_target_pairs={{0,4},{2,6},{4,0},{6,2},{1,5},{3,7},{5,1},{7,3},{8,12},{10,14},{12... | collective-permute-start | bytes 786440 | tf_op jit(solution)/shard_map/ppermute | solution.py:206
  35.7 10.8 %collective-permute-start.2 = (bf16[32,2,16,128]{3,2,1,0:T(8,128)(2,1)S(1)}, bf16[32,2,16,128]{3,2,1,0:T(8,128)(2,1)S(1)}, u32[]{:S(2)}, u32[]{:S(2)}) collective-permute-start(bf16[32,2,16,128]{3,2,1,0:T(8,128)(2,1)S(1)} %all-to-all-done), channel_id=1, source_target_pairs={{0,2},{2,4},{4,6},{6,0},{1,3},{3,5},{5,7},{7,1},{8,10},{10,12},{12... | collective-permute-start | bytes 786440 | tf_op jit(solution)/shard_map/ppermute | solution.py:206
  39.2 10.6 %collective-permute-start.10 = (bf16[32,2048]{1,0:T(8,128)(2,1)S(1)}, bf16[32,2048]{1,0:T(8,128)(2,1)S(1)}, u32[]{:S(2)}, u32[]{:S(2)}) collective-permute-start(bf16[32,2048]{1,0:T(8,128)(2,1)S(1)} %collective-permute-done.6), channel_id=1, source_target_pairs={{0,224},{64,0},{128,64},{192,128},{32,192},{96,32},{160,96},{224,1... | collective-permute-start | bytes 393224 | tf_op jit(solution)/shard_map/ppermute | solution.py:207
  41.1 9.3 %collective-permute-start.11 = (bf16[32,2048]{1,0:T(8,128)(2,1)}, bf16[32,2048]{1,0:T(8,128)(2,1)S(1)}, u32[]{:S(2)}, u32[]{:S(2)}) collective-permute-start(bf16[32,2048]{1,0:T(8,128)(2,1)} %collective-permute-done.9), channel_id=1, source_target_pairs={{0,64},{64,128},{128,192},{192,32},{32,96},{96,160},{160,224},{224... | collective-permute-start | bytes 393224 | tf_op jit(solution)/shard_map/ppermute | solution.py:209
  47.4 14.6 %copy-start.11 = (s32[16,4]{0,1:T(4,128)S(1)}, s32[16,4]{0,1:T(4,128)}, u32[]{:S(2)}) copy-start(s32[16,4]{0,1:T(4,128)} %param.9) | copy-start | bytes 772
  47.5 21.4 %collective-permute-start.18 = (bf16[4,32,2,16,128]{4,3,2,1,0:T(8,128)(2,1)S(1)}, bf16[4,32,2,16,128]{4,3,2,1,0:T(8,128)(2,1)S(1)}, u32[]{:S(2)}, u32[]{:S(2)}) collective-permute-start(bf16[4,32,2,16,128]{4,3,2,1,0:T(8,128)(2,1)S(1)} %pad_maximum_fusion.refs_11_), channel_id=1, source_target_pairs={{0,1},{1,0},{2,3},{3,2},{4,5},{5,4},{6,7},{7,6},{8,9},{9,8},{10,11... | collective-permute-start | bytes 3145736 | tf_op jit(solution)/shard_map/ppermute | solution.py:213
  51.1 6.8 %collective-permute-start.14 = (bf16[3,32,2048]{2,1,0:T(8,128)(2,1)}, bf16[3,32,2048]{2,1,0:T(8,128)(2,1)S(1)}, u32[]{:S(2)}, u32[]{:S(2)}) collective-permute-start(bf16[3,32,2048]{2,1,0:T(8,128)(2,1)} %bitcast_dynamic-update-slice_fusion.refs_0_), channel_id=1, source_target_pairs={{0,24},{8,0},{16,8},{24,16},{1,25},{9,1},{17,9},{25,17},{2,26},{10... | collective-permute-start | bytes 1179656 | tf_op jit(solution)/shard_map/ppermute | solution.py:176
  52.5 9.7 %collective-permute-start.12 = (bf16[3,32,2048]{2,1,0:T(8,128)(2,1)}, bf16[3,32,2048]{2,1,0:T(8,128)(2,1)}, u32[]{:S(2)}, u32[]{:S(2)}) collective-permute-start(bf16[3,32,2048]{2,1,0:T(8,128)(2,1)} %bitcast_dynamic-update-slice_fusion.refs_0_), channel_id=1, source_target_pairs={{0,8},{8,16},{16,24},{24,0},{1,9},{9,17},{17,25},{25,1},{2,10},{10... | collective-permute-start | bytes 1179656 | tf_op jit(solution)/shard_map/ppermute | solution.py:175
  53.3 15.5 %collective-permute-start.16 = (bf16[3,32,2048]{2,1,0:T(8,128)(2,1)}, bf16[3,32,2048]{2,1,0:T(8,128)(2,1)}, u32[]{:S(2)}, u32[]{:S(2)}) collective-permute-start(bf16[3,32,2048]{2,1,0:T(8,128)(2,1)} %slice.50), channel_id=1, source_target_pairs={{0,8},{8,16},{16,24},{24,0},{1,9},{9,17},{17,25},{25,1},{2,10},{10... | collective-permute-start | bytes 1179656 | tf_op jit(solution)/shard_map/ppermute | solution.py:177
  55.1 9.0 %collective-permute-start.17 = (bf16[2,32,2048]{2,1,0:T(8,128)(2,1)}, bf16[2,32,2048]{2,1,0:T(8,128)(2,1)}, u32[]{:S(2)}, u32[]{:S(2)}) collective-permute-start(bf16[2,32,2048]{2,1,0:T(8,128)(2,1)} %slice.51), channel_id=1, source_target_pairs={{0,24},{8,0},{16,8},{24,16},{1,25},{9,1},{17,9},{25,17},{2,26},{10... | collective-permute-start | bytes 786440 | tf_op jit(solution)/shard_map/ppermute | solution.py:178
  59.4 20.1 %collective-permute-start.15 = (bf16[2,32,2048]{2,1,0:T(8,128)(2,1)}, bf16[2,32,2048]{2,1,0:T(8,128)(2,1)}, u32[]{:S(2)}, u32[]{:S(2)}) collective-permute-start(bf16[2,32,2048]{2,1,0:T(8,128)(2,1)} %slice.49), channel_id=1, source_target_pairs={{0,24},{8,0},{16,8},{24,16},{1,25},{9,1},{17,9},{25,17},{2,26},{10... | collective-permute-start | bytes 786440 | tf_op jit(solution)/shard_map/ppermute | solution.py:178
  62.2 20.6 %copy-start.5 = (s32[6]{0:T(128)}, s32[6]{0:T(128)S(1)}, u32[]{:S(2)}) copy-start(s32[6]{0:T(128)S(1)} %stack.51.meta) | copy-start | bytes 76
  62.2 7.0 %copy-start.1 = (bf16[5,32,2048]{2,1,0:T(8,128)(2,1)S(1)}, bf16[5,32,2048]{2,1,0:T(8,128)(2,1)}, u32[]{:S(2)}) copy-start(bf16[5,32,2048]{2,1,0:T(8,128)(2,1)} %copy-done) | copy-start | bytes 1966084
  63.2 16.4 %collective-permute-start.13 = (bf16[1,32,2048]{2,1,0:T(8,128)(2,1)S(1)}, bf16[1,32,2048]{2,1,0:T(8,128)(2,1)S(1)}, u32[]{:S(2)}, u32[]{:S(2)}) collective-permute-start(bf16[1,32,2048]{2,1,0:T(8,128)(2,1)S(1)} %slice.48), channel_id=1, source_target_pairs={{0,8},{8,16},{16,24},{24,0},{1,9},{9,17},{17,25},{25,1},{2,10},{10... | collective-permute-start | bytes 393224 | tf_op jit(solution)/shard_map/ppermute | solution.py:177
  69.0 2.5 %copy-start.4 = (bf16[2048,512]{1,0:T(8,128)(2,1)S(1)}, bf16[2048,512]{1,0:T(8,128)(2,1)}, u32[]{:S(2)}) copy-start(bf16[2048,512]{1,0:T(8,128)(2,1)} %refs_10_.1) | copy-start | bytes 6291460
  71.6 10.1 %copy-start.3 = (bf16[3,32,2048]{2,1,0:T(8,128)(2,1)S(1)}, bf16[3,32,2048]{2,1,0:T(8,128)(2,1)}, u32[]{:S(2)}) copy-start(bf16[3,32,2048]{2,1,0:T(8,128)(2,1)} %copy-done.2) | copy-start | bytes 1179652
  88.8 8.8 %collective-permute-start.19 = (f32[4,512,128]{2,1,0:T(8,128)S(1)}, f32[4,512,128]{2,1,0:T(8,128)S(1)}, u32[]{:S(2)}, u32[]{:S(2)}) collective-permute-start(f32[4,512,128]{2,1,0:T(8,128)S(1)} %get-tuple-element.50), channel_id=1, source_target_pairs={{0,1},{1,0},{2,3},{3,2},{4,5},{5,4},{6,7},{7,6},{8,9},{9,8},{10,11... | collective-permute-start | bytes 3145736 | tf_op jit(solution)/shard_map/ppermute | solution.py:218
  98.6 8.8 %collective-permute-start.20 = (f32[512,128]{1,0:T(8,128)S(1)}, f32[512,128]{1,0:T(8,128)S(1)}, u32[]{:S(2)}, u32[]{:S(2)}) collective-permute-start(f32[512,128]{1,0:T(8,128)S(1)} %get-tuple-element.53), channel_id=1, source_target_pairs={{0,2},{2,4},{4,6},{6,0},{1,3},{3,5},{5,7},{7,1},{8,10},{10,12},{12... | collective-permute-start | bytes 786440 | tf_op jit(solution)/shard_map/ppermute | solution.py:221
  98.6 15.5 %collective-permute-start.21 = (f32[512,128]{1,0:T(8,128)S(1)}, f32[512,128]{1,0:T(8,128)S(1)}, u32[]{:S(2)}, u32[]{:S(2)}) collective-permute-start(f32[512,128]{1,0:T(8,128)S(1)} %get-tuple-element.52), channel_id=1, source_target_pairs={{0,4},{2,6},{4,0},{6,2},{1,5},{3,7},{5,1},{7,3},{8,12},{10,14},{12... | collective-permute-start | bytes 786440 | tf_op jit(solution)/shard_map/ppermute | solution.py:221
  102.4 11.7 %collective-permute-start.22 = (f32[512,128]{1,0:T(8,128)S(1)}, f32[512,128]{1,0:T(8,128)S(1)}, u32[]{:S(2)}, u32[]{:S(2)}) collective-permute-start(f32[512,128]{1,0:T(8,128)S(1)} %get-tuple-element.51), channel_id=1, source_target_pairs={{0,6},{2,0},{4,2},{6,4},{1,7},{3,1},{5,3},{7,5},{8,14},{10,8},{12,... | collective-permute-start | bytes 786440 | tf_op jit(solution)/shard_map/ppermute | solution.py:221
  107.3 6.8 %copy-start.6 = (f32[512,128]{1,0:T(8,128)}, f32[512,128]{1,0:T(8,128)S(1)}, u32[]{:S(2)}) copy-start(f32[512,128]{1,0:T(8,128)S(1)} %collective-permute-done.20.p2) | copy-start | bytes 786436
  (4 other events, 3.1 us)

commit v8 on v7

--- a/solution.py
+++ b/solution.py
@@ -26,29 +26,30 @@
 NEAR = (-2, 5)
 FAR = (3, 3)
 CUTS = {NEAR: 3, FAR: 1}
-
-
-def ladder_kernel(group, meta, live, *refs):
-    low, n = group
-    cut = CUTS[group]
-    ts, us, (v, wa, wb), refs = refs[:5], refs[5:10], refs[10:13], refs[13:]
-    blocks = [(p, d, q, d) for p, q in ((0, 0), (1, 1)) for d in range(n)]
-    blocks += [(2, d, 2, d) for d in range(cut)] + [(3, d - cut, 2, d) for d in range(cut, n)]
-    blocks += [(4, d, 3, d) for d in range(n)]
+FIRST = ((NEAR, 0, 0, 5), (NEAR, 1, 0, 5), (NEAR, 3, 0, 5), (FAR, 0, 0, 3))
+LAST = ((FAR, 1, 0, 3), (FAR, 3, 0, 3), (NEAR, 2, 0, 3), (NEAR, 2, 3, 2), (FAR, 2, 0, 1), (FAR, 2, 1, 2))
+
+
+def ladder_kernel(pieces, meta, live, *refs):
+    n = len(pieces)
+    ts, us, (v, wa, wb), refs = refs[:n], refs[n : 2 * n], refs[2 * n : 2 * n + 3], refs[2 * n + 3 :]
     prev = None
-    if group is FAR:
+    if pieces is LAST:
         vm = v
         prev, refs = refs[0], refs[1:]
     outs, (ladder, wm, o2) = refs[:-3], refs[-3:]
-    if group is NEAR:
+    if pieces is FIRST:
         vm = outs[1]
     x0, c0, y0, col, z0 = meta[0], meta[1], meta[2], meta[3], meta[5]
-    ys = [(y0 + 4 - q) & 3 for q in range(4)]
-    zs = [(z0 + low + 8 + lax.rem(e + 4 * n - z0, n)) & 7 for e in range(n)]
-    hs = [((z & 3) << 1) | (z >> 2) for z in zs]
-    at = [((((z >> 2) ^ c0) << 2) | (((z & 3) + 4 - x0) & 3)) for z in zs]
-
-    if group is NEAR:
+    blocks = []
+    for p, ((low, size), q, top, count) in enumerate(pieces):
+        for e in range(count):
+            z = (z0 + low + 8 + lax.rem(top + e + 4 * size - z0, size)) & 7
+            h = ((z & 3) << 1) | (z >> 2)
+            spot = (((z >> 2) ^ c0) << 2) | (((z & 3) + 4 - x0) & 3)
+            blocks.append((p, e, (y0 + 4 - q) & 3, h, spot))
+
+    if pieces is FIRST:
 
         @pl.loop(0, 16)
         def _(kt):
@@ -62,14 +63,14 @@
     def _(r):
         ladder[r] = jnp.zeros((512, 128), F32) if prev is None else prev[r]
 
-    half = 2 * n
+    half = len(blocks) // 2
     for part_of in (blocks[:half], blocks[half:]):
-        rows = jnp.concatenate([ts[p][e] for p, e, _, _ in part_of], 0)
+        rows = jnp.concatenate([ts[p][e] for p, e, *_ in part_of], 0)
         part = jnp.dot(rows, vm[...], preferred_element_type=F32)
-        for m, (_, _, q, d) in enumerate(part_of):
+        for m, (_, _, y, _, spot) in enumerate(part_of):
             for a in range(4):
-                rows = pl.ds(ys[q] * 4 + a, 32, stride=16)
-                ladder[at[d], rows, :] += part[m * 32 : m * 32 + 32, a * 128 : a * 128 + 128]
+                rows = pl.ds(y * 4 + a, 32, stride=16)
+                ladder[spot, rows, :] += part[m * 32 : m * 32 + 32, a * 128 : a * 128 + 128]
 
     lane = lax.broadcasted_iota(jnp.int32, (128, 128), 1)
 
@@ -79,21 +80,21 @@
 
     acc = jnp.zeros((512, 128), F32)
     w_all = None
-    for m in range(0, 4 * n, 2):
+    for m in range(0, len(blocks), 2):
         pair = blocks[m : m + 2]
-        lhs = jnp.concatenate([us[p][e].reshape(512, 128) for p, e, _, _ in pair], 1)
-        rhs = jnp.concatenate([spread(hs[d] * 4 + ys[q], 1) for _, _, q, d in pair], 1)
+        lhs = jnp.concatenate([us[p][e].reshape(512, 128) for p, e, *_ in pair], 1)
+        rhs = jnp.concatenate([spread(h * 4 + y, 1) for _, _, y, h, _ in pair], 1)
         acc = acc + lax.dot_general(lhs, rhs, (((1,), (1,)), ((), ())), preferred_element_type=F32)
         if m % 8 == 0:
             w_all = jnp.zeros((128, 128), F32)
-        for f, (_, _, q, d) in enumerate(pair):
+        for f, (_, _, y, h, _) in enumerate(pair):
             place = m % 8 + f
-            wk = spread(hs[d] * 4 + ys[q], 0).astype(F32)
+            wk = spread(h * 4 + y, 0).astype(F32)
             wk = pltpu.roll(wk, (16 * place + 128 - 16 * col) & 127, 1)
             w_all = jnp.where((lane >> 4) == place, wk, w_all)
-        if m % 8 == 6 or m + 2 == 4 * n:
+        if m % 8 == 6 or m + 2 == len(blocks):
             top = m // 8 * 128
-            width = min(128, 64 * n - top)
+            width = min(128, 16 * len(blocks) - top)
             wm[:, top : top + width] = w_all[:, :width].astype(BF16)
     o2[...] = acc.T
 
@@ -103,7 +104,7 @@
     def _(jj):
         j = jj * 2
         rhs = jnp.concatenate(
-            [jnp.concatenate([us[p][e, j + f] for p, e, _, _ in blocks], 0) for f in range(2)], 1
+            [jnp.concatenate([us[p][e, j + f] for p, e, *_ in blocks], 0) for f in range(2)], 1
         )
         one = jnp.dot(wm[...], rhs, preferred_element_type=F32)
         two = o2[:, pl.ds(pl.multiple_of((jj >> 2) * 128, 128), 128)]
@@ -119,23 +120,24 @@
                     outs[r // 4][r % 4, rows, :] = value
 
 
-def ladder_call(group, meta, live, ts, us, v, wa, wb, prev=()):
+def ladder_call(pieces, meta, live, ts, us, v, wa, wb, prev=()):
     smem = pl.BlockSpec(memory_space=pltpu.SMEM)
     vmem = pl.BlockSpec(memory_space=pltpu.VMEM)
+    count = sum(piece[3] for piece in pieces)
     whole = jax.ShapeDtypeStruct((8, 512, 128), F32)
     half = jax.ShapeDtypeStruct((4, 512, 128), F32)
     masked = jax.ShapeDtypeStruct((2048, 512), BF16)
     return pl.pallas_call(
-        functools.partial(ladder_kernel, group),
+        functools.partial(ladder_kernel, pieces),
         out_shape=(half, half) if prev else (whole, masked),
-        in_specs=[smem, smem] + [vmem] * (13 + len(prev)),
+        in_specs=[smem, smem] + [vmem] * (2 * len(pieces) + 3 + len(prev)),
         out_specs=(vmem, vmem),
         scratch_shapes=[
             pltpu.VMEM((8, 512, 128), F32),
-            pltpu.VMEM((128, 64 * group[1]), BF16),
+            pltpu.VMEM((128, 16 * count), BF16),
             pltpu.VMEM((128, 512), F32),
         ],
-        cost_estimate=pl.CostEstimate(flops=400_000_000 * group[1], bytes_accessed=10_000_000, transcendentals=0),
+        cost_estimate=pl.CostEstimate(flops=100_000_000 * count, bytes_accessed=10_000_000, transcendentals=0),
         compiler_params=pltpu.CompilerParams(vmem_limit_bytes=24 << 20),
         name="ladder",
     )(meta, live, *ts, *us, v, wa, wb, *prev)
@@ -171,12 +173,13 @@
     )
 
 
-def over_y(group, cut):
-    down = lax.ppermute(group, "y", shift(4, 1))
-    up = lax.ppermute(group, "y", shift(4, -1))
+def beside(group):
+    return lax.ppermute(group, "y", shift(4, 1)), lax.ppermute(group, "y", shift(4, -1))
+
+
+def onward(down, up, cut):
     first = lax.ppermute(down[:cut], "y", shift(4, 1))
-    rest = lax.ppermute(up[cut:], "y", shift(4, -1))
-    return [group, down, first, rest, up]
+    return first, lax.ppermute(up[cut:], "y", shift(4, -1))
 
 
 def split_rows(ts):
@@ -202,19 +205,22 @@
     for k in range(1, 3):
         fwd, bwd = lax.ppermute(fwd, Z, z_shift(1)), lax.ppermute(bwd, Z, z_shift(-1))
         near = place(place(near, NEAR, z0, -k, fwd), NEAR, z0, k, bwd)
-    ts_near = over_y(near, CUTS[NEAR])
+    near_down, near_up = beside(near)
     xs = [both] + [lax.ppermute(both, "x", shift(4, -s)) for s in (1, 2, 3)]
     fwd, bwd = lax.ppermute(fwd, Z, z_shift(1)), lax.ppermute(bwd, Z, z_shift(-1))
     far = place(place(far, FAR, z0, 5, fwd), FAR, z0, 3, bwd)
     far = place(far, FAR, z0, 4, lax.ppermute(fwd, Z, z_shift(1)))
-    ts_far = over_y(far, CUTS[FAR])
-    *xs, ts_near[1], ts_near[4], occ_col = lax.optimization_barrier((*xs, ts_near[1], ts_near[4], occ_col))
+    far_down, far_up = beside(far)
+    *xs, near_down, near_up, occ_col = lax.optimization_barrier((*xs, near_down, near_up, occ_col))
     wa = jnp.stack(xs)
     wb = lax.ppermute(wa, "core", shift(2, 1))
-    *ts_near, wb = lax.optimization_barrier((*ts_near, wb))
-    first, masked = ladder_call(NEAR, meta, tile_live, ts_near, split_rows(ts_near), ladder_ints, wa, wb)
-    *ts_far, first = lax.optimization_barrier((*ts_far, first))
-    keep, away = ladder_call(FAR, meta, tile_live, ts_far, split_rows(ts_far), masked, wa, wb, (first,))
+    near_two = onward(near_down, near_up, CUTS[NEAR])
+    first = [near, near_down, near_up, far]
+    *first, wb = lax.optimization_barrier((*first, wb))
+    prev, masked = ladder_call(FIRST, meta, tile_live, first, split_rows(first), ladder_ints, wa, wb)
+    far_down, far_up, prev = lax.optimization_barrier((far_down, far_up, prev))
+    last = [far_down, far_up, *near_two, *onward(far_down, far_up, CUTS[FAR])]
+    keep, away = ladder_call(LAST, meta, tile_live, last, split_rows(last), masked, wa, wb, (prev,))
     got = lax.ppermute(away, "core", shift(2, 1))
     parts = [keep[0], got[0]]
     for s in (1, 2, 3):

time: 118 us -> 110 us (0.932)
  waiting for transfers between devices: 35 us -> 30.4 us
  local copies, waits for them, and re-layouts: 17.1 us -> 13.3 us
    ppermute x8, waiting for transfers between devices: 5.92 us -> 1.33 us  [the longest x2 1.31 us: onward(): first = lax.ppermute(down[:cut], 'y', shift(4, 1))]
    unnamed x35 -> x31, local copies, waits for them, and re-layouts: 7.54 us -> 4.92 us
  transfers between devices with their start and end apart: 24 -> 24, of which waited for: 9 -> 7; matrix products, arithmetic and copies ran while one was open for 12% -> 13% of each run, Pallas kernels for 7% -> 7%
where the time goes in v8:
time: 110 us; the launch traced here: 109 us
  starting transfers between devices  46.9 us (43%)
  waiting for transfers between devices  30.4 us (28%)
  Pallas kernels  16.1 us (15%)
  local copies, waits for them, and re-layouts  13.3 us (12%)
  other arithmetic  2.24 us (2%)
    pallas_call x2, Pallas kernels, ladder_call(): pl.pallas_call(functools.partial(ladder_kernel, pieces), out_shape=(half,...  13.6 us
    ppermute x3, waiting for transfers between devices, local(): parts.append(lax.ppermute(keep[s] + got[s], 'x', shift(4, s)))  11.7 us
    ppermute x3, waiting for transfers between devices, local(): lax.ppermute(fwd, Z, z_shift(1))  9.84 us
    all_to_all x1, starting transfers between devices, local(): both = lax.all_to_all(both, G, 0, 0, tiled=True)  8.23 us
    ppermute x3, starting transfers between devices, local(): lax.ppermute(bwd, Z, z_shift(-1))  7.35 us
    ppermute x1, starting transfers between devices, local(): got = lax.ppermute(away, 'core', shift(2, 1))  6.25 us
    ppermute x3, waiting for transfers between devices, local(): xs = [both] + [lax.ppermute(both, 'x', shift(4, -s)) for s in (1, 2, 3)]  5.25 us
    unnamed x31, local copies, waits for them, and re-layouts  4.92 us
  transfers between devices with their start and end apart: 24, of which 7 were waited for; matrix products, arithmetic and copies ran while one was open for 13% of the time, Pallas kernels for 7%

profile of v8, /device:TPU:1, one launch (start us, length us, event | category | flops | bytes accessed | tf_op | source)
XLA Modules:
  0.0 109.3 jit_solution(1972476576136802102)
XLA Ops:
  0.0 2.5 %collective-permute-start.3 = (bf16[32,2048]{1,0:T(8,128)(2,1)}, bf16[32,2048]{1,0:T(8,128)(2,1)S(1)}, u32[]{:S(2)}, u32[]{:S(2)}) collective-permute-start(bf16[32,2048]{1,0:T(8,128)(2,1)} %param.7), channel_id=1, source_target_pairs={{0,64},{64,128},{128,192},{192,32},{32,96},{96,160},{160,224},{224... | collective-permute-start | bytes 393224 | tf_op jit(solution)/shard_map/ppermute | solution.py:206
  2.5 4.0 %collective-permute-start.4 = (bf16[32,2048]{1,0:T(8,128)(2,1)}, bf16[32,2048]{1,0:T(8,128)(2,1)S(1)}, u32[]{:S(2)}, u32[]{:S(2)}) collective-permute-start(bf16[32,2048]{1,0:T(8,128)(2,1)} %param.7), channel_id=1, source_target_pairs={{0,224},{64,0},{128,64},{192,128},{32,192},{96,32},{160,96},{224,1... | collective-permute-start | bytes 393224 | tf_op jit(solution)/shard_map/ppermute | solution.py:206
  6.5 1.2 %pad_maximum_fusion.1 = bf16[2,4,32,4,128]{4,3,2,1,0:T(4,128)(2,1)S(1)} fusion(bf16[1,4,32,4,128]{4,3,2,1,0:T(4,128)(2,1)} %bitcast.103, bf16[1,4,32,4,128]{4,3,2,1,0:T(4,128)(2,1)} %bitcast.104), kind=kLoop, calls=%fused_computation.8 | loop fusion | flops 131072 | bytes 524288 | tf_op jit(solution)/shard_map/stack | solution.py:198
  8.4 8.2 %all-to-all-start = ((bf16[32,2,16,128]{3,2,1,0:T(8,128)(2,1)}), bf16[32,2,16,128]{3,2,1,0:T(8,128)(2,1)S(1)}, u32[]{:S(2)}, u32[]{:S(2)}) async-start(bf16[32,2,16,128]{3,2,1,0:T(8,128)(2,1)} %bitcast.9), calls=%async_computation | async-start | bytes 524288 | tf_op jit(solution)/shard_map/all_to_all | solution.py:200
  16.9 1.3 %collective-permute-start.5 = (bf16[32,2048]{1,0:T(8,128)(2,1)S(1)}, bf16[32,2048]{1,0:T(8,128)(2,1)S(1)}, u32[]{:S(2)}, u32[]{:S(2)}) collective-permute-start(bf16[32,2048]{1,0:T(8,128)(2,1)S(1)} %collective-permute-done.3), channel_id=1, source_target_pairs={{0,64},{64,128},{128,192},{192,32},{32,96},{96,160},{160,224},{224... | collective-permute-start | bytes 393224 | tf_op jit(solution)/shard_map/ppermute | solution.py:206
  18.2 1.4 %collective-permute-start.6 = (bf16[32,2048]{1,0:T(8,128)(2,1)S(1)}, bf16[32,2048]{1,0:T(8,128)(2,1)S(1)}, u32[]{:S(2)}, u32[]{:S(2)}) collective-permute-start(bf16[32,2048]{1,0:T(8,128)(2,1)S(1)} %collective-permute-done.4), channel_id=1, source_target_pairs={{0,224},{64,0},{128,64},{192,128},{32,192},{96,32},{160,96},{224,1... | collective-permute-start | bytes 393224 | tf_op jit(solution)/shard_map/ppermute | solution.py:206
  19.7 7.5 %collective-permute-done.5 = bf16[32,2048]{1,0:T(8,128)(2,1)S(1)} collective-permute-done((bf16[32,2048]{1,0:T(8,128)(2,1)S(1)}, bf16[32,2048]{1,0:T(8,128)(2,1)S(1)}, u32[]{:S(2)}, u32[]{:S(2)}) %collective-permute-start.5) | collective-permute-done | bytes 131104 | tf_op jit(solution)/shard_map/ppermute | solution.py:206
  27.3 1.7 %collective-permute-start.7 = (bf16[5,32,2048]{2,1,0:T(8,128)(2,1)S(1)}, bf16[5,32,2048]{2,1,0:T(8,128)(2,1)S(1)}, u32[]{:S(2)}, u32[]{:S(2)}) collective-permute-start(bf16[5,32,2048]{2,1,0:T(8,128)(2,1)S(1)} %bitcast_dynamic-update-slice_fusion.3.refs_0_), channel_id=1, source_target_pairs={{0,8},{8,16},{16,24},{24,0},{1,9},{9,17},{17,25},{25,1},{2,10},{10... | collective-permute-start | bytes 1966088 | tf_op jit(solution)/shard_map/ppermute | solution.py:177
  28.9 1.4 %collective-permute-start.8 = (bf16[5,32,2048]{2,1,0:T(8,128)(2,1)S(1)}, bf16[5,32,2048]{2,1,0:T(8,128)(2,1)S(1)}, u32[]{:S(2)}, u32[]{:S(2)}) collective-permute-start(bf16[5,32,2048]{2,1,0:T(8,128)(2,1)S(1)} %bitcast_dynamic-update-slice_fusion.3.refs_0_), channel_id=1, source_target_pairs={{0,24},{8,0},{16,8},{24,16},{1,25},{9,1},{17,9},{25,17},{2,26},{10... | collective-permute-start | bytes 1966088 | tf_op jit(solution)/shard_map/ppermute | solution.py:177
  30.3 2.5 %collective-permute-start = (bf16[32,2,16,128]{3,2,1,0:T(8,128)(2,1)S(1)}, bf16[32,2,16,128]{3,2,1,0:T(8,128)(2,1)S(1)}, u32[]{:S(2)}, u32[]{:S(2)}) collective-permute-start(bf16[32,2,16,128]{3,2,1,0:T(8,128)(2,1)S(1)} %all-to-all-done), channel_id=1, source_target_pairs={{0,6},{2,0},{4,2},{6,4},{1,7},{3,1},{5,3},{7,5},{8,14},{10,8},{12,... | collective-permute-start | bytes 786440 | tf_op jit(solution)/shard_map/ppermute | solution.py:209
  33.3 2.3 %collective-permute-done.9 = bf16[32,2048]{1,0:T(8,128)(2,1)} collective-permute-done((bf16[32,2048]{1,0:T(8,128)(2,1)S(1)}, bf16[32,2048]{1,0:T(8,128)(2,1)}, u32[]{:S(2)}, u32[]{:S(2)}) %collective-permute-start.9) | collective-permute-done | bytes 131104 | tf_op jit(solution)/shard_map/ppermute | solution.py:210
  35.7 1.2 %collective-permute-start.2 = (bf16[32,2,16,128]{3,2,1,0:T(8,128)(2,1)S(1)}, bf16[32,2,16,128]{3,2,1,0:T(8,128)(2,1)S(1)}, u32[]{:S(2)}, u32[]{:S(2)}) collective-permute-start(bf16[32,2,16,128]{3,2,1,0:T(8,128)(2,1)S(1)} %all-to-all-done), channel_id=1, source_target_pairs={{0,2},{2,4},{4,6},{6,0},{1,3},{3,5},{5,7},{7,1},{8,10},{10,12},{12... | collective-permute-start | bytes 786440 | tf_op jit(solution)/shard_map/ppermute | solution.py:209
  37.7 1.6 %bitcast_dynamic-update-slice_fusion.2 = bf16[3,32,2048]{2,1,0:T(8,128)(2,1)} fusion(bf16[3,32,2048]{2,1,0:T(8,128)(2,1)} %broadcast_in_dim.47, s32[]{:T(128)S(6)} %select_n.29, bf16[32,2048]{1,0:T(8,128)(2,1)} %collective-permute-done.9), kind=kLoop, calls=%fused_computation.12 | loop fusion | bytes 262148 | tf_op jit(solution)/shard_map/dynamic_update_slice | solution.py:191
  39.2 1.9 %collective-permute-start.10 = (bf16[32,2048]{1,0:T(8,128)(2,1)S(1)}, bf16[32,2048]{1,0:T(8,128)(2,1)S(1)}, u32[]{:S(2)}, u32[]{:S(2)}) collective-permute-start(bf16[32,2048]{1,0:T(8,128)(2,1)S(1)} %collective-permute-done.6), channel_id=1, source_target_pairs={{0,224},{64,0},{128,64},{192,128},{32,192},{96,32},{160,96},{224,1... | collective-permute-start | bytes 393224 | tf_op jit(solution)/shard_map/ppermute | solution.py:210
  41.2 5.2 %collective-permute-done.2 = bf16[32,2,16,128]{3,2,1,0:T(8,128)(2,1)S(1)} collective-permute-done((bf16[32,2,16,128]{3,2,1,0:T(8,128)(2,1)S(1)}, bf16[32,2,16,128]{3,2,1,0:T(8,128)(2,1)S(1)}, u32[]{:S(2)}, u32[]{:S(2)}) %collective-permute-start.2) | collective-permute-done | bytes 262176 | tf_op jit(solution)/shard_map/ppermute | solution.py:209
  47.5 2.3 %collective-permute-start.14 = (bf16[4,32,2,16,128]{4,3,2,1,0:T(8,128)(2,1)S(1)}, bf16[4,32,2,16,128]{4,3,2,1,0:T(8,128)(2,1)S(1)}, u32[]{:S(2)}, u32[]{:S(2)}) collective-permute-start(bf16[4,32,2,16,128]{4,3,2,1,0:T(8,128)(2,1)S(1)} %pad_maximum_fusion.refs_9_.refs_13_), channel_id=1, source_target_pairs={{0,1},{1,0},{2,3},{3,2},{4,5},{5,4},{6,7},{7,6},{8,9},{9,8},{10,11... | collective-permute-start | bytes 3145736 | tf_op jit(solution)/shard_map/ppermute | solution.py:216
  51.2 2.6 %collective-permute-start.13 = (bf16[3,32,2048]{2,1,0:T(8,128)(2,1)}, bf16[3,32,2048]{2,1,0:T(8,128)(2,1)}, u32[]{:S(2)}, u32[]{:S(2)}) collective-permute-start(bf16[3,32,2048]{2,1,0:T(8,128)(2,1)} %bitcast_dynamic-update-slice_fusion.refs_3_), channel_id=1, source_target_pairs={{0,24},{8,0},{16,8},{24,16},{1,25},{9,1},{17,9},{25,17},{2,26},{10... | collective-permute-start | bytes 1179656 | tf_op jit(solution)/shard_map/ppermute | solution.py:177
  54.0 1.0 slice.37
  55.1 2.7 %collective-permute-start.16 = (bf16[2,32,2048]{2,1,0:T(8,128)(2,1)S(1)}, bf16[2,32,2048]{2,1,0:T(8,128)(2,1)S(1)}, u32[]{:S(2)}, u32[]{:S(2)}) collective-permute-start(bf16[2,32,2048]{2,1,0:T(8,128)(2,1)S(1)} %slice.37), channel_id=1, source_target_pairs={{0,24},{8,0},{16,8},{24,16},{1,25},{9,1},{17,9},{25,17},{2,26},{10... | collective-permute-start | bytes 786440 | tf_op jit(solution)/shard_map/ppermute | solution.py:182
  58.2 1.3 %copy.16 = bf16[12,8,16,128]{3,2,1,0:T(8,128)(2,1)S(1)} copy(bf16[12,8,16,128]{3,1,2,0:T(8,128)(2,1)} %bitcast.42) | data formatting | bytes 786432
  59.5 7.5 %ladder.2 = (f32[8,512,128]{2,1,0:T(8,128)S(1)}, bf16[2048,512]{1,0:T(8,128)(2,1)S(1)}) custom-call(s32[6]{0:T(128)S(1)} %stack.51.meta, s32[16,4]{1,0:T(8,128)S(1)} %copy.11.live, bf16[5,32,2048]{2,1,0:T(8,128)(2,1)S(1)} %bitcast_dynamic-update-slice_fusion.3.refs_0_, bf16[5,32,2048]{2,1,0:T(8,128)(2,1)S(1)} %collective-permute-done.7.refs_1_, ...), custom_call_target="tpu_custom_call" | custom-call | flops 1800000000 | bytes 10000000 | tf_op jit(solution)/shard_map/ladder/pallas_call | solution.py:130
  69.0 1.5 %collective-permute-start.17 = (bf16[1,32,2048]{2,1,0:T(8,128)(2,1)S(1)}, bf16[1,32,2048]{2,1,0:T(8,128)(2,1)S(1)}, u32[]{:S(2)}, u32[]{:S(2)}) collective-permute-start(bf16[1,32,2048]{2,1,0:T(8,128)(2,1)S(1)} %slice.38), channel_id=1, source_target_pairs={{0,8},{8,16},{16,24},{24,0},{1,9},{9,17},{17,25},{25,1},{2,10},{10... | collective-permute-start | bytes 393224 | tf_op jit(solution)/shard_map/ppermute | solution.py:181
  70.6 1.1 copy.17
  71.7 1.1 copy.18
  72.7 1.3 %collective-permute-done.17.refs_4_ = bf16[1,32,2048]{2,1,0:T(8,128)(2,1)S(1)} collective-permute-done((bf16[1,32,2048]{2,1,0:T(8,128)(2,1)S(1)}, bf16[1,32,2048]{2,1,0:T(8,128)(2,1)S(1)}, u32[]{:S(2)}, u32[]{:S(2)}) %collective-permute-start.17) | collective-permute-done | bytes 131104 | tf_op jit(solution)/shard_map/ppermute | solution.py:181
  74.1 6.2 %ladder.3 = (f32[4,512,128]{2,1,0:T(8,128)S(1)}, f32[4,512,128]{2,1,0:T(8,128)S(1)}) custom-call(s32[6]{0:T(128)S(1)} %stack.51.meta, s32[16,4]{1,0:T(8,128)S(1)} %copy.11.live, bf16[3,32,2048]{2,1,0:T(8,128)(2,1)} %collective-permute-done.12.refs_0_, bf16[3,32,2048]{2,1,0:T(8,128)(2,1)} %collective-permute-done.13.refs_1_, ...), custom_call_target="tpu_custom_call" | custom-call | flops 1400000000 | bytes 10000000 | tf_op jit(solution)/shard_map/ladder/pallas_call | solution.py:130
  80.3 6.3 %collective-permute-start.19 = (f32[4,512,128]{2,1,0:T(8,128)S(1)}, f32[4,512,128]{2,1,0:T(8,128)S(1)}, u32[]{:S(2)}, u32[]{:S(2)}) collective-permute-start(f32[4,512,128]{2,1,0:T(8,128)S(1)} %get-tuple-element.42), channel_id=1, source_target_pairs={{0,1},{1,0},{2,3},{3,2},{4,5},{5,4},{6,7},{7,6},{8,9},{9,8},{10,11... | collective-permute-start | bytes 3145736 | tf_op jit(solution)/shard_map/ppermute | solution.py:224
  86.6 2.3 %collective-permute-done.19 = f32[4,512,128]{2,1,0:T(8,128)S(1)} collective-permute-done((f32[4,512,128]{2,1,0:T(8,128)S(1)}, f32[4,512,128]{2,1,0:T(8,128)S(1)}, u32[]{:S(2)}, u32[]{:S(2)}) %collective-permute-start.19) | collective-permute-done | bytes 1048608 | tf_op jit(solution)/shard_map/ppermute | solution.py:224
  89.8 4.6 %collective-permute-start.21 = (f32[512,128]{1,0:T(8,128)S(1)}, f32[512,128]{1,0:T(8,128)S(1)}, u32[]{:S(2)}, u32[]{:S(2)}) collective-permute-start(f32[512,128]{1,0:T(8,128)S(1)} %get-tuple-element.44), channel_id=1, source_target_pairs={{0,4},{2,6},{4,0},{6,2},{1,5},{3,7},{5,1},{7,3},{8,12},{10,14},{12... | collective-permute-start | bytes 786440 | tf_op jit(solution)/shard_map/ppermute | solution.py:227
  94.4 5.2 %collective-permute-done.20.p2 = f32[512,128]{1,0:T(8,128)S(1)} collective-permute-done((f32[512,128]{1,0:T(8,128)S(1)}, f32[512,128]{1,0:T(8,128)S(1)}, u32[]{:S(2)}, u32[]{:S(2)}) %collective-permute-start.20) | collective-permute-done | bytes 262176 | tf_op jit(solution)/shard_map/ppermute | solution.py:227
  99.6 6.5 %collective-permute-done.21.p3 = f32[512,128]{1,0:T(8,128)S(1)} collective-permute-done((f32[512,128]{1,0:T(8,128)S(1)}, f32[512,128]{1,0:T(8,128)S(1)}, u32[]{:S(2)}, u32[]{:S(2)}) %collective-permute-start.21) | collective-permute-done | bytes 262176 | tf_op jit(solution)/shard_map/ppermute | solution.py:227
  106.8 2.4 %finish.1 = bf16[128,512]{1,0:T(8,128)(2,1)} custom-call(s32[6]{0:T(128)} %copy-done.3, f32[32]{0:T(128)} %occ.1, f32[128]{0:T(128)} %vir.1, f32[32,128]{1,0:T(8,128)} %broadcast_in_dim.45.occ_col, f32[1,128]{1,0:T(1,128)} %bitcast.105, f32[512,128]{1,0:T(8,128)} %get-tuple-element.46.p0, f32[512,128]{1,0:T(8,128)} %get-tuple-element.47.p1, ...), custom_call_target="tpu_custom_call" | custom-call | flops 400000 | bytes 1500000 | tf_op jit(solution)/shard_map/finish/pallas_call | solution.py:159
  (70 shorter events, 9.3 us)
Async XLA Ops:
  0.0 16.8 %copy-start.7 = (bf16[32,2048]{1,0:T(8,128)(2,1)S(1)}, bf16[32,2048]{1,0:T(8,128)(2,1)}, u32[]{:S(2)}) copy-start(bf16[32,2048]{1,0:T(8,128)(2,1)} %param.7) | copy-start | bytes 393220
  0.0 16.9 %collective-permute-start.3 = (bf16[32,2048]{1,0:T(8,128)(2,1)}, bf16[32,2048]{1,0:T(8,128)(2,1)S(1)}, u32[]{:S(2)}, u32[]{:S(2)}) collective-permute-start(bf16[32,2048]{1,0:T(8,128)(2,1)} %param.7), channel_id=1, source_target_pairs={{0,64},{64,128},{128,192},{192,32},{32,96},{96,160},{160,224},{224... | collective-permute-start | bytes 393224 | tf_op jit(solution)/shard_map/ppermute | solution.py:206
  2.5 15.7 %collective-permute-start.4 = (bf16[32,2048]{1,0:T(8,128)(2,1)}, bf16[32,2048]{1,0:T(8,128)(2,1)S(1)}, u32[]{:S(2)}, u32[]{:S(2)}) collective-permute-start(bf16[32,2048]{1,0:T(8,128)(2,1)} %param.7), channel_id=1, source_target_pairs={{0,224},{64,0},{128,64},{192,128},{32,192},{96,32},{160,96},{224,1... | collective-permute-start | bytes 393224 | tf_op jit(solution)/shard_map/ppermute | solution.py:206
  6.5 40.0 %copy-start.8 = (f32[32]{0:T(128)S(1)}, f32[32]{0:T(128)}, u32[]{:S(2)}) copy-start(f32[32]{0:T(128)} %occ.1) | copy-start | bytes 388
  8.4 21.9 %all-to-all-start = ((bf16[32,2,16,128]{3,2,1,0:T(8,128)(2,1)}), bf16[32,2,16,128]{3,2,1,0:T(8,128)(2,1)S(1)}, u32[]{:S(2)}, u32[]{:S(2)}) async-start(bf16[32,2,16,128]{3,2,1,0:T(8,128)(2,1)} %bitcast.9), calls=%async_computation | async-start | bytes 524288 | tf_op jit(solution)/shard_map/all_to_all | solution.py:200
  16.9 10.3 %collective-permute-start.5 = (bf16[32,2048]{1,0:T(8,128)(2,1)S(1)}, bf16[32,2048]{1,0:T(8,128)(2,1)S(1)}, u32[]{:S(2)}, u32[]{:S(2)}) collective-permute-start(bf16[32,2048]{1,0:T(8,128)(2,1)S(1)} %collective-permute-done.3), channel_id=1, source_target_pairs={{0,64},{64,128},{128,192},{192,32},{32,96},{96,160},{160,224},{224... | collective-permute-start | bytes 393224 | tf_op jit(solution)/shard_map/ppermute | solution.py:206
  18.2 9.0 %collective-permute-start.6 = (bf16[32,2048]{1,0:T(8,128)(2,1)S(1)}, bf16[32,2048]{1,0:T(8,128)(2,1)S(1)}, u32[]{:S(2)}, u32[]{:S(2)}) collective-permute-start(bf16[32,2048]{1,0:T(8,128)(2,1)S(1)} %collective-permute-done.4), channel_id=1, source_target_pairs={{0,224},{64,0},{128,64},{192,128},{32,192},{96,32},{160,96},{224,1... | collective-permute-start | bytes 393224 | tf_op jit(solution)/shard_map/ppermute | solution.py:206
  19.6 34.1 %copy-start.9 = (s32[16,4]{0,1:T(4,128)S(1)}, s32[16,4]{0,1:T(4,128)}, u32[]{:S(2)}) copy-start(s32[16,4]{0,1:T(4,128)} %param.9) | copy-start | bytes 772
  27.3 19.2 %collective-permute-start.7 = (bf16[5,32,2048]{2,1,0:T(8,128)(2,1)S(1)}, bf16[5,32,2048]{2,1,0:T(8,128)(2,1)S(1)}, u32[]{:S(2)}, u32[]{:S(2)}) collective-permute-start(bf16[5,32,2048]{2,1,0:T(8,128)(2,1)S(1)} %bitcast_dynamic-update-slice_fusion.3.refs_0_), channel_id=1, source_target_pairs={{0,8},{8,16},{16,24},{24,0},{1,9},{9,17},{17,25},{25,1},{2,10},{10... | collective-permute-start | bytes 1966088 | tf_op jit(solution)/shard_map/ppermute | solution.py:177
  28.9 17.5 %collective-permute-start.8 = (bf16[5,32,2048]{2,1,0:T(8,128)(2,1)S(1)}, bf16[5,32,2048]{2,1,0:T(8,128)(2,1)S(1)}, u32[]{:S(2)}, u32[]{:S(2)}) collective-permute-start(bf16[5,32,2048]{2,1,0:T(8,128)(2,1)S(1)} %bitcast_dynamic-update-slice_fusion.3.refs_0_), channel_id=1, source_target_pairs={{0,24},{8,0},{16,8},{24,16},{1,25},{9,1},{17,9},{25,17},{2,26},{10... | collective-permute-start | bytes 1966088 | tf_op jit(solution)/shard_map/ppermute | solution.py:177
  30.3 5.3 %collective-permute-start.9 = (bf16[32,2048]{1,0:T(8,128)(2,1)S(1)}, bf16[32,2048]{1,0:T(8,128)(2,1)}, u32[]{:S(2)}, u32[]{:S(2)}) collective-permute-start(bf16[32,2048]{1,0:T(8,128)(2,1)S(1)} %collective-permute-done.5), channel_id=1, source_target_pairs={{0,64},{64,128},{128,192},{192,32},{32,96},{96,160},{160,224},{224... | collective-permute-start | bytes 393224 | tf_op jit(solution)/shard_map/ppermute | solution.py:210
  30.3 8.9 %collective-permute-start = (bf16[32,2,16,128]{3,2,1,0:T(8,128)(2,1)S(1)}, bf16[32,2,16,128]{3,2,1,0:T(8,128)(2,1)S(1)}, u32[]{:S(2)}, u32[]{:S(2)}) collective-permute-start(bf16[32,2,16,128]{3,2,1,0:T(8,128)(2,1)S(1)} %all-to-all-done), channel_id=1, source_target_pairs={{0,6},{2,0},{4,2},{6,4},{1,7},{3,1},{5,3},{7,5},{8,14},{10,8},{12,... | collective-permute-start | bytes 786440 | tf_op jit(solution)/shard_map/ppermute | solution.py:209
  32.8 8.3 %collective-permute-start.1 = (bf16[32,2,16,128]{3,2,1,0:T(8,128)(2,1)S(1)}, bf16[32,2,16,128]{3,2,1,0:T(8,128)(2,1)S(1)}, u32[]{:S(2)}, u32[]{:S(2)}) collective-permute-start(bf16[32,2,16,128]{3,2,1,0:T(8,128)(2,1)S(1)} %all-to-all-done), channel_id=1, source_target_pairs={{0,4},{2,6},{4,0},{6,2},{1,5},{3,7},{5,1},{7,3},{8,12},{10,14},{12... | collective-permute-start | bytes 786440 | tf_op jit(solution)/shard_map/ppermute | solution.py:209
  35.7 10.8 %collective-permute-start.2 = (bf16[32,2,16,128]{3,2,1,0:T(8,128)(2,1)S(1)}, bf16[32,2,16,128]{3,2,1,0:T(8,128)(2,1)S(1)}, u32[]{:S(2)}, u32[]{:S(2)}) collective-permute-start(bf16[32,2,16,128]{3,2,1,0:T(8,128)(2,1)S(1)} %all-to-all-done), channel_id=1, source_target_pairs={{0,2},{2,4},{4,6},{6,0},{1,3},{3,5},{5,7},{7,1},{8,10},{10,12},{12... | collective-permute-start | bytes 786440 | tf_op jit(solution)/shard_map/ppermute | solution.py:209
  39.2 10.5 %collective-permute-start.10 = (bf16[32,2048]{1,0:T(8,128)(2,1)S(1)}, bf16[32,2048]{1,0:T(8,128)(2,1)S(1)}, u32[]{:S(2)}, u32[]{:S(2)}) collective-permute-start(bf16[32,2048]{1,0:T(8,128)(2,1)S(1)} %collective-permute-done.6), channel_id=1, source_target_pairs={{0,224},{64,0},{128,64},{192,128},{32,192},{96,32},{160,96},{224,1... | collective-permute-start | bytes 393224 | tf_op jit(solution)/shard_map/ppermute | solution.py:210
  41.1 9.3 %collective-permute-start.11 = (bf16[32,2048]{1,0:T(8,128)(2,1)}, bf16[32,2048]{1,0:T(8,128)(2,1)S(1)}, u32[]{:S(2)}, u32[]{:S(2)}) collective-permute-start(bf16[32,2048]{1,0:T(8,128)(2,1)} %collective-permute-done.9), channel_id=1, source_target_pairs={{0,64},{64,128},{128,192},{192,32},{32,96},{96,160},{160,224},{224... | collective-permute-start | bytes 393224 | tf_op jit(solution)/shard_map/ppermute | solution.py:212
  46.5 0.8 copy-start
  47.5 10.3 %collective-permute-start.14 = (bf16[4,32,2,16,128]{4,3,2,1,0:T(8,128)(2,1)S(1)}, bf16[4,32,2,16,128]{4,3,2,1,0:T(8,128)(2,1)S(1)}, u32[]{:S(2)}, u32[]{:S(2)}) collective-permute-start(bf16[4,32,2,16,128]{4,3,2,1,0:T(8,128)(2,1)S(1)} %pad_maximum_fusion.refs_9_.refs_13_), channel_id=1, source_target_pairs={{0,1},{1,0},{2,3},{3,2},{4,5},{5,4},{6,7},{7,6},{8,9},{9,8},{10,11... | collective-permute-start | bytes 3145736 | tf_op jit(solution)/shard_map/ppermute | solution.py:216
  51.1 15.9 %collective-permute-start.12 = (bf16[3,32,2048]{2,1,0:T(8,128)(2,1)}, bf16[3,32,2048]{2,1,0:T(8,128)(2,1)}, u32[]{:S(2)}, u32[]{:S(2)}) collective-permute-start(bf16[3,32,2048]{2,1,0:T(8,128)(2,1)} %bitcast_dynamic-update-slice_fusion.refs_3_), channel_id=1, source_target_pairs={{0,8},{8,16},{16,24},{24,0},{1,9},{9,17},{17,25},{25,1},{2,10},{10... | collective-permute-start | bytes 1179656 | tf_op jit(solution)/shard_map/ppermute | solution.py:177
  51.2 15.8 %collective-permute-start.13 = (bf16[3,32,2048]{2,1,0:T(8,128)(2,1)}, bf16[3,32,2048]{2,1,0:T(8,128)(2,1)}, u32[]{:S(2)}, u32[]{:S(2)}) collective-permute-start(bf16[3,32,2048]{2,1,0:T(8,128)(2,1)} %bitcast_dynamic-update-slice_fusion.refs_3_), channel_id=1, source_target_pairs={{0,24},{8,0},{16,8},{24,16},{1,25},{9,1},{17,9},{25,17},{2,26},{10... | collective-permute-start | bytes 1179656 | tf_op jit(solution)/shard_map/ppermute | solution.py:177
  53.9 20.2 %copy-start.3 = (s32[6]{0:T(128)}, s32[6]{0:T(128)S(1)}, u32[]{:S(2)}) copy-start(s32[6]{0:T(128)S(1)} %stack.51.meta) | copy-start | bytes 76
  53.9 4.1 %copy-start.1 = (bf16[5,32,2048]{2,1,0:T(8,128)(2,1)S(1)}, bf16[5,32,2048]{2,1,0:T(8,128)(2,1)}, u32[]{:S(2)}) copy-start(bf16[5,32,2048]{2,1,0:T(8,128)(2,1)} %copy-done) | copy-start | bytes 1966084
  54.0 16.6 %collective-permute-start.15 = (bf16[3,32,2048]{2,1,0:T(8,128)(2,1)S(1)}, bf16[3,32,2048]{2,1,0:T(8,128)(2,1)S(1)}, u32[]{:S(2)}, u32[]{:S(2)}) collective-permute-start(bf16[3,32,2048]{2,1,0:T(8,128)(2,1)S(1)} %slice.36), channel_id=1, source_target_pairs={{0,8},{8,16},{16,24},{24,0},{1,9},{9,17},{17,25},{25,1},{2,10},{10... | collective-permute-start | bytes 1179656 | tf_op jit(solution)/shard_map/ppermute | solution.py:181
  55.1 15.4 %collective-permute-start.16 = (bf16[2,32,2048]{2,1,0:T(8,128)(2,1)S(1)}, bf16[2,32,2048]{2,1,0:T(8,128)(2,1)S(1)}, u32[]{:S(2)}, u32[]{:S(2)}) collective-permute-start(bf16[2,32,2048]{2,1,0:T(8,128)(2,1)S(1)} %slice.37), channel_id=1, source_target_pairs={{0,24},{8,0},{16,8},{24,16},{1,25},{9,1},{17,9},{25,17},{2,26},{10... | collective-permute-start | bytes 786440 | tf_op jit(solution)/shard_map/ppermute | solution.py:182
  57.8 1.7 %copy-start.2 = (bf16[2048,512]{1,0:T(8,128)(2,1)S(1)}, bf16[2048,512]{1,0:T(8,128)(2,1)}, u32[]{:S(2)}) copy-start(bf16[2048,512]{1,0:T(8,128)(2,1)} %refs_8_.1) | copy-start | bytes 6291460
  67.9 6.2 %collective-permute-start.18 = (bf16[2,32,2048]{2,1,0:T(8,128)(2,1)S(1)}, bf16[2,32,2048]{2,1,0:T(8,128)(2,1)S(1)}, u32[]{:S(2)}, u32[]{:S(2)}) collective-permute-start(bf16[2,32,2048]{2,1,0:T(8,128)(2,1)S(1)} %slice.39), channel_id=1, source_target_pairs={{0,24},{8,0},{16,8},{24,16},{1,25},{9,1},{17,9},{25,17},{2,26},{10... | collective-permute-start | bytes 786440 | tf_op jit(solution)/shard_map/ppermute | solution.py:182
  69.0 5.1 %collective-permute-start.17 = (bf16[1,32,2048]{2,1,0:T(8,128)(2,1)S(1)}, bf16[1,32,2048]{2,1,0:T(8,128)(2,1)S(1)}, u32[]{:S(2)}, u32[]{:S(2)}) collective-permute-start(bf16[1,32,2048]{2,1,0:T(8,128)(2,1)S(1)} %slice.38), channel_id=1, source_target_pairs={{0,8},{8,16},{16,24},{24,0},{1,9},{9,17},{17,25},{25,1},{2,10},{10... | collective-permute-start | bytes 393224 | tf_op jit(solution)/shard_map/ppermute | solution.py:181
  80.3 8.5 %collective-permute-start.19 = (f32[4,512,128]{2,1,0:T(8,128)S(1)}, f32[4,512,128]{2,1,0:T(8,128)S(1)}, u32[]{:S(2)}, u32[]{:S(2)}) collective-permute-start(f32[4,512,128]{2,1,0:T(8,128)S(1)} %get-tuple-element.42), channel_id=1, source_target_pairs={{0,1},{1,0},{2,3},{3,2},{4,5},{5,4},{6,7},{7,6},{8,9},{9,8},{10,11... | collective-permute-start | bytes 3145736 | tf_op jit(solution)/shard_map/ppermute | solution.py:224
  89.8 9.8 %collective-permute-start.20 = (f32[512,128]{1,0:T(8,128)S(1)}, f32[512,128]{1,0:T(8,128)S(1)}, u32[]{:S(2)}, u32[]{:S(2)}) collective-permute-start(f32[512,128]{1,0:T(8,128)S(1)} %get-tuple-element.45), channel_id=1, source_target_pairs={{0,2},{2,4},{4,6},{6,0},{1,3},{3,5},{5,7},{7,1},{8,10},{10,12},{12... | collective-permute-start | bytes 786440 | tf_op jit(solution)/shard_map/ppermute | solution.py:227
  89.8 16.3 %collective-permute-start.21 = (f32[512,128]{1,0:T(8,128)S(1)}, f32[512,128]{1,0:T(8,128)S(1)}, u32[]{:S(2)}, u32[]{:S(2)}) collective-permute-start(f32[512,128]{1,0:T(8,128)S(1)} %get-tuple-element.44), channel_id=1, source_target_pairs={{0,4},{2,6},{4,0},{6,2},{1,5},{3,7},{5,1},{7,3},{8,12},{10,14},{12... | collective-permute-start | bytes 786440 | tf_op jit(solution)/shard_map/ppermute | solution.py:227
  94.4 11.7 %collective-permute-start.22 = (f32[512,128]{1,0:T(8,128)S(1)}, f32[512,128]{1,0:T(8,128)S(1)}, u32[]{:S(2)}, u32[]{:S(2)}) collective-permute-start(f32[512,128]{1,0:T(8,128)S(1)} %get-tuple-element.43), channel_id=1, source_target_pairs={{0,6},{2,0},{4,2},{6,4},{1,7},{3,1},{5,3},{7,5},{8,14},{10,8},{12,... | collective-permute-start | bytes 786440 | tf_op jit(solution)/shard_map/ppermute | solution.py:227
  99.6 6.5 %copy-start.4 = (f32[512,128]{1,0:T(8,128)}, f32[512,128]{1,0:T(8,128)S(1)}, u32[]{:S(2)}) copy-start(f32[512,128]{1,0:T(8,128)S(1)} %collective-permute-done.20.p2) | copy-start | bytes 786436
  (2 other events, 1.5 us)

commit v9 on v8

--- a/solution.py
+++ b/solution.py
@@ -10,6 +10,7 @@
 G = ("zl", "zh", "y")
 C = ("x", "core")
 Z = ("zl", "zh")
+UNROLL = 8
 F32 = jnp.float32
 BF16 = jnp.bfloat16
 
@@ -51,7 +52,7 @@
 
     if pieces is FIRST:
 
-        @pl.loop(0, 16)
+        @pl.loop(0, 16, unroll=4)
         def _(kt):
             rows = pl.ds(pl.multiple_of(kt * 128, 128), 128)
             for c in range(4):
@@ -61,7 +62,7 @@
 
     @pl.loop(0, 8)
     def _(r):
-        ladder[r] = jnp.zeros((512, 128), F32) if prev is None else prev[r]
+        ladder[r] = jnp.zeros((512, 128), F32)
 
     half = len(blocks) // 2
     for part_of in (blocks[:half], blocks[half:]):
@@ -70,7 +71,7 @@
         for m, (_, _, y, _, spot) in enumerate(part_of):
             for a in range(4):
                 rows = pl.ds(y * 4 + a, 32, stride=16)
-                ladder[spot, rows, :] += part[m * 32 : m * 32 + 32, a * 128 : a * 128 + 128]
+                ladder[spot, rows, :] = part[m * 32 : m * 32 + 32, a * 128 : a * 128 + 128]
 
     lane = lax.broadcasted_iota(jnp.int32, (128, 128), 1)
 
@@ -100,7 +101,7 @@
 
     own = (lane >> 4) == col
 
-    @pl.loop(0, 16)
+    @pl.loop(0, 16, unroll=UNROLL)
     def _(jj):
         j = jj * 2
         rhs = jnp.concatenate(
@@ -117,7 +118,7 @@
                 if prev is None:
                     outs[0][r, rows, :] = value
                 else:
-                    outs[r // 4][r % 4, rows, :] = value
+                    outs[r // 4][r % 4, rows, :] = value + prev[r, rows, :]
 
 
 def ladder_call(pieces, meta, live, ts, us, v, wa, wb, prev=()):
@@ -143,31 +144,35 @@
     )(meta, live, *ts, *us, v, wa, wb, *prev)
 
 
-def finish_kernel(meta, occ, vir, occ_col, vir_row, p0, p1, p2, p3, p4, out):
+def finish_kernel(meta, occ, vir, vir_row, p0, p1, p2, p3, p4, out, total):
     col, g = meta[3], meta[4]
+    row = lax.broadcasted_iota(jnp.int32, (32, 128), 0)
+    occ_col = jnp.zeros((32, 128), F32)
+    for j in range(32):
+        occ_col = jnp.where(row == j, occ[j], occ_col)
+    total[...] = ((p0[...] + p1[...]) + p2[...]) + (p3[...] + p4[...])
     for il in range(4):
         for a in range(4):
-            rows = pl.ds(il * 4 + a, 32, stride=16)
-            total = ((p0[rows, :] + p1[rows, :]) + p2[rows, :]) + (p3[rows, :] + p4[rows, :])
-            denom = ((vir[g * 4 + a] + vir_row[...]) - occ[col * 4 + il]) - occ_col[...]
-            out[il * 32 : il * 32 + 32, a * 128 : a * 128 + 128] = (total / denom).astype(BF16)
-
-
-def finish_call(meta, occ_col, eps_occ, eps_vir, parts):
+            value = total[pl.ds(il * 4 + a, 32, stride=16), :]
+            denom = ((vir[g * 4 + a] + vir_row[...]) - occ[col * 4 + il]) - occ_col
+            out[il * 32 : il * 32 + 32, a * 128 : a * 128 + 128] = (value / denom).astype(BF16)
+
+
+def finish_call(meta, eps_occ, eps_vir, parts):
     smem = pl.BlockSpec(memory_space=pltpu.SMEM)
     vmem = pl.BlockSpec(memory_space=pltpu.VMEM)
     return pl.pallas_call(
         finish_kernel,
         out_shape=jax.ShapeDtypeStruct((128, 512), BF16),
-        in_specs=[smem] * 3 + [vmem] * 7,
+        in_specs=[smem] * 3 + [vmem] * 6,
         out_specs=vmem,
+        scratch_shapes=[pltpu.VMEM((512, 128), F32)],
         cost_estimate=pl.CostEstimate(flops=400_000, bytes_accessed=1_500_000, transcendentals=0),
         name="finish",
     )(
         meta,
         eps_occ,
         eps_vir,
-        occ_col,
         eps_vir[None, :],
         *parts,
     )
@@ -198,7 +203,6 @@
     both = jnp.stack([cycle_direct, cycle_exchange]).reshape(2, 4, 32, 4, 128)
     both = both.transpose(2, 0, 1, 3, 4).reshape(32, 2, 16, 128)
     both = lax.all_to_all(both, G, 0, 0, tiled=True)
-    occ_col = jnp.broadcast_to(eps_occ[:, None], (32, 128))
     near = place(jnp.zeros((5, 32, 2048), BF16), NEAR, z0, 0, amplitudes)
     far = jnp.zeros((3, 32, 2048), BF16)
     fwd = bwd = amplitudes
@@ -211,7 +215,7 @@
     far = place(place(far, FAR, z0, 5, fwd), FAR, z0, 3, bwd)
     far = place(far, FAR, z0, 4, lax.ppermute(fwd, Z, z_shift(1)))
     far_down, far_up = beside(far)
-    *xs, near_down, near_up, occ_col = lax.optimization_barrier((*xs, near_down, near_up, occ_col))
+    *xs, near_down, near_up = lax.optimization_barrier((*xs, near_down, near_up))
     wa = jnp.stack(xs)
     wb = lax.ppermute(wa, "core", shift(2, 1))
     near_two = onward(near_down, near_up, CUTS[NEAR])
@@ -225,7 +229,7 @@
     parts = [keep[0], got[0]]
     for s in (1, 2, 3):
         parts.append(lax.ppermute(keep[s] + got[s], "x", shift(4, s)))
-    return finish_call(meta, occ_col, eps_occ, eps_vir, parts)
+    return finish_call(meta, eps_occ, eps_vir, parts)
 
 
 def solution(mesh):

time: 110 us -> 103 us (0.936)
  Pallas kernels: 16.1 us -> 11.1 us
  waiting for transfers between devices: 30.4 us -> 29.1 us
    pallas_call x2, Pallas kernels: 13.6 us -> 9.01 us  [ladder_call(): pl.pallas_call(functools.partial(ladder_kernel, pieces), out_shape=(half,...]
    ppermute x3, waiting for transfers between devices: 5.25 us -> 3.46 us  [local(): xs = [both] + [lax.ppermute(both, 'x', shift(4, -s)) for s in (1, 2, 3)]]
    ppermute x2, waiting for transfers between devices: 1.31 us -> 3.07 us  [onward(): first = lax.ppermute(down[:cut], 'y', shift(4, 1))]
    ppermute x3, starting transfers between devices: 7.35 us -> 5.78 us  [local(): lax.ppermute(bwd, Z, z_shift(-1))]
    ppermute x1, starting transfers between devices: 6.25 us -> 4.84 us  [local(): got = lax.ppermute(away, 'core', shift(2, 1))]
    ppermute x3, starting transfers between devices: 4.21 us -> 5.54 us  [local(): xs = [both] + [lax.ppermute(both, 'x', shift(4, -s)) for s in (1, 2, 3)]]
    ppermute x3, waiting for transfers between devices: 11.7 us -> 10.5 us  [local(): parts.append(lax.ppermute(keep[s] + got[s], 'x', shift(4, s)))]
    ppermute x1, starting transfers between devices: 0.09 us -> 1.21 us  [local(): far = place(far, FAR, z0, 4, lax.ppermute(fwd, Z, z_shift(1)))]
  transfers between devices with their start and end apart: 24 -> 24, of which waited for: 7 -> 9; matrix products, arithmetic and copies ran while one was open for 13% -> 13% of each run, Pallas kernels for 7% -> 5%
where the time goes in v9:
time: 103 us; the launch traced here: 102 us
  starting transfers between devices  46.3 us (45%)
  waiting for transfers between devices  29.1 us (28%)
  local copies, waits for them, and re-layouts  13.3 us (13%)
  Pallas kernels  11.1 us (11%)
  other arithmetic  2.23 us (2%)
    ppermute x3, waiting for transfers between devices, local(): parts.append(lax.ppermute(keep[s] + got[s], 'x', shift(4, s)))  10.5 us
    ppermute x3, waiting for transfers between devices, local(): lax.ppermute(fwd, Z, z_shift(1))  9.79 us
    pallas_call x2, Pallas kernels, ladder_call(): pl.pallas_call(functools.partial(ladder_kernel, pieces), out_shape=(half,...  9.01 us
    all_to_all x1, starting transfers between devices, local(): both = lax.all_to_all(both, G, 0, 0, tiled=True)  8.23 us
    ppermute x3, starting transfers between devices, local(): lax.ppermute(bwd, Z, z_shift(-1))  5.78 us
    unnamed x29, local copies, waits for them, and re-layouts  5.6 us
    ppermute x3, starting transfers between devices, local(): xs = [both] + [lax.ppermute(both, 'x', shift(4, -s)) for s in (1, 2, 3)]  5.54 us
    ppermute x1, starting transfers between devices, local(): got = lax.ppermute(away, 'core', shift(2, 1))  4.84 us
  transfers between devices with their start and end apart: 24, of which 9 were waited for; matrix products, arithmetic and copies ran while one was open for 13% of the time, Pallas kernels for 5%

profile of v9, /device:TPU:1, one launch (start us, length us, event | category | flops | bytes accessed | tf_op | source)
XLA Modules:
  0.0 102.4 jit_solution(9772009258961121857)
XLA Ops:
  0.0 2.5 %collective-permute-start = (bf16[32,2048]{1,0:T(8,128)(2,1)}, bf16[32,2048]{1,0:T(8,128)(2,1)S(1)}, u32[]{:S(2)}, u32[]{:S(2)}) collective-permute-start(bf16[32,2048]{1,0:T(8,128)(2,1)} %param.7), channel_id=1, source_target_pairs={{0,64},{64,128},{128,192},{192,32},{32,96},{96,160},{160,224},{224... | collective-permute-start | bytes 393224 | tf_op jit(solution)/shard_map/ppermute | solution.py:210
  2.5 4.0 %collective-permute-start.3 = (bf16[32,2048]{1,0:T(8,128)(2,1)}, bf16[32,2048]{1,0:T(8,128)(2,1)S(1)}, u32[]{:S(2)}, u32[]{:S(2)}) collective-permute-start(bf16[32,2048]{1,0:T(8,128)(2,1)} %param.7), channel_id=1, source_target_pairs={{0,224},{64,0},{128,64},{192,128},{32,192},{96,32},{160,96},{224,1... | collective-permute-start | bytes 393224 | tf_op jit(solution)/shard_map/ppermute | solution.py:210
  6.5 1.2 %pad_maximum_fusion.1 = bf16[2,4,32,4,128]{4,3,2,1,0:T(4,128)(2,1)S(1)} fusion(bf16[1,4,32,4,128]{4,3,2,1,0:T(4,128)(2,1)} %bitcast.103, bf16[1,4,32,4,128]{4,3,2,1,0:T(4,128)(2,1)} %bitcast.104), kind=kLoop, calls=%fused_computation.8 | loop fusion | flops 131072 | bytes 524288 | tf_op jit(solution)/shard_map/stack | solution.py:203
  8.4 8.2 %all-to-all-start = ((bf16[32,2,16,128]{3,2,1,0:T(8,128)(2,1)}), bf16[32,2,16,128]{3,2,1,0:T(8,128)(2,1)S(1)}, u32[]{:S(2)}, u32[]{:S(2)}) async-start(bf16[32,2,16,128]{3,2,1,0:T(8,128)(2,1)} %bitcast.18), calls=%async_computation | async-start | bytes 524288 | tf_op jit(solution)/shard_map/all_to_all | solution.py:205
  16.9 1.3 %collective-permute-start.1 = (bf16[32,2048]{1,0:T(8,128)(2,1)S(1)}, bf16[32,2048]{1,0:T(8,128)(2,1)S(1)}, u32[]{:S(2)}, u32[]{:S(2)}) collective-permute-start(bf16[32,2048]{1,0:T(8,128)(2,1)S(1)} %collective-permute-done), channel_id=1, source_target_pairs={{0,64},{64,128},{128,192},{192,32},{32,96},{96,160},{160,224},{224... | collective-permute-start | bytes 393224 | tf_op jit(solution)/shard_map/ppermute | solution.py:210
  18.2 1.4 %collective-permute-start.4 = (bf16[32,2048]{1,0:T(8,128)(2,1)S(1)}, bf16[32,2048]{1,0:T(8,128)(2,1)S(1)}, u32[]{:S(2)}, u32[]{:S(2)}) collective-permute-start(bf16[32,2048]{1,0:T(8,128)(2,1)S(1)} %collective-permute-done.3), channel_id=1, source_target_pairs={{0,224},{64,0},{128,64},{192,128},{32,192},{96,32},{160,96},{224,1... | collective-permute-start | bytes 393224 | tf_op jit(solution)/shard_map/ppermute | solution.py:210
  19.7 7.5 %collective-permute-done.1 = bf16[32,2048]{1,0:T(8,128)(2,1)S(1)} collective-permute-done((bf16[32,2048]{1,0:T(8,128)(2,1)S(1)}, bf16[32,2048]{1,0:T(8,128)(2,1)S(1)}, u32[]{:S(2)}, u32[]{:S(2)}) %collective-permute-start.1) | collective-permute-done | bytes 131104 | tf_op jit(solution)/shard_map/ppermute | solution.py:210
  27.2 1.7 %collective-permute-start.12 = (bf16[5,32,2048]{2,1,0:T(8,128)(2,1)S(1)}, bf16[5,32,2048]{2,1,0:T(8,128)(2,1)S(1)}, u32[]{:S(2)}, u32[]{:S(2)}) collective-permute-start(bf16[5,32,2048]{2,1,0:T(8,128)(2,1)S(1)} %bitcast_dynamic-update-slice_fusion.refs_0_), channel_id=1, source_target_pairs={{0,8},{8,16},{16,24},{24,0},{1,9},{9,17},{17,25},{25,1},{2,10},{10... | collective-permute-start | bytes 1966088 | tf_op jit(solution)/shard_map/ppermute | solution.py:182
  28.9 1.4 %collective-permute-start.13 = (bf16[5,32,2048]{2,1,0:T(8,128)(2,1)S(1)}, bf16[5,32,2048]{2,1,0:T(8,128)(2,1)S(1)}, u32[]{:S(2)}, u32[]{:S(2)}) collective-permute-start(bf16[5,32,2048]{2,1,0:T(8,128)(2,1)S(1)} %bitcast_dynamic-update-slice_fusion.refs_0_), channel_id=1, source_target_pairs={{0,24},{8,0},{16,8},{24,16},{1,25},{9,1},{17,9},{25,17},{2,26},{10... | collective-permute-start | bytes 1966088 | tf_op jit(solution)/shard_map/ppermute | solution.py:182
  30.3 2.7 %collective-permute-start.10 = (bf16[32,2,16,128]{3,2,1,0:T(8,128)(2,1)S(1)}, bf16[32,2,16,128]{3,2,1,0:T(8,128)(2,1)S(1)}, u32[]{:S(2)}, u32[]{:S(2)}) collective-permute-start(bf16[32,2,16,128]{3,2,1,0:T(8,128)(2,1)S(1)} %all-to-all-done), channel_id=1, source_target_pairs={{0,4},{2,6},{4,0},{6,2},{1,5},{3,7},{5,1},{7,3},{8,12},{10,14},{12... | collective-permute-start | bytes 786440 | tf_op jit(solution)/shard_map/ppermute | solution.py:213
  33.4 2.3 %collective-permute-done.2 = bf16[32,2048]{1,0:T(8,128)(2,1)} collective-permute-done((bf16[32,2048]{1,0:T(8,128)(2,1)S(1)}, bf16[32,2048]{1,0:T(8,128)(2,1)}, u32[]{:S(2)}, u32[]{:S(2)}) %collective-permute-start.2) | collective-permute-done | bytes 131104 | tf_op jit(solution)/shard_map/ppermute | solution.py:214
  35.6 2.5 %collective-permute-start.9 = (bf16[32,2,16,128]{3,2,1,0:T(8,128)(2,1)S(1)}, bf16[32,2,16,128]{3,2,1,0:T(8,128)(2,1)S(1)}, u32[]{:S(2)}, u32[]{:S(2)}) collective-permute-start(bf16[32,2,16,128]{3,2,1,0:T(8,128)(2,1)S(1)} %all-to-all-done), channel_id=1, source_target_pairs={{0,6},{2,0},{4,2},{6,4},{1,7},{3,1},{5,3},{7,5},{8,14},{10,8},{12,... | collective-permute-start | bytes 786440 | tf_op jit(solution)/shard_map/ppermute | solution.py:213
  38.9 1.6 %bitcast_dynamic-update-slice_fusion.7 = bf16[3,32,2048]{2,1,0:T(8,128)(2,1)} fusion(bf16[3,32,2048]{2,1,0:T(8,128)(2,1)} %broadcast_in_dim.34, s32[]{:T(128)S(6)} %select_n.24, bf16[32,2048]{1,0:T(8,128)(2,1)} %collective-permute-done.2), kind=kLoop, calls=%fused_computation.17 | loop fusion | bytes 262148 | tf_op jit(solution)/shard_map/dynamic_update_slice | solution.py:196
  40.8 3.5 %collective-permute-done.11 = bf16[32,2,16,128]{3,2,1,0:T(8,128)(2,1)S(1)} collective-permute-done((bf16[32,2,16,128]{3,2,1,0:T(8,128)(2,1)S(1)}, bf16[32,2,16,128]{3,2,1,0:T(8,128)(2,1)S(1)}, u32[]{:S(2)}, u32[]{:S(2)}) %collective-permute-start.11) | collective-permute-done | bytes 262176 | tf_op jit(solution)/shard_map/ppermute | solution.py:213
  44.3 1.2 %collective-permute-start.6 = (bf16[32,2048]{1,0:T(8,128)(2,1)}, bf16[32,2048]{1,0:T(8,128)(2,1)S(1)}, u32[]{:S(2)}, u32[]{:S(2)}) collective-permute-start(bf16[32,2048]{1,0:T(8,128)(2,1)} %collective-permute-done.2), channel_id=1, source_target_pairs={{0,64},{64,128},{128,192},{192,32},{32,96},{96,160},{160,224},{224... | collective-permute-start | bytes 393224 | tf_op jit(solution)/shard_map/ppermute | solution.py:216
  46.5 2.6 %collective-permute-start.14 = (bf16[4,32,2,16,128]{4,3,2,1,0:T(8,128)(2,1)S(1)}, bf16[4,32,2,16,128]{4,3,2,1,0:T(8,128)(2,1)S(1)}, u32[]{:S(2)}, u32[]{:S(2)}) collective-permute-start(bf16[4,32,2,16,128]{4,3,2,1,0:T(8,128)(2,1)S(1)} %pad_maximum_fusion.refs_9_.refs_13_), channel_id=1, source_target_pairs={{0,1},{1,0},{2,3},{3,2},{4,5},{5,4},{6,7},{7,6},{8,9},{9,8},{10,11... | collective-permute-start | bytes 3145736 | tf_op jit(solution)/shard_map/ppermute | solution.py:220
  50.6 2.6 %collective-permute-start.8 = (bf16[3,32,2048]{2,1,0:T(8,128)(2,1)}, bf16[3,32,2048]{2,1,0:T(8,128)(2,1)}, u32[]{:S(2)}, u32[]{:S(2)}) collective-permute-start(bf16[3,32,2048]{2,1,0:T(8,128)(2,1)} %bitcast_dynamic-update-slice_fusion.5.refs_3_), channel_id=1, source_target_pairs={{0,24},{8,0},{16,8},{24,16},{1,25},{9,1},{17,9},{25,17},{2,26},{10... | collective-permute-start | bytes 1179656 | tf_op jit(solution)/shard_map/ppermute | solution.py:182
  54.5 2.7 %collective-permute-start.16 = (bf16[2,32,2048]{2,1,0:T(8,128)(2,1)S(1)}, bf16[2,32,2048]{2,1,0:T(8,128)(2,1)S(1)}, u32[]{:S(2)}, u32[]{:S(2)}) collective-permute-start(bf16[2,32,2048]{2,1,0:T(8,128)(2,1)S(1)} %slice.37), channel_id=1, source_target_pairs={{0,24},{8,0},{16,8},{24,16},{1,25},{9,1},{17,9},{25,17},{2,26},{10... | collective-permute-start | bytes 786440 | tf_op jit(solution)/shard_map/ppermute | solution.py:187
  57.6 1.3 %copy.16 = bf16[12,8,16,128]{3,2,1,0:T(8,128)(2,1)S(1)} copy(bf16[12,8,16,128]{3,1,2,0:T(8,128)(2,1)} %bitcast.42) | data formatting | bytes 786432
  58.9 5.0 %ladder.2 = (f32[8,512,128]{2,1,0:T(8,128)S(1)}, bf16[2048,512]{1,0:T(8,128)(2,1)S(1)}) custom-call(s32[6]{0:T(128)S(1)} %stack.51.meta, s32[16,4]{1,0:T(8,128)S(1)} %copy.11.live, bf16[5,32,2048]{2,1,0:T(8,128)(2,1)S(1)} %bitcast_dynamic-update-slice_fusion.refs_0_, bf16[5,32,2048]{2,1,0:T(8,128)(2,1)S(1)} %collective-permute-done.12.refs_1_, ...), custom_call_target="tpu_custom_call" | custom-call | flops 1800000000 | bytes 10000000 | tf_op jit(solution)/shard_map/ladder/pallas_call | solution.py:131
  65.9 1.5 %collective-permute-start.17 = (bf16[1,32,2048]{2,1,0:T(8,128)(2,1)S(1)}, bf16[1,32,2048]{2,1,0:T(8,128)(2,1)S(1)}, u32[]{:S(2)}, u32[]{:S(2)}) collective-permute-start(bf16[1,32,2048]{2,1,0:T(8,128)(2,1)S(1)} %slice.38), channel_id=1, source_target_pairs={{0,8},{8,16},{16,24},{24,0},{1,9},{9,17},{17,25},{25,1},{2,10},{10... | collective-permute-start | bytes 393224 | tf_op jit(solution)/shard_map/ppermute | solution.py:186
  69.1 1.1 %copy.18 = bf16[12,8,16,128]{3,2,1,0:T(8,128)(2,1)S(1)} copy(bf16[12,8,16,128]{3,1,2,0:T(8,128)(2,1)} %bitcast.50) | data formatting | bytes 786432
  70.2 2.6 %collective-permute-done.17.refs_4_ = bf16[1,32,2048]{2,1,0:T(8,128)(2,1)S(1)} collective-permute-done((bf16[1,32,2048]{2,1,0:T(8,128)(2,1)S(1)}, bf16[1,32,2048]{2,1,0:T(8,128)(2,1)S(1)}, u32[]{:S(2)}, u32[]{:S(2)}) %collective-permute-start.17) | collective-permute-done | bytes 131104 | tf_op jit(solution)/shard_map/ppermute | solution.py:186
  72.8 4.0 %ladder.3 = (f32[4,512,128]{2,1,0:T(8,128)S(1)}, f32[4,512,128]{2,1,0:T(8,128)S(1)}) custom-call(s32[6]{0:T(128)S(1)} %stack.51.meta, s32[16,4]{1,0:T(8,128)S(1)} %copy.11.live, bf16[3,32,2048]{2,1,0:T(8,128)(2,1)} %collective-permute-done.7.refs_0_, bf16[3,32,2048]{2,1,0:T(8,128)(2,1)} %collective-permute-done.8.refs_1_, ...), custom_call_target="tpu_custom_call" | custom-call | flops 1400000000 | bytes 10000000 | tf_op jit(solution)/shard_map/ladder/pallas_call | solution.py:131
  76.8 4.8 %collective-permute-start.19 = (f32[4,512,128]{2,1,0:T(8,128)S(1)}, f32[4,512,128]{2,1,0:T(8,128)S(1)}, u32[]{:S(2)}, u32[]{:S(2)}) collective-permute-start(f32[4,512,128]{2,1,0:T(8,128)S(1)} %get-tuple-element.40), channel_id=1, source_target_pairs={{0,1},{1,0},{2,3},{3,2},{4,5},{5,4},{6,7},{7,6},{8,9},{9,8},{10,11... | collective-permute-start | bytes 3145736 | tf_op jit(solution)/shard_map/ppermute | solution.py:228
  81.7 2.3 %collective-permute-done.19 = f32[4,512,128]{2,1,0:T(8,128)S(1)} collective-permute-done((f32[4,512,128]{2,1,0:T(8,128)S(1)}, f32[4,512,128]{2,1,0:T(8,128)S(1)}, u32[]{:S(2)}, u32[]{:S(2)}) %collective-permute-start.19) | collective-permute-done | bytes 1048608 | tf_op jit(solution)/shard_map/ppermute | solution.py:228
  84.9 1.3 %collective-permute-start.20 = (f32[512,128]{1,0:T(8,128)S(1)}, f32[512,128]{1,0:T(8,128)S(1)}, u32[]{:S(2)}, u32[]{:S(2)}) collective-permute-start(f32[512,128]{1,0:T(8,128)S(1)} %get-tuple-element.43), channel_id=1, source_target_pairs={{0,2},{2,4},{4,6},{6,0},{1,3},{3,5},{5,7},{7,1},{8,10},{10,12},{12... | collective-permute-start | bytes 786440 | tf_op jit(solution)/shard_map/ppermute | solution.py:231
  86.2 1.2 %collective-permute-start.21 = (f32[512,128]{1,0:T(8,128)S(1)}, f32[512,128]{1,0:T(8,128)S(1)}, u32[]{:S(2)}, u32[]{:S(2)}) collective-permute-start(f32[512,128]{1,0:T(8,128)S(1)} %get-tuple-element.42), channel_id=1, source_target_pairs={{0,4},{2,6},{4,0},{6,2},{1,5},{3,7},{5,1},{7,3},{8,12},{10,14},{12... | collective-permute-start | bytes 786440 | tf_op jit(solution)/shard_map/ppermute | solution.py:231
  87.4 1.7 %collective-permute-start.22 = (f32[512,128]{1,0:T(8,128)S(1)}, f32[512,128]{1,0:T(8,128)S(1)}, u32[]{:S(2)}, u32[]{:S(2)}) collective-permute-start(f32[512,128]{1,0:T(8,128)S(1)} %get-tuple-element.41), channel_id=1, source_target_pairs={{0,6},{2,0},{4,2},{6,4},{1,7},{3,1},{5,3},{7,5},{8,14},{10,8},{12,... | collective-permute-start | bytes 786440 | tf_op jit(solution)/shard_map/ppermute | solution.py:231
  89.1 4.8 %collective-permute-done.20.p2 = f32[512,128]{1,0:T(8,128)S(1)} collective-permute-done((f32[512,128]{1,0:T(8,128)S(1)}, f32[512,128]{1,0:T(8,128)S(1)}, u32[]{:S(2)}, u32[]{:S(2)}) %collective-permute-start.20) | collective-permute-done | bytes 262176 | tf_op jit(solution)/shard_map/ppermute | solution.py:231
  93.8 5.3 %collective-permute-done.21.p3 = f32[512,128]{1,0:T(8,128)S(1)} collective-permute-done((f32[512,128]{1,0:T(8,128)S(1)}, f32[512,128]{1,0:T(8,128)S(1)}, u32[]{:S(2)}, u32[]{:S(2)}) %collective-permute-start.21) | collective-permute-done | bytes 262176 | tf_op jit(solution)/shard_map/ppermute | solution.py:231
  100.3 2.1 %finish.1 = bf16[128,512]{1,0:T(8,128)(2,1)} custom-call(s32[6]{0:T(128)} %copy-done.3, f32[32]{0:T(128)} %occ.1, f32[128]{0:T(128)} %vir.1, f32[1,128]{1,0:T(1,128)} %bitcast.105, f32[512,128]{1,0:T(8,128)} %get-tuple-element.44.p0, f32[512,128]{1,0:T(8,128)} %get-tuple-element.45.p1, f32[512,128]{1,0:T(8,128)} %copy-done.4, f32[512,128]{1,0:T(8,128)} %copy-done.5, ...), custom_call_target="tpu_custom_call" | custom-call | flops 400000 | bytes 1500000 | tf_op jit(solution)/shard_map/finish/pallas_call | solution.py:164
  (67 shorter events, 12.4 us)
Async XLA Ops:
  0.0 16.8 %copy-start.7 = (bf16[32,2048]{1,0:T(8,128)(2,1)S(1)}, bf16[32,2048]{1,0:T(8,128)(2,1)}, u32[]{:S(2)}) copy-start(bf16[32,2048]{1,0:T(8,128)(2,1)} %param.7) | copy-start | bytes 393220
  0.0 16.8 %collective-permute-start = (bf16[32,2048]{1,0:T(8,128)(2,1)}, bf16[32,2048]{1,0:T(8,128)(2,1)S(1)}, u32[]{:S(2)}, u32[]{:S(2)}) collective-permute-start(bf16[32,2048]{1,0:T(8,128)(2,1)} %param.7), channel_id=1, source_target_pairs={{0,64},{64,128},{128,192},{192,32},{32,96},{96,160},{160,224},{224... | collective-permute-start | bytes 393224 | tf_op jit(solution)/shard_map/ppermute | solution.py:210
  2.5 15.7 %collective-permute-start.3 = (bf16[32,2048]{1,0:T(8,128)(2,1)}, bf16[32,2048]{1,0:T(8,128)(2,1)S(1)}, u32[]{:S(2)}, u32[]{:S(2)}) collective-permute-start(bf16[32,2048]{1,0:T(8,128)(2,1)} %param.7), channel_id=1, source_target_pairs={{0,224},{64,0},{128,64},{192,128},{32,192},{96,32},{160,96},{224,1... | collective-permute-start | bytes 393224 | tf_op jit(solution)/shard_map/ppermute | solution.py:210
  8.4 21.9 %all-to-all-start = ((bf16[32,2,16,128]{3,2,1,0:T(8,128)(2,1)}), bf16[32,2,16,128]{3,2,1,0:T(8,128)(2,1)S(1)}, u32[]{:S(2)}, u32[]{:S(2)}) async-start(bf16[32,2,16,128]{3,2,1,0:T(8,128)(2,1)} %bitcast.18), calls=%async_computation | async-start | bytes 524288 | tf_op jit(solution)/shard_map/all_to_all | solution.py:205
  16.9 10.3 %collective-permute-start.1 = (bf16[32,2048]{1,0:T(8,128)(2,1)S(1)}, bf16[32,2048]{1,0:T(8,128)(2,1)S(1)}, u32[]{:S(2)}, u32[]{:S(2)}) collective-permute-start(bf16[32,2048]{1,0:T(8,128)(2,1)S(1)} %collective-permute-done), channel_id=1, source_target_pairs={{0,64},{64,128},{128,192},{192,32},{32,96},{96,160},{160,224},{224... | collective-permute-start | bytes 393224 | tf_op jit(solution)/shard_map/ppermute | solution.py:210
  18.2 9.0 %collective-permute-start.4 = (bf16[32,2048]{1,0:T(8,128)(2,1)S(1)}, bf16[32,2048]{1,0:T(8,128)(2,1)S(1)}, u32[]{:S(2)}, u32[]{:S(2)}) collective-permute-start(bf16[32,2048]{1,0:T(8,128)(2,1)S(1)} %collective-permute-done.3), channel_id=1, source_target_pairs={{0,224},{64,0},{128,64},{192,128},{32,192},{96,32},{160,96},{224,1... | collective-permute-start | bytes 393224 | tf_op jit(solution)/shard_map/ppermute | solution.py:210
  19.6 33.5 %copy-start.8 = (s32[16,4]{0,1:T(4,128)S(1)}, s32[16,4]{0,1:T(4,128)}, u32[]{:S(2)}) copy-start(s32[16,4]{0,1:T(4,128)} %param.9) | copy-start | bytes 772
  27.2 18.2 %collective-permute-start.12 = (bf16[5,32,2048]{2,1,0:T(8,128)(2,1)S(1)}, bf16[5,32,2048]{2,1,0:T(8,128)(2,1)S(1)}, u32[]{:S(2)}, u32[]{:S(2)}) collective-permute-start(bf16[5,32,2048]{2,1,0:T(8,128)(2,1)S(1)} %bitcast_dynamic-update-slice_fusion.refs_0_), channel_id=1, source_target_pairs={{0,8},{8,16},{16,24},{24,0},{1,9},{9,17},{17,25},{25,1},{2,10},{10... | collective-permute-start | bytes 1966088 | tf_op jit(solution)/shard_map/ppermute | solution.py:182
  28.9 16.6 %collective-permute-start.13 = (bf16[5,32,2048]{2,1,0:T(8,128)(2,1)S(1)}, bf16[5,32,2048]{2,1,0:T(8,128)(2,1)S(1)}, u32[]{:S(2)}, u32[]{:S(2)}) collective-permute-start(bf16[5,32,2048]{2,1,0:T(8,128)(2,1)S(1)} %bitcast_dynamic-update-slice_fusion.refs_0_), channel_id=1, source_target_pairs={{0,24},{8,0},{16,8},{24,16},{1,25},{9,1},{17,9},{25,17},{2,26},{10... | collective-permute-start | bytes 1966088 | tf_op jit(solution)/shard_map/ppermute | solution.py:182
  30.3 5.3 %collective-permute-start.2 = (bf16[32,2048]{1,0:T(8,128)(2,1)S(1)}, bf16[32,2048]{1,0:T(8,128)(2,1)}, u32[]{:S(2)}, u32[]{:S(2)}) collective-permute-start(bf16[32,2048]{1,0:T(8,128)(2,1)S(1)} %collective-permute-done.1), channel_id=1, source_target_pairs={{0,64},{64,128},{128,192},{192,32},{32,96},{96,160},{160,224},{224... | collective-permute-start | bytes 393224 | tf_op jit(solution)/shard_map/ppermute | solution.py:214
  30.3 10.2 %collective-permute-start.10 = (bf16[32,2,16,128]{3,2,1,0:T(8,128)(2,1)S(1)}, bf16[32,2,16,128]{3,2,1,0:T(8,128)(2,1)S(1)}, u32[]{:S(2)}, u32[]{:S(2)}) collective-permute-start(bf16[32,2,16,128]{3,2,1,0:T(8,128)(2,1)S(1)} %all-to-all-done), channel_id=1, source_target_pairs={{0,4},{2,6},{4,0},{6,2},{1,5},{3,7},{5,1},{7,3},{8,12},{10,14},{12... | collective-permute-start | bytes 786440 | tf_op jit(solution)/shard_map/ppermute | solution.py:213
  33.1 11.2 %collective-permute-start.11 = (bf16[32,2,16,128]{3,2,1,0:T(8,128)(2,1)S(1)}, bf16[32,2,16,128]{3,2,1,0:T(8,128)(2,1)S(1)}, u32[]{:S(2)}, u32[]{:S(2)}) collective-permute-start(bf16[32,2,16,128]{3,2,1,0:T(8,128)(2,1)S(1)} %all-to-all-done), channel_id=1, source_target_pairs={{0,2},{2,4},{4,6},{6,0},{1,3},{3,5},{5,7},{7,1},{8,10},{10,12},{12... | collective-permute-start | bytes 786440 | tf_op jit(solution)/shard_map/ppermute | solution.py:213
  35.6 9.8 %collective-permute-start.9 = (bf16[32,2,16,128]{3,2,1,0:T(8,128)(2,1)S(1)}, bf16[32,2,16,128]{3,2,1,0:T(8,128)(2,1)S(1)}, u32[]{:S(2)}, u32[]{:S(2)}) collective-permute-start(bf16[32,2,16,128]{3,2,1,0:T(8,128)(2,1)S(1)} %all-to-all-done), channel_id=1, source_target_pairs={{0,6},{2,0},{4,2},{6,4},{1,7},{3,1},{5,3},{7,5},{8,14},{10,8},{12,... | collective-permute-start | bytes 786440 | tf_op jit(solution)/shard_map/ppermute | solution.py:213
  40.5 8.6 %collective-permute-start.5 = (bf16[32,2048]{1,0:T(8,128)(2,1)S(1)}, bf16[32,2048]{1,0:T(8,128)(2,1)S(1)}, u32[]{:S(2)}, u32[]{:S(2)}) collective-permute-start(bf16[32,2048]{1,0:T(8,128)(2,1)S(1)} %collective-permute-done.4), channel_id=1, source_target_pairs={{0,224},{64,0},{128,64},{192,128},{32,192},{96,32},{160,96},{224,1... | collective-permute-start | bytes 393224 | tf_op jit(solution)/shard_map/ppermute | solution.py:214
  44.3 5.5 %collective-permute-start.6 = (bf16[32,2048]{1,0:T(8,128)(2,1)}, bf16[32,2048]{1,0:T(8,128)(2,1)S(1)}, u32[]{:S(2)}, u32[]{:S(2)}) collective-permute-start(bf16[32,2048]{1,0:T(8,128)(2,1)} %collective-permute-done.2), channel_id=1, source_target_pairs={{0,64},{64,128},{128,192},{192,32},{32,96},{96,160},{160,224},{224... | collective-permute-start | bytes 393224 | tf_op jit(solution)/shard_map/ppermute | solution.py:216
  45.5 0.9 copy-start
  46.5 10.7 %collective-permute-start.14 = (bf16[4,32,2,16,128]{4,3,2,1,0:T(8,128)(2,1)S(1)}, bf16[4,32,2,16,128]{4,3,2,1,0:T(8,128)(2,1)S(1)}, u32[]{:S(2)}, u32[]{:S(2)}) collective-permute-start(bf16[4,32,2,16,128]{4,3,2,1,0:T(8,128)(2,1)S(1)} %pad_maximum_fusion.refs_9_.refs_13_), channel_id=1, source_target_pairs={{0,1},{1,0},{2,3},{3,2},{4,5},{5,4},{6,7},{7,6},{8,9},{9,8},{10,11... | collective-permute-start | bytes 3145736 | tf_op jit(solution)/shard_map/ppermute | solution.py:220
  50.5 13.4 %collective-permute-start.7 = (bf16[3,32,2048]{2,1,0:T(8,128)(2,1)}, bf16[3,32,2048]{2,1,0:T(8,128)(2,1)}, u32[]{:S(2)}, u32[]{:S(2)}) collective-permute-start(bf16[3,32,2048]{2,1,0:T(8,128)(2,1)} %bitcast_dynamic-update-slice_fusion.5.refs_3_), channel_id=1, source_target_pairs={{0,8},{8,16},{16,24},{24,0},{1,9},{9,17},{17,25},{25,1},{2,10},{10... | collective-permute-start | bytes 1179656 | tf_op jit(solution)/shard_map/ppermute | solution.py:182
  50.6 13.3 %collective-permute-start.8 = (bf16[3,32,2048]{2,1,0:T(8,128)(2,1)}, bf16[3,32,2048]{2,1,0:T(8,128)(2,1)}, u32[]{:S(2)}, u32[]{:S(2)}) collective-permute-start(bf16[3,32,2048]{2,1,0:T(8,128)(2,1)} %bitcast_dynamic-update-slice_fusion.5.refs_3_), channel_id=1, source_target_pairs={{0,24},{8,0},{16,8},{24,16},{1,25},{9,1},{17,9},{25,17},{2,26},{10... | collective-permute-start | bytes 1179656 | tf_op jit(solution)/shard_map/ppermute | solution.py:182
  53.3 19.5 %copy-start.3 = (s32[6]{0:T(128)}, s32[6]{0:T(128)S(1)}, u32[]{:S(2)}) copy-start(s32[6]{0:T(128)S(1)} %stack.51.meta) | copy-start | bytes 76
  53.3 4.1 %copy-start.1 = (bf16[5,32,2048]{2,1,0:T(8,128)(2,1)S(1)}, bf16[5,32,2048]{2,1,0:T(8,128)(2,1)}, u32[]{:S(2)}) copy-start(bf16[5,32,2048]{2,1,0:T(8,128)(2,1)} %copy-done) | copy-start | bytes 1966084
  53.3 14.6 %collective-permute-start.15 = (bf16[3,32,2048]{2,1,0:T(8,128)(2,1)S(1)}, bf16[3,32,2048]{2,1,0:T(8,128)(2,1)S(1)}, u32[]{:S(2)}, u32[]{:S(2)}) collective-permute-start(bf16[3,32,2048]{2,1,0:T(8,128)(2,1)S(1)} %slice.36), channel_id=1, source_target_pairs={{0,8},{8,16},{16,24},{24,0},{1,9},{9,17},{17,25},{25,1},{2,10},{10... | collective-permute-start | bytes 1179656 | tf_op jit(solution)/shard_map/ppermute | solution.py:186
  54.5 12.9 %collective-permute-start.16 = (bf16[2,32,2048]{2,1,0:T(8,128)(2,1)S(1)}, bf16[2,32,2048]{2,1,0:T(8,128)(2,1)S(1)}, u32[]{:S(2)}, u32[]{:S(2)}) collective-permute-start(bf16[2,32,2048]{2,1,0:T(8,128)(2,1)S(1)} %slice.37), channel_id=1, source_target_pairs={{0,24},{8,0},{16,8},{24,16},{1,25},{9,1},{17,9},{25,17},{2,26},{10... | collective-permute-start | bytes 786440 | tf_op jit(solution)/shard_map/ppermute | solution.py:187
  57.1 1.7 %copy-start.2 = (bf16[2048,512]{1,0:T(8,128)(2,1)S(1)}, bf16[2048,512]{1,0:T(8,128)(2,1)}, u32[]{:S(2)}) copy-start(bf16[2048,512]{1,0:T(8,128)(2,1)} %refs_8_.1) | copy-start | bytes 6291460
  64.9 7.9 %collective-permute-start.18 = (bf16[2,32,2048]{2,1,0:T(8,128)(2,1)S(1)}, bf16[2,32,2048]{2,1,0:T(8,128)(2,1)S(1)}, u32[]{:S(2)}, u32[]{:S(2)}) collective-permute-start(bf16[2,32,2048]{2,1,0:T(8,128)(2,1)S(1)} %slice.39), channel_id=1, source_target_pairs={{0,24},{8,0},{16,8},{24,16},{1,25},{9,1},{17,9},{25,17},{2,26},{10... | collective-permute-start | bytes 786440 | tf_op jit(solution)/shard_map/ppermute | solution.py:187
  65.9 6.9 %collective-permute-start.17 = (bf16[1,32,2048]{2,1,0:T(8,128)(2,1)S(1)}, bf16[1,32,2048]{2,1,0:T(8,128)(2,1)S(1)}, u32[]{:S(2)}, u32[]{:S(2)}) collective-permute-start(bf16[1,32,2048]{2,1,0:T(8,128)(2,1)S(1)} %slice.38), channel_id=1, source_target_pairs={{0,8},{8,16},{16,24},{24,0},{1,9},{9,17},{17,25},{25,1},{2,10},{10... | collective-permute-start | bytes 393224 | tf_op jit(solution)/shard_map/ppermute | solution.py:186
  76.8 7.1 %collective-permute-start.19 = (f32[4,512,128]{2,1,0:T(8,128)S(1)}, f32[4,512,128]{2,1,0:T(8,128)S(1)}, u32[]{:S(2)}, u32[]{:S(2)}) collective-permute-start(f32[4,512,128]{2,1,0:T(8,128)S(1)} %get-tuple-element.40), channel_id=1, source_target_pairs={{0,1},{1,0},{2,3},{3,2},{4,5},{5,4},{6,7},{7,6},{8,9},{9,8},{10,11... | collective-permute-start | bytes 3145736 | tf_op jit(solution)/shard_map/ppermute | solution.py:228
  84.9 8.9 %collective-permute-start.20 = (f32[512,128]{1,0:T(8,128)S(1)}, f32[512,128]{1,0:T(8,128)S(1)}, u32[]{:S(2)}, u32[]{:S(2)}) collective-permute-start(f32[512,128]{1,0:T(8,128)S(1)} %get-tuple-element.43), channel_id=1, source_target_pairs={{0,2},{2,4},{4,6},{6,0},{1,3},{3,5},{5,7},{7,1},{8,10},{10,12},{12... | collective-permute-start | bytes 786440 | tf_op jit(solution)/shard_map/ppermute | solution.py:231
  86.2 12.9 %collective-permute-start.21 = (f32[512,128]{1,0:T(8,128)S(1)}, f32[512,128]{1,0:T(8,128)S(1)}, u32[]{:S(2)}, u32[]{:S(2)}) collective-permute-start(f32[512,128]{1,0:T(8,128)S(1)} %get-tuple-element.42), channel_id=1, source_target_pairs={{0,4},{2,6},{4,0},{6,2},{1,5},{3,7},{5,1},{7,3},{8,12},{10,14},{12... | collective-permute-start | bytes 786440 | tf_op jit(solution)/shard_map/ppermute | solution.py:231
  87.4 12.2 %collective-permute-start.22 = (f32[512,128]{1,0:T(8,128)S(1)}, f32[512,128]{1,0:T(8,128)S(1)}, u32[]{:S(2)}, u32[]{:S(2)}) collective-permute-start(f32[512,128]{1,0:T(8,128)S(1)} %get-tuple-element.41), channel_id=1, source_target_pairs={{0,6},{2,0},{4,2},{6,4},{1,7},{3,1},{5,3},{7,5},{8,14},{10,8},{12,... | collective-permute-start | bytes 786440 | tf_op jit(solution)/shard_map/ppermute | solution.py:231
  93.8 5.7 %copy-start.4 = (f32[512,128]{1,0:T(8,128)}, f32[512,128]{1,0:T(8,128)S(1)}, u32[]{:S(2)}) copy-start(f32[512,128]{1,0:T(8,128)S(1)} %collective-permute-done.20.p2) | copy-start | bytes 786436
  99.1 0.7 copy-start.5
  (1 other events, 0.7 us)

commit v10 on v9

--- a/solution.py
+++ b/solution.py
@@ -150,7 +150,7 @@
     occ_col = jnp.zeros((32, 128), F32)
     for j in range(32):
         occ_col = jnp.where(row == j, occ[j], occ_col)
-    total[...] = ((p0[...] + p1[...]) + p2[...]) + (p3[...] + p4[...])
+    total[...] = ((p0[0] + p1[0]) + p2[...]) + (p3[...] + p4[...])
     for il in range(4):
         for a in range(4):
             value = total[pl.ds(il * 4 + a, 32, stride=16), :]
@@ -202,12 +202,14 @@
     meta = jnp.stack([x0, c0, y0, lax.axis_index(C), lax.axis_index(G), z0]).astype(jnp.int32)
     both = jnp.stack([cycle_direct, cycle_exchange]).reshape(2, 4, 32, 4, 128)
     both = both.transpose(2, 0, 1, 3, 4).reshape(32, 2, 16, 128)
-    both = lax.all_to_all(both, G, 0, 0, tiled=True)
     near = place(jnp.zeros((5, 32, 2048), BF16), NEAR, z0, 0, amplitudes)
     far = jnp.zeros((3, 32, 2048), BF16)
     fwd = bwd = amplitudes
     for k in range(1, 3):
         fwd, bwd = lax.ppermute(fwd, Z, z_shift(1)), lax.ppermute(bwd, Z, z_shift(-1))
+        if k == 1:
+            fwd, bwd, both = lax.optimization_barrier((fwd, bwd, both))
+            both = lax.all_to_all(both, G, 0, 0, tiled=True)
         near = place(place(near, NEAR, z0, -k, fwd), NEAR, z0, k, bwd)
     near_down, near_up = beside(near)
     xs = [both] + [lax.ppermute(both, "x", shift(4, -s)) for s in (1, 2, 3)]
@@ -226,7 +228,7 @@
     last = [far_down, far_up, *near_two, *onward(far_down, far_up, CUTS[FAR])]
     keep, away = ladder_call(LAST, meta, tile_live, last, split_rows(last), masked, wa, wb, (prev,))
     got = lax.ppermute(away, "core", shift(2, 1))
-    parts = [keep[0], got[0]]
+    parts = [keep, got]
     for s in (1, 2, 3):
         parts.append(lax.ppermute(keep[s] + got[s], "x", shift(4, s)))
     return finish_call(meta, eps_occ, eps_vir, parts)

time: 103 us -> 103 us (level)
  waiting for transfers between devices: 29.1 us -> 24.9 us
  starting transfers between devices: 46.3 us -> 50 us
    ppermute x3, waiting for transfers between devices: 9.79 us -> 0.45 us  [local(): lax.ppermute(fwd, Z, z_shift(1))]
    all_to_all x1, waiting for transfers between devices: 0.01 us -> 6.62 us  [local(): both = lax.all_to_all(both, G, 0, 0, tiled=True)]
    ppermute x1, starting transfers between devices: 1.21 us -> 4.01 us  [local(): far = place(far, FAR, z0, 4, lax.ppermute(fwd, Z, z_shift(1)))]
    ppermute x3, waiting for transfers between devices: 3.46 us -> 1.7 us  [local(): xs = [both] + [lax.ppermute(both, 'x', shift(4, -s)) for s in (1, 2, 3)]]
    ppermute x3, starting transfers between devices: 5.78 us -> 6.95 us  [local(): lax.ppermute(bwd, Z, z_shift(-1))]
    unnamed x29 -> x31, local copies, waits for them, and re-layouts: 5.6 us -> 5.67 us
  transfers between devices with their start and end apart: 24 -> 24, of which waited for: 9 -> 7; matrix products, arithmetic and copies ran while one was open for 13% -> 14% of each run, Pallas kernels for 5% -> 5%
where the time goes in v10:
time: 103 us; the launch traced here: 102 us
  starting transfers between devices  50 us (49%)
  waiting for transfers between devices  24.9 us (24%)
  local copies, waits for them, and re-layouts  14.2 us (14%)
  Pallas kernels  11.6 us (11%)
  other arithmetic  1.38 us (1%)
    ppermute x3, waiting for transfers between devices, local(): parts.append(lax.ppermute(keep[s] + got[s], 'x', shift(4, s)))  10.7 us
    pallas_call x2, Pallas kernels, ladder_call(): pl.pallas_call(functools.partial(ladder_kernel, pieces), out_shape=(half,...  9.01 us
    all_to_all x1, starting transfers between devices, local(): both = lax.all_to_all(both, G, 0, 0, tiled=True)  7.98 us
    ppermute x3, starting transfers between devices, local(): lax.ppermute(bwd, Z, z_shift(-1))  6.95 us
    all_to_all x1, waiting for transfers between devices, local(): both = lax.all_to_all(both, G, 0, 0, tiled=True)  6.62 us
    unnamed x31, local copies, waits for them, and re-layouts  5.67 us
    ppermute x3, starting transfers between devices, local(): xs = [both] + [lax.ppermute(both, 'x', shift(4, -s)) for s in (1, 2, 3)]  5.42 us
    ppermute x1, starting transfers between devices, local(): got = lax.ppermute(away, 'core', shift(2, 1))  4.85 us
  transfers between devices with their start and end apart: 24, of which 7 were waited for; matrix products, arithmetic and copies ran while one was open for 14% of the time, Pallas kernels for 5%

profile of v10, /device:TPU:1, one launch (start us, length us, event | category | flops | bytes accessed | tf_op | source)
XLA Modules:
  0.0 102.4 jit_solution(5218405773269777471)
XLA Ops:
  0.0 2.5 %collective-permute-start = (bf16[32,2048]{1,0:T(8,128)(2,1)}, bf16[32,2048]{1,0:T(8,128)(2,1)S(1)}, u32[]{:S(2)}, u32[]{:S(2)}) collective-permute-start(bf16[32,2048]{1,0:T(8,128)(2,1)} %param.7), channel_id=1, source_target_pairs={{0,64},{64,128},{128,192},{192,32},{32,96},{96,160},{160,224},{224... | collective-permute-start | bytes 393224 | tf_op jit(solution)/shard_map/ppermute | solution.py:209
  2.5 3.9 %collective-permute-start.1 = (bf16[32,2048]{1,0:T(8,128)(2,1)}, bf16[32,2048]{1,0:T(8,128)(2,1)S(1)}, u32[]{:S(2)}, u32[]{:S(2)}) collective-permute-start(bf16[32,2048]{1,0:T(8,128)(2,1)} %param.7), channel_id=1, source_target_pairs={{0,224},{64,0},{128,64},{192,128},{32,192},{96,32},{160,96},{224,1... | collective-permute-start | bytes 393224 | tf_op jit(solution)/shard_map/ppermute | solution.py:209
  7.4 1.2 %pad_maximum_fusion.1 = bf16[2,4,32,4,128]{4,3,2,1,0:T(4,128)(2,1)S(1)} fusion(bf16[1,4,32,4,128]{4,3,2,1,0:T(4,128)(2,1)} %bitcast.99, bf16[1,4,32,4,128]{4,3,2,1,0:T(4,128)(2,1)} %bitcast.100), kind=kLoop, calls=%fused_computation.7 | loop fusion | flops 131072 | bytes 524288 | tf_op jit(solution)/shard_map/stack | solution.py:203
  9.8 2.7 %collective-permute-start.4 = (bf16[32,2048]{1,0:T(8,128)(2,1)S(1)}, bf16[32,2048]{1,0:T(8,128)(2,1)S(1)}, u32[]{:S(2)}, u32[]{:S(2)}) collective-permute-start(bf16[32,2048]{1,0:T(8,128)(2,1)S(1)} %collective-permute-done.1), channel_id=1, source_target_pairs={{0,224},{64,0},{128,64},{192,128},{32,192},{96,32},{160,96},{224,1... | collective-permute-start | bytes 393224 | tf_op jit(solution)/shard_map/ppermute | solution.py:209
  12.5 8.0 %all-to-all-start = ((bf16[32,2,16,128]{3,2,1,0:T(8,128)(2,1)}), bf16[32,2,16,128]{3,2,1,0:T(8,128)(2,1)S(1)}, u32[]{:S(2)}, u32[]{:S(2)}) async-start(bf16[32,2,16,128]{3,2,1,0:T(8,128)(2,1)} %bitcast.10), calls=%async_computation | async-start | bytes 524288 | tf_op jit(solution)/shard_map/all_to_all | solution.py:212
  20.6 1.3 %collective-permute-start.12 = (bf16[5,32,2048]{2,1,0:T(8,128)(2,1)S(1)}, bf16[5,32,2048]{2,1,0:T(8,128)(2,1)S(1)}, u32[]{:S(2)}, u32[]{:S(2)}) collective-permute-start(bf16[5,32,2048]{2,1,0:T(8,128)(2,1)S(1)} %bitcast_dynamic-update-slice_fusion.refs_0_), channel_id=1, source_target_pairs={{0,8},{8,16},{16,24},{24,0},{1,9},{9,17},{17,25},{25,1},{2,10},{10... | collective-permute-start | bytes 1966088 | tf_op jit(solution)/shard_map/ppermute | solution.py:182
  21.9 1.4 %collective-permute-start.13 = (bf16[5,32,2048]{2,1,0:T(8,128)(2,1)S(1)}, bf16[5,32,2048]{2,1,0:T(8,128)(2,1)S(1)}, u32[]{:S(2)}, u32[]{:S(2)}) collective-permute-start(bf16[5,32,2048]{2,1,0:T(8,128)(2,1)S(1)} %bitcast_dynamic-update-slice_fusion.refs_0_), channel_id=1, source_target_pairs={{0,24},{8,0},{16,8},{24,16},{1,25},{9,1},{17,9},{25,17},{2,26},{10... | collective-permute-start | bytes 1966088 | tf_op jit(solution)/shard_map/ppermute | solution.py:182
  23.4 1.2 %collective-permute-start.3 = (bf16[32,2048]{1,0:T(8,128)(2,1)S(1)}, bf16[32,2048]{1,0:T(8,128)(2,1)}, u32[]{:S(2)}, u32[]{:S(2)}) collective-permute-start(bf16[32,2048]{1,0:T(8,128)(2,1)S(1)} %collective-permute-done.2), channel_id=1, source_target_pairs={{0,64},{64,128},{128,192},{192,32},{32,96},{96,160},{160,224},{224... | collective-permute-start | bytes 393224 | tf_op jit(solution)/shard_map/ppermute | solution.py:216
  24.6 6.6 %all-to-all-done = bf16[32,2,16,128]{3,2,1,0:T(8,128)(2,1)S(1)} async-done(((bf16[32,2,16,128]{3,2,1,0:T(8,128)(2,1)}), bf16[32,2,16,128]{3,2,1,0:T(8,128)(2,1)S(1)}, u32[]{:S(2)}, u32[]{:S(2)}) %all-to-all-start) | async-done | bytes 262176 | tf_op jit(solution)/shard_map/all_to_all | solution.py:212
  31.2 2.7 %collective-permute-start.10 = (bf16[32,2,16,128]{3,2,1,0:T(8,128)(2,1)S(1)}, bf16[32,2,16,128]{3,2,1,0:T(8,128)(2,1)S(1)}, u32[]{:S(2)}, u32[]{:S(2)}) collective-permute-start(bf16[32,2,16,128]{3,2,1,0:T(8,128)(2,1)S(1)} %all-to-all-done), channel_id=1, source_target_pairs={{0,4},{2,6},{4,0},{6,2},{1,5},{3,7},{5,1},{7,3},{8,12},{10,14},{12... | collective-permute-start | bytes 786440 | tf_op jit(solution)/shard_map/ppermute | solution.py:215
  34.3 2.4 %collective-permute-start.9 = (bf16[32,2,16,128]{3,2,1,0:T(8,128)(2,1)S(1)}, bf16[32,2,16,128]{3,2,1,0:T(8,128)(2,1)S(1)}, u32[]{:S(2)}, u32[]{:S(2)}) collective-permute-start(bf16[32,2,16,128]{3,2,1,0:T(8,128)(2,1)S(1)} %all-to-all-done), channel_id=1, source_target_pairs={{0,6},{2,0},{4,2},{6,4},{1,7},{3,1},{5,3},{7,5},{8,14},{10,8},{12,... | collective-permute-start | bytes 786440 | tf_op jit(solution)/shard_map/ppermute | solution.py:215
  37.5 1.6 %bitcast_dynamic-update-slice_fusion.7 = bf16[3,32,2048]{2,1,0:T(8,128)(2,1)} fusion(bf16[3,32,2048]{2,1,0:T(8,128)(2,1)} %broadcast_in_dim.34, s32[]{:T(128)S(6)} %select_n.24, bf16[32,2048]{1,0:T(8,128)(2,1)} %collective-permute-done.3), kind=kLoop, calls=%fused_computation.15 | loop fusion | bytes 262148 | tf_op jit(solution)/shard_map/dynamic_update_slice | solution.py:196
  39.4 1.7 %collective-permute-done.11 = bf16[32,2,16,128]{3,2,1,0:T(8,128)(2,1)S(1)} collective-permute-done((bf16[32,2,16,128]{3,2,1,0:T(8,128)(2,1)S(1)}, bf16[32,2,16,128]{3,2,1,0:T(8,128)(2,1)S(1)}, u32[]{:S(2)}, u32[]{:S(2)}) %collective-permute-start.11) | collective-permute-done | bytes 262176 | tf_op jit(solution)/shard_map/ppermute | solution.py:215
  41.1 4.0 %collective-permute-start.6 = (bf16[32,2048]{1,0:T(8,128)(2,1)}, bf16[32,2048]{1,0:T(8,128)(2,1)S(1)}, u32[]{:S(2)}, u32[]{:S(2)}) collective-permute-start(bf16[32,2048]{1,0:T(8,128)(2,1)} %collective-permute-done.3), channel_id=1, source_target_pairs={{0,64},{64,128},{128,192},{192,32},{32,96},{96,160},{160,224},{224... | collective-permute-start | bytes 393224 | tf_op jit(solution)/shard_map/ppermute | solution.py:218
  46.1 3.2 %collective-permute-start.14 = (bf16[4,32,2,16,128]{4,3,2,1,0:T(8,128)(2,1)S(1)}, bf16[4,32,2,16,128]{4,3,2,1,0:T(8,128)(2,1)S(1)}, u32[]{:S(2)}, u32[]{:S(2)}) collective-permute-start(bf16[4,32,2,16,128]{4,3,2,1,0:T(8,128)(2,1)S(1)} %pad_maximum_fusion.refs_9_.refs_13_), channel_id=1, source_target_pairs={{0,1},{1,0},{2,3},{3,2},{4,5},{5,4},{6,7},{7,6},{8,9},{9,8},{10,11... | collective-permute-start | bytes 3145736 | tf_op jit(solution)/shard_map/ppermute | solution.py:222
  50.8 2.5 %collective-permute-start.8 = (bf16[3,32,2048]{2,1,0:T(8,128)(2,1)}, bf16[3,32,2048]{2,1,0:T(8,128)(2,1)}, u32[]{:S(2)}, u32[]{:S(2)}) collective-permute-start(bf16[3,32,2048]{2,1,0:T(8,128)(2,1)} %bitcast_dynamic-update-slice_fusion.5.refs_3_), channel_id=1, source_target_pairs={{0,24},{8,0},{16,8},{24,16},{1,25},{9,1},{17,9},{25,17},{2,26},{10... | collective-permute-start | bytes 1179656 | tf_op jit(solution)/shard_map/ppermute | solution.py:182
  53.6 1.0 %slice.31 = bf16[2,32,2048]{2,1,0:T(8,128)(2,1)S(1)} slice(bf16[5,32,2048]{2,1,0:T(8,128)(2,1)} %copy-done), slice={[3:5], [0:32], [0:2048]} | slice | bytes 524288 | tf_op jit(solution)/shard_map/slice | solution.py:187
  54.7 2.7 %collective-permute-start.16 = (bf16[2,32,2048]{2,1,0:T(8,128)(2,1)S(1)}, bf16[2,32,2048]{2,1,0:T(8,128)(2,1)S(1)}, u32[]{:S(2)}, u32[]{:S(2)}) collective-permute-start(bf16[2,32,2048]{2,1,0:T(8,128)(2,1)S(1)} %slice.31), channel_id=1, source_target_pairs={{0,24},{8,0},{16,8},{24,16},{1,25},{9,1},{17,9},{25,17},{2,26},{10... | collective-permute-start | bytes 786440 | tf_op jit(solution)/shard_map/ppermute | solution.py:187
  57.8 1.3 %copy.16 = bf16[12,8,16,128]{3,2,1,0:T(8,128)(2,1)S(1)} copy(bf16[12,8,16,128]{3,1,2,0:T(8,128)(2,1)} %bitcast.40) | data formatting | bytes 786432
  59.1 5.0 %ladder.2 = (f32[8,512,128]{2,1,0:T(8,128)S(1)}, bf16[2048,512]{1,0:T(8,128)(2,1)S(1)}) custom-call(s32[6]{0:T(128)S(1)} %stack.51.meta, s32[16,4]{1,0:T(8,128)S(1)} %copy.11.live, bf16[5,32,2048]{2,1,0:T(8,128)(2,1)S(1)} %bitcast_dynamic-update-slice_fusion.refs_0_, bf16[5,32,2048]{2,1,0:T(8,128)(2,1)S(1)} %collective-permute-done.12.refs_1_, ...), custom_call_target="tpu_custom_call" | custom-call | flops 1800000000 | bytes 10000000 | tf_op jit(solution)/shard_map/ladder/pallas_call | solution.py:131
  66.1 1.5 %collective-permute-start.17 = (bf16[1,32,2048]{2,1,0:T(8,128)(2,1)S(1)}, bf16[1,32,2048]{2,1,0:T(8,128)(2,1)S(1)}, u32[]{:S(2)}, u32[]{:S(2)}) collective-permute-start(bf16[1,32,2048]{2,1,0:T(8,128)(2,1)S(1)} %slice.32), channel_id=1, source_target_pairs={{0,8},{8,16},{16,24},{24,0},{1,9},{9,17},{17,25},{25,1},{2,10},{10... | collective-permute-start | bytes 393224 | tf_op jit(solution)/shard_map/ppermute | solution.py:186
  67.7 1.1 %copy.17 = bf16[12,8,16,128]{3,2,1,0:T(8,128)(2,1)S(1)} copy(bf16[12,8,16,128]{3,1,2,0:T(8,128)(2,1)} %bitcast.44) | data formatting | bytes 786432
  68.8 1.1 %copy.18 = bf16[12,8,16,128]{3,2,1,0:T(8,128)(2,1)S(1)} copy(bf16[12,8,16,128]{3,1,2,0:T(8,128)(2,1)} %bitcast.48) | data formatting | bytes 786432
  69.9 3.1 %collective-permute-done.17.refs_4_ = bf16[1,32,2048]{2,1,0:T(8,128)(2,1)S(1)} collective-permute-done((bf16[1,32,2048]{2,1,0:T(8,128)(2,1)S(1)}, bf16[1,32,2048]{2,1,0:T(8,128)(2,1)S(1)}, u32[]{:S(2)}, u32[]{:S(2)}) %collective-permute-start.17) | collective-permute-done | bytes 131104 | tf_op jit(solution)/shard_map/ppermute | solution.py:186
  73.0 4.0 %ladder.3 = (f32[4,512,128]{2,1,0:T(8,128)S(1)}, f32[4,512,128]{2,1,0:T(8,128)S(1)}) custom-call(s32[6]{0:T(128)S(1)} %stack.51.meta, s32[16,4]{1,0:T(8,128)S(1)} %copy.11.live, bf16[3,32,2048]{2,1,0:T(8,128)(2,1)} %collective-permute-done.7.refs_0_, bf16[3,32,2048]{2,1,0:T(8,128)(2,1)} %collective-permute-done.8.refs_1_, ...), custom_call_target="tpu_custom_call" | custom-call | flops 1400000000 | bytes 10000000 | tf_op jit(solution)/shard_map/ladder/pallas_call | solution.py:131
  77.1 4.9 %collective-permute-start.19 = (f32[4,512,128]{2,1,0:T(8,128)S(1)}, f32[4,512,128]{2,1,0:T(8,128)S(1)}, u32[]{:S(2)}, u32[]{:S(2)}) collective-permute-start(f32[4,512,128]{2,1,0:T(8,128)S(1)} %get-tuple-element.46), channel_id=1, source_target_pairs={{0,1},{1,0},{2,3},{3,2},{4,5},{5,4},{6,7},{7,6},{8,9},{9,8},{10,11... | collective-permute-start | bytes 3145736 | tf_op jit(solution)/shard_map/ppermute | solution.py:230
  81.9 2.3 %collective-permute-done.19.p1 = f32[4,512,128]{2,1,0:T(8,128)S(1)} collective-permute-done((f32[4,512,128]{2,1,0:T(8,128)S(1)}, f32[4,512,128]{2,1,0:T(8,128)S(1)}, u32[]{:S(2)}, u32[]{:S(2)}) %collective-permute-start.19) | collective-permute-done | bytes 1048608 | tf_op jit(solution)/shard_map/ppermute | solution.py:230
  84.3 1.4 %collective-permute-start.20 = (f32[512,128]{1,0:T(8,128)S(1)}, f32[512,128]{1,0:T(8,128)S(1)}, u32[]{:S(2)}, u32[]{:S(2)}) collective-permute-start(f32[512,128]{1,0:T(8,128)S(1)} %get-tuple-element.49), channel_id=1, source_target_pairs={{0,2},{2,4},{4,6},{6,0},{1,3},{3,5},{5,7},{7,1},{8,10},{10,12},{12... | collective-permute-start | bytes 786440 | tf_op jit(solution)/shard_map/ppermute | solution.py:233
  85.7 1.7 %collective-permute-start.21 = (f32[512,128]{1,0:T(8,128)S(1)}, f32[512,128]{1,0:T(8,128)S(1)}, u32[]{:S(2)}, u32[]{:S(2)}) collective-permute-start(f32[512,128]{1,0:T(8,128)S(1)} %get-tuple-element.48), channel_id=1, source_target_pairs={{0,4},{2,6},{4,0},{6,2},{1,5},{3,7},{5,1},{7,3},{8,12},{10,14},{12... | collective-permute-start | bytes 786440 | tf_op jit(solution)/shard_map/ppermute | solution.py:233
  88.3 4.8 %collective-permute-done.20.p2 = f32[512,128]{1,0:T(8,128)S(1)} collective-permute-done((f32[512,128]{1,0:T(8,128)S(1)}, f32[512,128]{1,0:T(8,128)S(1)}, u32[]{:S(2)}, u32[]{:S(2)}) %collective-permute-start.20) | collective-permute-done | bytes 262176 | tf_op jit(solution)/shard_map/ppermute | solution.py:233
  93.1 5.9 %collective-permute-done.21.p3 = f32[512,128]{1,0:T(8,128)S(1)} collective-permute-done((f32[512,128]{1,0:T(8,128)S(1)}, f32[512,128]{1,0:T(8,128)S(1)}, u32[]{:S(2)}, u32[]{:S(2)}) %collective-permute-start.21) | collective-permute-done | bytes 262176 | tf_op jit(solution)/shard_map/ppermute | solution.py:233
  99.8 2.6 %finish.1 = bf16[128,512]{1,0:T(8,128)(2,1)} custom-call(s32[6]{0:T(128)} %copy-done.4, f32[32]{0:T(128)} %occ.1, f32[128]{0:T(128)} %vir.1, f32[1,128]{1,0:T(1,128)} %bitcast.101, f32[4,512,128]{2,1,0:T(8,128)} %copy-done.2, f32[4,512,128]{2,1,0:T(8,128)} %copy-done.5, f32[512,128]{1,0:T(8,128)} %copy-done.6, f32[512,128]{1,0:T(8,128)} %copy-done.7, ...), custom_call_target="tpu_custom_call" | custom-call | flops 400000 | bytes 1500000 | tf_op jit(solution)/shard_map/finish/pallas_call | solution.py:164
  (69 shorter events, 10.9 us)
Async XLA Ops:
  0.0 9.8 %collective-permute-start = (bf16[32,2048]{1,0:T(8,128)(2,1)}, bf16[32,2048]{1,0:T(8,128)(2,1)S(1)}, u32[]{:S(2)}, u32[]{:S(2)}) collective-permute-start(bf16[32,2048]{1,0:T(8,128)(2,1)} %param.7), channel_id=1, source_target_pairs={{0,64},{64,128},{128,192},{192,32},{32,96},{96,160},{160,224},{224... | collective-permute-start | bytes 393224 | tf_op jit(solution)/shard_map/ppermute | solution.py:209
  2.5 7.4 %collective-permute-start.1 = (bf16[32,2048]{1,0:T(8,128)(2,1)}, bf16[32,2048]{1,0:T(8,128)(2,1)S(1)}, u32[]{:S(2)}, u32[]{:S(2)}) collective-permute-start(bf16[32,2048]{1,0:T(8,128)(2,1)} %param.7), channel_id=1, source_target_pairs={{0,224},{64,0},{128,64},{192,128},{32,192},{96,32},{160,96},{224,1... | collective-permute-start | bytes 393224 | tf_op jit(solution)/shard_map/ppermute | solution.py:209
  9.8 10.7 %collective-permute-start.2 = (bf16[32,2048]{1,0:T(8,128)(2,1)S(1)}, bf16[32,2048]{1,0:T(8,128)(2,1)S(1)}, u32[]{:S(2)}, u32[]{:S(2)}) collective-permute-start(bf16[32,2048]{1,0:T(8,128)(2,1)S(1)} %collective-permute-done), channel_id=1, source_target_pairs={{0,64},{64,128},{128,192},{192,32},{32,96},{96,160},{160,224},{224... | collective-permute-start | bytes 393224 | tf_op jit(solution)/shard_map/ppermute | solution.py:209
  9.8 10.8 %collective-permute-start.4 = (bf16[32,2048]{1,0:T(8,128)(2,1)S(1)}, bf16[32,2048]{1,0:T(8,128)(2,1)S(1)}, u32[]{:S(2)}, u32[]{:S(2)}) collective-permute-start(bf16[32,2048]{1,0:T(8,128)(2,1)S(1)} %collective-permute-done.1), channel_id=1, source_target_pairs={{0,224},{64,0},{128,64},{192,128},{32,192},{96,32},{160,96},{224,1... | collective-permute-start | bytes 393224 | tf_op jit(solution)/shard_map/ppermute | solution.py:209
  12.5 18.7 %all-to-all-start = ((bf16[32,2,16,128]{3,2,1,0:T(8,128)(2,1)}), bf16[32,2,16,128]{3,2,1,0:T(8,128)(2,1)S(1)}, u32[]{:S(2)}, u32[]{:S(2)}) async-start(bf16[32,2,16,128]{3,2,1,0:T(8,128)(2,1)} %bitcast.10), calls=%async_computation | async-start | bytes 524288 | tf_op jit(solution)/shard_map/all_to_all | solution.py:212
  20.5 32.8 %copy-start.9 = (s32[16,4]{0,1:T(4,128)S(1)}, s32[16,4]{0,1:T(4,128)}, u32[]{:S(2)}) copy-start(s32[16,4]{0,1:T(4,128)} %param.9) | copy-start | bytes 772
  20.6 24.5 %collective-permute-start.12 = (bf16[5,32,2048]{2,1,0:T(8,128)(2,1)S(1)}, bf16[5,32,2048]{2,1,0:T(8,128)(2,1)S(1)}, u32[]{:S(2)}, u32[]{:S(2)}) collective-permute-start(bf16[5,32,2048]{2,1,0:T(8,128)(2,1)S(1)} %bitcast_dynamic-update-slice_fusion.refs_0_), channel_id=1, source_target_pairs={{0,8},{8,16},{16,24},{24,0},{1,9},{9,17},{17,25},{25,1},{2,10},{10... | collective-permute-start | bytes 1966088 | tf_op jit(solution)/shard_map/ppermute | solution.py:182
  21.9 23.2 %collective-permute-start.13 = (bf16[5,32,2048]{2,1,0:T(8,128)(2,1)S(1)}, bf16[5,32,2048]{2,1,0:T(8,128)(2,1)S(1)}, u32[]{:S(2)}, u32[]{:S(2)}) collective-permute-start(bf16[5,32,2048]{2,1,0:T(8,128)(2,1)S(1)} %bitcast_dynamic-update-slice_fusion.refs_0_), channel_id=1, source_target_pairs={{0,24},{8,0},{16,8},{24,16},{1,25},{9,1},{17,9},{25,17},{2,26},{10... | collective-permute-start | bytes 1966088 | tf_op jit(solution)/shard_map/ppermute | solution.py:182
  23.4 10.9 %collective-permute-start.3 = (bf16[32,2048]{1,0:T(8,128)(2,1)S(1)}, bf16[32,2048]{1,0:T(8,128)(2,1)}, u32[]{:S(2)}, u32[]{:S(2)}) collective-permute-start(bf16[32,2048]{1,0:T(8,128)(2,1)S(1)} %collective-permute-done.2), channel_id=1, source_target_pairs={{0,64},{64,128},{128,192},{192,32},{32,96},{96,160},{160,224},{224... | collective-permute-start | bytes 393224 | tf_op jit(solution)/shard_map/ppermute | solution.py:216
  31.2 7.8 %collective-permute-start.10 = (bf16[32,2,16,128]{3,2,1,0:T(8,128)(2,1)S(1)}, bf16[32,2,16,128]{3,2,1,0:T(8,128)(2,1)S(1)}, u32[]{:S(2)}, u32[]{:S(2)}) collective-permute-start(bf16[32,2,16,128]{3,2,1,0:T(8,128)(2,1)S(1)} %all-to-all-done), channel_id=1, source_target_pairs={{0,4},{2,6},{4,0},{6,2},{1,5},{3,7},{5,1},{7,3},{8,12},{10,14},{12... | collective-permute-start | bytes 786440 | tf_op jit(solution)/shard_map/ppermute | solution.py:215
  34.0 7.1 %collective-permute-start.11 = (bf16[32,2,16,128]{3,2,1,0:T(8,128)(2,1)S(1)}, bf16[32,2,16,128]{3,2,1,0:T(8,128)(2,1)S(1)}, u32[]{:S(2)}, u32[]{:S(2)}) collective-permute-start(bf16[32,2,16,128]{3,2,1,0:T(8,128)(2,1)S(1)} %all-to-all-done), channel_id=1, source_target_pairs={{0,2},{2,4},{4,6},{6,0},{1,3},{3,5},{5,7},{7,1},{8,10},{10,12},{12... | collective-permute-start | bytes 786440 | tf_op jit(solution)/shard_map/ppermute | solution.py:215
  34.3 10.8 %collective-permute-start.9 = (bf16[32,2,16,128]{3,2,1,0:T(8,128)(2,1)S(1)}, bf16[32,2,16,128]{3,2,1,0:T(8,128)(2,1)S(1)}, u32[]{:S(2)}, u32[]{:S(2)}) collective-permute-start(bf16[32,2,16,128]{3,2,1,0:T(8,128)(2,1)S(1)} %all-to-all-done), channel_id=1, source_target_pairs={{0,6},{2,0},{4,2},{6,4},{1,7},{3,1},{5,3},{7,5},{8,14},{10,8},{12,... | collective-permute-start | bytes 786440 | tf_op jit(solution)/shard_map/ppermute | solution.py:215
  39.0 10.3 %collective-permute-start.5 = (bf16[32,2048]{1,0:T(8,128)(2,1)S(1)}, bf16[32,2048]{1,0:T(8,128)(2,1)S(1)}, u32[]{:S(2)}, u32[]{:S(2)}) collective-permute-start(bf16[32,2048]{1,0:T(8,128)(2,1)S(1)} %collective-permute-done.4), channel_id=1, source_target_pairs={{0,224},{64,0},{128,64},{192,128},{32,192},{96,32},{160,96},{224,1... | collective-permute-start | bytes 393224 | tf_op jit(solution)/shard_map/ppermute | solution.py:216
  41.1 8.9 %collective-permute-start.6 = (bf16[32,2048]{1,0:T(8,128)(2,1)}, bf16[32,2048]{1,0:T(8,128)(2,1)S(1)}, u32[]{:S(2)}, u32[]{:S(2)}) collective-permute-start(bf16[32,2048]{1,0:T(8,128)(2,1)} %collective-permute-done.3), channel_id=1, source_target_pairs={{0,64},{64,128},{128,192},{192,32},{32,96},{96,160},{160,224},{224... | collective-permute-start | bytes 393224 | tf_op jit(solution)/shard_map/ppermute | solution.py:218
  45.1 0.8 copy-start
  46.1 11.3 %collective-permute-start.14 = (bf16[4,32,2,16,128]{4,3,2,1,0:T(8,128)(2,1)S(1)}, bf16[4,32,2,16,128]{4,3,2,1,0:T(8,128)(2,1)S(1)}, u32[]{:S(2)}, u32[]{:S(2)}) collective-permute-start(bf16[4,32,2,16,128]{4,3,2,1,0:T(8,128)(2,1)S(1)} %pad_maximum_fusion.refs_9_.refs_13_), channel_id=1, source_target_pairs={{0,1},{1,0},{2,3},{3,2},{4,5},{5,4},{6,7},{7,6},{8,9},{9,8},{10,11... | collective-permute-start | bytes 3145736 | tf_op jit(solution)/shard_map/ppermute | solution.py:222
  50.7 13.4 %collective-permute-start.7 = (bf16[3,32,2048]{2,1,0:T(8,128)(2,1)}, bf16[3,32,2048]{2,1,0:T(8,128)(2,1)}, u32[]{:S(2)}, u32[]{:S(2)}) collective-permute-start(bf16[3,32,2048]{2,1,0:T(8,128)(2,1)} %bitcast_dynamic-update-slice_fusion.5.refs_3_), channel_id=1, source_target_pairs={{0,8},{8,16},{16,24},{24,0},{1,9},{9,17},{17,25},{25,1},{2,10},{10... | collective-permute-start | bytes 1179656 | tf_op jit(solution)/shard_map/ppermute | solution.py:182
  50.8 13.2 %collective-permute-start.8 = (bf16[3,32,2048]{2,1,0:T(8,128)(2,1)}, bf16[3,32,2048]{2,1,0:T(8,128)(2,1)}, u32[]{:S(2)}, u32[]{:S(2)}) collective-permute-start(bf16[3,32,2048]{2,1,0:T(8,128)(2,1)} %bitcast_dynamic-update-slice_fusion.5.refs_3_), channel_id=1, source_target_pairs={{0,24},{8,0},{16,8},{24,16},{1,25},{9,1},{17,9},{25,17},{2,26},{10... | collective-permute-start | bytes 1179656 | tf_op jit(solution)/shard_map/ppermute | solution.py:182
  53.5 19.5 %copy-start.4 = (s32[6]{0:T(128)}, s32[6]{0:T(128)S(1)}, u32[]{:S(2)}) copy-start(s32[6]{0:T(128)S(1)} %stack.51.meta) | copy-start | bytes 76
  53.5 4.1 %copy-start.1 = (bf16[5,32,2048]{2,1,0:T(8,128)(2,1)S(1)}, bf16[5,32,2048]{2,1,0:T(8,128)(2,1)}, u32[]{:S(2)}) copy-start(bf16[5,32,2048]{2,1,0:T(8,128)(2,1)} %copy-done) | copy-start | bytes 1966084
  53.5 14.1 %collective-permute-start.15 = (bf16[3,32,2048]{2,1,0:T(8,128)(2,1)S(1)}, bf16[3,32,2048]{2,1,0:T(8,128)(2,1)S(1)}, u32[]{:S(2)}, u32[]{:S(2)}) collective-permute-start(bf16[3,32,2048]{2,1,0:T(8,128)(2,1)S(1)} %slice.30), channel_id=1, source_target_pairs={{0,8},{8,16},{16,24},{24,0},{1,9},{9,17},{17,25},{25,1},{2,10},{10... | collective-permute-start | bytes 1179656 | tf_op jit(solution)/shard_map/ppermute | solution.py:186
  54.7 12.9 %collective-permute-start.16 = (bf16[2,32,2048]{2,1,0:T(8,128)(2,1)S(1)}, bf16[2,32,2048]{2,1,0:T(8,128)(2,1)S(1)}, u32[]{:S(2)}, u32[]{:S(2)}) collective-permute-start(bf16[2,32,2048]{2,1,0:T(8,128)(2,1)S(1)} %slice.31), channel_id=1, source_target_pairs={{0,24},{8,0},{16,8},{24,16},{1,25},{9,1},{17,9},{25,17},{2,26},{10... | collective-permute-start | bytes 786440 | tf_op jit(solution)/shard_map/ppermute | solution.py:187
  57.3 1.7 %copy-start.3 = (bf16[2048,512]{1,0:T(8,128)(2,1)S(1)}, bf16[2048,512]{1,0:T(8,128)(2,1)}, u32[]{:S(2)}) copy-start(bf16[2048,512]{1,0:T(8,128)(2,1)} %refs_8_.1) | copy-start | bytes 6291460
  65.1 7.9 %collective-permute-start.18 = (bf16[2,32,2048]{2,1,0:T(8,128)(2,1)S(1)}, bf16[2,32,2048]{2,1,0:T(8,128)(2,1)S(1)}, u32[]{:S(2)}, u32[]{:S(2)}) collective-permute-start(bf16[2,32,2048]{2,1,0:T(8,128)(2,1)S(1)} %slice.33), channel_id=1, source_target_pairs={{0,24},{8,0},{16,8},{24,16},{1,25},{9,1},{17,9},{25,17},{2,26},{10... | collective-permute-start | bytes 786440 | tf_op jit(solution)/shard_map/ppermute | solution.py:187
  66.1 6.9 %collective-permute-start.17 = (bf16[1,32,2048]{2,1,0:T(8,128)(2,1)S(1)}, bf16[1,32,2048]{2,1,0:T(8,128)(2,1)S(1)}, u32[]{:S(2)}, u32[]{:S(2)}) collective-permute-start(bf16[1,32,2048]{2,1,0:T(8,128)(2,1)S(1)} %slice.32), channel_id=1, source_target_pairs={{0,8},{8,16},{16,24},{24,0},{1,9},{9,17},{17,25},{25,1},{2,10},{10... | collective-permute-start | bytes 393224 | tf_op jit(solution)/shard_map/ppermute | solution.py:186
  77.0 7.2 %copy-start.2 = (f32[4,512,128]{2,1,0:T(8,128)}, f32[4,512,128]{2,1,0:T(8,128)S(1)}, u32[]{:S(2)}) copy-start(f32[4,512,128]{2,1,0:T(8,128)S(1)} %get-tuple-element.45.p0) | copy-start | bytes 3145732
  77.1 7.1 %collective-permute-start.19 = (f32[4,512,128]{2,1,0:T(8,128)S(1)}, f32[4,512,128]{2,1,0:T(8,128)S(1)}, u32[]{:S(2)}, u32[]{:S(2)}) collective-permute-start(f32[4,512,128]{2,1,0:T(8,128)S(1)} %get-tuple-element.46), channel_id=1, source_target_pairs={{0,1},{1,0},{2,3},{3,2},{4,5},{5,4},{6,7},{7,6},{8,9},{9,8},{10,11... | collective-permute-start | bytes 3145736 | tf_op jit(solution)/shard_map/ppermute | solution.py:230
  84.2 14.8 %copy-start.5 = (f32[4,512,128]{2,1,0:T(8,128)}, f32[4,512,128]{2,1,0:T(8,128)S(1)}, u32[]{:S(2)}) copy-start(f32[4,512,128]{2,1,0:T(8,128)S(1)} %collective-permute-done.19.p1) | copy-start | bytes 3145732
  84.3 8.8 %collective-permute-start.20 = (f32[512,128]{1,0:T(8,128)S(1)}, f32[512,128]{1,0:T(8,128)S(1)}, u32[]{:S(2)}, u32[]{:S(2)}) collective-permute-start(f32[512,128]{1,0:T(8,128)S(1)} %get-tuple-element.49), channel_id=1, source_target_pairs={{0,2},{2,4},{4,6},{6,0},{1,3},{3,5},{5,7},{7,1},{8,10},{10,12},{12... | collective-permute-start | bytes 786440 | tf_op jit(solution)/shard_map/ppermute | solution.py:233
  85.7 13.3 %collective-permute-start.21 = (f32[512,128]{1,0:T(8,128)S(1)}, f32[512,128]{1,0:T(8,128)S(1)}, u32[]{:S(2)}, u32[]{:S(2)}) collective-permute-start(f32[512,128]{1,0:T(8,128)S(1)} %get-tuple-element.48), channel_id=1, source_target_pairs={{0,4},{2,6},{4,0},{6,2},{1,5},{3,7},{5,1},{7,3},{8,12},{10,14},{12... | collective-permute-start | bytes 786440 | tf_op jit(solution)/shard_map/ppermute | solution.py:233
  87.4 11.7 %collective-permute-start.22 = (f32[512,128]{1,0:T(8,128)S(1)}, f32[512,128]{1,0:T(8,128)S(1)}, u32[]{:S(2)}, u32[]{:S(2)}) collective-permute-start(f32[512,128]{1,0:T(8,128)S(1)} %get-tuple-element.47), channel_id=1, source_target_pairs={{0,6},{2,0},{4,2},{6,4},{1,7},{3,1},{5,3},{7,5},{8,14},{10,8},{12,... | collective-permute-start | bytes 786440 | tf_op jit(solution)/shard_map/ppermute | solution.py:233
  93.1 6.0 %copy-start.6 = (f32[512,128]{1,0:T(8,128)}, f32[512,128]{1,0:T(8,128)S(1)}, u32[]{:S(2)}) copy-start(f32[512,128]{1,0:T(8,128)S(1)} %collective-permute-done.20.p2) | copy-start | bytes 786436
  (2 other events, 1.5 us)

commit v11 on v10

--- a/solution.py
+++ b/solution.py
@@ -164,7 +164,8 @@
     return pl.pallas_call(
         finish_kernel,
         out_shape=jax.ShapeDtypeStruct((128, 512), BF16),
-        in_specs=[smem] * 3 + [vmem] * 6,
+        grid=(1,),
+        in_specs=[smem] * 3 + [vmem] + [pl.BlockSpec((1, 512, 128), lambda n: (0, 0, 0))] * 2 + [vmem] * 3,
         out_specs=vmem,
         scratch_shapes=[pltpu.VMEM((512, 128), F32)],
         cost_estimate=pl.CostEstimate(flops=400_000, bytes_accessed=1_500_000, transcendentals=0),

time: 103 us -> 103 us (level)
  no operation moved by 1% of the time
where the time goes in v11:
time: 103 us; the launch traced here: 102 us
  starting transfers between devices  50 us (49%)
  waiting for transfers between devices  24.9 us (24%)
  local copies, waits for them, and re-layouts  14.2 us (14%)
  Pallas kernels  11.1 us (11%)
  other arithmetic  1.38 us (1%)
    ppermute x3, waiting for transfers between devices, local(): parts.append(lax.ppermute(keep[s] + got[s], 'x', shift(4, s)))  10.7 us
    pallas_call x2, Pallas kernels, ladder_call(): pl.pallas_call(functools.partial(ladder_kernel, pieces), out_shape=(half,...  9.01 us
    all_to_all x1, starting transfers between devices, local(): both = lax.all_to_all(both, G, 0, 0, tiled=True)  7.98 us
    ppermute x3, starting transfers between devices, local(): lax.ppermute(bwd, Z, z_shift(-1))  6.95 us
    all_to_all x1, waiting for transfers between devices, local(): both = lax.all_to_all(both, G, 0, 0, tiled=True)  6.62 us
    unnamed x31, local copies, waits for them, and re-layouts  5.67 us
    ppermute x3, starting transfers between devices, local(): xs = [both] + [lax.ppermute(both, 'x', shift(4, -s)) for s in (1, 2, 3)]  5.42 us
    ppermute x1, starting transfers between devices, local(): got = lax.ppermute(away, 'core', shift(2, 1))  4.85 us
  transfers between devices with their start and end apart: 24, of which 7 were waited for; matrix products, arithmetic and copies ran while one was open for 14% of the time, Pallas kernels for 5%

profile of v11, /device:TPU:1, one launch (start us, length us, event | category | flops | bytes accessed | tf_op | source)
XLA Modules:
  0.0 102.0 jit_solution(11259587242014398643)
XLA Ops:
  0.0 2.5 %collective-permute-start = (bf16[32,2048]{1,0:T(8,128)(2,1)}, bf16[32,2048]{1,0:T(8,128)(2,1)S(1)}, u32[]{:S(2)}, u32[]{:S(2)}) collective-permute-start(bf16[32,2048]{1,0:T(8,128)(2,1)} %param.7), channel_id=1, source_target_pairs={{0,64},{64,128},{128,192},{192,32},{32,96},{96,160},{160,224},{224... | collective-permute-start | bytes 393224 | tf_op jit(solution)/shard_map/ppermute | solution.py:210
  2.5 3.9 %collective-permute-start.1 = (bf16[32,2048]{1,0:T(8,128)(2,1)}, bf16[32,2048]{1,0:T(8,128)(2,1)S(1)}, u32[]{:S(2)}, u32[]{:S(2)}) collective-permute-start(bf16[32,2048]{1,0:T(8,128)(2,1)} %param.7), channel_id=1, source_target_pairs={{0,224},{64,0},{128,64},{192,128},{32,192},{96,32},{160,96},{224,1... | collective-permute-start | bytes 393224 | tf_op jit(solution)/shard_map/ppermute | solution.py:210
  7.4 1.2 %pad_maximum_fusion.1 = bf16[2,4,32,4,128]{4,3,2,1,0:T(4,128)(2,1)S(1)} fusion(bf16[1,4,32,4,128]{4,3,2,1,0:T(4,128)(2,1)} %bitcast.99, bf16[1,4,32,4,128]{4,3,2,1,0:T(4,128)(2,1)} %bitcast.100), kind=kLoop, calls=%fused_computation.7 | loop fusion | flops 131072 | bytes 524288 | tf_op jit(solution)/shard_map/stack | solution.py:204
  9.8 2.7 %collective-permute-start.4 = (bf16[32,2048]{1,0:T(8,128)(2,1)S(1)}, bf16[32,2048]{1,0:T(8,128)(2,1)S(1)}, u32[]{:S(2)}, u32[]{:S(2)}) collective-permute-start(bf16[32,2048]{1,0:T(8,128)(2,1)S(1)} %collective-permute-done.1), channel_id=1, source_target_pairs={{0,224},{64,0},{128,64},{192,128},{32,192},{96,32},{160,96},{224,1... | collective-permute-start | bytes 393224 | tf_op jit(solution)/shard_map/ppermute | solution.py:210
  12.5 8.0 %all-to-all-start = ((bf16[32,2,16,128]{3,2,1,0:T(8,128)(2,1)}), bf16[32,2,16,128]{3,2,1,0:T(8,128)(2,1)S(1)}, u32[]{:S(2)}, u32[]{:S(2)}) async-start(bf16[32,2,16,128]{3,2,1,0:T(8,128)(2,1)} %bitcast.10), calls=%async_computation | async-start | bytes 524288 | tf_op jit(solution)/shard_map/all_to_all | solution.py:213
  20.6 1.3 %collective-permute-start.12 = (bf16[5,32,2048]{2,1,0:T(8,128)(2,1)S(1)}, bf16[5,32,2048]{2,1,0:T(8,128)(2,1)S(1)}, u32[]{:S(2)}, u32[]{:S(2)}) collective-permute-start(bf16[5,32,2048]{2,1,0:T(8,128)(2,1)S(1)} %bitcast_dynamic-update-slice_fusion.refs_0_), channel_id=1, source_target_pairs={{0,8},{8,16},{16,24},{24,0},{1,9},{9,17},{17,25},{25,1},{2,10},{10... | collective-permute-start | bytes 1966088 | tf_op jit(solution)/shard_map/ppermute | solution.py:183
  21.9 1.4 %collective-permute-start.13 = (bf16[5,32,2048]{2,1,0:T(8,128)(2,1)S(1)}, bf16[5,32,2048]{2,1,0:T(8,128)(2,1)S(1)}, u32[]{:S(2)}, u32[]{:S(2)}) collective-permute-start(bf16[5,32,2048]{2,1,0:T(8,128)(2,1)S(1)} %bitcast_dynamic-update-slice_fusion.refs_0_), channel_id=1, source_target_pairs={{0,24},{8,0},{16,8},{24,16},{1,25},{9,1},{17,9},{25,17},{2,26},{10... | collective-permute-start | bytes 1966088 | tf_op jit(solution)/shard_map/ppermute | solution.py:183
  23.4 1.2 %collective-permute-start.3 = (bf16[32,2048]{1,0:T(8,128)(2,1)S(1)}, bf16[32,2048]{1,0:T(8,128)(2,1)}, u32[]{:S(2)}, u32[]{:S(2)}) collective-permute-start(bf16[32,2048]{1,0:T(8,128)(2,1)S(1)} %collective-permute-done.2), channel_id=1, source_target_pairs={{0,64},{64,128},{128,192},{192,32},{32,96},{96,160},{160,224},{224... | collective-permute-start | bytes 393224 | tf_op jit(solution)/shard_map/ppermute | solution.py:217
  24.6 6.6 %all-to-all-done = bf16[32,2,16,128]{3,2,1,0:T(8,128)(2,1)S(1)} async-done(((bf16[32,2,16,128]{3,2,1,0:T(8,128)(2,1)}), bf16[32,2,16,128]{3,2,1,0:T(8,128)(2,1)S(1)}, u32[]{:S(2)}, u32[]{:S(2)}) %all-to-all-start) | async-done | bytes 262176 | tf_op jit(solution)/shard_map/all_to_all | solution.py:213
  31.2 2.7 %collective-permute-start.10 = (bf16[32,2,16,128]{3,2,1,0:T(8,128)(2,1)S(1)}, bf16[32,2,16,128]{3,2,1,0:T(8,128)(2,1)S(1)}, u32[]{:S(2)}, u32[]{:S(2)}) collective-permute-start(bf16[32,2,16,128]{3,2,1,0:T(8,128)(2,1)S(1)} %all-to-all-done), channel_id=1, source_target_pairs={{0,4},{2,6},{4,0},{6,2},{1,5},{3,7},{5,1},{7,3},{8,12},{10,14},{12... | collective-permute-start | bytes 786440 | tf_op jit(solution)/shard_map/ppermute | solution.py:216
  34.3 2.4 %collective-permute-start.9 = (bf16[32,2,16,128]{3,2,1,0:T(8,128)(2,1)S(1)}, bf16[32,2,16,128]{3,2,1,0:T(8,128)(2,1)S(1)}, u32[]{:S(2)}, u32[]{:S(2)}) collective-permute-start(bf16[32,2,16,128]{3,2,1,0:T(8,128)(2,1)S(1)} %all-to-all-done), channel_id=1, source_target_pairs={{0,6},{2,0},{4,2},{6,4},{1,7},{3,1},{5,3},{7,5},{8,14},{10,8},{12,... | collective-permute-start | bytes 786440 | tf_op jit(solution)/shard_map/ppermute | solution.py:216
  37.5 1.6 %bitcast_dynamic-update-slice_fusion.7 = bf16[3,32,2048]{2,1,0:T(8,128)(2,1)} fusion(bf16[3,32,2048]{2,1,0:T(8,128)(2,1)} %broadcast_in_dim.34, s32[]{:T(128)S(6)} %select_n.24, bf16[32,2048]{1,0:T(8,128)(2,1)} %collective-permute-done.3), kind=kLoop, calls=%fused_computation.15 | loop fusion | bytes 262148 | tf_op jit(solution)/shard_map/dynamic_update_slice | solution.py:197
  39.4 1.7 %collective-permute-done.11 = bf16[32,2,16,128]{3,2,1,0:T(8,128)(2,1)S(1)} collective-permute-done((bf16[32,2,16,128]{3,2,1,0:T(8,128)(2,1)S(1)}, bf16[32,2,16,128]{3,2,1,0:T(8,128)(2,1)S(1)}, u32[]{:S(2)}, u32[]{:S(2)}) %collective-permute-start.11) | collective-permute-done | bytes 262176 | tf_op jit(solution)/shard_map/ppermute | solution.py:216
  41.1 4.0 %collective-permute-start.6 = (bf16[32,2048]{1,0:T(8,128)(2,1)}, bf16[32,2048]{1,0:T(8,128)(2,1)S(1)}, u32[]{:S(2)}, u32[]{:S(2)}) collective-permute-start(bf16[32,2048]{1,0:T(8,128)(2,1)} %collective-permute-done.3), channel_id=1, source_target_pairs={{0,64},{64,128},{128,192},{192,32},{32,96},{96,160},{160,224},{224... | collective-permute-start | bytes 393224 | tf_op jit(solution)/shard_map/ppermute | solution.py:219
  46.1 3.2 %collective-permute-start.14 = (bf16[4,32,2,16,128]{4,3,2,1,0:T(8,128)(2,1)S(1)}, bf16[4,32,2,16,128]{4,3,2,1,0:T(8,128)(2,1)S(1)}, u32[]{:S(2)}, u32[]{:S(2)}) collective-permute-start(bf16[4,32,2,16,128]{4,3,2,1,0:T(8,128)(2,1)S(1)} %pad_maximum_fusion.refs_9_.refs_13_), channel_id=1, source_target_pairs={{0,1},{1,0},{2,3},{3,2},{4,5},{5,4},{6,7},{7,6},{8,9},{9,8},{10,11... | collective-permute-start | bytes 3145736 | tf_op jit(solution)/shard_map/ppermute | solution.py:223
  50.8 2.5 %collective-permute-start.8 = (bf16[3,32,2048]{2,1,0:T(8,128)(2,1)}, bf16[3,32,2048]{2,1,0:T(8,128)(2,1)}, u32[]{:S(2)}, u32[]{:S(2)}) collective-permute-start(bf16[3,32,2048]{2,1,0:T(8,128)(2,1)} %bitcast_dynamic-update-slice_fusion.5.refs_3_), channel_id=1, source_target_pairs={{0,24},{8,0},{16,8},{24,16},{1,25},{9,1},{17,9},{25,17},{2,26},{10... | collective-permute-start | bytes 1179656 | tf_op jit(solution)/shard_map/ppermute | solution.py:183
  53.6 1.0 %slice.31 = bf16[2,32,2048]{2,1,0:T(8,128)(2,1)S(1)} slice(bf16[5,32,2048]{2,1,0:T(8,128)(2,1)} %copy-done), slice={[3:5], [0:32], [0:2048]} | slice | bytes 524288 | tf_op jit(solution)/shard_map/slice | solution.py:188
  54.7 2.7 %collective-permute-start.16 = (bf16[2,32,2048]{2,1,0:T(8,128)(2,1)S(1)}, bf16[2,32,2048]{2,1,0:T(8,128)(2,1)S(1)}, u32[]{:S(2)}, u32[]{:S(2)}) collective-permute-start(bf16[2,32,2048]{2,1,0:T(8,128)(2,1)S(1)} %slice.31), channel_id=1, source_target_pairs={{0,24},{8,0},{16,8},{24,16},{1,25},{9,1},{17,9},{25,17},{2,26},{10... | collective-permute-start | bytes 786440 | tf_op jit(solution)/shard_map/ppermute | solution.py:188
  57.8 1.3 %copy.16 = bf16[12,8,16,128]{3,2,1,0:T(8,128)(2,1)S(1)} copy(bf16[12,8,16,128]{3,1,2,0:T(8,128)(2,1)} %bitcast.40) | data formatting | bytes 786432
  59.1 5.0 %ladder.2 = (f32[8,512,128]{2,1,0:T(8,128)S(1)}, bf16[2048,512]{1,0:T(8,128)(2,1)S(1)}) custom-call(s32[6]{0:T(128)S(1)} %stack.51.meta, s32[16,4]{1,0:T(8,128)S(1)} %copy.11.live, bf16[5,32,2048]{2,1,0:T(8,128)(2,1)S(1)} %bitcast_dynamic-update-slice_fusion.refs_0_, bf16[5,32,2048]{2,1,0:T(8,128)(2,1)S(1)} %collective-permute-done.12.refs_1_, ...), custom_call_target="tpu_custom_call" | custom-call | flops 1800000000 | bytes 10000000 | tf_op jit(solution)/shard_map/ladder/pallas_call | solution.py:131
  66.1 1.5 %collective-permute-start.17 = (bf16[1,32,2048]{2,1,0:T(8,128)(2,1)S(1)}, bf16[1,32,2048]{2,1,0:T(8,128)(2,1)S(1)}, u32[]{:S(2)}, u32[]{:S(2)}) collective-permute-start(bf16[1,32,2048]{2,1,0:T(8,128)(2,1)S(1)} %slice.32), channel_id=1, source_target_pairs={{0,8},{8,16},{16,24},{24,0},{1,9},{9,17},{17,25},{25,1},{2,10},{10... | collective-permute-start | bytes 393224 | tf_op jit(solution)/shard_map/ppermute | solution.py:187
  67.7 1.1 %copy.17 = bf16[12,8,16,128]{3,2,1,0:T(8,128)(2,1)S(1)} copy(bf16[12,8,16,128]{3,1,2,0:T(8,128)(2,1)} %bitcast.44) | data formatting | bytes 786432
  68.8 1.1 %copy.18 = bf16[12,8,16,128]{3,2,1,0:T(8,128)(2,1)S(1)} copy(bf16[12,8,16,128]{3,1,2,0:T(8,128)(2,1)} %bitcast.48) | data formatting | bytes 786432
  69.9 3.1 %collective-permute-done.17.refs_4_ = bf16[1,32,2048]{2,1,0:T(8,128)(2,1)S(1)} collective-permute-done((bf16[1,32,2048]{2,1,0:T(8,128)(2,1)S(1)}, bf16[1,32,2048]{2,1,0:T(8,128)(2,1)S(1)}, u32[]{:S(2)}, u32[]{:S(2)}) %collective-permute-start.17) | collective-permute-done | bytes 131104 | tf_op jit(solution)/shard_map/ppermute | solution.py:187
  73.0 4.0 %ladder.3 = (f32[4,512,128]{2,1,0:T(8,128)S(1)}, f32[4,512,128]{2,1,0:T(8,128)S(1)}) custom-call(s32[6]{0:T(128)S(1)} %stack.51.meta, s32[16,4]{1,0:T(8,128)S(1)} %copy.11.live, bf16[3,32,2048]{2,1,0:T(8,128)(2,1)} %collective-permute-done.7.refs_0_, bf16[3,32,2048]{2,1,0:T(8,128)(2,1)} %collective-permute-done.8.refs_1_, ...), custom_call_target="tpu_custom_call" | custom-call | flops 1400000000 | bytes 10000000 | tf_op jit(solution)/shard_map/ladder/pallas_call | solution.py:131
  77.1 4.9 %collective-permute-start.19 = (f32[4,512,128]{2,1,0:T(8,128)S(1)}, f32[4,512,128]{2,1,0:T(8,128)S(1)}, u32[]{:S(2)}, u32[]{:S(2)}) collective-permute-start(f32[4,512,128]{2,1,0:T(8,128)S(1)} %get-tuple-element.46), channel_id=1, source_target_pairs={{0,1},{1,0},{2,3},{3,2},{4,5},{5,4},{6,7},{7,6},{8,9},{9,8},{10,11... | collective-permute-start | bytes 3145736 | tf_op jit(solution)/shard_map/ppermute | solution.py:231
  81.9 2.3 %collective-permute-done.19.p1 = f32[4,512,128]{2,1,0:T(8,128)S(1)} collective-permute-done((f32[4,512,128]{2,1,0:T(8,128)S(1)}, f32[4,512,128]{2,1,0:T(8,128)S(1)}, u32[]{:S(2)}, u32[]{:S(2)}) %collective-permute-start.19) | collective-permute-done | bytes 1048608 | tf_op jit(solution)/shard_map/ppermute | solution.py:231
  84.3 1.4 %collective-permute-start.20 = (f32[512,128]{1,0:T(8,128)S(1)}, f32[512,128]{1,0:T(8,128)S(1)}, u32[]{:S(2)}, u32[]{:S(2)}) collective-permute-start(f32[512,128]{1,0:T(8,128)S(1)} %get-tuple-element.49), channel_id=1, source_target_pairs={{0,2},{2,4},{4,6},{6,0},{1,3},{3,5},{5,7},{7,1},{8,10},{10,12},{12... | collective-permute-start | bytes 786440 | tf_op jit(solution)/shard_map/ppermute | solution.py:234
  85.7 1.7 %collective-permute-start.21 = (f32[512,128]{1,0:T(8,128)S(1)}, f32[512,128]{1,0:T(8,128)S(1)}, u32[]{:S(2)}, u32[]{:S(2)}) collective-permute-start(f32[512,128]{1,0:T(8,128)S(1)} %get-tuple-element.48), channel_id=1, source_target_pairs={{0,4},{2,6},{4,0},{6,2},{1,5},{3,7},{5,1},{7,3},{8,12},{10,14},{12... | collective-permute-start | bytes 786440 | tf_op jit(solution)/shard_map/ppermute | solution.py:234
  88.3 4.8 %collective-permute-done.20.p2 = f32[512,128]{1,0:T(8,128)S(1)} collective-permute-done((f32[512,128]{1,0:T(8,128)S(1)}, f32[512,128]{1,0:T(8,128)S(1)}, u32[]{:S(2)}, u32[]{:S(2)}) %collective-permute-start.20) | collective-permute-done | bytes 262176 | tf_op jit(solution)/shard_map/ppermute | solution.py:234
  93.1 5.9 %collective-permute-done.21.p3 = f32[512,128]{1,0:T(8,128)S(1)} collective-permute-done((f32[512,128]{1,0:T(8,128)S(1)}, f32[512,128]{1,0:T(8,128)S(1)}, u32[]{:S(2)}, u32[]{:S(2)}) %collective-permute-start.21) | collective-permute-done | bytes 262176 | tf_op jit(solution)/shard_map/ppermute | solution.py:234
  99.8 2.1 %finish.1 = bf16[128,512]{1,0:T(8,128)(2,1)} custom-call(s32[6]{0:T(128)} %copy-done.4, f32[32]{0:T(128)} %occ.1, f32[128]{0:T(128)} %vir.1, f32[1,128]{1,0:T(1,128)} %bitcast.101, f32[4,512,128]{2,1,0:T(8,128)} %copy-done.2, f32[4,512,128]{2,1,0:T(8,128)} %copy-done.5, f32[512,128]{1,0:T(8,128)} %copy-done.6, f32[512,128]{1,0:T(8,128)} %copy-done.7, ...), custom_call_target="tpu_custom_call" | custom-call | flops 400000 | bytes 1500000 | tf_op jit(solution)/shard_map/finish/pallas_call | solution.py:164
  (69 shorter events, 10.9 us)
Async XLA Ops:
  0.0 9.8 %collective-permute-start = (bf16[32,2048]{1,0:T(8,128)(2,1)}, bf16[32,2048]{1,0:T(8,128)(2,1)S(1)}, u32[]{:S(2)}, u32[]{:S(2)}) collective-permute-start(bf16[32,2048]{1,0:T(8,128)(2,1)} %param.7), channel_id=1, source_target_pairs={{0,64},{64,128},{128,192},{192,32},{32,96},{96,160},{160,224},{224... | collective-permute-start | bytes 393224 | tf_op jit(solution)/shard_map/ppermute | solution.py:210
  2.5 7.4 %collective-permute-start.1 = (bf16[32,2048]{1,0:T(8,128)(2,1)}, bf16[32,2048]{1,0:T(8,128)(2,1)S(1)}, u32[]{:S(2)}, u32[]{:S(2)}) collective-permute-start(bf16[32,2048]{1,0:T(8,128)(2,1)} %param.7), channel_id=1, source_target_pairs={{0,224},{64,0},{128,64},{192,128},{32,192},{96,32},{160,96},{224,1... | collective-permute-start | bytes 393224 | tf_op jit(solution)/shard_map/ppermute | solution.py:210
  9.8 10.7 %collective-permute-start.2 = (bf16[32,2048]{1,0:T(8,128)(2,1)S(1)}, bf16[32,2048]{1,0:T(8,128)(2,1)S(1)}, u32[]{:S(2)}, u32[]{:S(2)}) collective-permute-start(bf16[32,2048]{1,0:T(8,128)(2,1)S(1)} %collective-permute-done), channel_id=1, source_target_pairs={{0,64},{64,128},{128,192},{192,32},{32,96},{96,160},{160,224},{224... | collective-permute-start | bytes 393224 | tf_op jit(solution)/shard_map/ppermute | solution.py:210
  9.8 10.8 %collective-permute-start.4 = (bf16[32,2048]{1,0:T(8,128)(2,1)S(1)}, bf16[32,2048]{1,0:T(8,128)(2,1)S(1)}, u32[]{:S(2)}, u32[]{:S(2)}) collective-permute-start(bf16[32,2048]{1,0:T(8,128)(2,1)S(1)} %collective-permute-done.1), channel_id=1, source_target_pairs={{0,224},{64,0},{128,64},{192,128},{32,192},{96,32},{160,96},{224,1... | collective-permute-start | bytes 393224 | tf_op jit(solution)/shard_map/ppermute | solution.py:210
  12.5 18.7 %all-to-all-start = ((bf16[32,2,16,128]{3,2,1,0:T(8,128)(2,1)}), bf16[32,2,16,128]{3,2,1,0:T(8,128)(2,1)S(1)}, u32[]{:S(2)}, u32[]{:S(2)}) async-start(bf16[32,2,16,128]{3,2,1,0:T(8,128)(2,1)} %bitcast.10), calls=%async_computation | async-start | bytes 524288 | tf_op jit(solution)/shard_map/all_to_all | solution.py:213
  20.5 32.8 %copy-start.9 = (s32[16,4]{0,1:T(4,128)S(1)}, s32[16,4]{0,1:T(4,128)}, u32[]{:S(2)}) copy-start(s32[16,4]{0,1:T(4,128)} %param.9) | copy-start | bytes 772
  20.6 24.5 %collective-permute-start.12 = (bf16[5,32,2048]{2,1,0:T(8,128)(2,1)S(1)}, bf16[5,32,2048]{2,1,0:T(8,128)(2,1)S(1)}, u32[]{:S(2)}, u32[]{:S(2)}) collective-permute-start(bf16[5,32,2048]{2,1,0:T(8,128)(2,1)S(1)} %bitcast_dynamic-update-slice_fusion.refs_0_), channel_id=1, source_target_pairs={{0,8},{8,16},{16,24},{24,0},{1,9},{9,17},{17,25},{25,1},{2,10},{10... | collective-permute-start | bytes 1966088 | tf_op jit(solution)/shard_map/ppermute | solution.py:183
  21.9 23.2 %collective-permute-start.13 = (bf16[5,32,2048]{2,1,0:T(8,128)(2,1)S(1)}, bf16[5,32,2048]{2,1,0:T(8,128)(2,1)S(1)}, u32[]{:S(2)}, u32[]{:S(2)}) collective-permute-start(bf16[5,32,2048]{2,1,0:T(8,128)(2,1)S(1)} %bitcast_dynamic-update-slice_fusion.refs_0_), channel_id=1, source_target_pairs={{0,24},{8,0},{16,8},{24,16},{1,25},{9,1},{17,9},{25,17},{2,26},{10... | collective-permute-start | bytes 1966088 | tf_op jit(solution)/shard_map/ppermute | solution.py:183
  23.4 10.9 %collective-permute-start.3 = (bf16[32,2048]{1,0:T(8,128)(2,1)S(1)}, bf16[32,2048]{1,0:T(8,128)(2,1)}, u32[]{:S(2)}, u32[]{:S(2)}) collective-permute-start(bf16[32,2048]{1,0:T(8,128)(2,1)S(1)} %collective-permute-done.2), channel_id=1, source_target_pairs={{0,64},{64,128},{128,192},{192,32},{32,96},{96,160},{160,224},{224... | collective-permute-start | bytes 393224 | tf_op jit(solution)/shard_map/ppermute | solution.py:217
  31.2 7.8 %collective-permute-start.10 = (bf16[32,2,16,128]{3,2,1,0:T(8,128)(2,1)S(1)}, bf16[32,2,16,128]{3,2,1,0:T(8,128)(2,1)S(1)}, u32[]{:S(2)}, u32[]{:S(2)}) collective-permute-start(bf16[32,2,16,128]{3,2,1,0:T(8,128)(2,1)S(1)} %all-to-all-done), channel_id=1, source_target_pairs={{0,4},{2,6},{4,0},{6,2},{1,5},{3,7},{5,1},{7,3},{8,12},{10,14},{12... | collective-permute-start | bytes 786440 | tf_op jit(solution)/shard_map/ppermute | solution.py:216
  34.0 7.1 %collective-permute-start.11 = (bf16[32,2,16,128]{3,2,1,0:T(8,128)(2,1)S(1)}, bf16[32,2,16,128]{3,2,1,0:T(8,128)(2,1)S(1)}, u32[]{:S(2)}, u32[]{:S(2)}) collective-permute-start(bf16[32,2,16,128]{3,2,1,0:T(8,128)(2,1)S(1)} %all-to-all-done), channel_id=1, source_target_pairs={{0,2},{2,4},{4,6},{6,0},{1,3},{3,5},{5,7},{7,1},{8,10},{10,12},{12... | collective-permute-start | bytes 786440 | tf_op jit(solution)/shard_map/ppermute | solution.py:216
  34.3 10.8 %collective-permute-start.9 = (bf16[32,2,16,128]{3,2,1,0:T(8,128)(2,1)S(1)}, bf16[32,2,16,128]{3,2,1,0:T(8,128)(2,1)S(1)}, u32[]{:S(2)}, u32[]{:S(2)}) collective-permute-start(bf16[32,2,16,128]{3,2,1,0:T(8,128)(2,1)S(1)} %all-to-all-done), channel_id=1, source_target_pairs={{0,6},{2,0},{4,2},{6,4},{1,7},{3,1},{5,3},{7,5},{8,14},{10,8},{12,... | collective-permute-start | bytes 786440 | tf_op jit(solution)/shard_map/ppermute | solution.py:216
  39.0 10.3 %collective-permute-start.5 = (bf16[32,2048]{1,0:T(8,128)(2,1)S(1)}, bf16[32,2048]{1,0:T(8,128)(2,1)S(1)}, u32[]{:S(2)}, u32[]{:S(2)}) collective-permute-start(bf16[32,2048]{1,0:T(8,128)(2,1)S(1)} %collective-permute-done.4), channel_id=1, source_target_pairs={{0,224},{64,0},{128,64},{192,128},{32,192},{96,32},{160,96},{224,1... | collective-permute-start | bytes 393224 | tf_op jit(solution)/shard_map/ppermute | solution.py:217
  41.1 8.9 %collective-permute-start.6 = (bf16[32,2048]{1,0:T(8,128)(2,1)}, bf16[32,2048]{1,0:T(8,128)(2,1)S(1)}, u32[]{:S(2)}, u32[]{:S(2)}) collective-permute-start(bf16[32,2048]{1,0:T(8,128)(2,1)} %collective-permute-done.3), channel_id=1, source_target_pairs={{0,64},{64,128},{128,192},{192,32},{32,96},{96,160},{160,224},{224... | collective-permute-start | bytes 393224 | tf_op jit(solution)/shard_map/ppermute | solution.py:219
  45.1 0.8 copy-start
  46.1 11.3 %collective-permute-start.14 = (bf16[4,32,2,16,128]{4,3,2,1,0:T(8,128)(2,1)S(1)}, bf16[4,32,2,16,128]{4,3,2,1,0:T(8,128)(2,1)S(1)}, u32[]{:S(2)}, u32[]{:S(2)}) collective-permute-start(bf16[4,32,2,16,128]{4,3,2,1,0:T(8,128)(2,1)S(1)} %pad_maximum_fusion.refs_9_.refs_13_), channel_id=1, source_target_pairs={{0,1},{1,0},{2,3},{3,2},{4,5},{5,4},{6,7},{7,6},{8,9},{9,8},{10,11... | collective-permute-start | bytes 3145736 | tf_op jit(solution)/shard_map/ppermute | solution.py:223
  50.7 13.4 %collective-permute-start.7 = (bf16[3,32,2048]{2,1,0:T(8,128)(2,1)}, bf16[3,32,2048]{2,1,0:T(8,128)(2,1)}, u32[]{:S(2)}, u32[]{:S(2)}) collective-permute-start(bf16[3,32,2048]{2,1,0:T(8,128)(2,1)} %bitcast_dynamic-update-slice_fusion.5.refs_3_), channel_id=1, source_target_pairs={{0,8},{8,16},{16,24},{24,0},{1,9},{9,17},{17,25},{25,1},{2,10},{10... | collective-permute-start | bytes 1179656 | tf_op jit(solution)/shard_map/ppermute | solution.py:183
  50.8 13.2 %collective-permute-start.8 = (bf16[3,32,2048]{2,1,0:T(8,128)(2,1)}, bf16[3,32,2048]{2,1,0:T(8,128)(2,1)}, u32[]{:S(2)}, u32[]{:S(2)}) collective-permute-start(bf16[3,32,2048]{2,1,0:T(8,128)(2,1)} %bitcast_dynamic-update-slice_fusion.5.refs_3_), channel_id=1, source_target_pairs={{0,24},{8,0},{16,8},{24,16},{1,25},{9,1},{17,9},{25,17},{2,26},{10... | collective-permute-start | bytes 1179656 | tf_op jit(solution)/shard_map/ppermute | solution.py:183
  53.5 19.5 %copy-start.4 = (s32[6]{0:T(128)}, s32[6]{0:T(128)S(1)}, u32[]{:S(2)}) copy-start(s32[6]{0:T(128)S(1)} %stack.51.meta) | copy-start | bytes 76
  53.5 4.1 %copy-start.1 = (bf16[5,32,2048]{2,1,0:T(8,128)(2,1)S(1)}, bf16[5,32,2048]{2,1,0:T(8,128)(2,1)}, u32[]{:S(2)}) copy-start(bf16[5,32,2048]{2,1,0:T(8,128)(2,1)} %copy-done) | copy-start | bytes 1966084
  53.5 14.1 %collective-permute-start.15 = (bf16[3,32,2048]{2,1,0:T(8,128)(2,1)S(1)}, bf16[3,32,2048]{2,1,0:T(8,128)(2,1)S(1)}, u32[]{:S(2)}, u32[]{:S(2)}) collective-permute-start(bf16[3,32,2048]{2,1,0:T(8,128)(2,1)S(1)} %slice.30), channel_id=1, source_target_pairs={{0,8},{8,16},{16,24},{24,0},{1,9},{9,17},{17,25},{25,1},{2,10},{10... | collective-permute-start | bytes 1179656 | tf_op jit(solution)/shard_map/ppermute | solution.py:187
  54.7 12.9 %collective-permute-start.16 = (bf16[2,32,2048]{2,1,0:T(8,128)(2,1)S(1)}, bf16[2,32,2048]{2,1,0:T(8,128)(2,1)S(1)}, u32[]{:S(2)}, u32[]{:S(2)}) collective-permute-start(bf16[2,32,2048]{2,1,0:T(8,128)(2,1)S(1)} %slice.31), channel_id=1, source_target_pairs={{0,24},{8,0},{16,8},{24,16},{1,25},{9,1},{17,9},{25,17},{2,26},{10... | collective-permute-start | bytes 786440 | tf_op jit(solution)/shard_map/ppermute | solution.py:188
  57.3 1.7 %copy-start.3 = (bf16[2048,512]{1,0:T(8,128)(2,1)S(1)}, bf16[2048,512]{1,0:T(8,128)(2,1)}, u32[]{:S(2)}) copy-start(bf16[2048,512]{1,0:T(8,128)(2,1)} %refs_8_.1) | copy-start | bytes 6291460
  65.1 7.9 %collective-permute-start.18 = (bf16[2,32,2048]{2,1,0:T(8,128)(2,1)S(1)}, bf16[2,32,2048]{2,1,0:T(8,128)(2,1)S(1)}, u32[]{:S(2)}, u32[]{:S(2)}) collective-permute-start(bf16[2,32,2048]{2,1,0:T(8,128)(2,1)S(1)} %slice.33), channel_id=1, source_target_pairs={{0,24},{8,0},{16,8},{24,16},{1,25},{9,1},{17,9},{25,17},{2,26},{10... | collective-permute-start | bytes 786440 | tf_op jit(solution)/shard_map/ppermute | solution.py:188
  66.1 6.9 %collective-permute-start.17 = (bf16[1,32,2048]{2,1,0:T(8,128)(2,1)S(1)}, bf16[1,32,2048]{2,1,0:T(8,128)(2,1)S(1)}, u32[]{:S(2)}, u32[]{:S(2)}) collective-permute-start(bf16[1,32,2048]{2,1,0:T(8,128)(2,1)S(1)} %slice.32), channel_id=1, source_target_pairs={{0,8},{8,16},{16,24},{24,0},{1,9},{9,17},{17,25},{25,1},{2,10},{10... | collective-permute-start | bytes 393224 | tf_op jit(solution)/shard_map/ppermute | solution.py:187
  77.0 7.2 %copy-start.2 = (f32[4,512,128]{2,1,0:T(8,128)}, f32[4,512,128]{2,1,0:T(8,128)S(1)}, u32[]{:S(2)}) copy-start(f32[4,512,128]{2,1,0:T(8,128)S(1)} %get-tuple-element.45.p0) | copy-start | bytes 3145732
  77.1 7.1 %collective-permute-start.19 = (f32[4,512,128]{2,1,0:T(8,128)S(1)}, f32[4,512,128]{2,1,0:T(8,128)S(1)}, u32[]{:S(2)}, u32[]{:S(2)}) collective-permute-start(f32[4,512,128]{2,1,0:T(8,128)S(1)} %get-tuple-element.46), channel_id=1, source_target_pairs={{0,1},{1,0},{2,3},{3,2},{4,5},{5,4},{6,7},{7,6},{8,9},{9,8},{10,11... | collective-permute-start | bytes 3145736 | tf_op jit(solution)/shard_map/ppermute | solution.py:231
  84.2 14.8 %copy-start.5 = (f32[4,512,128]{2,1,0:T(8,128)}, f32[4,512,128]{2,1,0:T(8,128)S(1)}, u32[]{:S(2)}) copy-start(f32[4,512,128]{2,1,0:T(8,128)S(1)} %collective-permute-done.19.p1) | copy-start | bytes 3145732
  84.3 8.8 %collective-permute-start.20 = (f32[512,128]{1,0:T(8,128)S(1)}, f32[512,128]{1,0:T(8,128)S(1)}, u32[]{:S(2)}, u32[]{:S(2)}) collective-permute-start(f32[512,128]{1,0:T(8,128)S(1)} %get-tuple-element.49), channel_id=1, source_target_pairs={{0,2},{2,4},{4,6},{6,0},{1,3},{3,5},{5,7},{7,1},{8,10},{10,12},{12... | collective-permute-start | bytes 786440 | tf_op jit(solution)/shard_map/ppermute | solution.py:234
  85.7 13.3 %collective-permute-start.21 = (f32[512,128]{1,0:T(8,128)S(1)}, f32[512,128]{1,0:T(8,128)S(1)}, u32[]{:S(2)}, u32[]{:S(2)}) collective-permute-start(f32[512,128]{1,0:T(8,128)S(1)} %get-tuple-element.48), channel_id=1, source_target_pairs={{0,4},{2,6},{4,0},{6,2},{1,5},{3,7},{5,1},{7,3},{8,12},{10,14},{12... | collective-permute-start | bytes 786440 | tf_op jit(solution)/shard_map/ppermute | solution.py:234
  87.4 11.7 %collective-permute-start.22 = (f32[512,128]{1,0:T(8,128)S(1)}, f32[512,128]{1,0:T(8,128)S(1)}, u32[]{:S(2)}, u32[]{:S(2)}) collective-permute-start(f32[512,128]{1,0:T(8,128)S(1)} %get-tuple-element.47), channel_id=1, source_target_pairs={{0,6},{2,0},{4,2},{6,4},{1,7},{3,1},{5,3},{7,5},{8,14},{10,8},{12,... | collective-permute-start | bytes 786440 | tf_op jit(solution)/shard_map/ppermute | solution.py:234
  93.1 6.0 %copy-start.6 = (f32[512,128]{1,0:T(8,128)}, f32[512,128]{1,0:T(8,128)S(1)}, u32[]{:S(2)}) copy-start(f32[512,128]{1,0:T(8,128)S(1)} %collective-permute-done.20.p2) | copy-start | bytes 786436
  (2 other events, 1.5 us)
